TPU v7x, 32 devices: a whole 2x2x4 slice. The times are simulated.
32 devices in a mesh: dp: 8 (over z, x), seq: 4 (over y, core).
Axes of the slice: x: 2, y: 2, z: 4, core: 2. Of those that a mesh axis runs over, the one named last changes fastest.
Arguments:
- hidden_in: bfloat16 [8192, 2048], P(('dp', 'seq')), may hold values from -6 to 6
- cotangent: bfloat16 [8192, 2048], P(('dp', 'seq')), may hold values from -6 to 6
- gain_attn: bfloat16 [2048], P('dp'), may hold values from 0.099609375 to 1.8984375
- w_query: bfloat16 [2048, 2048], P('dp'), may hold values from -0.125 to 0.125
- w_key: bfloat16 [2048, 256], P('dp'), may hold values from -0.125 to 0.125
- w_value: bfloat16 [2048, 256], P('dp'), may hold values from -0.125 to 0.125
- w_out: bfloat16 [2048, 2048], P(None, 'dp'), may hold values from -0.5 to 0.5
- gain_mlp: bfloat16 [2048], P('dp'), may hold values from 0.099609375 to 1.8984375
- w_gate: bfloat16 [2048, 5632], P('dp'), may hold values from -0.125 to 0.125
- w_up: bfloat16 [2048, 5632], P('dp'), may hold values from -0.125 to 0.125
- w_down: bfloat16 [5632, 2048], P(None, 'dp'), may hold values from -0.15625 to 0.15625
- doc_lengths: int32 [8, 6], P('dp'), may hold values from 0 to 1024, as said below
- valid_count: int32 [8], P('dp'), may hold values from 512 to 1024, as said below
Outputs:
- hidden_out: bfloat16 [8192, 2048], P(('dp', 'seq'))
- grad_in: bfloat16 [8192, 2048], P(('dp', 'seq'))
- grad_gain_attn: float32 [2048], P('dp')
- grad_query: float32 [2048, 2048], P('dp')
- grad_key: float32 [2048, 256], P('dp')
- grad_value: float32 [2048, 256], P('dp')
- grad_out: float32 [2048, 2048], P(None, 'dp')
- grad_gain_mlp: float32 [2048], P('dp')
- grad_gate: float32 [2048, 5632], P('dp')
- grad_up: float32 [2048, 5632], P('dp')
- grad_down: float32 [5632, 2048], P(None, 'dp')
Inputs may be any that keep to these rules, and one draw needn't show every extreme that they name: `valid_count`: in every draw at least one pack has no padding. `doc_lengths`: the 6 lengths of a pack add up to 1024; a pack is either 6 documents of one token or more, or one whole document of 1024 tokens followed by empty slots, and every draw has at least one whole pack.
All inputs are finite; a program needn't handle non-finite values.
Results may differ from a plain program's by a relative error of at most 0.02.
Values may be sent and summed in bfloat16 or wider, within the bound.
No kernel may reach another device: no remote copies, remote signals or barrier semaphores. Data moves between devices by JAX's collectives and lax.ppermute only.
A program may use at most 384 MiB of HBM per device.

v0:
```python
import jax
import jax.numpy as jnp
from jax import lax
from jax.sharding import PartitionSpec as P

HEADS = 32
HD = 64
KVH = 4


epsilon = 1e-05


def doc_layout(lengths, pack_size):
    doc_ends = jnp.cumsum(lengths)
    doc_starts = doc_ends - lengths
    places = jnp.arange(pack_size, dtype=jnp.int32)
    segment = jnp.sum((places[:, None] >= doc_ends[None, :]).astype(jnp.int32), axis=1)
    doc_first = jnp.max(
        jnp.where(places[:, None] >= doc_starts[None, :], doc_starts[None, :], 0), axis=1
    )
    return (segment, places - doc_first)


def rotary_tables(positions):
    half_dim = HD // 2
    frequency = 10000.0 ** (-2.0 * jnp.arange(half_dim, dtype=jnp.float32) / HD)
    angle_table = positions.astype(jnp.float32)[:, None] * frequency[None, :]
    return (jnp.cos(angle_table), jnp.sin(angle_table))


def rotate(values, cosine, sine_part, head_count):
    row_count = values.shape[0]
    shaped = values.reshape(row_count, head_count, -1)
    half_dim = shaped.shape[2] // 2
    first_half = shaped[:, :, :half_dim]
    second = shaped[:, :, half_dim:]
    cos_rows = cosine[:, None, :]
    sin_rows = sine_part[:, None, :]
    turned = jnp.concatenate(
        [first_half * cos_rows - second * sin_rows, second * cos_rows + first_half * sin_rows],
        axis=2,
    )
    return turned.reshape(row_count, -1)


def mask_block(begin_row, block_rows, segment, live_count):
    key_ids = jnp.arange(segment.shape[0], dtype=jnp.int32)
    row_ids = begin_row + jnp.arange(block_rows, dtype=jnp.int32)
    row_seg = lax.dynamic_slice_in_dim(segment, begin_row, block_rows)
    same_doc = row_seg[:, None] == segment[None, :]
    causal = key_ids[None, :] <= row_ids[:, None]
    not_padded = (key_ids[None, :] < live_count) | (key_ids[None, :] == row_ids[:, None])
    return same_doc & causal & not_padded


def forward_dot(left_side, right_side):
    return jnp.dot(left_side, right_side, preferred_element_type=jnp.float32)


def cross(left_side, right_side):
    return lax.dot_general(
        left_side, right_side, (((0,), (0,)), ((), ())), preferred_element_type=jnp.float32
    )


def against(left_side, right_side):
    return lax.dot_general(
        left_side, right_side, (((1,), (1,)), ((), ())), preferred_element_type=jnp.float32
    )


def rms_back(grad_normed, values, inverse, gain_vec):
    scaled = grad_normed * gain_vec
    return inverse * (
        scaled - values * inverse * inverse * jnp.mean(scaled * values, axis=1, keepdims=True)
    )


def split_heads(head_query, head_key, head_value):
    pack_size = head_query.shape[0]
    kv_local = head_key.shape[1] // HD
    groups = HEADS // KVH
    return (
        head_query.reshape(pack_size, kv_local, groups, HD),
        head_key.reshape(pack_size, kv_local, HD),
        head_value.reshape(pack_size, kv_local, HD),
    )


def masked_scores(query_block, key3, begin_row, block_rows, segment, live_count):
    scores = jnp.einsum(
        "bkgd,tkd->kgbt", query_block, key3, preferred_element_type=jnp.float32
    ) * HD ** (-0.5)
    permit = mask_block(begin_row, block_rows, segment, live_count)
    return jnp.where(permit[None, None], scores, -1e30)


def attention_forward(query4, key3, value3, segment, live_count, block_rows):
    pack_size = query4.shape[0]

    def attend(begin_row):
        query_block = lax.dynamic_slice_in_dim(query4, begin_row, block_rows, 0)
        scores = masked_scores(query_block, key3, begin_row, block_rows, segment, live_count)
        row_peak = jnp.max(scores, axis=-1, keepdims=True)
        exponent = jnp.exp(scores - row_peak)
        row_total = jnp.sum(exponent, axis=-1, keepdims=True)
        weights = (exponent / row_total).astype(jnp.bfloat16)
        mixed = jnp.einsum("kgbt,tkd->bkgd", weights, value3, preferred_element_type=jnp.float32)
        return (mixed.reshape(block_rows, -1).astype(jnp.bfloat16), row_peak + jnp.log(row_total))

    block_starts = jnp.arange(pack_size // block_rows, dtype=jnp.int32) * block_rows
    mixed_blocks, log_totals = lax.map(attend, block_starts)
    return (mixed_blocks.reshape(pack_size, -1), log_totals, block_starts)


def attention_backward(
    query4, key3, value3, grad4, block_starts, log_totals, segment, live_count, block_rows
):
    pack_size = query4.shape[0]
    score_scale = HD ** (-0.5)

    def attend_back(running, block_item):
        begin_row, log_total = block_item
        key_acc, value_acc = running
        query_block = lax.dynamic_slice_in_dim(query4, begin_row, block_rows, 0)
        grad_block = lax.dynamic_slice_in_dim(grad4, begin_row, block_rows, 0)
        scores = masked_scores(query_block, key3, begin_row, block_rows, segment, live_count)
        probs = jnp.exp(scores - log_total)
        weights = probs.astype(jnp.bfloat16)
        grad_probs = jnp.einsum(
            "bkgd,tkd->kgbt", grad_block, value3, preferred_element_type=jnp.float32
        )
        inner_sum = jnp.sum(probs * grad_probs, axis=-1, keepdims=True)
        grad_scores = (probs * (grad_probs - inner_sum)).astype(jnp.bfloat16)
        grad_query_block = (
            jnp.einsum("kgbt,tkd->bkgd", grad_scores, key3, preferred_element_type=jnp.float32)
            * score_scale
        )
        key_acc = (
            key_acc
            + jnp.einsum(
                "kgbt,bkgd->tkd", grad_scores, query_block, preferred_element_type=jnp.float32
            )
            * score_scale
        )
        value_acc = value_acc + jnp.einsum(
            "kgbt,bkgd->tkd", weights, grad_block, preferred_element_type=jnp.float32
        )
        return ((key_acc, value_acc), grad_query_block.reshape(block_rows, -1).astype(jnp.bfloat16))

    zero_acc = jnp.zeros(key3.shape, jnp.float32)
    (key_acc, value_acc), grad_query_blocks = lax.scan(
        attend_back, (zero_acc, zero_acc), (block_starts, log_totals)
    )
    grad_q_heads = grad_query_blocks.reshape(pack_size, -1)
    return (
        grad_q_heads,
        key_acc.reshape(pack_size, -1).astype(jnp.bfloat16),
        value_acc.reshape(pack_size, -1).astype(jnp.bfloat16),
    )


def on_device(
    hidden_in,
    cotangent,
    gain_attn,
    w_query,
    w_key,
    w_value,
    w_out,
    gain_mlp,
    w_gate,
    w_up,
    w_down,
    doc_lengths,
    valid_count,
):
    seq_count = lax.axis_size("seq")
    seq_place = lax.axis_index("seq")
    tok_rows = hidden_in.shape[0]
    pack_size = tok_rows * seq_count
    block_rows = min(512, pack_size)
    live_count = valid_count[0]
    segment, positions = doc_layout(doc_lengths[0], pack_size)
    inputs = hidden_in.astype(jnp.float32)
    inverse_one = lax.rsqrt(jnp.mean(inputs * inputs, axis=1, keepdims=True) + epsilon)
    local_pos = lax.dynamic_slice_in_dim(positions, seq_place * tok_rows, tok_rows)
    cosine, sine_part = rotary_tables(local_pos)
    gain_one, query_w, key_w, value_w, out_w = (
        lax.all_gather(gain_attn, "dp", axis=0, tiled=True),
        lax.all_gather(w_query, "dp", axis=0, tiled=True),
        lax.all_gather(w_key, "dp", axis=0, tiled=True),
        lax.all_gather(w_value, "dp", axis=0, tiled=True),
        lax.all_gather(w_out, "dp", axis=1, tiled=True),
    )
    gain_one = gain_one.astype(jnp.float32)
    normed_one = (inputs * inverse_one * gain_one).astype(jnp.bfloat16)
    queries = rotate(forward_dot(normed_one, query_w), cosine, sine_part, HEADS).astype(
        jnp.bfloat16
    )
    keys_rot = rotate(forward_dot(normed_one, key_w), cosine, sine_part, KVH).astype(jnp.bfloat16)
    values = forward_dot(normed_one, value_w).astype(jnp.bfloat16)
    head_query, head_key, head_value = (
        lax.all_to_all(queries, "seq", split_axis=1, concat_axis=0, tiled=True),
        lax.all_to_all(keys_rot, "seq", split_axis=1, concat_axis=0, tiled=True),
        lax.all_to_all(values, "seq", split_axis=1, concat_axis=0, tiled=True),
    )
    query4, key3, value3 = split_heads(head_query, head_key, head_value)
    mixed_heads, log_totals, block_starts = attention_forward(
        query4, key3, value3, segment, live_count, block_rows
    )
    mixed_tok = lax.all_to_all(mixed_heads, "seq", split_axis=0, concat_axis=1, tiled=True)
    hidden = inputs + forward_dot(mixed_tok, out_w)
    gain_two, gate_w, up_w, down_w = (
        lax.all_gather(gain_mlp, "dp", axis=0, tiled=True),
        lax.all_gather(w_gate, "dp", axis=0, tiled=True),
        lax.all_gather(w_up, "dp", axis=0, tiled=True),
        lax.all_gather(w_down, "dp", axis=1, tiled=True),
    )
    gain_two = gain_two.astype(jnp.float32)
    inverse_two = lax.rsqrt(jnp.mean(hidden * hidden, axis=1, keepdims=True) + epsilon)
    normed_two = (hidden * inverse_two * gain_two).astype(jnp.bfloat16)
    gate_pre = forward_dot(normed_two, gate_w)
    up_pre = forward_dot(normed_two, up_w)
    sigmoid_gate = jax.nn.sigmoid(gate_pre)
    active = gate_pre * sigmoid_gate
    hidden_act = (active * up_pre).astype(jnp.bfloat16)
    result = (hidden + forward_dot(hidden_act, down_w)).astype(jnp.bfloat16)
    grad_act = against(cotangent, down_w)
    grad_up_pre = (grad_act * active).astype(jnp.bfloat16)
    grad_gate_pre = (
        grad_act * up_pre * sigmoid_gate * (1.0 + gate_pre * (1.0 - sigmoid_gate))
    ).astype(jnp.bfloat16)
    grad_normed_two = against(grad_gate_pre, gate_w) + against(grad_up_pre, up_w)
    term_gain_two = jnp.sum(grad_normed_two * hidden * inverse_two, axis=0)
    mlp_terms = (
        lax.psum_scatter(
            term_gain_two.astype(jnp.bfloat16), "dp", scatter_dimension=0, tiled=True
        ).astype(jnp.float32),
        lax.psum_scatter(
            cross(normed_two, grad_gate_pre).astype(jnp.bfloat16),
            "dp",
            scatter_dimension=0,
            tiled=True,
        ).astype(jnp.float32),
        lax.psum_scatter(
            cross(normed_two, grad_up_pre).astype(jnp.bfloat16),
            "dp",
            scatter_dimension=0,
            tiled=True,
        ).astype(jnp.float32),
        lax.psum_scatter(
            cross(hidden_act, cotangent).astype(jnp.bfloat16), "dp", scatter_dimension=1, tiled=True
        ).astype(jnp.float32),
    )
    grad_gain_mlp, grad_gate, grad_up, grad_down = (
        lax.psum(mlp_terms[0].astype(jnp.bfloat16), "seq").astype(jnp.float32),
        lax.psum(mlp_terms[1].astype(jnp.bfloat16), "seq").astype(jnp.float32),
        lax.psum(mlp_terms[2].astype(jnp.bfloat16), "seq").astype(jnp.float32),
        lax.psum(mlp_terms[3].astype(jnp.bfloat16), "seq").astype(jnp.float32),
    )
    grad_hidden = cotangent.astype(jnp.float32) + rms_back(
        grad_normed_two, hidden, inverse_two, gain_two
    )
    grad_branch = grad_hidden.astype(jnp.bfloat16)
    term_out = cross(mixed_tok, grad_branch)
    grad_mixed = against(grad_branch, out_w).astype(jnp.bfloat16)
    grad_heads = lax.all_to_all(grad_mixed, "seq", split_axis=1, concat_axis=0, tiled=True)
    grad4 = grad_heads.reshape(query4.shape)
    grad_q_heads, grad_k_heads, grad_v_heads = attention_backward(
        query4, key3, value3, grad4, block_starts, log_totals, segment, live_count, block_rows
    )
    grad_q_tok, grad_k_tok, grad_v_tok = (
        lax.all_to_all(grad_q_heads, "seq", split_axis=0, concat_axis=1, tiled=True),
        lax.all_to_all(grad_k_heads, "seq", split_axis=0, concat_axis=1, tiled=True),
        lax.all_to_all(grad_v_heads, "seq", split_axis=0, concat_axis=1, tiled=True),
    )
    grad_q_pre = rotate(grad_q_tok.astype(jnp.float32), cosine, -sine_part, HEADS).astype(
        jnp.bfloat16
    )
    grad_k_pre = rotate(grad_k_tok.astype(jnp.float32), cosine, -sine_part, KVH).astype(
        jnp.bfloat16
    )
    grad_normed_one = (
        against(grad_q_pre, query_w) + against(grad_k_pre, key_w) + against(grad_v_tok, value_w)
    )
    term_gain_one = jnp.sum(grad_normed_one * inputs * inverse_one, axis=0)
    attn_terms = (
        lax.psum_scatter(
            term_gain_one.astype(jnp.bfloat16), "dp", scatter_dimension=0, tiled=True
        ).astype(jnp.float32),
        lax.psum_scatter(
            cross(normed_one, grad_q_pre).astype(jnp.bfloat16),
            "dp",
            scatter_dimension=0,
            tiled=True,
        ).astype(jnp.float32),
        lax.psum_scatter(
            cross(normed_one, grad_k_pre).astype(jnp.bfloat16),
            "dp",
            scatter_dimension=0,
            tiled=True,
        ).astype(jnp.float32),
        lax.psum_scatter(
            cross(normed_one, grad_v_tok).astype(jnp.bfloat16),
            "dp",
            scatter_dimension=0,
            tiled=True,
        ).astype(jnp.float32),
        lax.psum_scatter(
            term_out.astype(jnp.bfloat16), "dp", scatter_dimension=1, tiled=True
        ).astype(jnp.float32),
    )
    grad_gain_attn, grad_query, grad_key, grad_value, grad_out = (
        lax.psum(attn_terms[0].astype(jnp.bfloat16), "seq").astype(jnp.float32),
        lax.psum(attn_terms[1].astype(jnp.bfloat16), "seq").astype(jnp.float32),
        lax.psum(attn_terms[2].astype(jnp.bfloat16), "seq").astype(jnp.float32),
        lax.psum(attn_terms[3].astype(jnp.bfloat16), "seq").astype(jnp.float32),
        lax.psum(attn_terms[4].astype(jnp.bfloat16), "seq").astype(jnp.float32),
    )
    grad_input = (grad_hidden + rms_back(grad_normed_one, inputs, inverse_one, gain_one)).astype(
        jnp.bfloat16
    )
    return (
        result,
        grad_input,
        grad_gain_attn,
        grad_query,
        grad_key,
        grad_value,
        grad_out,
        grad_gain_mlp,
        grad_gate,
        grad_up,
        grad_down,
    )


def solution(mesh):
    return jax.shard_map(
        on_device,
        mesh=mesh,
        in_specs=(
            P(("dp", "seq"), None),
            P(("dp", "seq"), None),
            P("dp"),
            P("dp", None),
            P("dp", None),
            P("dp", None),
            P(None, "dp"),
            P("dp"),
            P("dp", None),
            P("dp", None),
            P(None, "dp"),
            P("dp", None),
            P("dp"),
        ),
        out_specs=(
            P(("dp", "seq"), None),
            P(("dp", "seq"), None),
            P("dp"),
            P("dp", None),
            P("dp", None),
            P("dp", None),
            P(None, "dp"),
            P("dp"),
            P("dp", None),
            P("dp", None),
            P(None, "dp"),
        ),
        check_vma=False,
    )
```

profile of v0, /device:TPU:0, one launch (start us, length us, event | category | flops | bytes accessed | tf_op | source)
XLA Modules:
  0.0 3653.1 jit_solution(11690651880786060198)
XLA Ops:
  11.9 22.2 all-gather
  35.7 17.3 all-gather.12.cloned.1.call-done
  58.9 35.1 all-gather.14.cloned.1.call-done
  96.6 123.3 %all-gather.10.cloned.1.call-done = bf16[2048,2048]{1,0:T(8,128)(2,1)} async-done(((bf16[256,2048]{1,0:T(8,128)(2,1)}), bf16[2048,2048]{1,0:T(8,128)(2,1)}) %all-gather.10.cloned.1.call-update) | async-done | bytes 8388624 | tf_op jit(solution)/shard_map/all_gather | solution.py:192
  219.9 6.8 fusion.80
  240.6 12.7 all-to-all-done
  255.0 40.3 %while.27 = (s32[]{:T(128)}, bf16[2,512,512]{2,1,0:T(8,128)(2,1)S(1)}, f32[2,1,8,512,1]{3,2,4,1,0:T(8,128)}, s32[2]{0:T(128)}, s32[1024]{0:T(1024)S(1)}, /*index...) while((s32[]{:T(128)}, ...), condition=%wide.region_7.8_spmd, body=%wide.region_4.7_spmd.sunk | while | flops 1127478784 | bytes 55984320 | solution.py:113
  299.8 18.3 all-gather.1
  320.6 25.0 all-gather.16.cloned.1.call-done
  345.6 5.8 multiply_reduce_fusion.2
  353.0 433.3 %all-gather.18.cloned.1.call-done = bf16[2048,5632]{1,0:T(8,128)(2,1)} async-done(((bf16[256,5632]{1,0:T(8,128)(2,1)}), bf16[2048,5632]{1,0:T(8,128)(2,1)}) %all-gather.18.cloned.1.call-update) | async-done | bytes 23068688 | tf_op jit(solution)/shard_map/all_gather | solution.py:217
  786.4 13.3 fusion.82
  799.6 429.2 %all-gather.20.cloned.1.call-done = bf16[2048,5632]{1,0:T(8,128)(2,1)} async-done(((bf16[256,5632]{1,0:T(8,128)(2,1)}), bf16[2048,5632]{1,0:T(8,128)(2,1)}) %all-gather.20.cloned.1.call-update) | async-done | bytes 23068688 | tf_op jit(solution)/shard_map/all_gather | solution.py:218
  1228.9 13.2 fusion.83
  1242.1 430.7 %all-gather.22.cloned.1.call-done = bf16[5632,2048]{1,0:T(8,128)(2,1)} async-done(((bf16[5632,256]{1,0:T(8,128)(2,1)}), bf16[5632,2048]{1,0:T(8,128)(2,1)}) %all-gather.22.cloned.1.call-update) | async-done | bytes 23068688 | tf_op jit(solution)/shard_map/all_gather | solution.py:219
  1672.8 25.8 multiply_convert_fusion
  1698.5 12.9 fusion.84
  1711.4 13.8 multiply_reduce_fusion
  1727.8 6.5 convolution_convert_fusion.7
  1739.0 14.4 all-to-all-done.4
  1756.8 99.3 %while.28 = (s32[]{:T(128)}, f32[1024,1,64]{0,2,1:T(8,128)}, f32[1024,1,64]{0,2,1:T(8,128)}, bf16[2,512,512]{2,1,0:T(8,128)(2,1)}, s32[2]{0:T(128)}, /*index=5*/...) while((s32[]{:T(128)}, f32[1024,1,64]{0,2,1:T(8,128)}, ...), condition=%wide.region_12.13_spmd.clone, body=%wide.region_10.12_spmd.clone.sunk | while | flops 2726098432 | bytes 172982736 | solution.py:153
  1768.0 10.8 fusion.159
  1778.7 9.3 fusion.160
  1788.0 5.9 fusion.161
  1793.9 7.6 fusion.162
  1817.6 10.8 fusion.159
  1828.4 9.3 fusion.160
  1837.7 5.9 fusion.161
  1843.6 7.6 fusion.162
  1857.2 7.0 all_to_all.116
  1868.3 7.4 all_to_all.117
  1877.4 6.8 convolution_convert_fusion.3
  1884.3 18.0 all_to_all.118
  1909.7 5.8 convolution_convert_fusion.4
  1915.5 12.7 convolution_convert_fusion.2
  1928.3 13.1 convolution_convert_fusion.1
  1941.4 12.7 convolution_convert_fusion
  1954.2 43.4 %reduce-scatter.12.cloned.1.call-done = bf16[256,256]{1,0:T(8,128)(2,1)} async-done(((bf16[2048,256]{1,0:T(8,128)(2,1)}), bf16[256,256]{1,0:T(8,128)(2,1)}) %reduce-scatter.12.cloned.1.call-update) | async-done | bytes 131088 | tf_op jit(solution)/shard_map/reduce_scatter | solution.py:305
  1997.6 151.9 %reduce-scatter.14.cloned.1.call-done = bf16[2048,256]{1,0:T(8,128)(2,1)} async-done(((bf16[2048,2048]{1,0:T(8,128)(2,1)}), bf16[2048,256]{1,0:T(8,128)(2,1)}) %reduce-scatter.14.cloned.1.call-update) | async-done | bytes 1048592 | tf_op jit(solution)/shard_map/reduce_scatter | solution.py:311
  2149.5 152.1 %reduce-scatter.8.cloned.1.call-done = bf16[256,2048]{1,0:T(8,128)(2,1)} async-done(((bf16[2048,2048]{1,0:T(8,128)(2,1)}), bf16[256,2048]{1,0:T(8,128)(2,1)}) %reduce-scatter.8.cloned.1.call-update) | async-done | bytes 1048592 | tf_op jit(solution)/shard_map/reduce_scatter | solution.py:293
  2301.7 376.4 %reduce-scatter.16.cloned.1.call-done = bf16[256,5632]{1,0:T(8,128)(2,1)} async-done(((bf16[2048,5632]{1,0:T(8,128)(2,1)}), bf16[256,5632]{1,0:T(8,128)(2,1)}) %reduce-scatter.16.cloned.1.call-update) | async-done | bytes 2883600 | tf_op jit(solution)/shard_map/reduce_scatter | solution.py:241
  2678.1 376.6 %reduce-scatter.18.cloned.1.call-done = bf16[256,5632]{1,0:T(8,128)(2,1)} async-done(((bf16[2048,5632]{1,0:T(8,128)(2,1)}), bf16[256,5632]{1,0:T(8,128)(2,1)}) %reduce-scatter.18.cloned.1.call-update) | async-done | bytes 2883600 | tf_op jit(solution)/shard_map/reduce_scatter | solution.py:247
  3054.6 376.6 %reduce-scatter.20.cloned.1.call-done = bf16[5632,256]{1,0:T(8,128)(2,1)} async-done(((bf16[5632,2048]{1,0:T(8,128)(2,1)}), bf16[5632,256]{1,0:T(8,128)(2,1)}) %reduce-scatter.20.cloned.1.call-update) | async-done | bytes 2883600 | tf_op jit(solution)/shard_map/reduce_scatter | solution.py:253
  3433.2 14.3 fusion.57
  3447.5 6.0 fusion.85
  3457.1 19.6 all-reduce.2
  3476.8 6.5 all-reduce.3
  3487.7 143.4 %all-reduce.7.cloned.1.call-done = (bf16[256,2048]{1,0:T(8,128)(2,1)}, bf16[256,256]{1,0:T(8,128)(2,1)}, bf16[256,256]{1,0:T(8,128)(2,1)}, bf16[2048,256]{1,0:T(...) async-done(((bf16[256,2048]{1,0:T(8,128)(2,1)}, bf16[256,256]{1,0:T(8,128)(2,1)}, bf16[256,256]{1,0:T(8,128)(2,1)}, ...) | async-done | bytes 11010064 | tf_op jit(solution)/shard_map/psum | solution.py:317
  (258 shorter events, 152.6 us)
Async XLA Ops:
  7.2 45.8 %all-gather.12.cloned.1.call-start = ((), (), s32[]{:S(2)}) async-start(), calls=%async_computation.16 | async-start | bytes 1179648 | tf_op jit(solution)/shard_map/all_gather | solution.py:193
  7.9 86.2 %all-gather.14.cloned.1.call-start = ((), (), s32[]{:S(2)}) async-start(), calls=%async_computation.17 | async-start | bytes 1179648 | tf_op jit(solution)/shard_map/all_gather | solution.py:194
  8.7 211.3 %all-gather.10.cloned.1.call-start = ((), (), s32[]{:S(2)}) async-start(), calls=%async_computation.15 | async-start | bytes 9437184 | tf_op jit(solution)/shard_map/all_gather | solution.py:192
  9.4 336.2 %all-gather.16.cloned.1.call-start = ((), (), s32[]{:S(2)}) async-start(), calls=%async_computation.18 | async-start | bytes 9437184 | tf_op jit(solution)/shard_map/all_gather | solution.py:195
  10.0 776.4 %all-gather.18.cloned.1.call-start = ((), (), s32[]{:S(2)}) async-start(), calls=%async_computation.19 | async-start | bytes 25952256 | tf_op jit(solution)/shard_map/all_gather | solution.py:217
  10.6 23.6 copy-start.40
  10.6 24.0 copy-start.1
  10.6 1218.3 %all-gather.20.cloned.1.call-start = ((), (), s32[]{:S(2)}) async-start(), calls=%async_computation.20 | async-start | bytes 25952256 | tf_op jit(solution)/shard_map/all_gather | solution.py:218
  11.2 1661.6 %all-gather.22.cloned.1.call-start = ((), (), s32[]{:S(2)}) async-start(), calls=%async_computation.21 | async-start | bytes 25952256 | tf_op jit(solution)/shard_map/all_gather | solution.py:219
  34.2 185.7 %copy-start.32 = (f32[8,1,256]{2,1,0:T(1,128)}, f32[8,1,256]{2,1,0:T(1,128)S(1)}, u32[]{:S(2)}) copy-start(f32[8,1,256]{2,1,0:T(1,128)S(1)} %convert_element_type.268) | copy-start | bytes 24580
  34.9 185.0 %copy-start.36 = (f32[256]{0:T(256)}, f32[256]{0:T(256)S(1)}, u32[]{:S(2)}) copy-start(f32[256]{0:T(256)S(1)} %add_rsqrt_fusion.1) | copy-start | bytes 3076
  35.7 191.1 %copy-start.27 = (f32[256,32]{0,1:T(8,128)}, f32[256,32]{0,1:T(8,128)S(1)}, u32[]{:S(2)}) copy-start(f32[256,32]{0,1:T(8,128)S(1)} %get-tuple-element.253) | copy-start | bytes 98308
  55.6 171.5 %all-to-all-start.1 = ((bf16[256,4,64]{0,2,1:T(8,128)(2,1)}), bf16[256,4,64]{0,2,1:T(8,128)(2,1)S(1)}, u32[]{:S(2)}, u32[]{:S(2)}) async-start(bf16[256,4,64]{0,2,1:T(8,128)(2,1)} %pad_maximum_fusion.2), calls=%async_computation.1 | async-start | bytes 262144 | tf_op jit(solution)/shard_map/all_to_all | solution.py:206
  227.1 7.9 all-to-all-start.2
  235.1 18.2 all-to-all-start
  255.0 44.8 %copy-start.41 = (bf16[256]{0:T(256)(128)(2,1)S(1)}, bf16[256]{0:T(256)(128)(2,1)}, u32[]{:S(2)}) copy-start(bf16[256]{0:T(256)(128)(2,1)} %param.24) | copy-start | bytes 1540
  295.3 22.8 copy-start.13
  295.3 50.3 %copy-start.2 = (bf16[256,2048]{1,0:T(8,128)(2,1)S(1)}, bf16[256,2048]{1,0:T(8,128)(2,1)}, u32[]{:S(2)}) copy-start(bf16[256,2048]{1,0:T(8,128)(2,1)} %param.17) | copy-start | bytes 3145732
  296.3 21.8 all-to-all-start.3
  320.6 30.8 copy-start.8
  353.0 875.9 %copy-start.9 = (bf16[256,2048]{1,0:T(8,128)(2,1)}, bf16[256,2048]{1,0:T(8,128)(2,1)S(1)}, u32[]{:S(2)}) copy-start(bf16[256,2048]{1,0:T(8,128)(2,1)S(1)} %multiply_convert_fusion.3) | copy-start | bytes 3145732
  799.6 873.1 %copy-start.14 = (bf16[256,2048]{1,0:T(8,128)(2,1)S(1)}, bf16[256,2048]{1,0:T(8,128)(2,1)}, u32[]{:S(2)}) copy-start(bf16[256,2048]{1,0:T(8,128)(2,1)} %param.18) | copy-start | bytes 3145732
  1698.5 12.9 copy-start.7
  1727.8 6.5 copy-start.4
  1735.4 18.0 all-to-all-start.4
  1738.9 215.3 %reduce-scatter.10.cloned.1.call-start = ((), (), s32[]{:S(2)}) async-start(), calls=%async_computation.23 | async-start | bytes 1179648 | tf_op jit(solution)/shard_map/reduce_scatter | solution.py:299
  1756.8 108.4 %copy-start.33 = (f32[8,1,256]{2,1,0:T(1,128)S(1)}, f32[8,1,256]{2,1,0:T(1,128)}, u32[]{:S(2)}) copy-start(f32[8,1,256]{2,1,0:T(1,128)} %copy-done.32) | copy-start | bytes 24580
  1788.0 5.9 copy-start
  1788.0 5.9 copy-start.10
  1788.0 13.5 slice-start
  1793.9 7.6 slice-start.1
  1837.7 5.9 copy-start.10
  1837.7 13.5 slice-start
  1843.5 7.6 slice-start.1
  1856.1 12.0 copy-start.12
  1864.3 11.4 copy-start.3
  1864.3 11.4 copy-start.37
  1868.1 9.3 copy-start.5
  1868.1 129.5 %reduce-scatter.12.cloned.1.call-start = ((), (), s32[]{:S(2)}) async-start(), calls=%async_computation.24 | async-start | bytes 1179648 | tf_op jit(solution)/shard_map/reduce_scatter | solution.py:305
  1877.3 272.2 %reduce-scatter.14.cloned.1.call-start = ((), (), s32[]{:S(2)}) async-start(), calls=%async_computation.25 | async-start | bytes 9437184 | tf_op jit(solution)/shard_map/reduce_scatter | solution.py:311
  1884.2 417.5 %reduce-scatter.8.cloned.1.call-start = ((), (), s32[]{:S(2)}) async-start(), calls=%async_computation.22 | async-start | bytes 9437184 | tf_op jit(solution)/shard_map/reduce_scatter | solution.py:293
  1915.5 762.6 %reduce-scatter.16.cloned.1.call-start = ((), (), s32[]{:S(2)}) async-start(), calls=%async_computation.26 | async-start | bytes 25952256 | tf_op jit(solution)/shard_map/reduce_scatter | solution.py:241
  1928.2 1126.4 %reduce-scatter.18.cloned.1.call-start = ((), (), s32[]{:S(2)}) async-start(), calls=%async_computation.27 | async-start | bytes 25952256 | tf_op jit(solution)/shard_map/reduce_scatter | solution.py:247
  1941.4 1489.9 %reduce-scatter.20.cloned.1.call-start = ((), (), s32[]{:S(2)}) async-start(), calls=%async_computation.28 | async-start | bytes 25952256 | tf_op jit(solution)/shard_map/reduce_scatter | solution.py:253
  1954.2 1676.9 %all-reduce.7.cloned.1.call-start = ((), (), s32[]{:S(2)}) async-start(), calls=%async_computation.29 | async-start | bytes 22020096 | tf_op jit(solution)/shard_map/psum | solution.py:317
  3433.2 14.4 copy-start.20
  3447.5 6.0 copy-start.25
  3447.5 6.0 copy-start.30
  (24 other events, 64.8 us)
Sparse Core Ops, SparseCore 0:
  10.1 42.8 all-gather.11
  55.1 38.8 all-gather.13
  96.2 123.6 all-gather.9
  221.8 123.7 all-gather.15
  347.0 439.3 all-gather.17
  787.7 441.0 all-gather.19
  1230.3 442.3 all-gather.21
  1868.2 62.5 reduce-scatter.9
  1935.2 62.3 reduce-scatter.11
  2001.1 148.3 reduce-scatter.13
  2153.6 148.0 reduce-scatter.7
  2305.4 372.6 reduce-scatter.15
  2681.9 372.6 reduce-scatter.17
  3058.4 372.8 reduce-scatter.19
  3434.4 196.6 all-reduce.6
where the time goes:
time: 3660 us; the launch traced here: 3650 us
  waiting for transfers between devices  3150 us (86%)
  matrix products  263 us (7%)
  blocking collectives  99 us (3%)
  other arithmetic  71 us (2%)
    all_gather x1, waiting for transfers between devices, on_device(): lax.all_gather(w_gate, 'dp', axis=0, tiled=True)  433 us
    all_gather x1, waiting for transfers between devices, on_device(): lax.all_gather(w_down, 'dp', axis=1, tiled=True)  431 us
    all_gather x1, waiting for transfers between devices, on_device(): lax.all_gather(w_up, 'dp', axis=0, tiled=True)  429 us
    reduce_scatter x1, waiting for transfers between devices, on_device(): lax.psum_scatter(cross(hidden_act, cotangent).astype(jnp.bfloat16), 'dp',...  377 us
    reduce_scatter x1, waiting for transfers between devices, on_device(): lax.psum_scatter(cross(normed_two, grad_up_pre).astype(jnp.bfloat16), 'dp...  377 us
    reduce_scatter x1, waiting for transfers between devices, on_device(): lax.psum_scatter(cross(normed_two, grad_gate_pre).astype(jnp.bfloat16), '...  376 us
    reduce_scatter x1, waiting for transfers between devices, on_device(): lax.psum_scatter(cross(normed_one, grad_q_pre).astype(jnp.bfloat16), 'dp'...  152 us
    reduce_scatter x1, waiting for transfers between devices, on_device(): lax.psum_scatter(term_out.astype(jnp.bfloat16), 'dp', scatter_dimension=1...  152 us
  transfers between devices with their start and end apart: 20, of which 17 were waited for; matrix products, arithmetic and copies ran while one was open for 5% of the time, Pallas kernels for 0%

commit v1 on v0

v1 whole, which is shorter than its diff:
```python
import jax
import jax.numpy as jnp
from jax import lax
from jax.sharding import PartitionSpec as P

HEADS = 32
HD = 64
KVH = 4
EPS = 1e-05
BF = jnp.bfloat16
F32 = jnp.float32


class Ring:
    def __init__(self, size):
        self.size = size
        self.half = size // 2
        self.order = list(range(0, size, 2)) + list(range(size - 1, 0, -2))
        place = [0] * size
        for position, device in enumerate(self.order):
            place[device] = position
        self.place = place
        walk = [(self.order[i], self.order[(i + 1) % size]) for i in range(size)]
        self.up = walk
        self.down = [(b, a) for a, b in walk]
        self.steps = (
            [-t for t in range(self.half)] + [t for t in range(1, self.half)] + [self.half]
        )

    def slot_owners(self):
        mine = jnp.asarray(self.place, jnp.int32)[lax.axis_index("dp")]
        wanted = (mine + jnp.asarray(self.steps, jnp.int32)) % self.size
        return jnp.asarray(self.order, jnp.int32)[wanted]

    def owner_slots(self):
        mine = jnp.asarray(self.place, jnp.int32)[lax.axis_index("dp")]
        slot_of_step = [0] * self.size
        for slot, step in enumerate(self.steps):
            slot_of_step[step % self.size] = slot
        step = (jnp.asarray(self.place, jnp.int32) - mine) % self.size
        return jnp.asarray(slot_of_step, jnp.int32)[step]

    def gather(self, block):
        rows = block.shape[0] // 2
        from_down, from_up = [block], [block]
        for _ in range(1, self.half):
            from_down.append(lax.ppermute(from_down[-1], "dp", self.up))
            from_up.append(lax.ppermute(from_up[-1], "dp", self.down))
        last = jnp.concatenate(
            [
                lax.ppermute(from_down[-1][:rows], "dp", self.up),
                lax.ppermute(from_up[-1][rows:], "dp", self.down),
            ],
            axis=0,
        )
        return from_down + from_up[1:] + [last]

    def scatter(self, term, add_to):
        far = term(self.size - 1)
        rows = far.shape[0] // 2
        going_up, going_down = far[:rows].astype(BF), far[rows:].astype(BF)
        for step in range(self.half - 1, 0, -1):
            going_up = lax.ppermute(going_up, "dp", self.up)
            going_down = lax.ppermute(going_down, "dp", self.down)
            up_term = term(self.half - 1 + step)
            down_term = term(step)
            if step == self.half - 1:
                going_up = jnp.concatenate(
                    [(up_term[:rows] + going_up).astype(BF), up_term[rows:].astype(BF)], axis=0
                )
                going_down = jnp.concatenate(
                    [down_term[:rows].astype(BF), (down_term[rows:] + going_down).astype(BF)], axis=0
                )
            else:
                going_up = (up_term + going_up).astype(BF)
                going_down = (down_term + going_down).astype(BF)
        going_up = lax.ppermute(going_up, "dp", self.up)
        going_down = lax.ppermute(going_down, "dp", self.down)
        return term(0) + going_up + going_down


def swap(block, distance, size):
    return lax.ppermute(block, "seq", [(i, i ^ distance) for i in range(size)])


def seq_gather(block, size):
    blocks = [block]
    distance = size // 2
    held = {0: block}
    while distance >= 1:
        for offset in list(held):
            held[offset ^ distance] = swap(held[offset], distance, size)
        distance //= 2
    blocks = [held[offset] for offset in range(size)]
    return blocks


def seq_scatter(parts, size):
    parts = list(parts)
    distance = 1
    held = {offset: parts[offset] for offset in range(size)}
    while distance < size:
        keep = {}
        for offset in held:
            if offset & distance:
                continue
            got = swap(held[offset | distance].astype(BF), distance, size)
            keep[offset] = held[offset].astype(F32) + got.astype(F32)
        held = keep
        distance *= 2
    return held[0]


def doc_layout(lengths, pack_size):
    doc_ends = jnp.cumsum(lengths)
    doc_starts = doc_ends - lengths
    places = jnp.arange(pack_size, dtype=jnp.int32)
    segment = jnp.sum((places[:, None] >= doc_ends[None, :]).astype(jnp.int32), axis=1)
    doc_first = jnp.max(
        jnp.where(places[:, None] >= doc_starts[None, :], doc_starts[None, :], 0), axis=1
    )
    return (segment, places - doc_first)


def rotary_tables(positions):
    half_dim = HD // 2
    frequency = 10000.0 ** (-2.0 * jnp.arange(half_dim, dtype=F32) / HD)
    angle_table = positions.astype(F32)[:, None] * frequency[None, :]
    return (jnp.cos(angle_table), jnp.sin(angle_table))


def rotate(values, cosine, sine_part):
    row_count = values.shape[0]
    shaped = values.reshape(row_count, -1, HD)
    half_dim = HD // 2
    first_half = shaped[:, :, :half_dim]
    second = shaped[:, :, half_dim:]
    cos_rows = cosine[:, None, :]
    sin_rows = sine_part[:, None, :]
    turned = jnp.concatenate(
        [first_half * cos_rows - second * sin_rows, second * cos_rows + first_half * sin_rows],
        axis=2,
    )
    return turned.reshape(row_count, -1)


def mask_block(begin_row, block_rows, segment, live_count):
    key_ids = jnp.arange(segment.shape[0], dtype=jnp.int32)
    row_ids = begin_row + jnp.arange(block_rows, dtype=jnp.int32)
    row_seg = lax.dynamic_slice_in_dim(segment, begin_row, block_rows)
    same_doc = row_seg[:, None] == segment[None, :]
    causal = key_ids[None, :] <= row_ids[:, None]
    not_padded = (key_ids[None, :] < live_count) | (key_ids[None, :] == row_ids[:, None])
    return same_doc & causal & not_padded


def dot(left_side, right_side):
    return jnp.dot(left_side, right_side, preferred_element_type=F32)


def cross(left_side, right_side):
    return lax.dot_general(
        left_side, right_side, (((0,), (0,)), ((), ())), preferred_element_type=F32
    )


def against(left_side, right_side):
    return lax.dot_general(
        left_side, right_side, (((1,), (1,)), ((), ())), preferred_element_type=F32
    )


def rms_back(grad_normed, values, inverse, gain_vec):
    scaled = grad_normed * gain_vec
    return inverse * (
        scaled - values * inverse * inverse * jnp.mean(scaled * values, axis=1, keepdims=True)
    )


def masked_scores(query_block, key3, begin_row, block_rows, segment, live_count):
    scores = jnp.einsum(
        "bkgd,tkd->kgbt", query_block, key3, preferred_element_type=F32
    ) * HD ** (-0.5)
    permit = mask_block(begin_row, block_rows, segment, live_count)
    return jnp.where(permit[None, None], scores, -1e30)


def attention_forward(query4, key3, value3, segment, live_count, block_rows):
    pack_size = query4.shape[0]

    def attend(begin_row):
        query_block = lax.dynamic_slice_in_dim(query4, begin_row, block_rows, 0)
        scores = masked_scores(query_block, key3, begin_row, block_rows, segment, live_count)
        row_peak = jnp.max(scores, axis=-1, keepdims=True)
        exponent = jnp.exp(scores - row_peak)
        row_total = jnp.sum(exponent, axis=-1, keepdims=True)
        weights = (exponent / row_total).astype(BF)
        mixed = jnp.einsum("kgbt,tkd->bkgd", weights, value3, preferred_element_type=F32)
        return (mixed.reshape(block_rows, -1).astype(BF), row_peak + jnp.log(row_total))

    block_starts = jnp.arange(pack_size // block_rows, dtype=jnp.int32) * block_rows
    mixed_blocks, log_totals = lax.map(attend, block_starts)
    return (mixed_blocks.reshape(pack_size, -1), log_totals, block_starts)


def attention_backward(
    query4, key3, value3, grad4, block_starts, log_totals, segment, live_count, block_rows
):
    pack_size = query4.shape[0]
    score_scale = HD ** (-0.5)

    def attend_back(running, block_item):
        begin_row, log_total = block_item
        key_acc, value_acc = running
        query_block = lax.dynamic_slice_in_dim(query4, begin_row, block_rows, 0)
        grad_block = lax.dynamic_slice_in_dim(grad4, begin_row, block_rows, 0)
        scores = masked_scores(query_block, key3, begin_row, block_rows, segment, live_count)
        probs = jnp.exp(scores - log_total)
        weights = probs.astype(BF)
        grad_probs = jnp.einsum("bkgd,tkd->kgbt", grad_block, value3, preferred_element_type=F32)
        inner_sum = jnp.sum(probs * grad_probs, axis=-1, keepdims=True)
        grad_scores = (probs * (grad_probs - inner_sum)).astype(BF)
        grad_query_block = (
            jnp.einsum("kgbt,tkd->bkgd", grad_scores, key3, preferred_element_type=F32)
            * score_scale
        )
        key_acc = (
            key_acc
            + jnp.einsum("kgbt,bkgd->tkd", grad_scores, query_block, preferred_element_type=F32)
            * score_scale
        )
        value_acc = value_acc + jnp.einsum(
            "kgbt,bkgd->tkd", weights, grad_block, preferred_element_type=F32
        )
        return ((key_acc, value_acc), grad_query_block.reshape(block_rows, -1).astype(BF))

    zero_acc = jnp.zeros(key3.shape, F32)
    (key_acc, value_acc), grad_query_blocks = lax.scan(
        attend_back, (zero_acc, zero_acc), (block_starts, log_totals)
    )
    return (
        grad_query_blocks.reshape(pack_size, -1),
        key_acc.reshape(pack_size, -1).astype(BF),
        value_acc.reshape(pack_size, -1).astype(BF),
    )


def take_blocks(array, order, axis, size):
    width = array.shape[axis] // size
    return jnp.concatenate(
        [lax.dynamic_slice_in_dim(array, order[i] * width, width, axis) for i in range(size)],
        axis=axis,
    )


def layer(
    hidden_in,
    cotangent,
    gain_attn,
    w_query,
    w_key,
    w_value,
    w_out,
    gain_mlp,
    w_gate,
    w_up,
    w_down,
    doc_lengths,
    valid_count,
):
    seq = lax.axis_size("seq")
    n_dp = lax.axis_size("dp")
    here = lax.axis_index("seq")
    ring = Ring(n_dp)
    rows = hidden_in.shape[0]
    pack_size = rows * seq
    width = gain_attn.shape[0]
    model = width * n_dp
    q_cols = w_query.shape[1] // seq
    k_cols = w_key.shape[1] // seq
    ff = w_gate.shape[1] // seq
    block_rows = min(512, pack_size)

    owners = ring.slot_owners()
    slots = ring.owner_slots()
    seq_order = here ^ jnp.arange(seq, dtype=jnp.int32)

    def part(array, axis, cols):
        return lax.dynamic_slice_in_dim(array, here * cols, cols, axis)

    def slot(array, j):
        return lax.slice_in_dim(array, j * width, (j + 1) * width, axis=1)

    gains = jnp.concatenate(
        [gain_attn, gain_mlp, jnp.zeros((q_cols + 2 * k_cols - 2 * width,), BF)]
    )
    head_block = jnp.concatenate(
        [
            jnp.concatenate(
                [part(w_query, 1, q_cols), part(w_key, 1, k_cols), part(w_value, 1, k_cols)], axis=1
            ),
            jnp.broadcast_to(gains[None], (16, gains.shape[0])),
        ],
        axis=0,
    )
    head_blocks = ring.gather(head_block)
    w_heads = jnp.concatenate([b[:width] for b in head_blocks], axis=0)
    gain_one = jnp.concatenate([b[width, :width] for b in head_blocks]).astype(F32)
    gain_two = jnp.concatenate([b[width, width : 2 * width] for b in head_blocks]).astype(F32)
    w_out_all = jnp.concatenate(ring.gather(part(w_out, 0, q_cols)), axis=1)
    my_gate, my_up, my_down = part(w_gate, 1, ff), part(w_up, 1, ff), part(w_down, 0, ff)
    first = (ff // 2 + 127) // 128 * 128
    bounds = [(0, first), (first, ff)]
    w_gate_up, w_down_all = [], []
    for a, b in bounds:
        w_gate_up.append(
            jnp.concatenate(
                ring.gather(jnp.concatenate([my_gate[:, a:b], my_up[:, a:b]], axis=1)), axis=0
            )
        )
        w_down_all.append(jnp.concatenate(ring.gather(my_down[a:b]), axis=1))

    mine = take_blocks(hidden_in, owners, 1, n_dp)
    my_cot = take_blocks(cotangent, owners, 1, n_dp)
    inputs = jnp.concatenate(seq_gather(mine, seq), axis=0).astype(F32)
    cot = jnp.concatenate(seq_gather(my_cot, seq), axis=0)

    live_count = valid_count[0]
    segment, positions = doc_layout(doc_lengths[0], pack_size)
    cosine, sine_part = rotary_tables(take_blocks(positions, seq_order, 0, seq))

    inverse_one = lax.rsqrt(jnp.mean(inputs * inputs, axis=1, keepdims=True) + EPS)
    normed_one = (inputs * inverse_one * gain_one).astype(BF)
    heads_pre = dot(normed_one, w_heads)
    queries = rotate(heads_pre[:, :q_cols], cosine, sine_part).astype(BF)
    keys_rot = rotate(heads_pre[:, q_cols : q_cols + k_cols], cosine, sine_part).astype(BF)
    values = heads_pre[:, q_cols + k_cols :].astype(BF)

    def natural(array):
        return take_blocks(array, seq_order, 0, seq)

    kv_local = k_cols // HD
    query4 = natural(queries).reshape(pack_size, kv_local, -1, HD)
    key3 = natural(keys_rot).reshape(pack_size, kv_local, HD)
    value3 = natural(values).reshape(pack_size, kv_local, HD)
    mixed_nat, log_totals, block_starts = attention_forward(
        query4, key3, value3, segment, live_count, block_rows
    )
    mixed = natural(mixed_nat)

    def token_parts(array):
        return [array[j * rows : (j + 1) * rows] for j in range(seq)]

    branch = dot(mixed, w_out_all)
    my_inputs = mine.astype(F32)
    hidden = my_inputs + seq_scatter(token_parts(branch), seq)
    inverse_two = lax.rsqrt(jnp.mean(hidden * hidden, axis=1, keepdims=True) + EPS)
    my_normed_two = (hidden * inverse_two * gain_two).astype(BF)
    normed_two = jnp.concatenate(seq_gather(my_normed_two, seq), axis=0)

    down = 0.0
    grad_normed = 0.0
    gate_up_sums, down_sums = [], []
    for (a, b), gate_up_w, down_w in zip(bounds, w_gate_up, w_down_all):
        size = b - a
        both = dot(normed_two, gate_up_w)
        gate_pre, up_pre = both[:, :size], both[:, size:]
        sigmoid_gate = jax.nn.sigmoid(gate_pre)
        active = gate_pre * sigmoid_gate
        hidden_act = (active * up_pre).astype(BF)
        grad_act = against(cot, down_w)
        grad_up_pre = (grad_act * active).astype(BF)
        grad_gate_pre = (
            grad_act * up_pre * sigmoid_gate * (1.0 + gate_pre * (1.0 - sigmoid_gate))
        ).astype(BF)
        grad_both = jnp.concatenate([grad_gate_pre, grad_up_pre], axis=1)
        down = down + dot(hidden_act, down_w)
        grad_normed = grad_normed + against(grad_both, gate_up_w)
        gate_up_sums.append(
            ring.scatter(lambda j: cross(slot(normed_two, j), grad_both), None).astype(BF)
        )
        down_sums.append(ring.scatter(lambda j: cross(hidden_act, slot(cot, j)), None).astype(BF))

    result = (hidden + seq_scatter(token_parts(down), seq)).astype(BF)
    grad_normed_two = seq_scatter(token_parts(grad_normed), seq)
    term_gain_two = jnp.sum(grad_normed_two * hidden * inverse_two, axis=0)
    grad_hidden = my_cot.astype(F32) + rms_back(grad_normed_two, hidden, inverse_two, gain_two)
    my_grad_branch = grad_hidden.astype(BF)
    grad_branch = jnp.concatenate(seq_gather(my_grad_branch, seq), axis=0)
    out_sum = ring.scatter(lambda j: cross(mixed, slot(grad_branch, j)), None).astype(BF)
    grad_mixed = against(grad_branch, w_out_all).astype(BF)
    grad4 = natural(grad_mixed).reshape(query4.shape)
    grad_q, grad_k, grad_v = attention_backward(
        query4, key3, value3, grad4, block_starts, log_totals, segment, live_count, block_rows
    )
    grad_q_pre = rotate(natural(grad_q).astype(F32), cosine, -sine_part).astype(BF)
    grad_k_pre = rotate(natural(grad_k).astype(F32), cosine, -sine_part).astype(BF)
    grad_heads = jnp.concatenate([grad_q_pre, grad_k_pre, natural(grad_v)], axis=1)
    grad_normed_one = against(grad_heads, w_heads)
    term_gain_one = jnp.sum(grad_normed_one * inputs * inverse_one, axis=0)

    def head_term(j):
        gain_terms = jnp.concatenate(
            [
                term_gain_one[j * width : (j + 1) * width],
                term_gain_two[j * width : (j + 1) * width],
                jnp.zeros((q_cols + 2 * k_cols - 2 * width,), F32),
            ]
        )
        return jnp.concatenate(
            [
                cross(slot(normed_one, j), grad_heads),
                jnp.broadcast_to(gain_terms[None], (16, gain_terms.shape[0])),
            ],
            axis=0,
        )

    head_sum = ring.scatter(head_term, None).astype(BF)
    grad_input = (
        grad_hidden
        + rms_back(
            seq_scatter(token_parts(grad_normed_one), seq),
            my_inputs,
            inverse_one[:rows],
            gain_one,
        )
    ).astype(BF)

    def whole(array, axis):
        return take_blocks(
            jnp.concatenate(seq_gather(array, seq), axis=axis).astype(F32), seq_order, axis, seq
        )

    gate_sum = jnp.concatenate([g[:, : g.shape[1] // 2] for g in gate_up_sums], axis=1)
    up_sum = jnp.concatenate([g[:, g.shape[1] // 2 :] for g in gate_up_sums], axis=1)
    grad_gate, grad_up = whole(gate_sum, 1), whole(up_sum, 1)
    grad_down = whole(jnp.concatenate(down_sums, axis=0), 0)
    grad_out = whole(out_sum, 0)
    head_sums = seq_gather(head_sum, seq)
    gain_sum = sum(h[width, : 2 * width].astype(F32) for h in head_sums)

    def head_whole(begin, end):
        return take_blocks(
            jnp.concatenate([h[:width, begin:end] for h in head_sums], axis=1).astype(F32),
            seq_order,
            1,
            seq,
        )

    grad_query = head_whole(0, q_cols)
    grad_key = head_whole(q_cols, q_cols + k_cols)
    grad_value = head_whole(q_cols + k_cols, q_cols + 2 * k_cols)

    return (
        take_blocks(result, slots, 1, n_dp),
        take_blocks(grad_input, slots, 1, n_dp),
        gain_sum[:width],
        grad_query,
        grad_key,
        grad_value,
        grad_out,
        gain_sum[width:],
        grad_gate,
        grad_up,
        grad_down,
    )


def solution(mesh):
    return jax.shard_map(
        layer,
        mesh=mesh,
        in_specs=(
            P(("dp", "seq"), None),
            P(("dp", "seq"), None),
            P("dp"),
            P("dp", None),
            P("dp", None),
            P("dp", None),
            P(None, "dp"),
            P("dp"),
            P("dp", None),
            P("dp", None),
            P(None, "dp"),
            P("dp", None),
            P("dp"),
        ),
        out_specs=(
            P(("dp", "seq"), None),
            P(("dp", "seq"), None),
            P("dp"),
            P("dp", None),
            P("dp", None),
            P("dp", None),
            P(None, "dp"),
            P("dp"),
            P("dp", None),
            P("dp", None),
            P(None, "dp"),
        ),
        check_vma=False,
    )
```

time: 3660 us -> 986 us (0.27)
  waiting for transfers between devices: 3150 us -> 332 us
  local copies, waits for them, and re-layouts: 29.2 us -> 150 us
  starting transfers between devices: 18.1 us -> 130 us
  blocking collectives: 99 us -> 0 us
    all_gather x7 -> x0, waiting for transfers between devices: 1490 us -> none  [the longest x1 433 us: on_device(): lax.all_gather(w_gate, 'dp', axis=0, tiled=True)]
    reduce_scatter x7 -> x0, waiting for transfers between devices: 1480 us -> none  [the longest x1 377 us: on_device(): lax.psum_scatter(cross(hidden_act, cotangent).astype(jnp.bfloat16), 'dp',...]
    ppermute x0 -> x135, waiting for transfers between devices: none -> 332 us  [the longest x39 115 us: swap(): return lax.ppermute(block, 'seq', [(i, i ^ distance) for i in range(size)])]
    psum x1 -> x0, waiting for transfers between devices: 143 us -> none  [on_device(): lax.psum(attn_terms[1].astype(jnp.bfloat16), 'seq').astype(jnp.float32)]
    ppermute x0 -> x135, starting transfers between devices: none -> 130 us  [the longest x24 39.1 us: scatter(): going_up = lax.ppermute(going_up, 'dp', self.up)]
    unnamed x81 -> x403, local copies, waits for them, and re-layouts: 6.47 us -> 91.4 us
    all_gather x2 -> x0, blocking collectives: 40.5 us -> none  [the longest x1 22.2 us: on_device(): lax.all_gather(gain_attn, 'dp', axis=0, tiled=True)]
    dot_general x17 -> x16, matrix products: 113 us -> 94.5 us  [the longest x6 43.5 us: dot(): return jnp.dot(left_side, right_side, preferred_element_type=F32)]
  transfers between devices with their start and end apart: 20 -> 135, of which waited for: 17 -> 52; matrix products, arithmetic and copies ran while one was open for 5% -> 39% of each run, Pallas kernels for 0% -> 0%
where the time goes in v1:
time: 986 us; the launch traced here: 975 us
  waiting for transfers between devices  332 us (34%)
  matrix products  228 us (23%)
  local copies, waits for them, and re-layouts  150 us (15%)
  starting transfers between devices  130 us (13%)
  other arithmetic  101 us (10%)
  between operations  25.3 us (3%)
    ppermute x39, waiting for transfers between devices, swap(): return lax.ppermute(block, 'seq', [(i, i ^ distance) for i in range(size)])  115 us
    unnamed x403, local copies, waits for them, and re-layouts  91.4 us
    ppermute x24, waiting for transfers between devices, scatter(): going_up = lax.ppermute(going_up, 'dp', self.up)  61.1 us
    dot_general x48, matrix products, cross(): lax.dot_general(left_side, right_side, (((0,), (0,)), ((), ())), preferre...  59.2 us
    dot_general x6, matrix products, against(): lax.dot_general(left_side, right_side, (((1,), (1,)), ((), ())), preferre...  55.5 us
    ppermute x18, waiting for transfers between devices, gather(): from_down.append(lax.ppermute(from_down[-1], 'dp', self.up))  49.5 us
    dot_general x6, matrix products, dot(): return jnp.dot(left_side, right_side, preferred_element_type=F32)  43.5 us
    ppermute x24, waiting for transfers between devices, scatter(): going_down = lax.ppermute(going_down, 'dp', self.down)  41.5 us
  transfers between devices with their start and end apart: 135, of which 52 were waited for; matrix products, arithmetic and copies ran while one was open for 39% of the time, Pallas kernels for 0%

profile of v1, /device:TPU:0, one launch (start us, length us, event | category | flops | bytes accessed | tf_op | source)
XLA Modules:
  0.0 974.9 jit_solution(8247749254160852445)
XLA Ops:
  83.8 15.4 %collective-permute-done.12 = bf16[512,256]{1,0:T(8,128)(2,1)S(1)} collective-permute-done((bf16[512,256]{1,0:T(8,128)(2,1)}, bf16[512,256]{1,0:T(8,128)(2,1)S(1)}, u32[]{:S(2)}, u32[]{:S(2)}) %collective-permute-start.12) | collective-permute-done | bytes 262176 | tf_op jit(solution)/shard_map/ppermute | solution.py:47
  99.9 6.3 collective-permute-done.50
  112.6 18.0 %collective-permute-done.4 = bf16[272,640]{1,0:T(8,128)(2,1)S(1)} collective-permute-done((bf16[272,640]{1,0:T(8,128)(2,1)}, bf16[272,640]{1,0:T(8,128)(2,1)S(1)}, u32[]{:S(2)}, u32[]{:S(2)}) %collective-permute-start.4) | collective-permute-done | bytes 348192 | tf_op jit(solution)/shard_map/ppermute | solution.py:47
  168.5 10.6 %collective-permute-done.8 = bf16[272,640]{1,0:T(8,128)(2,1)S(1)} collective-permute-done((bf16[272,640]{1,0:T(8,128)(2,1)S(1)}, bf16[272,640]{1,0:T(8,128)(2,1)S(1)}, u32[]{:S(2)}, u32[]{:S(2)}) %collective-permute-start.8) | collective-permute-done | bytes 348192 | tf_op jit(solution)/shard_map/ppermute | solution.py:48
  199.2 6.4 fusion.58
  205.6 6.3 fusion.267
  213.8 37.6 %while.27 = (s32[]{:T(128)}, bf16[2,512,512]{2,1,0:T(8,128)(2,1)S(1)}, f32[2,1,8,512,1]{3,2,4,1,0:T(8,128)}, s32[2]{0:T(128)S(1)}, s32[1024]{0:T(1024)S(1)}, /*i...) while((s32[]{:T(128)}, ...), condition=%wide.region_7.8_spmd, body=%wide.region_4.7_spmd.sunk | while | flops 1127478784 | bytes 55984320 | solution.py:202
  226.5 5.4 fusion.337
  245.1 5.4 fusion.337
  253.8 5.7 fusion.263
  279.0 24.2 %collective-permute-done.40 = bf16[384,256]{1,0:T(8,128)(2,1)} collective-permute-done((bf16[384,256]{1,0:T(8,128)(2,1)S(1)}, bf16[384,256]{1,0:T(8,128)(2,1)}, u32[]{:S(2)}, u32[]{:S(2)}) %collective-permute-start.40) | collective-permute-done | bytes 196640 | tf_op jit(solution)/shard_map/ppermute | solution.py:52
  319.1 9.8 %collective-permute-done.43 = bf16[256,1280]{1,0:T(8,128)(2,1)S(1)} collective-permute-done((bf16[256,1280]{1,0:T(8,128)(2,1)}, bf16[256,1280]{1,0:T(8,128)(2,1)S(1)}, u32[]{:S(2)}, u32[]{:S(2)}) %collective-permute-start.43) | collective-permute-done | bytes 655392 | tf_op jit(solution)/shard_map/ppermute | solution.py:47
  329.2 6.7 collective-permute-done.61
  338.8 8.3 collective-permute-done.29
  349.2 7.3 collective-permute-done.21
  364.8 6.3 collective-permute-done.47
  375.8 9.3 collective-permute-done.23
  390.6 10.4 %fusion.235 = f32[1024,1280]{1,0:T(8,128)} fusion(bf16[2048,1280]{1,0:T(8,128)(2,1)S(1)} %constant_dynamic-update-slice_fusion.33, bf16[256,2048]{1,0:T(8,128)(2,1)S(1)} %collective-permute-done.24, bf16[256,2048]{1,0:T(8,128)(2,1)S(1)} %collective-permute-done.23, bf16[256,2048]{1,0:T(8,128)(2,1)S(1)} %collective-permute-done.22, ...), kind=kOutput, calls=%fused_computation.619 | convolution fusion | flops 5385486336 | bytes 14680064 | tf_op jit(solution)/shard_map/dot_general | solution.py:158
  401.0 10.9 %multiply_convert_fusion.4 = (bf16[1024,640]{1,0:T(8,128)(2,1)S(1)}, bf16[1024,640]{1,0:T(8,128)(2,1)}, bf16[1024,640]{1,0:T(8,128)(2,1)S(1)}) fusion(f32[1024,1280]{1,0:T(8,128)} %fusion.235, bf16[640,2048]{1,0:T(8,128)(2,1)S(1)} %copy-done.112, bf16[256,2048]{1,0:T(8,128)(2,1)S(1)} %collective-permute-done.62, ...), kind=kOutput, calls=%fused_computation.112 | convolution fusion | flops 2710962176 | bytes 15990784 | tf_op jit(solution)/shard_map/dot_general | solution.py:168
  423.5 8.1 fusion.233
  431.6 14.3 %fusion.236 = f32[1024,1536]{1,0:T(8,128)} fusion(bf16[2048,1536]{1,0:T(8,128)(2,1)} %constant_dynamic-update-slice_fusion.17, bf16[256,2048]{1,0:T(8,128)(2,1)S(1)} %collective-permute-done.24, bf16[256,2048]{1,0:T(8,128)(2,1)S(1)} %collective-permute-done.23, bf16[256,2048]{1,0:T(8,128)(2,1)S(1)} %collective-permute-done.22, ...), kind=kOutput, calls=%fused_computation.620 | convolution fusion | flops 6459228160 | bytes 16777216 | tf_op jit(solution)/shard_map/dot_general | solution.py:158
  445.9 12.0 %multiply_convert_fusion.1 = (bf16[1024,768]{1,0:T(8,128)(2,1)}, bf16[1024,768]{1,0:T(8,128)(2,1)}, bf16[1024,768]{1,0:T(8,128)(2,1)S(1)}) fusion(f32[1024,1536]{1,0:T(8,128)} %fusion.236, bf16[768,2048]{1,0:T(8,128)(2,1)S(1)} %copy-done.39, bf16[256,2048]{1,0:T(8,128)(2,1)S(1)} %copy-done.73, bf16[256,2048]{1,0:T(8,128)(2,1)S(1)} %copy-done.69, ...), kind=kOutput, calls=%fused_computation.91 | convolution fusion | flops 3249799168 | bytes 18350080 | tf_op jit(solution)/shard_map/dot_general | solution.py:168
  479.0 13.6 %fusion.264 = (bf16[1024,2048]{1,0:T(8,128)(2,1)}, f32[1024,2048]{1,0:T(8,128)}) fusion(f32[1024,2048]{1,0:T(8,128)} %fusion.233, bf16[2048,1536]{1,0:T(8,128)(2,1)} %constant_dynamic-update-slice_fusion.17, bf16[1024,768]{1,0:T(8,128)(2,1)} %get-tuple-element.252, bf16[1024,768]{1,0:T(8,128)(2,1)} %get-tuple-element.251), kind=kOutput, calls=%fused_computation.648 | convolution fusion | flops 6452936704 | bytes 30408704 | tf_op jit(solution)/shard_map/dot_general | solution.py:168
  528.4 6.5 collective-permute-done.129
  541.5 5.4 collective-permute-done.117
  550.2 13.4 %collective-permute-done.126 = bf16[640,256]{1,0:T(8,128)(2,1)S(1)} collective-permute-done((bf16[640,256]{1,0:T(8,128)(2,1)S(1)}, bf16[640,256]{1,0:T(8,128)(2,1)S(1)}, u32[]{:S(2)}, u32[]{:S(2)}) %collective-permute-start.126) | collective-permute-done | bytes 327712 | tf_op jit(solution)/shard_map/ppermute | solution.py:63
  568.0 4.8 collective-permute-done.118
  582.6 7.9 collective-permute-done.95
  614.4 9.7 collective-permute-done.104
  631.0 9.6 collective-permute-done.96
  647.6 5.8 collective-permute-done.65
  656.9 18.9 %collective-permute-done.59 = bf16[256,2048]{1,0:T(8,128)(2,1)S(1)} collective-permute-done((bf16[256,2048]{1,0:T(8,128)(2,1)S(1)}, bf16[256,2048]{1,0:T(8,128)(2,1)S(1)}, u32[]{:S(2)}, u32[]{:S(2)}) %collective-permute-start.59) | collective-permute-done | bytes 1048608 | tf_op jit(solution)/shard_map/ppermute | solution.py:83
  678.2 5.0 fusion.237
  706.3 9.4 collective-permute-done.67
  715.7 15.6 %collective-permute-done.111 = bf16[256,1408]{1,0:T(8,128)(2,1)} collective-permute-done((bf16[256,1408]{1,0:T(8,128)(2,1)S(1)}, bf16[256,1408]{1,0:T(8,128)(2,1)}, u32[]{:S(2)}, u32[]{:S(2)}) %collective-permute-start.111) | collective-permute-done | bytes 720928 | tf_op jit(solution)/shard_map/ppermute | solution.py:83
  734.4 9.5 collective-permute-done.114
  753.7 5.2 convolution_convert_fusion.2
  761.4 82.3 %while.28 = (s32[]{:T(128)}, f32[1024,1,64]{0,2,1:T(8,128)}, f32[1024,1,64]{0,2,1:T(8,128)}, bf16[2,512,512]{2,1,0:T(8,128)(2,1)}, s32[2]{0:T(128)S(1)}, /*index...) while((s32[]{:T(128)}, f32[1024,1,64]{0,2,1:T(8,128)}, ...), condition=%wide.region_12.13_spmd.clone, body=%wide.region_10.12_spmd.clone.sunk | while | flops 2726098432 | bytes 150438384 | solution.py:238
  771.6 10.8 %fusion.348 = (f32[8,512]{1,0:T(8,128)}, f32[1,8,512,1024]{3,2,1,0:T(8,128)}) fusion(f32[512,8,1024]{2,0,1:T(8,128)S(1)} %fusion.346, f32[8,512]{1,0:T(8,128)} %dynamic-slice_bitcast_fusion.6, bf16[1024,1,64]{0,2,1:T(8,128)(2,1)} %get-tuple-element.652, bf16[1024,1,8,64]{0,3,2,1:T(8,128)(2,1)S(1)} %get-tuple-element.649, s32[]{:T(128)S(6)} %select_n.292, ...), kind=kOutput, calls=%fused_computation.32.clone.1 | convolution fusion | flops 557838336 | bytes 34766852 | tf_op jit(solution)/shard_map/while/body/eval_jaxpr/bkgd,tkd->kgbt/dot_general | solution.py:181
  782.4 6.9 fusion.349
  789.4 7.5 fusion.351
  812.6 10.8 %fusion.348 = (f32[8,512]{1,0:T(8,128)}, f32[1,8,512,1024]{3,2,1,0:T(8,128)}) fusion(f32[512,8,1024]{2,0,1:T(8,128)S(1)} %fusion.346, f32[8,512]{1,0:T(8,128)} %dynamic-slice_bitcast_fusion.6, bf16[1024,1,64]{0,2,1:T(8,128)(2,1)} %get-tuple-element.652, bf16[1024,1,8,64]{0,3,2,1:T(8,128)(2,1)S(1)} %get-tuple-element.649, s32[]{:T(128)S(6)} %select_n.292, ...), kind=kOutput, calls=%fused_computation.32.clone.1 | convolution fusion | flops 557838336 | bytes 34766852 | tf_op jit(solution)/shard_map/while/body/eval_jaxpr/bkgd,tkd->kgbt/dot_general | solution.py:181
  823.4 6.9 fusion.349
  830.4 7.5 fusion.351
  858.2 5.7 fusion.60
  896.9 5.5 collective-permute-done.77
  929.2 6.1 collective-permute-done.92
  941.1 22.5 %collective-permute-done.81 = bf16[272,640]{1,0:T(8,128)(2,1)S(1)} collective-permute-done((bf16[272,640]{1,0:T(8,128)(2,1)S(1)}, bf16[272,640]{1,0:T(8,128)(2,1)S(1)}, u32[]{:S(2)}, u32[]{:S(2)}) %collective-permute-start.81) | collective-permute-done | bytes 348192 | tf_op jit(solution)/shard_map/ppermute | solution.py:83
  (999 shorter events, 504.0 us)
Async XLA Ops:
  4.4 73.8 %collective-permute-start.6 = (bf16[272,640]{1,0:T(8,128)(2,1)}, bf16[272,640]{1,0:T(8,128)(2,1)}, u32[]{:S(2)}, u32[]{:S(2)}) collective-permute-start(bf16[272,640]{1,0:T(8,128)(2,1)} %pad_maximum_fusion.28), channel_id=1, source_target_pairs={{8,0},{16,8},{24,16},{28,24},{20,28},{12,20},{4,12},{0,4},{9,1},{1... | collective-permute-start | bytes 1044488 | tf_op jit(solution)/shard_map/ppermute | solution.py:48
  7.4 66.5 %collective-permute-start.3 = (bf16[272,640]{1,0:T(8,128)(2,1)}, bf16[272,640]{1,0:T(8,128)(2,1)}, u32[]{:S(2)}, u32[]{:S(2)}) collective-permute-start(bf16[272,640]{1,0:T(8,128)(2,1)} %pad_maximum_fusion.28), channel_id=1, source_target_pairs={{0,8},{8,16},{16,24},{24,28},{28,20},{20,12},{12,4},{4,0},{1,9},{9... | collective-permute-start | bytes 1044488 | tf_op jit(solution)/shard_map/ppermute | solution.py:47
  9.2 74.1 %collective-permute-start.14 = (bf16[512,256]{1,0:T(8,128)(2,1)}, bf16[512,256]{1,0:T(8,128)(2,1)}, u32[]{:S(2)}, u32[]{:S(2)}) collective-permute-start(bf16[512,256]{1,0:T(8,128)(2,1)} %get-tuple-element.246), channel_id=1, source_target_pairs={{8,0},{16,8},{24,16},{28,24},{20,28},{12,20},{4,12},{0,4},{9,1},{1... | collective-permute-start | bytes 786440 | tf_op jit(solution)/shard_map/ppermute | solution.py:48
  11.2 56.0 %collective-permute-start.11 = (bf16[512,256]{1,0:T(8,128)(2,1)}, bf16[512,256]{1,0:T(8,128)(2,1)}, u32[]{:S(2)}, u32[]{:S(2)}) collective-permute-start(bf16[512,256]{1,0:T(8,128)(2,1)} %get-tuple-element.246), channel_id=1, source_target_pairs={{0,8},{8,16},{16,24},{24,28},{28,20},{20,12},{12,4},{4,0},{1,9},{9... | collective-permute-start | bytes 786440 | tf_op jit(solution)/shard_map/ppermute | solution.py:47
  13.1 57.4 %collective-permute-start.49 = (bf16[640,256]{1,0:T(8,128)(2,1)}, bf16[640,256]{1,0:T(8,128)(2,1)}, u32[]{:S(2)}, u32[]{:S(2)}) collective-permute-start(bf16[640,256]{1,0:T(8,128)(2,1)} %get-tuple-element.242), channel_id=1, source_target_pairs={{0,8},{8,16},{16,24},{24,28},{28,20},{20,12},{12,4},{4,0},{1,9},{9... | collective-permute-start | bytes 983048 | tf_op jit(solution)/shard_map/ppermute | solution.py:47
  70.5 38.1 %collective-permute-start.41 = (bf16[256,1280]{1,0:T(8,128)(2,1)}, bf16[256,1280]{1,0:T(8,128)(2,1)}, u32[]{:S(2)}, u32[]{:S(2)}) collective-permute-start(bf16[256,1280]{1,0:T(8,128)(2,1)} %get-tuple-element.322), channel_id=1, source_target_pairs={{0,8},{8,16},{16,24},{24,28},{28,20},{20,12},{12,4},{4,0},{1,9},{9... | collective-permute-start | bytes 1966088 | tf_op jit(solution)/shard_map/ppermute | solution.py:47
  80.0 55.9 %collective-permute-start.52 = (bf16[640,256]{1,0:T(8,128)(2,1)}, bf16[640,256]{1,0:T(8,128)(2,1)}, u32[]{:S(2)}, u32[]{:S(2)}) collective-permute-start(bf16[640,256]{1,0:T(8,128)(2,1)} %get-tuple-element.242), channel_id=1, source_target_pairs={{8,0},{16,8},{24,16},{28,24},{20,28},{12,20},{4,12},{0,4},{9,1},{1... | collective-permute-start | bytes 983048 | tf_op jit(solution)/shard_map/ppermute | solution.py:48
  83.4 71.0 %collective-permute-start.25 = (bf16[256,1536]{1,0:T(8,128)(2,1)}, bf16[256,1536]{1,0:T(8,128)(2,1)S(1)}, u32[]{:S(2)}, u32[]{:S(2)}) collective-permute-start(bf16[256,1536]{1,0:T(8,128)(2,1)} %get-tuple-element.314), channel_id=1, source_target_pairs={{0,8},{8,16},{16,24},{24,28},{28,20},{20,12},{12,4},{4,0},{1,9},{9... | collective-permute-start | bytes 2359304 | tf_op jit(solution)/shard_map/ppermute | solution.py:47
  135.9 47.4 %collective-permute-start.1 = (bf16[256,2048]{1,0:T(8,128)(2,1)S(1)}, bf16[256,2048]{1,0:T(8,128)(2,1)S(1)}, u32[]{:S(2)}, u32[]{:S(2)}) collective-permute-start(bf16[256,2048]{1,0:T(8,128)(2,1)S(1)} %constant_dynamic-update-slice_fusion.2), channel_id=1, source_target_pairs={{0,2},{1,3},{2,0},{3,1},{4,6},{5,7},{6,4},{7,5},{8,10},{9,11},{10,... | collective-permute-start | bytes 3145736 | tf_op jit(solution)/shard_map/ppermute | solution.py:83
  159.9 35.0 %collective-permute-start = (bf16[256,2048]{1,0:T(8,128)(2,1)S(1)}, bf16[256,2048]{1,0:T(8,128)(2,1)S(1)}, u32[]{:S(2)}, u32[]{:S(2)}) collective-permute-start(bf16[256,2048]{1,0:T(8,128)(2,1)S(1)} %constant_dynamic-update-slice_fusion.2), channel_id=1, source_target_pairs={{0,1},{1,0},{2,3},{3,2},{4,5},{5,4},{6,7},{7,6},{8,9},{9,8},{10,11... | collective-permute-start | bytes 3145736 | tf_op jit(solution)/shard_map/ppermute | solution.py:83
  159.9 31.2 %collective-permute-start.37 = (bf16[768,256]{1,0:T(8,128)(2,1)}, bf16[768,256]{1,0:T(8,128)(2,1)}, u32[]{:S(2)}, u32[]{:S(2)}) collective-permute-start(bf16[768,256]{1,0:T(8,128)(2,1)} %collective-permute-done.36), channel_id=1, source_target_pairs={{8,0},{16,8},{24,16},{28,24},{20,28},{12,20},{4,12},{0,4},{9,1},{1... | collective-permute-start | bytes 1179656 | tf_op jit(solution)/shard_map/ppermute | solution.py:48
  189.3 75.0 %collective-permute-start.44 = (bf16[256,1280]{1,0:T(8,128)(2,1)}, bf16[256,1280]{1,0:T(8,128)(2,1)}, u32[]{:S(2)}, u32[]{:S(2)}) collective-permute-start(bf16[256,1280]{1,0:T(8,128)(2,1)} %get-tuple-element.322), channel_id=1, source_target_pairs={{8,0},{16,8},{24,16},{28,24},{20,28},{12,20},{4,12},{0,4},{9,1},{1... | collective-permute-start | bytes 1966088 | tf_op jit(solution)/shard_map/ppermute | solution.py:48
  191.1 77.4 %collective-permute-start.35 = (bf16[768,256]{1,0:T(8,128)(2,1)}, bf16[768,256]{1,0:T(8,128)(2,1)}, u32[]{:S(2)}, u32[]{:S(2)}) collective-permute-start(bf16[768,256]{1,0:T(8,128)(2,1)} %copy-done.89), channel_id=1, source_target_pairs={{0,8},{8,16},{16,24},{24,28},{28,20},{20,12},{12,4},{4,0},{1,9},{9... | collective-permute-start | bytes 1179656 | tf_op jit(solution)/shard_map/ppermute | solution.py:47
  192.2 73.6 %collective-permute-start.38 = (bf16[768,256]{1,0:T(8,128)(2,1)}, bf16[768,256]{1,0:T(8,128)(2,1)}, u32[]{:S(2)}, u32[]{:S(2)}) collective-permute-start(bf16[768,256]{1,0:T(8,128)(2,1)} %collective-permute-done.37), channel_id=1, source_target_pairs={{8,0},{16,8},{24,16},{28,24},{20,28},{12,20},{4,12},{0,4},{9,1},{1... | collective-permute-start | bytes 1179656 | tf_op jit(solution)/shard_map/ppermute | solution.py:48
  194.9 64.9 %collective-permute-start.56 = (bf16[320,256]{1,0:T(8,128)(2,1)}, bf16[320,256]{1,0:T(8,128)(2,1)}, u32[]{:S(2)}, u32[]{:S(2)}) collective-permute-start(bf16[320,256]{1,0:T(8,128)(2,1)} %slice.977), channel_id=1, source_target_pairs={{8,0},{16,8},{24,16},{28,24},{20,28},{12,20},{4,12},{0,4},{9,1},{1... | collective-permute-start | bytes 491528 | tf_op jit(solution)/shard_map/ppermute | solution.py:52
  196.8 64.1 %collective-permute-start.55 = (bf16[320,256]{1,0:T(8,128)(2,1)}, bf16[320,256]{1,0:T(8,128)(2,1)}, u32[]{:S(2)}, u32[]{:S(2)}) collective-permute-start(bf16[320,256]{1,0:T(8,128)(2,1)} %slice.976), channel_id=1, source_target_pairs={{0,8},{8,16},{16,24},{24,28},{28,20},{20,12},{12,4},{4,0},{1,9},{9... | collective-permute-start | bytes 491528 | tf_op jit(solution)/shard_map/ppermute | solution.py:51
  260.9 54.2 %collective-permute-start.20 = (bf16[256,2048]{1,0:T(8,128)(2,1)S(1)}, bf16[256,2048]{1,0:T(8,128)(2,1)}, u32[]{:S(2)}, u32[]{:S(2)}) collective-permute-start(bf16[256,2048]{1,0:T(8,128)(2,1)S(1)} %get-tuple-element.278), channel_id=1, source_target_pairs={{0,1},{1,0},{2,3},{3,2},{4,5},{5,4},{6,7},{7,6},{8,9},{9,8},{10,11... | collective-permute-start | bytes 3145736 | tf_op jit(solution)/shard_map/ppermute | solution.py:83
  264.3 53.6 %collective-permute-start.28 = (bf16[256,1536]{1,0:T(8,128)(2,1)}, bf16[256,1536]{1,0:T(8,128)(2,1)}, u32[]{:S(2)}, u32[]{:S(2)}) collective-permute-start(bf16[256,1536]{1,0:T(8,128)(2,1)} %get-tuple-element.314), channel_id=1, source_target_pairs={{8,0},{16,8},{24,16},{28,24},{20,28},{12,20},{4,12},{0,4},{9,1},{1... | collective-permute-start | bytes 2359304 | tf_op jit(solution)/shard_map/ppermute | solution.py:48
  265.8 47.7 %collective-permute-start.45 = (bf16[256,1280]{1,0:T(8,128)(2,1)}, bf16[256,1280]{1,0:T(8,128)(2,1)}, u32[]{:S(2)}, u32[]{:S(2)}) collective-permute-start(bf16[256,1280]{1,0:T(8,128)(2,1)} %collective-permute-done.44), channel_id=1, source_target_pairs={{8,0},{16,8},{24,16},{28,24},{20,28},{12,20},{4,12},{0,4},{9,1},{1... | collective-permute-start | bytes 1966088 | tf_op jit(solution)/shard_map/ppermute | solution.py:48
  268.4 34.7 %collective-permute-start.40 = (bf16[384,256]{1,0:T(8,128)(2,1)S(1)}, bf16[384,256]{1,0:T(8,128)(2,1)}, u32[]{:S(2)}, u32[]{:S(2)}) collective-permute-start(bf16[384,256]{1,0:T(8,128)(2,1)S(1)} %slice.971), channel_id=1, source_target_pairs={{8,0},{16,8},{24,16},{28,24},{20,28},{12,20},{4,12},{0,4},{9,1},{1... | collective-permute-start | bytes 589832 | tf_op jit(solution)/shard_map/ppermute | solution.py:52
  278.5 39.5 %collective-permute-start.26 = (bf16[256,1536]{1,0:T(8,128)(2,1)}, bf16[256,1536]{1,0:T(8,128)(2,1)S(1)}, u32[]{:S(2)}, u32[]{:S(2)}) collective-permute-start(bf16[256,1536]{1,0:T(8,128)(2,1)} %copy-done.77), channel_id=1, source_target_pairs={{0,8},{8,16},{16,24},{24,28},{28,20},{20,12},{12,4},{4,0},{1,9},{9... | collective-permute-start | bytes 2359304 | tf_op jit(solution)/shard_map/ppermute | solution.py:47
  317.9 31.0 %collective-permute-start.19 = (bf16[256,2048]{1,0:T(8,128)(2,1)S(1)}, bf16[256,2048]{1,0:T(8,128)(2,1)S(1)}, u32[]{:S(2)}, u32[]{:S(2)}) collective-permute-start(bf16[256,2048]{1,0:T(8,128)(2,1)S(1)} %get-tuple-element.277), channel_id=1, source_target_pairs={{0,1},{1,0},{2,3},{3,2},{4,5},{5,4},{6,7},{7,6},{8,9},{9,8},{10,11... | collective-permute-start | bytes 3145736 | tf_op jit(solution)/shard_map/ppermute | solution.py:83
  318.0 38.5 %collective-permute-start.21 = (bf16[256,2048]{1,0:T(8,128)(2,1)S(1)}, bf16[256,2048]{1,0:T(8,128)(2,1)S(1)}, u32[]{:S(2)}, u32[]{:S(2)}) collective-permute-start(bf16[256,2048]{1,0:T(8,128)(2,1)S(1)} %fusion.91), channel_id=1, source_target_pairs={{0,2},{1,3},{2,0},{3,1},{4,6},{5,7},{6,4},{7,5},{8,10},{9,11},{10,... | collective-permute-start | bytes 3145736 | tf_op jit(solution)/shard_map/ppermute | solution.py:83
  469.8 41.4 %collective-permute-start.124 = (bf16[320,256]{1,0:T(8,128)(2,1)}, bf16[320,256]{1,0:T(8,128)(2,1)}, u32[]{:S(2)}, u32[]{:S(2)}) collective-permute-start(bf16[320,256]{1,0:T(8,128)(2,1)} %get-tuple-element.334), channel_id=1, source_target_pairs={{0,8},{8,16},{16,24},{24,28},{28,20},{20,12},{12,4},{4,0},{1,9},{9... | collective-permute-start | bytes 491528 | tf_op jit(solution)/shard_map/ppermute | solution.py:63
  471.5 38.3 %collective-permute-start.128 = (bf16[320,256]{1,0:T(8,128)(2,1)}, bf16[320,256]{1,0:T(8,128)(2,1)}, u32[]{:S(2)}, u32[]{:S(2)}) collective-permute-start(bf16[320,256]{1,0:T(8,128)(2,1)} %get-tuple-element.335), channel_id=1, source_target_pairs={{8,0},{16,8},{24,16},{28,24},{20,28},{12,20},{4,12},{0,4},{9,1},{1... | collective-permute-start | bytes 491528 | tf_op jit(solution)/shard_map/ppermute | solution.py:64
  474.7 42.6 %collective-permute-start.102 = (bf16[128,1280]{1,0:T(8,128)(2,1)}, bf16[128,1280]{1,0:T(8,128)(2,1)}, u32[]{:S(2)}, u32[]{:S(2)}) collective-permute-start(bf16[128,1280]{1,0:T(8,128)(2,1)} %get-tuple-element.320), channel_id=1, source_target_pairs={{0,8},{8,16},{16,24},{24,28},{28,20},{20,12},{12,4},{4,0},{1,9},{9... | collective-permute-start | bytes 983048 | tf_op jit(solution)/shard_map/ppermute | solution.py:63
  476.5 42.5 %collective-permute-start.106 = (bf16[128,1280]{1,0:T(8,128)(2,1)}, bf16[128,1280]{1,0:T(8,128)(2,1)}, u32[]{:S(2)}, u32[]{:S(2)}) collective-permute-start(bf16[128,1280]{1,0:T(8,128)(2,1)} %get-tuple-element.321), channel_id=1, source_target_pairs={{8,0},{16,8},{24,16},{28,24},{20,28},{12,20},{4,12},{0,4},{9,1},{1... | collective-permute-start | bytes 983048 | tf_op jit(solution)/shard_map/ppermute | solution.py:64
  516.2 131.3 %collective-permute-start.63 = (bf16[256,2048]{1,0:T(8,128)(2,1)}, bf16[256,2048]{1,0:T(8,128)(2,1)S(1)}, u32[]{:S(2)}, u32[]{:S(2)}) collective-permute-start(bf16[256,2048]{1,0:T(8,128)(2,1)} %get-tuple-element.273), channel_id=1, source_target_pairs={{0,1},{1,0},{2,3},{3,2},{4,5},{5,4},{6,7},{7,6},{8,9},{9,8},{10,11... | collective-permute-start | bytes 3145736 | tf_op jit(solution)/shard_map/ppermute | solution.py:83
  517.4 60.6 %collective-permute-start.64 = (bf16[256,2048]{1,0:T(8,128)(2,1)S(1)}, bf16[256,2048]{1,0:T(8,128)(2,1)S(1)}, u32[]{:S(2)}, u32[]{:S(2)}) collective-permute-start(bf16[256,2048]{1,0:T(8,128)(2,1)S(1)} %get-tuple-element.274), channel_id=1, source_target_pairs={{0,1},{1,0},{2,3},{3,2},{4,5},{5,4},{6,7},{7,6},{8,9},{9,8},{10,11... | collective-permute-start | bytes 3145736 | tf_op jit(solution)/shard_map/ppermute | solution.py:83
  536.9 30.1 %collective-permute-start.103 = (bf16[256,1280]{1,0:T(8,128)(2,1)S(1)}, bf16[256,1280]{1,0:T(8,128)(2,1)S(1)}, u32[]{:S(2)}, u32[]{:S(2)}) collective-permute-start(bf16[256,1280]{1,0:T(8,128)(2,1)S(1)} %pad_maximum_fusion.23), channel_id=1, source_target_pairs={{0,8},{8,16},{16,24},{24,28},{28,20},{20,12},{12,4},{4,0},{1,9},{9... | collective-permute-start | bytes 1966088 | tf_op jit(solution)/shard_map/ppermute | solution.py:63
  577.9 32.0 %collective-permute-start.131 = (bf16[640,256]{1,0:T(8,128)(2,1)S(1)}, bf16[640,256]{1,0:T(8,128)(2,1)S(1)}, u32[]{:S(2)}, u32[]{:S(2)}) collective-permute-start(bf16[640,256]{1,0:T(8,128)(2,1)S(1)} %fusion.104), channel_id=1, source_target_pairs={{8,0},{16,8},{24,16},{28,24},{20,28},{12,20},{4,12},{0,4},{9,1},{1... | collective-permute-start | bytes 983048 | tf_op jit(solution)/shard_map/ppermute | solution.py:78
  606.5 49.7 %collective-permute-start.57 = (bf16[256,2048]{1,0:T(8,128)(2,1)S(1)}, bf16[256,2048]{1,0:T(8,128)(2,1)S(1)}, u32[]{:S(2)}, u32[]{:S(2)}) collective-permute-start(bf16[256,2048]{1,0:T(8,128)(2,1)S(1)} %get-tuple-element.275), channel_id=1, source_target_pairs={{0,1},{1,0},{2,3},{3,2},{4,5},{5,4},{6,7},{7,6},{8,9},{9,8},{10,11... | collective-permute-start | bytes 3145736 | tf_op jit(solution)/shard_map/ppermute | solution.py:83
  610.0 30.6 %collective-permute-start.96 = (bf16[256,1536]{1,0:T(8,128)(2,1)S(1)}, bf16[256,1536]{1,0:T(8,128)(2,1)S(1)}, u32[]{:S(2)}, u32[]{:S(2)}) collective-permute-start(bf16[256,1536]{1,0:T(8,128)(2,1)S(1)} %fusion.66), channel_id=1, source_target_pairs={{0,8},{8,16},{16,24},{24,28},{28,20},{20,12},{12,4},{4,0},{1,9},{9... | collective-permute-start | bytes 2359304 | tf_op jit(solution)/shard_map/ppermute | solution.py:63
  640.6 35.3 %collective-permute-start.59 = (bf16[256,2048]{1,0:T(8,128)(2,1)S(1)}, bf16[256,2048]{1,0:T(8,128)(2,1)S(1)}, u32[]{:S(2)}, u32[]{:S(2)}) collective-permute-start(bf16[256,2048]{1,0:T(8,128)(2,1)S(1)} %fusion.87), channel_id=1, source_target_pairs={{0,2},{1,3},{2,0},{3,1},{4,6},{5,7},{6,4},{7,5},{8,10},{9,11},{10,... | collective-permute-start | bytes 3145736 | tf_op jit(solution)/shard_map/ppermute | solution.py:83
  644.5 45.1 %collective-permute-start.133 = (bf16[1408,256]{1,0:T(8,128)(2,1)}, bf16[1408,256]{1,0:T(8,128)(2,1)}, u32[]{:S(2)}, u32[]{:S(2)}) collective-permute-start(bf16[1408,256]{1,0:T(8,128)(2,1)} %pad_maximum_fusion.21), channel_id=1, source_target_pairs={{0,2},{1,3},{2,0},{3,1},{4,6},{5,7},{6,4},{7,5},{8,10},{9,11},{10,... | collective-permute-start | bytes 2162696 | tf_op jit(solution)/shard_map/ppermute | solution.py:83
  647.6 36.6 %collective-permute-start.132 = (bf16[1408,256]{1,0:T(8,128)(2,1)}, bf16[1408,256]{1,0:T(8,128)(2,1)}, u32[]{:S(2)}, u32[]{:S(2)}) collective-permute-start(bf16[1408,256]{1,0:T(8,128)(2,1)} %pad_maximum_fusion.21), channel_id=1, source_target_pairs={{0,1},{1,0},{2,3},{3,2},{4,5},{5,4},{6,7},{7,6},{8,9},{9,8},{10,11... | collective-permute-start | bytes 2162696 | tf_op jit(solution)/shard_map/ppermute | solution.py:83
  653.4 40.0 %collective-permute-start.105 = (bf16[256,1280]{1,0:T(8,128)(2,1)S(1)}, bf16[256,1280]{1,0:T(8,128)(2,1)}, u32[]{:S(2)}, u32[]{:S(2)}) collective-permute-start(bf16[256,1280]{1,0:T(8,128)(2,1)S(1)} %fusion.71), channel_id=1, source_target_pairs={{0,8},{8,16},{16,24},{24,28},{28,20},{20,12},{12,4},{4,0},{1,9},{9... | collective-permute-start | bytes 1966088 | tf_op jit(solution)/shard_map/ppermute | solution.py:77
  656.3 37.1 %collective-permute-start.109 = (bf16[256,1280]{1,0:T(8,128)(2,1)}, bf16[256,1280]{1,0:T(8,128)(2,1)}, u32[]{:S(2)}, u32[]{:S(2)}) collective-permute-start(bf16[256,1280]{1,0:T(8,128)(2,1)} %fusion.73), channel_id=1, source_target_pairs={{8,0},{16,8},{24,16},{28,24},{20,28},{12,20},{4,12},{0,4},{9,1},{1... | collective-permute-start | bytes 1966088 | tf_op jit(solution)/shard_map/ppermute | solution.py:78
  693.3 53.8 %collective-permute-start.66 = (bf16[256,2048]{1,0:T(8,128)(2,1)S(1)}, bf16[256,2048]{1,0:T(8,128)(2,1)S(1)}, u32[]{:S(2)}, u32[]{:S(2)}) collective-permute-start(bf16[256,2048]{1,0:T(8,128)(2,1)S(1)} %copy-done.38), channel_id=1, source_target_pairs={{0,1},{1,0},{2,3},{3,2},{4,5},{5,4},{6,7},{7,6},{8,9},{9,8},{10,11... | collective-permute-start | bytes 3145736 | tf_op jit(solution)/shard_map/ppermute | solution.py:83
  703.0 28.2 %collective-permute-start.111 = (bf16[256,1408]{1,0:T(8,128)(2,1)S(1)}, bf16[256,1408]{1,0:T(8,128)(2,1)}, u32[]{:S(2)}, u32[]{:S(2)}) collective-permute-start(bf16[256,1408]{1,0:T(8,128)(2,1)S(1)} %pad_maximum_fusion.19), channel_id=1, source_target_pairs={{0,2},{1,3},{2,0},{3,1},{4,6},{5,7},{6,4},{7,5},{8,10},{9,11},{10,... | collective-permute-start | bytes 2162696 | tf_op jit(solution)/shard_map/ppermute | solution.py:83
  704.7 29.3 %collective-permute-start.110 = (bf16[256,1408]{1,0:T(8,128)(2,1)S(1)}, bf16[256,1408]{1,0:T(8,128)(2,1)S(1)}, u32[]{:S(2)}, u32[]{:S(2)}) collective-permute-start(bf16[256,1408]{1,0:T(8,128)(2,1)S(1)} %pad_maximum_fusion.19), channel_id=1, source_target_pairs={{0,1},{1,0},{2,3},{3,2},{4,5},{5,4},{6,7},{7,6},{8,9},{9,8},{10,11... | collective-permute-start | bytes 2162696 | tf_op jit(solution)/shard_map/ppermute | solution.py:83
  704.7 39.2 %collective-permute-start.114 = (bf16[256,1408]{1,0:T(8,128)(2,1)S(1)}, bf16[256,1408]{1,0:T(8,128)(2,1)}, u32[]{:S(2)}, u32[]{:S(2)}) collective-permute-start(bf16[256,1408]{1,0:T(8,128)(2,1)S(1)} %pad_maximum_fusion.20), channel_id=1, source_target_pairs={{0,2},{1,3},{2,0},{3,1},{4,6},{5,7},{6,4},{7,5},{8,10},{9,11},{10,... | collective-permute-start | bytes 2162696 | tf_op jit(solution)/shard_map/ppermute | solution.py:83
  715.7 29.6 %collective-permute-start.113 = (bf16[256,1408]{1,0:T(8,128)(2,1)S(1)}, bf16[256,1408]{1,0:T(8,128)(2,1)S(1)}, u32[]{:S(2)}, u32[]{:S(2)}) collective-permute-start(bf16[256,1408]{1,0:T(8,128)(2,1)S(1)} %pad_maximum_fusion.20), channel_id=1, source_target_pairs={{0,1},{1,0},{2,3},{3,2},{4,5},{5,4},{6,7},{7,6},{8,9},{9,8},{10,11... | collective-permute-start | bytes 2162696 | tf_op jit(solution)/shard_map/ppermute | solution.py:83
  733.9 139.2 %collective-permute-start.112 = (bf16[256,1408]{1,0:T(8,128)(2,1)}, bf16[256,1408]{1,0:T(8,128)(2,1)}, u32[]{:S(2)}, u32[]{:S(2)}) collective-permute-start(bf16[256,1408]{1,0:T(8,128)(2,1)} %collective-permute-done.111), channel_id=1, source_target_pairs={{0,1},{1,0},{2,3},{3,2},{4,5},{5,4},{6,7},{7,6},{8,9},{9,8},{10,11... | collective-permute-start | bytes 2162696 | tf_op jit(solution)/shard_map/ppermute | solution.py:83
  743.9 125.9 %collective-permute-start.115 = (bf16[256,1408]{1,0:T(8,128)(2,1)}, bf16[256,1408]{1,0:T(8,128)(2,1)}, u32[]{:S(2)}, u32[]{:S(2)}) collective-permute-start(bf16[256,1408]{1,0:T(8,128)(2,1)} %collective-permute-done.114), channel_id=1, source_target_pairs={{0,1},{1,0},{2,3},{3,2},{4,5},{5,4},{6,7},{7,6},{8,9},{9,8},{10,11... | collective-permute-start | bytes 2162696 | tf_op jit(solution)/shard_map/ppermute | solution.py:83
  873.2 97.4 %collective-permute-start.69 = (bf16[256,2048]{1,0:T(8,128)(2,1)}, bf16[256,2048]{1,0:T(8,128)(2,1)S(1)}, u32[]{:S(2)}, u32[]{:S(2)}) collective-permute-start(bf16[256,2048]{1,0:T(8,128)(2,1)} %get-tuple-element.271), channel_id=1, source_target_pairs={{0,1},{1,0},{2,3},{3,2},{4,5},{5,4},{6,7},{7,6},{8,9},{9,8},{10,11... | collective-permute-start | bytes 3145736 | tf_op jit(solution)/shard_map/ppermute | solution.py:83
  882.6 46.4 %collective-permute-start.70 = (bf16[256,2048]{1,0:T(8,128)(2,1)S(1)}, bf16[256,2048]{1,0:T(8,128)(2,1)S(1)}, u32[]{:S(2)}, u32[]{:S(2)}) collective-permute-start(bf16[256,2048]{1,0:T(8,128)(2,1)S(1)} %copy-done.67), channel_id=1, source_target_pairs={{0,1},{1,0},{2,3},{3,2},{4,5},{5,4},{6,7},{7,6},{8,9},{9,8},{10,11... | collective-permute-start | bytes 3145736 | tf_op jit(solution)/shard_map/ppermute | solution.py:83
  935.3 35.2 %collective-permute-start.71 = (bf16[256,2048]{1,0:T(8,128)(2,1)S(1)}, bf16[256,2048]{1,0:T(8,128)(2,1)S(1)}, u32[]{:S(2)}, u32[]{:S(2)}) collective-permute-start(bf16[256,2048]{1,0:T(8,128)(2,1)S(1)} %fusion.82), channel_id=1, source_target_pairs={{0,2},{1,3},{2,0},{3,1},{4,6},{5,7},{6,4},{7,5},{8,10},{9,11},{10,... | collective-permute-start | bytes 3145736 | tf_op jit(solution)/shard_map/ppermute | solution.py:83
  (261 other events, 3535.4 us)

commit v2 on v0

v2 whole, which is shorter than its diff:
```python
import functools

import jax
import jax.numpy as jnp
from jax import lax
from jax.experimental import pallas as pl
from jax.experimental.pallas import tpu as pltpu
from jax.sharding import PartitionSpec as P

HEADS = 32
HD = 64
KVH = 4
EPS = 1e-05
TOP = 16
BF = jnp.bfloat16
F32 = jnp.float32
NEG = -1e30
VMEM_LIMIT = 60 << 20


def dot(left_side, right_side):
    return jnp.dot(left_side, right_side, preferred_element_type=F32)


def cross(left_side, right_side):
    return lax.dot_general(
        left_side, right_side, (((0,), (0,)), ((), ())), preferred_element_type=F32
    )


def against(left_side, right_side):
    return lax.dot_general(
        left_side, right_side, (((1,), (1,)), ((), ())), preferred_element_type=F32
    )


def kernel_call(body, outs, scratch=(), flops=0, moved=0, smem=0, args=(), name=None):
    vmem = pl.BlockSpec(memory_space=pltpu.VMEM)
    return pl.pallas_call(
        body,
        out_shape=tuple(jax.ShapeDtypeStruct(s, d) for s, d in outs),
        in_specs=[pl.BlockSpec(memory_space=pltpu.SMEM)] * smem + [vmem] * (len(args) - smem),
        out_specs=tuple(vmem for _ in outs),
        scratch_shapes=list(scratch),
        compiler_params=pltpu.CompilerParams(vmem_limit_bytes=VMEM_LIMIT),
        cost_estimate=pl.CostEstimate(flops=int(flops), transcendentals=0, bytes_accessed=int(moved)),
        name=name,
    )(*args)


class Ring:
    def __init__(self, size):
        self.size = size
        self.half = size // 2
        self.order = list(range(0, size, 2)) + list(range(size - 1, 0, -2))
        place = [0] * size
        for position, device in enumerate(self.order):
            place[device] = position
        self.place = place
        walk = [(self.order[i], self.order[(i + 1) % size]) for i in range(size)]
        self.up = walk
        self.down = [(b, a) for a, b in walk]
        self.steps = (
            [-t for t in range(self.half)] + [t for t in range(1, self.half)] + [self.half]
        )

    def slot_owners(self):
        mine = jnp.asarray(self.place, jnp.int32)[lax.axis_index("dp")]
        wanted = (mine + jnp.asarray(self.steps, jnp.int32)) % self.size
        return jnp.asarray(self.order, jnp.int32)[wanted]

    def owner_slots(self):
        mine = jnp.asarray(self.place, jnp.int32)[lax.axis_index("dp")]
        slot_of_step = [0] * self.size
        for slot, step in enumerate(self.steps):
            slot_of_step[step % self.size] = slot
        step = (jnp.asarray(self.place, jnp.int32) - mine) % self.size
        return jnp.asarray(slot_of_step, jnp.int32)[step]

    def go_up(self, block):
        return lax.ppermute(block, "dp", self.up)

    def go_down(self, block):
        return lax.ppermute(block, "dp", self.down)

    def gather(self, block, cut):
        from_down, from_up = [block], [block]
        for _ in range(1, self.half):
            from_down.append(self.go_up(from_down[-1]))
            from_up.append(self.go_down(from_up[-1]))
        return (
            from_down
            + from_up[1:]
            + [self.go_up(from_down[-1][:cut]), self.go_down(from_up[-1][cut:])]
        )

    def scatter(self, far, step, last):
        up, down = far(self.size - 1)
        for t in range(self.half - 1, 0, -1):
            up, down = self.go_up(up), self.go_down(down)
            up, down = step(self.half - 1 + t, t, up, down)
        return last(self.go_up(up), self.go_down(down))


def swap(block, distance):
    return lax.ppermute(block, "seq", [(i, i ^ distance) for i in range(4)])


def seq_gather(block):
    near = jnp.concatenate([block, swap(block, 2)], axis=0)
    return near, swap(near, 1)


def seq_scatter(terms):
    half = terms.shape[0] // 2
    quarter = half // 2
    near = terms[:half].astype(F32) + swap(terms[half:], 1).astype(F32)
    return near[:quarter] + swap(near[quarter:].astype(BF), 2).astype(F32)


def fill_weights(pieces, scratch, top, width, columns):
    begin = 0
    for index, piece in enumerate(pieces):
        skip = top if index < len(pieces) - 1 else 0
        count = piece.shape[0] - skip
        scratch[begin : begin + count, :] = piece[skip:, columns]
        begin += count


def permute_features(arrays, order, size):
    rows, features = arrays[0].shape
    width = features // size
    if width % 128:
        return [
            jnp.concatenate(
                [lax.dynamic_slice_in_dim(a, order[i] * width, width, 1) for i in range(size)],
                axis=1,
            )
            for a in arrays
        ]

    def body(order_ref, *refs):
        count = len(refs) // 2
        for source, target in zip(refs[:count], refs[count:]):
            target[...] = source[...]

    return pl.pallas_call(
        body,
        out_shape=tuple(jax.ShapeDtypeStruct(a.shape, a.dtype) for a in arrays),
        grid_spec=pltpu.PrefetchScalarGridSpec(
            num_scalar_prefetch=1,
            grid=(size,),
            in_specs=[pl.BlockSpec((rows, width), lambda i, o: (0, o[i])) for _ in arrays],
            out_specs=tuple(pl.BlockSpec((rows, width), lambda i, o: (0, i)) for _ in arrays),
        ),
        name="permute_features",
    )(order, *arrays)


def pack_heads(here, w_query, w_key, w_value, w_out, gain_attn, gain_mlp, seq):
    width = w_query.shape[0]
    q_cols, k_cols = w_query.shape[1] // seq, w_key.shape[1] // seq
    total = 2 * q_cols + 2 * k_cols

    def body(here_ref, query_ref, key_ref, value_ref, out_ref, one_ref, two_ref, block_ref):
        s = here_ref[0]
        block_ref[:TOP, :] = jnp.zeros((TOP, total), BF)
        block_ref[:1, :width] = one_ref[...]
        block_ref[:1, width : 2 * width] = two_ref[...]
        block_ref[TOP:, :q_cols] = query_ref[...]

        def mine(ref):
            part = jnp.zeros((width, k_cols), F32)
            for place in range(seq):
                piece = ref[:, place * k_cols : (place + 1) * k_cols].astype(F32)
                part = jnp.where(s == place, piece, part)
            return part

        both = jnp.concatenate([mine(key_ref), mine(value_ref)], axis=1)
        block_ref[TOP:, q_cols : q_cols + 2 * k_cols] = both.astype(BF)
        block_ref[TOP:, q_cols + 2 * k_cols :] = out_ref[...].astype(F32).T.astype(BF)

    whole = lambda shape: pl.BlockSpec(shape, lambda i, o: (0, 0))
    return pl.pallas_call(
        body,
        out_shape=jax.ShapeDtypeStruct((TOP + width, total), BF),
        grid_spec=pltpu.PrefetchScalarGridSpec(
            num_scalar_prefetch=1,
            grid=(1,),
            in_specs=[
                pl.BlockSpec((width, q_cols), lambda i, o: (0, o[0])),
                whole(w_key.shape),
                whole(w_value.shape),
                pl.BlockSpec((q_cols, width), lambda i, o: (o[0], 0)),
                whole((1, width)),
                whole((1, width)),
            ],
            out_specs=whole((TOP + width, total)),
        ),
        name="pack_heads",
    )(here, w_query, w_key, w_value, w_out, gain_attn[None], gain_mlp[None])


def pack_mlp(here, w_gate, w_up, w_down, bounds, seq):
    width, ff = w_gate.shape[0], w_gate.shape[1] // seq

    def body(here_ref, gate_ref, up_ref, down_ref, *blocks):
        for (a, b), block in zip(bounds, blocks):
            size = b - a
            block[:, :size] = gate_ref[:, a:b]
            block[:, size : 2 * size] = up_ref[:, a:b]
            block[:, 2 * size :] = down_ref[a:b, :].astype(F32).T.astype(BF)

    columns = pl.BlockSpec((width, ff), lambda i, o: (0, o[0]))
    return pl.pallas_call(
        body,
        out_shape=tuple(jax.ShapeDtypeStruct((width, 3 * (b - a)), BF) for a, b in bounds),
        grid_spec=pltpu.PrefetchScalarGridSpec(
            num_scalar_prefetch=1,
            grid=(1,),
            in_specs=[columns, columns, pl.BlockSpec((ff, width), lambda i, o: (o[0], 0))],
            out_specs=tuple(
                pl.BlockSpec((width, 3 * (b - a)), lambda i, o: (0, 0)) for a, b in bounds
            ),
        ),
        name="pack_mlp",
    )(here, w_gate, w_up, w_down)


def turn(values, cosine, sine_part):
    half_dim = HD // 2
    pieces = []
    for h in range(values.shape[0] // HD):
        first = values[h * HD : h * HD + half_dim]
        second = values[h * HD + half_dim : (h + 1) * HD]
        pieces.append(first * cosine - second * sine_part)
        pieces.append(second * cosine + first * sine_part)
    return jnp.concatenate(pieces, axis=0)


def rounded(values):
    return values.astype(BF).astype(F32)


def token_block(near_ref, far_ref, place, rows):
    begin = pl.multiple_of((place % 2) * rows, rows)
    near = near_ref[pl.ds(begin, rows), :].astype(F32)
    far = far_ref[pl.ds(begin, rows), :].astype(F32)
    return jnp.where(place < 2, near, far)


def write_bias(bias_ref, lengths_ref, live, block, rows):
    keys = (block + 1) * rows
    query = lax.broadcasted_iota(jnp.int32, (1, rows), 1) + block * rows
    low = jnp.zeros((1, rows), jnp.int32)
    start = 0
    for slot in range(lengths_ref.shape[0]):
        low = jnp.where(query >= start, jnp.maximum(low, start), low)
        start = start + lengths_ref[slot]
    high = jnp.minimum(query, live - 1)
    key = lax.broadcasted_iota(jnp.int32, (keys, rows), 0)
    allowed = ((key >= low) & (key <= high)) | (key == query)
    bias_ref[:keys, :] = jnp.where(allowed, 0.0, NEG)


def attention_forward(places, lengths, live, near, far, pieces, cosine, sine_part, rows, q_cols):
    pack_size = 4 * rows
    model = near.shape[1]
    n_heads = q_cols // HD
    heads_cols = q_cols + 2 * HD
    width = pieces[0].shape[0] - TOP

    def body(places_ref, lengths_ref, live_ref, near_ref, far_ref, cos_ref, sin_ref, *refs):
        piece_refs, refs = refs[: len(pieces)], refs[len(pieces) :]
        (
            normed_ref, query_ref, kv_ref, kvt_ref, lse_ref, mixed_t_ref, mixed_ref, branch_ref,
            gains_ref, w_ref, bias_ref, query_s, mixed_s,
        ) = refs
        live_count = live_ref[0]
        fill_weights(piece_refs, w_ref, TOP, width, slice(None))
        gains_ref[...] = jnp.zeros_like(gains_ref)
        for index, piece in enumerate(piece_refs[:-1]):
            at = slice(index * width, (index + 1) * width)
            gains_ref[0:1, at] = piece[0:1, :width].astype(F32)
            gains_ref[1:2, at] = piece[0:1, width : 2 * width].astype(F32)
        ones = jnp.ones((HD, rows), BF)
        for block in range(4):
            place = places_ref[block]
            at = slice(block * rows, (block + 1) * rows)
            keys = (block + 1) * rows
            to = pl.ds(pl.multiple_of(place * rows, rows), rows)
            inputs = token_block(near_ref, far_ref, place, rows)
            inverse = lax.rsqrt(jnp.mean(inputs * inputs, axis=1, keepdims=True) + EPS)
            normed = (inputs * inverse * gains_ref[0:1, :]).astype(BF)
            normed_ref[to, :] = normed
            pre = dot(normed, w_ref[:, :heads_cols]).T
            cos_b, sin_b = cos_ref[:, at], sin_ref[:, at]
            query = (rounded(turn(pre[:q_cols], cos_b, sin_b)) * HD**-0.5).astype(BF)
            query_s[...] = query
            query_ref[:, at] = query
            key_t = rounded(turn(pre[q_cols : q_cols + HD], cos_b, sin_b))
            value_t = rounded(pre[q_cols + HD :])
            kv_t = jnp.concatenate([key_t, value_t], axis=0)
            kv_ref[at, :] = kv_t.T.astype(BF)
            kvt_ref[: 2 * HD, at] = kv_t.astype(BF)
            kvt_ref[2 * HD :, at] = ones
            write_bias(bias_ref, lengths_ref, live_count, block, rows)

            def attend(h, _):
                mine = pl.ds(pl.multiple_of(h * HD, HD), HD)
                scores = dot(kv_ref[:keys, :HD], query_s[mine, :]) + bias_ref[:keys, :]
                peak = jnp.max(scores, axis=0, keepdims=True)
                weights = jnp.exp(scores - peak).astype(BF)
                summed = dot(kvt_ref[HD:, :keys], weights)
                total = summed[HD : HD + 1]
                mixed = summed[:HD] * (1.0 / total)
                mixed_s[mine, :] = mixed
                lse_ref[pl.ds(h, 1), at] = peak + jnp.log(total)
                return 0

            lax.fori_loop(0, n_heads, attend, 0, unroll=2)
            mixed_t = mixed_s[...]
            mixed_t_ref[:, at] = mixed_t
            mixed = mixed_t.T.astype(BF)
            mixed_ref[to, :] = mixed
            branch_ref[to, :] = against(mixed, w_ref[:, heads_cols:]).astype(BF)

    args = [places, lengths, live, near, far, cosine, sine_part, *pieces]
    flops = 2 * pack_size * model * (heads_cols + q_cols) + 4 * n_heads * pack_size**2 * HD * 3
    return kernel_call(
        body,
        [
            ((pack_size, model), BF),
            ((q_cols, pack_size), BF),
            ((pack_size, 2 * HD), BF),
            ((3 * HD, pack_size), BF),
            ((n_heads, pack_size), F32),
            ((q_cols, pack_size), F32),
            ((pack_size, q_cols), BF),
            ((pack_size, model), BF),
            ((8, model), F32),
        ],
        scratch=[
            pltpu.VMEM((model, heads_cols + q_cols), BF),
            pltpu.VMEM((pack_size, rows), F32),
            pltpu.VMEM((q_cols, rows), BF),
            pltpu.VMEM((q_cols, rows), F32),
        ],
        flops=flops,
        moved=30 << 20,
        smem=3,
        args=args,
        name="attention_forward",
    )


def attention_backward(
    places, lengths, live, near, far, pieces, cosine, sine_part, query, kv, kvt, lse, mixed_t, rows
):
    q_cols, pack_size = query.shape
    model = near.shape[1]
    n_heads = q_cols // HD
    heads_cols = q_cols + 2 * HD
    width = pieces[0].shape[0] - TOP

    def body(
        places_ref, lengths_ref, live_ref, near_ref, far_ref, cos_ref, sin_ref,
        query_ref, kv_ref, kvt_ref, lse_ref, mixed_t_ref, *refs
    ):
        piece_refs, refs = refs[: len(pieces)], refs[len(pieces) :]
        grad_q_ref, grad_kv_ref, w_ref, bias_ref, grad_s, grad_q_s, key_acc, value_acc, inner_s = refs
        live_count = live_ref[0]
        fill_weights(piece_refs, w_ref, TOP, width, slice(heads_cols, heads_cols + q_cols))
        key_acc[...] = jnp.zeros_like(key_acc)
        value_acc[...] = jnp.zeros_like(value_acc)
        for block in range(4):
            place = places_ref[block]
            at = slice(block * rows, (block + 1) * rows)
            keys = (block + 1) * rows
            to = pl.ds(pl.multiple_of(place * rows, rows), rows)
            branch = token_block(near_ref, far_ref, place, rows).astype(BF)
            grad_t = rounded(dot(branch, w_ref[...]).T)
            grad_s[...] = grad_t.astype(BF)
            product = grad_t * mixed_t_ref[:, at]
            for h in range(n_heads):
                inner_s[h : h + 1, :] = jnp.sum(
                    product[h * HD : (h + 1) * HD], axis=0, keepdims=True
                )
            write_bias(bias_ref, lengths_ref, live_count, block, rows)

            def attend(h, _):
                mine = pl.ds(pl.multiple_of(h * HD, HD), HD)
                query_h = query_ref[mine, at]
                grad_h = grad_s[mine, :]
                scores = dot(kv_ref[:keys, :HD], query_h) + bias_ref[:keys, :]
                probs = jnp.exp(scores - lse_ref[pl.ds(h, 1), at])
                grad_probs = dot(kv_ref[:keys, HD:], grad_h)
                grad_scores = (probs * (grad_probs - inner_s[pl.ds(h, 1), :])).astype(BF)
                grad_q_s[mine, :] = dot(kvt_ref[:HD, :keys], grad_scores) * HD**-0.5
                key_acc[:keys, :] += against(grad_scores, query_h)
                value_acc[:keys, :] += against(probs.astype(BF), grad_h)
                return 0

            lax.fori_loop(0, n_heads, attend, 0, unroll=2)
            turned = turn(rounded(grad_q_s[...]), cos_ref[:, at], -sin_ref[:, at])
            grad_q_ref[to, :] = turned.T.astype(BF)
        for block in range(4):
            at = slice(block * rows, (block + 1) * rows)
            to = pl.ds(pl.multiple_of(places_ref[block] * rows, rows), rows)
            key_t = turn(rounded(key_acc[at, :]).T, cos_ref[:, at], -sin_ref[:, at])
            grad_kv_ref[to, :] = jnp.concatenate([key_t.T, value_acc[at, :]], axis=1).astype(BF)

    args = [
        places, lengths, live, near, far, cosine, sine_part, query, kv, kvt, lse, mixed_t, *pieces
    ]
    return kernel_call(
        body,
        [((pack_size, q_cols), BF), ((pack_size, 2 * HD), BF)],
        scratch=[
            pltpu.VMEM((model, q_cols), BF),
            pltpu.VMEM((pack_size, rows), F32),
            pltpu.VMEM((q_cols, rows), BF),
            pltpu.VMEM((q_cols, rows), F32),
            pltpu.VMEM((pack_size, HD), F32),
            pltpu.VMEM((pack_size, HD), F32),
            pltpu.VMEM((n_heads, rows), F32),
        ],
        flops=2 * pack_size * model * q_cols + 10 * n_heads * pack_size**2 * HD * 3,
        moved=20 << 20,
        smem=3,
        args=args,
        name="attention_backward",
    )


def heads_back(grad_q, grad_kv, near, far, pieces, rows):
    pack_size, q_cols = grad_q.shape
    model = near.shape[1]
    heads_cols = q_cols + 2 * HD
    width = pieces[0].shape[0] - TOP

    def body(grad_q_ref, grad_kv_ref, near_ref, far_ref, *refs):
        piece_refs, (grad_ref, gain_ref, w_ref) = refs[: len(pieces)], refs[len(pieces) :]
        fill_weights(piece_refs, w_ref, TOP, width, slice(0, heads_cols))
        total = jnp.zeros((1, model), F32)
        for block in range(4):
            at = slice(block * rows, (block + 1) * rows)
            source = near_ref if block < 2 else far_ref
            inputs = source[(block % 2) * rows : (block % 2 + 1) * rows, :].astype(F32)
            inverse = lax.rsqrt(jnp.mean(inputs * inputs, axis=1, keepdims=True) + EPS)
            grad = against(grad_q_ref[at, :], w_ref[:, :q_cols]) + against(
                grad_kv_ref[at, :], w_ref[:, q_cols:]
            )
            grad_ref[at, :] = grad.astype(BF)
            total = total + jnp.sum(grad * inputs * inverse, axis=0, keepdims=True)
        gain_ref[...] = jnp.broadcast_to(total, gain_ref.shape)

    args = [grad_q, grad_kv, near, far, *pieces]
    return kernel_call(
        body,
        [((pack_size, model), BF), ((8, model), F32)],
        scratch=[pltpu.VMEM((model, heads_cols), BF)],
        flops=2 * pack_size * model * heads_cols,
        moved=14 << 20,
        args=args,
        name="heads_back",
    )


def mlp_chunk(near, far, cot_near, cot_far, pieces, before, rows, size):
    model = near.shape[1]
    pack_size = 4 * rows
    n_in = 4 + len(pieces) + len(before)

    def body(near_ref, far_ref, cot_near_ref, cot_far_ref, *refs):
        piece_refs = refs[: len(pieces)]
        before_refs = refs[len(pieces) : n_in - 4]
        down_ref, grad_ref, both_ref, act_ref, w_ref = refs[n_in - 4 :]
        step = pl.program_id(0)

        @pl.when(step == 0)
        def _():
            fill_weights(piece_refs, w_ref, 0, model, slice(None))

        def work(normed, cot):
            both = dot(normed, w_ref[:, : 2 * size])
            grad_act = dot(cot, w_ref[:, 2 * size :])
            gate_pre, up_pre = both[:, :size], both[:, size:]
            sig = 1.0 / (1.0 + jnp.exp(-gate_pre))
            active = gate_pre * sig
            act = (active * up_pre).astype(BF)
            act_ref[...] = act
            grad_up = (grad_act * active).astype(BF)
            grad_gate = (grad_act * up_pre * (sig + active * (1.0 - sig))).astype(BF)
            both_ref[:, :size] = grad_gate
            both_ref[:, size:] = grad_up
            down = against(act, w_ref[:, 2 * size :])
            grad = against(both_ref[...], w_ref[:, : 2 * size])
            if before_refs:
                down = down + before_refs[0][...].astype(F32)
                grad = grad + before_refs[1][...].astype(F32)
            down_ref[...] = down.astype(BF)
            grad_ref[...] = grad.astype(BF)

        @pl.when(step < 2)
        def _():
            work(near_ref[...], cot_near_ref[...])

        @pl.when(step >= 2)
        def _():
            work(far_ref[...], cot_far_ref[...])

    first = pl.BlockSpec((rows, model), lambda i: (jnp.minimum(i, 1), 0))
    second = pl.BlockSpec((rows, model), lambda i: (jnp.maximum(i - 2, 0), 0))
    each = lambda cols: pl.BlockSpec((rows, cols), lambda i: (i, 0))
    return pl.pallas_call(
        body,
        grid=(4,),
        out_shape=(
            jax.ShapeDtypeStruct((pack_size, model), BF),
            jax.ShapeDtypeStruct((pack_size, model), BF),
            jax.ShapeDtypeStruct((pack_size, 2 * size), BF),
            jax.ShapeDtypeStruct((pack_size, size), BF),
        ),
        in_specs=[first, second, first, second]
        + [
            pl.BlockSpec(p.shape, lambda i: (0, 0), pipeline_mode=pl.Buffered(1)) for p in pieces
        ]
        + [each(model) for _ in before],
        out_specs=(each(model), each(model), each(2 * size), each(size)),
        scratch_shapes=[pltpu.VMEM((model, 3 * size), BF)],
        compiler_params=pltpu.CompilerParams(vmem_limit_bytes=VMEM_LIMIT),
        cost_estimate=pl.CostEstimate(
            flops=12 * pack_size * model * size,
            transcendentals=0,
            bytes_accessed=2 * (model * 3 * size + pack_size * (4 * model + 3 * size)),
        ),
        name="mlp_chunk",
    )(near, far, cot_near, cot_far, *pieces, *before)


def ring_terms(pairs, slots, width, came, top, kind):
    columns = [sum(g.shape[1] for g in gs) for _, gs in pairs]
    total = sum(columns)
    head = 0 if top is None else TOP
    cut = head + width // 2
    full = head + width

    args, specs = [], []

    def add(array, spec=None):
        args.append(array)
        specs.append(spec or pl.BlockSpec(array.shape, lambda i: (0,) * array.ndim))

    for (near, far), gs in pairs:
        for s in slots:
            for half in (near, far):
                if width % 128:
                    add(half[:, s * width : (s + 1) * width])
                else:
                    add(half, pl.BlockSpec((half.shape[0], width), lambda i, s=s: (0, s)))
        for g in gs:
            add(g)
    if top is not None:
        for s in slots:
            add(top[s])
    for c in came:
        add(c)

    if kind == "far":
        outs = [((cut, total), BF), ((width // 2, total), BF)]
    elif kind == "step":
        outs = [((full, total), BF)] * 2
    else:
        outs = [((full, total), BF)]

    def body(*refs):
        n_in = len(args)
        ins, out_refs = list(refs[:n_in]), refs[n_in:]
        sums = [[] for _ in slots]
        at = 0
        for (near, _), gs in pairs:
            halves = [(ins[at + 2 * i], ins[at + 2 * i + 1]) for i in range(len(slots))]
            at += 2 * len(slots)
            g_refs = ins[at : at + len(gs)]
            at += len(gs)
            half_rows = near.shape[0]
            for i, (near_ref, far_ref) in enumerate(halves):
                for g_ref in g_refs:
                    sums[i].append(
                        cross(near_ref[...], g_ref[:half_rows, :])
                        + cross(far_ref[...], g_ref[half_rows:, :])
                    )
        tops = [None] * len(slots)
        if top is not None:
            tops = ins[at : at + len(slots)]
            at += len(slots)
        came_refs = ins[at:]

        def put(target, row, term, lane, extra):
            value = term if extra is None else term + extra.astype(F32)
            target[row : row + term.shape[0], lane : lane + term.shape[1]] = value.astype(BF)

        for i in range(len(slots)):
            lane = 0
            pieces = ([(0, tops[i][...].astype(F32))] if head else []) + [None]
            if head:
                value = tops[i][...].astype(F32)
                if kind == "far":
                    out_refs[0][:head, :] = value.astype(BF)
                elif kind == "step":
                    extra = None
                    if i == 0 or came_refs[i].shape[0] == full:
                        extra = came_refs[i][:head, :]
                    put(out_refs[i], 0, value, 0, extra)
                else:
                    put(
                        out_refs[0],
                        0,
                        value + came_refs[0][:head, :].astype(F32),
                        0,
                        came_refs[1][:head, :],
                    )
            for term in sums[i]:
                lanes = slice(lane, lane + term.shape[1])
                middle = width // 2
                if kind == "far":
                    put(out_refs[0], head, term[:middle], lane, None)
                    put(out_refs[1], 0, term[middle:], lane, None)
                elif kind == "step":
                    if came_refs[i].shape[0] == full:
                        put(out_refs[i], head, term, lane, came_refs[i][head:, lanes])
                    elif i == 0:
                        put(out_refs[i], head, term[:middle], lane, came_refs[i][head:, lanes])
                        put(out_refs[i], cut, term[middle:], lane, None)
                    else:
                        put(out_refs[i], head, term[:middle], lane, None)
                        put(out_refs[i], cut, term[middle:], lane, came_refs[i][:, lanes])
                else:
                    put(
                        out_refs[0],
                        head,
                        term + came_refs[0][head:, lanes].astype(F32),
                        lane,
                        came_refs[1][head:, lanes],
                    )
                lane += term.shape[1]

    tokens = 2 * pairs[0][0][0].shape[0]
    return pl.pallas_call(
        body,
        grid=(1,),
        out_shape=tuple(jax.ShapeDtypeStruct(s, d) for s, d in outs),
        in_specs=specs,
        out_specs=tuple(pl.BlockSpec(s, lambda i: (0, 0)) for s, _ in outs),
        compiler_params=pltpu.CompilerParams(vmem_limit_bytes=VMEM_LIMIT),
        cost_estimate=pl.CostEstimate(
            flops=2 * len(slots) * tokens * width * total,
            transcendentals=0,
            bytes_accessed=2 * (tokens * total + len(slots) * width * (tokens + 2 * total)),
        ),
        name="ring_terms",
    )(*args)


def reduce_over_dp(ring, pairs, width, top=None):
    def far(slot):
        return ring_terms(pairs, [slot], width, [], top, "far")

    def step(up_slot, down_slot, up, down):
        return ring_terms(pairs, [up_slot, down_slot], width, [up, down], top, "step")

    def last(up, down):
        return ring_terms(pairs, [0], width, [up, down], top, "last")[0]

    return ring.scatter(far, step, last)


def unpack_mlp(places, halves, bounds, width, ff):
    count = len(bounds)
    flat = [h for pair in halves for h in pair]

    def body(places_ref, *refs):
        ins, (gate_ref, up_ref, down_ref) = refs[: 2 * count], refs[2 * count :]
        place = places_ref[pl.program_id(0)]
        begin = pl.multiple_of((place % 2) * width, width)
        for c, (a, b) in enumerate(bounds):
            size = b - a
            near = ins[2 * c][pl.ds(begin, width), :].astype(F32)
            far = ins[2 * c + 1][pl.ds(begin, width), :].astype(F32)
            block = jnp.where(place < 2, near, far)
            gate_ref[:, a:b] = block[:, :size]
            up_ref[:, a:b] = block[:, size : 2 * size]
            down_ref[a:b, :] = block[:, 2 * size :].T

    columns = pl.BlockSpec((width, ff), lambda i, p: (0, i))
    return pl.pallas_call(
        body,
        out_shape=(
            jax.ShapeDtypeStruct((width, 4 * ff), F32),
            jax.ShapeDtypeStruct((width, 4 * ff), F32),
            jax.ShapeDtypeStruct((4 * ff, width), F32),
        ),
        grid_spec=pltpu.PrefetchScalarGridSpec(
            num_scalar_prefetch=1,
            grid=(4,),
            in_specs=[pl.BlockSpec(h.shape, lambda i, p: (0, 0)) for h in flat],
            out_specs=(columns, columns, pl.BlockSpec((ff, width), lambda i, p: (i, 0))),
        ),
        compiler_params=pltpu.CompilerParams(vmem_limit_bytes=VMEM_LIMIT),
        name="unpack_mlp",
    )(places, *flat)


def unpack_heads(places, heads, outs, width, q_cols):
    full = TOP + width

    def body(places_ref, near_ref, far_ref, out_near_ref, out_far_ref, *refs):
        query_ref, key_ref, value_ref, out_ref, gain_ref = refs
        gain = jnp.zeros((8, 2 * width), F32)
        for place in range(4):
            at = places_ref[place]
            begin = pl.multiple_of((at % 2) * full, 16)
            near = near_ref[pl.ds(begin, full), :].astype(F32)
            far = far_ref[pl.ds(begin, full), :].astype(F32)
            block = jnp.where(at < 2, near, far)
            gain = gain + block[:8, : 2 * width]
            query_ref[:, place * q_cols : (place + 1) * q_cols] = block[TOP:, :q_cols]
            key_ref[:, place * HD : (place + 1) * HD] = block[TOP:, q_cols : q_cols + HD]
            value_ref[:, place * HD : (place + 1) * HD] = block[TOP:, q_cols + HD :]
            begin = pl.multiple_of((at % 2) * width, 16)
            near = out_near_ref[pl.ds(begin, width), :].astype(F32)
            far = out_far_ref[pl.ds(begin, width), :].astype(F32)
            out_ref[place * q_cols : (place + 1) * q_cols, :] = jnp.where(at < 2, near, far).T
        gain_ref[...] = gain

    args = [places, *heads, *outs]
    return kernel_call(
        body,
        [
            ((width, 4 * q_cols), F32),
            ((width, 4 * HD), F32),
            ((width, 4 * HD), F32),
            ((4 * q_cols, width), F32),
            ((8, 2 * width), F32),
        ],
        moved=8 << 20,
        smem=1,
        args=args,
        name="unpack_heads",
    )


def doc_positions(lengths, pack_size):
    doc_starts = jnp.cumsum(lengths) - lengths
    places = jnp.arange(pack_size, dtype=jnp.int32)
    doc_first = jnp.max(
        jnp.where(places[:, None] >= doc_starts[None, :], doc_starts[None, :], 0), axis=1
    )
    return places - doc_first


def rotary_tables(positions):
    half_dim = HD // 2
    frequency = 10000.0 ** (-2.0 * jnp.arange(half_dim, dtype=F32) / HD)
    angle_table = frequency[:, None] * positions.astype(F32)[None, :]
    return (jnp.cos(angle_table), jnp.sin(angle_table))


def rms_back(grad_normed, values, inverse, gain_vec):
    scaled = grad_normed * gain_vec
    return inverse * (
        scaled - values * inverse * inverse * jnp.mean(scaled * values, axis=1, keepdims=True)
    )


def layer(
    hidden_in,
    cotangent,
    gain_attn,
    w_query,
    w_key,
    w_value,
    w_out,
    gain_mlp,
    w_gate,
    w_up,
    w_down,
    doc_lengths,
    valid_count,
):
    seq = lax.axis_size("seq")
    n_dp = lax.axis_size("dp")
    here = lax.axis_index("seq").astype(jnp.int32)
    ring = Ring(n_dp)
    rows = hidden_in.shape[0]
    pack_size = rows * seq
    width = gain_attn.shape[0]
    q_cols = w_query.shape[1] // seq
    ff = w_gate.shape[1] // seq
    here_1 = here.reshape(1)
    lengths, live = doc_lengths[0], valid_count[:1]

    offset = here ^ jnp.arange(4, dtype=jnp.int32)
    places = (offset % 2) * 2 + offset // 2

    first = (ff // 2 + 127) // 128 * 128
    bounds = [(0, first), (first, ff)]
    head_block = pack_heads(here_1, w_query, w_key, w_value, w_out, gain_attn, gain_mlp, seq)
    head_pieces = ring.gather(head_block, TOP + width // 2)
    mlp_pieces = [
        ring.gather(block, width // 2)
        for block in pack_mlp(here_1, w_gate, w_up, w_down, bounds, seq)
    ]

    mine, my_cot = permute_features([hidden_in, cotangent], ring.slot_owners(), n_dp)
    near, far = seq_gather(mine)
    cot_near, cot_far = seq_gather(my_cot)
    cosine, sine_part = rotary_tables(doc_positions(lengths, pack_size))

    normed, query, kv, kvt, lse, mixed_t, mixed, branch, gains = attention_forward(
        places, lengths, live, near, far, head_pieces, cosine, sine_part, rows, q_cols
    )
    gain_one, gain_two = gains[0:1], gains[1:2]

    my_inputs = mine.astype(F32)
    hidden = my_inputs + seq_scatter(branch)
    inverse_two = lax.rsqrt(jnp.mean(hidden * hidden, axis=1, keepdims=True) + EPS)
    my_normed_two = (hidden * inverse_two * gain_two).astype(BF)
    two_near, two_far = seq_gather(my_normed_two)

    before = ()
    chunk_sums = []
    for (a, b), pieces in zip(bounds, mlp_pieces):
        down, grad_normed, grad_both, act = mlp_chunk(
            two_near, two_far, cot_near, cot_far, pieces, before, rows, b - a
        )
        before = (down, grad_normed)
        chunk_sums.append(
            reduce_over_dp(
                ring, [((two_near, two_far), [grad_both]), ((cot_near, cot_far), [act])], width
            )
        )

    grad_normed_two = seq_scatter(grad_normed)
    term_gain_two = jnp.sum(grad_normed_two * hidden * inverse_two, axis=0)
    grad_hidden = my_cot.astype(F32) + rms_back(grad_normed_two, hidden, inverse_two, gain_two)
    branch_near, branch_far = seq_gather(grad_hidden.astype(BF))
    result = (hidden + seq_scatter(down)).astype(BF)

    out_sum = reduce_over_dp(ring, [((branch_near, branch_far), [mixed])], width)
    grad_q, grad_kv = attention_backward(
        places, lengths, live, branch_near, branch_far, head_pieces, cosine, sine_part,
        query, kv, kvt, lse, mixed_t, rows
    )
    grad_normed_one, gain_terms = heads_back(grad_q, grad_kv, near, far, head_pieces, rows)
    tops = jnp.concatenate(
        [
            gain_terms[0].reshape(n_dp, width),
            term_gain_two.reshape(n_dp, width),
            jnp.zeros((n_dp, q_cols + 2 * HD - 2 * width), F32),
        ],
        axis=1,
    ).astype(BF)
    tops = [
        jnp.concatenate([tops[j : j + 1], jnp.zeros((TOP - 1, tops.shape[1]), BF)], axis=0)
        for j in range(n_dp)
    ]
    half = pack_size // 2
    head_sum = reduce_over_dp(
        ring, [((normed[:half], normed[half:]), [grad_q, grad_kv])], width, tops
    )
    inverse_one = lax.rsqrt(jnp.mean(my_inputs * my_inputs, axis=1, keepdims=True) + EPS)
    grad_input = (
        grad_hidden + rms_back(seq_scatter(grad_normed_one), my_inputs, inverse_one, gain_one)
    ).astype(BF)

    grad_gate, grad_up, grad_down = unpack_mlp(
        places, [seq_gather(c) for c in chunk_sums], bounds, width, ff
    )
    grad_query, grad_key, grad_value, grad_out, gain_sums = unpack_heads(
        places, seq_gather(head_sum), seq_gather(out_sum), width, q_cols
    )
    result, grad_input = permute_features([result, grad_input], ring.owner_slots(), n_dp)

    return (
        result,
        grad_input,
        gain_sums[0, :width],
        grad_query,
        grad_key,
        grad_value,
        grad_out,
        gain_sums[0, width:],
        grad_gate,
        grad_up,
        grad_down,
    )


def solution(mesh):
    return jax.shard_map(
        layer,
        mesh=mesh,
        in_specs=(
            P(("dp", "seq"), None),
            P(("dp", "seq"), None),
            P("dp"),
            P("dp", None),
            P("dp", None),
            P("dp", None),
            P(None, "dp"),
            P("dp"),
            P("dp", None),
            P("dp", None),
            P(None, "dp"),
            P("dp", None),
            P("dp"),
        ),
        out_specs=(
            P(("dp", "seq"), None),
            P(("dp", "seq"), None),
            P("dp"),
            P("dp", None),
            P("dp", None),
            P("dp", None),
            P(None, "dp"),
            P("dp"),
            P("dp", None),
            P("dp", None),
            P(None, "dp"),
        ),
        check_vma=False,
    )
```

time: 3660 us -> 712 us (0.19)
  waiting for transfers between devices: 3150 us -> 296 us
  matrix products: 263 us -> 0 us
  Pallas kernels: 0 us -> 255 us
  blocking collectives: 99 us -> 0 us
  starting transfers between devices: 18.1 us -> 76.7 us
    all_gather x7 -> x0, waiting for transfers between devices: 1490 us -> none  [the longest x1 433 us: on_device(): lax.all_gather(w_gate, 'dp', axis=0, tiled=True)]
    reduce_scatter x7 -> x0, waiting for transfers between devices: 1480 us -> none  [the longest x1 377 us: on_device(): lax.psum_scatter(cross(hidden_act, cotangent).astype(jnp.bfloat16), 'dp',...]
    ppermute x0 -> x80, waiting for transfers between devices: none -> 296 us  [the longest x28 188 us: go_up(): return lax.ppermute(block, 'dp', self.up)]
    dot_general x35 -> x0, matrix products: 263 us -> none  [the longest x7 67.7 us: against(): lax.dot_general(left_side, right_side, (((1,), (1,)), ((), ())), preferre...]
    pallas_call x0 -> x31, Pallas kernels: none -> 255 us  [the longest x20 93.9 us: ring_terms(): pl.pallas_call(body, grid=(1,), out_shape=tuple((jax.ShapeDtypeStruct(s,...]
    psum x1 -> x0, waiting for transfers between devices: 143 us -> none  [on_device(): lax.psum(attn_terms[1].astype(jnp.bfloat16), 'seq').astype(jnp.float32)]
    ppermute x0 -> x80, starting transfers between devices: none -> 76.7 us  [the longest x28 39.4 us: go_up(): return lax.ppermute(block, 'dp', self.up)]
    all_gather x2 -> x0, blocking collectives: 40.5 us -> none  [the longest x1 22.2 us: on_device(): lax.all_gather(gain_attn, 'dp', axis=0, tiled=True)]
  transfers between devices with their start and end apart: 20 -> 80, of which waited for: 17 -> 34; matrix products, arithmetic and copies ran while one was open for 5% -> 8% of each run, Pallas kernels for 0% -> 26%
where the time goes in v2:
time: 712 us; the launch traced here: 708 us
  waiting for transfers between devices  296 us (42%)
  Pallas kernels  255 us (36%)
  starting transfers between devices  76.7 us (11%)
  local copies, waits for them, and re-layouts  40.7 us (6%)
  other arithmetic  37.1 us (5%)
    ppermute x28, waiting for transfers between devices, go_up(): return lax.ppermute(block, 'dp', self.up)  188 us
    pallas_call x20, Pallas kernels, ring_terms(): pl.pallas_call(body, grid=(1,), out_shape=tuple((jax.ShapeDtypeStruct(s,...  93.9 us
    pallas_call x4, Pallas kernels, kernel_call(): pl.pallas_call(body, out_shape=tuple((jax.ShapeDtypeStruct(s, d) for s, d...  77.2 us
    ppermute x28, waiting for transfers between devices, go_down(): return lax.ppermute(block, 'dp', self.down)  56.4 us
    pallas_call x2, Pallas kernels, mlp_chunk(): pl.pallas_call(body, grid=(4,), out_shape=(jax.ShapeDtypeStruct((pack_siz...  54.3 us
    ppermute x24, waiting for transfers between devices, swap(): return lax.ppermute(block, 'seq', [(i, i ^ distance) for i in range(4)])  51.5 us
    ppermute x28, starting transfers between devices, go_up(): return lax.ppermute(block, 'dp', self.up)  39.4 us
    ppermute x28, starting transfers between devices, go_down(): return lax.ppermute(block, 'dp', self.down)  19.9 us
  transfers between devices with their start and end apart: 80, of which 34 were waited for; matrix products, arithmetic and copies ran while one was open for 8% of the time, Pallas kernels for 26%

profile of v2, /device:TPU:0, one launch (start us, length us, event | category | flops | bytes accessed | tf_op | source)
XLA Modules:
  0.0 707.7 jit_solution(3242481453383824754)
XLA Ops:
  5.6 6.4 permute_features.2
  20.8 17.8 %collective-permute-done = bf16[256,2048]{1,0:T(8,128)(2,1)} collective-permute-done((bf16[256,2048]{1,0:T(8,128)(2,1)}, bf16[256,2048]{1,0:T(8,128)(2,1)}, u32[]{:S(2)}, u32[]{:S(2)}) %collective-permute-start) | collective-permute-done | bytes 1048608 | tf_op jit(solution)/shard_map/ppermute | solution.py:106
  42.9 13.9 %collective-permute-done.3.refs_2_ = bf16[272,1152]{1,0:T(8,128)(2,1)} collective-permute-done((bf16[272,1152]{1,0:T(8,128)(2,1)}, bf16[272,1152]{1,0:T(8,128)(2,1)}, u32[]{:S(2)}, u32[]{:S(2)}) %collective-permute-start.3) | collective-permute-done | bytes 626720 | tf_op jit(solution)/shard_map/ppermute | solution.py:81
  59.5 13.2 %collective-permute-done.4.refs_3_ = bf16[272,1152]{1,0:T(8,128)(2,1)S(1)} collective-permute-done((bf16[272,1152]{1,0:T(8,128)(2,1)}, bf16[272,1152]{1,0:T(8,128)(2,1)S(1)}, u32[]{:S(2)}, u32[]{:S(2)}) %collective-permute-start.4) | collective-permute-done | bytes 626720 | tf_op jit(solution)/shard_map/ppermute | solution.py:81
  76.2 5.8 collective-permute-done.9.refs_8_
  82.8 33.8 %attention_forward.1 = (bf16[1024,2048]{1,0:T(8,128)(2,1)}, bf16[512,1024]{1,0:T(8,128)(2,1)}, bf16[1024,128]{1,0:T(8,128)(2,1)}, bf16[192,1024]{1,0:T(8,128)(2,...) custom-call(s32[4]{0:T(128)} %fusion.15.places_ref, ...), custom_call_target="tpu_custom_call" | custom-call | flops 11274289152 | bytes 31457280 | tf_op jit(solution)/shard_map/attention_forward/pallas_call | solution.py:39
  132.0 18.5 %collective-permute-done.24.refs_1_ = bf16[256,2304]{1,0:T(8,128)(2,1)S(1)} collective-permute-done((bf16[256,2304]{1,0:T(8,128)(2,1)}, bf16[256,2304]{1,0:T(8,128)(2,1)S(1)}, u32[]{:S(2)}, u32[]{:S(2)}) %collective-permute-start.24) | collective-permute-done | bytes 1179680 | tf_op jit(solution)/shard_map/ppermute | solution.py:81
  154.7 16.9 %collective-permute-done.16.refs_1_ = bf16[256,1920]{1,0:T(8,128)(2,1)S(1)} collective-permute-done((bf16[256,1920]{1,0:T(8,128)(2,1)S(1)}, bf16[256,1920]{1,0:T(8,128)(2,1)S(1)}, u32[]{:S(2)}, u32[]{:S(2)}) %collective-permute-start.16) | collective-permute-done | bytes 983072 | tf_op jit(solution)/shard_map/ppermute | solution.py:81
  174.7 3.5 collective-permute-done.27.refs_4_
  179.5 17.4 %collective-permute-done.25.refs_2_ = bf16[256,2304]{1,0:T(8,128)(2,1)S(1)} collective-permute-done((bf16[256,2304]{1,0:T(8,128)(2,1)S(1)}, bf16[256,2304]{1,0:T(8,128)(2,1)S(1)}, u32[]{:S(2)}, u32[]{:S(2)}) %collective-permute-start.25) | collective-permute-done | bytes 1179680 | tf_op jit(solution)/shard_map/ppermute | solution.py:81
  199.2 18.7 %collective-permute-done.17.refs_2_ = bf16[256,1920]{1,0:T(8,128)(2,1)S(1)} collective-permute-done((bf16[256,1920]{1,0:T(8,128)(2,1)S(1)}, bf16[256,1920]{1,0:T(8,128)(2,1)S(1)}, u32[]{:S(2)}, u32[]{:S(2)}) %collective-permute-start.17) | collective-permute-done | bytes 983072 | tf_op jit(solution)/shard_map/ppermute | solution.py:81
  218.8 9.4 %collective-permute-done.20.refs_5_ = bf16[256,1920]{1,0:T(8,128)(2,1)S(1)} collective-permute-done((bf16[256,1920]{1,0:T(8,128)(2,1)S(1)}, bf16[256,1920]{1,0:T(8,128)(2,1)S(1)}, u32[]{:S(2)}, u32[]{:S(2)}) %collective-permute-start.20) | collective-permute-done | bytes 983072 | tf_op jit(solution)/shard_map/ppermute | solution.py:84
  229.7 13.5 %collective-permute-done.26.refs_3_ = bf16[256,2304]{1,0:T(8,128)(2,1)S(1)} collective-permute-done((bf16[256,2304]{1,0:T(8,128)(2,1)S(1)}, bf16[256,2304]{1,0:T(8,128)(2,1)S(1)}, u32[]{:S(2)}, u32[]{:S(2)}) %collective-permute-start.26) | collective-permute-done | bytes 1179680 | tf_op jit(solution)/shard_map/ppermute | solution.py:81
  244.1 9.4 %collective-permute-done.29.refs_6_ = bf16[256,2304]{1,0:T(8,128)(2,1)S(1)} collective-permute-done((bf16[256,2304]{1,0:T(8,128)(2,1)S(1)}, bf16[256,2304]{1,0:T(8,128)(2,1)S(1)}, u32[]{:S(2)}, u32[]{:S(2)}) %collective-permute-start.29) | collective-permute-done | bytes 1179680 | tf_op jit(solution)/shard_map/ppermute | solution.py:84
  255.0 9.3 %collective-permute-done.18.refs_3_ = bf16[256,1920]{1,0:T(8,128)(2,1)S(1)} collective-permute-done((bf16[256,1920]{1,0:T(8,128)(2,1)S(1)}, bf16[256,1920]{1,0:T(8,128)(2,1)S(1)}, u32[]{:S(2)}, u32[]{:S(2)}) %collective-permute-start.18) | collective-permute-done | bytes 983072 | tf_op jit(solution)/shard_map/ppermute | solution.py:81
  265.1 9.4 %collective-permute-done.21.refs_6_ = bf16[256,1920]{1,0:T(8,128)(2,1)S(1)} collective-permute-done((bf16[256,1920]{1,0:T(8,128)(2,1)S(1)}, bf16[256,1920]{1,0:T(8,128)(2,1)S(1)}, u32[]{:S(2)}, u32[]{:S(2)}) %collective-permute-start.21) | collective-permute-done | bytes 983072 | tf_op jit(solution)/shard_map/ppermute | solution.py:84
  278.0 9.2 %collective-permute-done.31.refs_8_ = bf16[128,2304]{1,0:T(8,128)(2,1)S(1)} collective-permute-done((bf16[128,2304]{1,0:T(8,128)(2,1)S(1)}, bf16[128,2304]{1,0:T(8,128)(2,1)S(1)}, u32[]{:S(2)}, u32[]{:S(2)}) %collective-permute-start.31) | collective-permute-done | bytes 589856 | tf_op jit(solution)/shard_map/ppermute | solution.py:84
  288.1 28.0 %mlp_chunk.2 = (bf16[1024,2048]{1,0:T(8,128)(2,1)}, bf16[1024,2048]{1,0:T(8,128)(2,1)}, bf16[1024,1536]{1,0:T(8,128)(2,1)}, bf16[1024,768]{1,0:T(8,128)(2,1)}) custom-call(bf16[512,2048]{1,0:T(8,128)(2,1)} %copy-done, bf16[512,2048]{1,0:T(8,128)(2,1)} %collective-permute-done.13.far_ref.refs_1_.refs_3_, bf16[512,2048]{1,0:T(8,128)(2,1)} %copy-done.1, ...), custom_call_target="tpu_custom_call" | custom-call | flops 19327352832 | bytes 30932992 | tf_op jit(solution)/shard_map/mlp_chunk/pallas_call | solution.py:516
  316.2 26.2 %mlp_chunk.3 = (bf16[1024,2048]{1,0:T(8,128)(2,1)}, bf16[1024,2048]{1,0:T(8,128)(2,1)}, bf16[1024,1280]{1,0:T(8,128)(2,1)}, bf16[1024,640]{1,0:T(8,128)(2,1)}) custom-call(bf16[512,2048]{1,0:T(8,128)(2,1)} %copy-done, bf16[512,2048]{1,0:T(8,128)(2,1)} %collective-permute-done.13.far_ref.refs_1_.refs_3_, bf16[512,2048]{1,0:T(8,128)(2,1)} %copy-done.1, ...), custom_call_target="tpu_custom_call" | custom-call | flops 16106127360 | bytes 28573696 | tf_op jit(solution)/shard_map/mlp_chunk/pallas_call | solution.py:516
  342.4 3.3 slice.132
  346.4 5.1 ring_terms.30
  368.7 7.1 %ring_terms.31 = (bf16[256,2304]{1,0:T(8,128)(2,1)}, bf16[256,2304]{1,0:T(8,128)(2,1)}) custom-call(bf16[512,2048]{1,0:T(8,128)(2,1)} %copy-done, bf16[512,2048]{1,0:T(8,128)(2,1)} %collective-permute-done.13.far_ref.refs_1_.refs_3_, bf16[512,2048]{1,0:T(8,128)(2,1)} %copy-done, bf16[512,2048]{1,0:T(8,128)(2,1)} %collective-permute-done.13.far_ref.refs_1_.refs_3_, ...), custom_call_target="tpu_custom_call" | custom-call | flops 2415919104 | bytes 10485760 | tf_op jit(solution)/shard_map/ring_terms/pallas_call | solution.py:650
  377.8 7.0 collective-permute-done.35
  387.4 18.3 %collective-permute-done.33 = bf16[256,2048]{1,0:T(8,128)(2,1)} collective-permute-done((bf16[256,2048]{1,0:T(8,128)(2,1)}, bf16[256,2048]{1,0:T(8,128)(2,1)}, u32[]{:S(2)}, u32[]{:S(2)}) %collective-permute-start.33) | collective-permute-done | bytes 1048608 | tf_op jit(solution)/shard_map/ppermute | solution.py:106
  405.7 5.3 fusion.16
  412.2 4.7 ring_terms.35
  418.9 7.4 %ring_terms.32 = (bf16[256,2304]{1,0:T(8,128)(2,1)}, bf16[256,2304]{1,0:T(8,128)(2,1)}) custom-call(bf16[512,2048]{1,0:T(8,128)(2,1)} %copy-done, bf16[512,2048]{1,0:T(8,128)(2,1)} %collective-permute-done.13.far_ref.refs_1_.refs_3_, bf16[512,2048]{1,0:T(8,128)(2,1)} %copy-done, bf16[512,2048]{1,0:T(8,128)(2,1)} %collective-permute-done.13.far_ref.refs_1_.refs_3_, ...), custom_call_target="tpu_custom_call" | custom-call | flops 2415919104 | bytes 10485760 | tf_op jit(solution)/shard_map/ring_terms/pallas_call | solution.py:650
  432.0 6.3 ring_terms.36
  442.3 13.1 %collective-permute-done.64.refs_10_ = bf16[256,2304]{1,0:T(8,128)(2,1)S(1)} collective-permute-done((bf16[256,2304]{1,0:T(8,128)(2,1)}, bf16[256,2304]{1,0:T(8,128)(2,1)S(1)}, u32[]{:S(2)}, u32[]{:S(2)}) %collective-permute-start.64) | collective-permute-done | bytes 1179680 | tf_op jit(solution)/shard_map/ppermute | solution.py:81
  457.0 7.5 %ring_terms.33 = (bf16[256,2304]{1,0:T(8,128)(2,1)}, bf16[256,2304]{1,0:T(8,128)(2,1)}) custom-call(bf16[512,2048]{1,0:T(8,128)(2,1)} %copy-done, bf16[512,2048]{1,0:T(8,128)(2,1)} %collective-permute-done.13.far_ref.refs_1_.refs_3_, bf16[512,2048]{1,0:T(8,128)(2,1)} %copy-done, bf16[512,2048]{1,0:T(8,128)(2,1)} %collective-permute-done.13.far_ref.refs_1_.refs_3_, ...), custom_call_target="tpu_custom_call" | custom-call | flops 2415919104 | bytes 10485760 | tf_op jit(solution)/shard_map/ring_terms/pallas_call | solution.py:650
  466.5 10.1 %collective-permute-done.72.refs_10_ = bf16[256,1920]{1,0:T(8,128)(2,1)} collective-permute-done((bf16[256,1920]{1,0:T(8,128)(2,1)}, bf16[256,1920]{1,0:T(8,128)(2,1)}, u32[]{:S(2)}, u32[]{:S(2)}) %collective-permute-start.72) | collective-permute-done | bytes 983072 | tf_op jit(solution)/shard_map/ppermute | solution.py:81
  478.1 6.7 ring_terms.37
  486.8 4.8 fusion.17
  491.6 29.6 %collective-permute-done.74.refs_10_ = bf16[256,1920]{1,0:T(8,128)(2,1)} collective-permute-done((bf16[256,1920]{1,0:T(8,128)(2,1)}, bf16[256,1920]{1,0:T(8,128)(2,1)}, u32[]{:S(2)}, u32[]{:S(2)}) %collective-permute-start.74) | collective-permute-done | bytes 983072 | tf_op jit(solution)/shard_map/ppermute | solution.py:81
  522.4 6.7 ring_terms.38
  532.2 5.8 ring_terms.34
  538.8 29.1 %attention_backward.1 = (bf16[1024,512]{1,0:T(8,128)(2,1)}, bf16[1024,128]{1,0:T(8,128)(2,1)}) custom-call(s32[4]{0:T(128)} %fusion.15.places_ref, s32[6]{0:T(128)} %bitcast.17, s32[1]{0:T(128)S(6)} %copy.32.live_ref, bf16[512,2048]{1,0:T(8,128)(2,1)} %copy-done.4, bf16[512,2048]{1,0:T(8,128)(2,1)} %collective-permute-done.37.far_ref.refs_1_.refs_3_, ...), custom_call_target="tpu_custom_call" | custom-call | flops 18253611008 | bytes 20971520 | tf_op jit(solution)/shard_map/attention_backward/pallas_call | solution.py:39
  568.0 10.0 %heads_back.1 = (bf16[1024,2048]{1,0:T(8,128)(2,1)}, f32[8,2048]{1,0:T(8,128)}) custom-call(bf16[1024,512]{1,0:T(8,128)(2,1)} %get-tuple-element.93.grad_q_ref.refs_2_.refs_4_, bf16[1024,128]{1,0:T(8,128)(2,1)} %get-tuple-element.94.grad_kv_ref.refs_3_.refs_5_, bf16[512,2048]{1,0:T(8,128)(2,1)} %copy-done.17, ...), custom_call_target="tpu_custom_call" | custom-call | flops 2684354560 | bytes 14680064 | tf_op jit(solution)/shard_map/heads_back/pallas_call | solution.py:39
  598.1 5.3 ring_terms.39
  608.1 3.5 ring_terms.21
  623.0 3.7 ring_terms.22
  630.3 3.4 ring_terms.28
  642.0 3.7 ring_terms.23
  651.3 5.2 collective-permute-done.46.refs_5_
  667.5 5.7 collective-permute-done.48
  676.0 10.8 %unpack_mlp.1 = (f32[256,5632]{1,0:T(8,128)}, f32[256,5632]{1,0:T(8,128)}, f32[5632,256]{1,0:T(8,128)}) custom-call(s32[4]{0:T(128)} %fusion.15.places_ref, bf16[512,2304]{1,0:T(8,128)(2,1)} %copy-done.14, bf16[512,2304]{1,0:T(8,128)(2,1)} %collective-permute-done.69.refs_1_, bf16[512,1920]{1,0:T(8,128)(2,1)} %pad_maximum_fusion.3.refs_2_, ...), custom_call_target="tpu_custom_call" | custom-call | tf_op jit(solution)/shard_map/unpack_mlp/pallas_call | solution.py:697
  686.8 4.3 unpack_heads.1
  700.8 6.4 permute_features.3
  (356 shorter events, 185.0 us)
Async XLA Ops:
  12.1 26.5 %collective-permute-start = (bf16[256,2048]{1,0:T(8,128)(2,1)}, bf16[256,2048]{1,0:T(8,128)(2,1)}, u32[]{:S(2)}, u32[]{:S(2)}) collective-permute-start(bf16[256,2048]{1,0:T(8,128)(2,1)} %get-tuple-element.78), channel_id=1, source_target_pairs={{0,2},{1,3},{2,0},{3,1},{4,6},{5,7},{6,4},{7,5},{8,10},{9,11},{10,... | collective-permute-start | bytes 3145736 | tf_op jit(solution)/shard_map/ppermute | solution.py:106
  18.7 21.3 %collective-permute-start.2 = (bf16[272,1152]{1,0:T(8,128)(2,1)}, bf16[272,1152]{1,0:T(8,128)(2,1)}, u32[]{:S(2)}, u32[]{:S(2)}) collective-permute-start(bf16[272,1152]{1,0:T(8,128)(2,1)} %pack_heads.1.refs_0_), channel_id=1, source_target_pairs={{0,8},{8,16},{16,24},{24,28},{28,20},{20,12},{12,4},{4,0},{1,9},{9... | collective-permute-start | bytes 1880072 | tf_op jit(solution)/shard_map/ppermute | solution.py:81
  20.3 21.5 %collective-permute-start.5 = (bf16[272,1152]{1,0:T(8,128)(2,1)}, bf16[272,1152]{1,0:T(8,128)(2,1)}, u32[]{:S(2)}, u32[]{:S(2)}) collective-permute-start(bf16[272,1152]{1,0:T(8,128)(2,1)} %pack_heads.1.refs_0_), channel_id=1, source_target_pairs={{8,0},{16,8},{24,16},{28,24},{20,28},{12,20},{4,12},{0,4},{9,1},{1... | collective-permute-start | bytes 1880072 | tf_op jit(solution)/shard_map/ppermute | solution.py:84
  39.9 42.1 %collective-permute-start.1 = (bf16[512,2048]{1,0:T(8,128)(2,1)S(1)}, bf16[512,2048]{1,0:T(8,128)(2,1)}, u32[]{:S(2)}, u32[]{:S(2)}) collective-permute-start(bf16[512,2048]{1,0:T(8,128)(2,1)S(1)} %constant_dynamic-update-slice_fusion.near_ref), channel_id=1, source_target_pairs={{0,1},{1,0},{2,3},{3,2},{4,5},{5,4},{6,7},{7,6},{8,9},{9,8},{10,11... | collective-permute-start | bytes 6291464 | tf_op jit(solution)/shard_map/ppermute | solution.py:106
  121.6 29.0 %collective-permute-start.24 = (bf16[256,2304]{1,0:T(8,128)(2,1)}, bf16[256,2304]{1,0:T(8,128)(2,1)S(1)}, u32[]{:S(2)}, u32[]{:S(2)}) collective-permute-start(bf16[256,2304]{1,0:T(8,128)(2,1)} %get-tuple-element.83.refs_0_), channel_id=1, source_target_pairs={{0,8},{8,16},{16,24},{24,28},{28,20},{20,12},{12,4},{4,0},{1,9},{9... | collective-permute-start | bytes 3538952 | tf_op jit(solution)/shard_map/ppermute | solution.py:81
  126.4 25.6 %collective-permute-start.11 = (bf16[256,2048]{1,0:T(8,128)(2,1)S(1)}, bf16[256,2048]{1,0:T(8,128)(2,1)S(1)}, u32[]{:S(2)}, u32[]{:S(2)}) collective-permute-start(bf16[256,2048]{1,0:T(8,128)(2,1)S(1)} %slice.216), channel_id=1, source_target_pairs={{0,2},{1,3},{2,0},{3,1},{4,6},{5,7},{6,4},{7,5},{8,10},{9,11},{10,... | collective-permute-start | bytes 3145736 | tf_op jit(solution)/shard_map/ppermute | solution.py:106
  128.0 43.6 %collective-permute-start.16 = (bf16[256,1920]{1,0:T(8,128)(2,1)S(1)}, bf16[256,1920]{1,0:T(8,128)(2,1)S(1)}, u32[]{:S(2)}, u32[]{:S(2)}) collective-permute-start(bf16[256,1920]{1,0:T(8,128)(2,1)S(1)} %copy-done.60), channel_id=1, source_target_pairs={{0,8},{8,16},{16,24},{24,28},{28,20},{20,12},{12,4},{4,0},{1,9},{9... | collective-permute-start | bytes 2949128 | tf_op jit(solution)/shard_map/ppermute | solution.py:81
  129.6 43.5 %collective-permute-start.19 = (bf16[256,1920]{1,0:T(8,128)(2,1)S(1)}, bf16[256,1920]{1,0:T(8,128)(2,1)S(1)}, u32[]{:S(2)}, u32[]{:S(2)}) collective-permute-start(bf16[256,1920]{1,0:T(8,128)(2,1)S(1)} %copy-done.60), channel_id=1, source_target_pairs={{8,0},{16,8},{24,16},{28,24},{20,28},{12,20},{4,12},{0,4},{9,1},{1... | collective-permute-start | bytes 2949128 | tf_op jit(solution)/shard_map/ppermute | solution.py:84
  130.1 48.1 %collective-permute-start.27 = (bf16[256,2304]{1,0:T(8,128)(2,1)S(1)}, bf16[256,2304]{1,0:T(8,128)(2,1)S(1)}, u32[]{:S(2)}, u32[]{:S(2)}) collective-permute-start(bf16[256,2304]{1,0:T(8,128)(2,1)S(1)} %copy-done.55), channel_id=1, source_target_pairs={{8,0},{16,8},{24,16},{28,24},{20,28},{12,20},{4,12},{0,4},{9,1},{1... | collective-permute-start | bytes 3538952 | tf_op jit(solution)/shard_map/ppermute | solution.py:84
  150.5 28.3 %collective-permute-start.14 = (bf16[256,2048]{1,0:T(8,128)(2,1)S(1)}, bf16[256,2048]{1,0:T(8,128)(2,1)S(1)}, u32[]{:S(2)}, u32[]{:S(2)}) collective-permute-start(bf16[256,2048]{1,0:T(8,128)(2,1)S(1)} %copy-done.18), channel_id=1, source_target_pairs={{0,2},{1,3},{2,0},{3,1},{4,6},{5,7},{6,4},{7,5},{8,10},{9,11},{10,... | collective-permute-start | bytes 3145736 | tf_op jit(solution)/shard_map/ppermute | solution.py:106
  152.1 44.8 %collective-permute-start.25 = (bf16[256,2304]{1,0:T(8,128)(2,1)S(1)}, bf16[256,2304]{1,0:T(8,128)(2,1)S(1)}, u32[]{:S(2)}, u32[]{:S(2)}) collective-permute-start(bf16[256,2304]{1,0:T(8,128)(2,1)S(1)} %collective-permute-done.24.refs_1_), channel_id=1, source_target_pairs={{0,8},{8,16},{16,24},{24,28},{28,20},{20,12},{12,4},{4,0},{1,9},{9... | collective-permute-start | bytes 3538952 | tf_op jit(solution)/shard_map/ppermute | solution.py:81
  171.6 25.8 %collective-permute-start.12 = (bf16[256,2048]{1,0:T(8,128)(2,1)S(1)}, bf16[256,2048]{1,0:T(8,128)(2,1)S(1)}, u32[]{:S(2)}, u32[]{:S(2)}) collective-permute-start(bf16[256,2048]{1,0:T(8,128)(2,1)S(1)} %multiply_convert_fusion), channel_id=1, source_target_pairs={{0,2},{1,3},{2,0},{3,1},{4,6},{5,7},{6,4},{7,5},{8,10},{9,11},{10,... | collective-permute-start | bytes 3145736 | tf_op jit(solution)/shard_map/ppermute | solution.py:106
  173.1 44.8 %collective-permute-start.17 = (bf16[256,1920]{1,0:T(8,128)(2,1)S(1)}, bf16[256,1920]{1,0:T(8,128)(2,1)S(1)}, u32[]{:S(2)}, u32[]{:S(2)}) collective-permute-start(bf16[256,1920]{1,0:T(8,128)(2,1)S(1)} %collective-permute-done.16.refs_1_), channel_id=1, source_target_pairs={{0,8},{8,16},{16,24},{24,28},{28,20},{20,12},{12,4},{4,0},{1,9},{9... | collective-permute-start | bytes 2949128 | tf_op jit(solution)/shard_map/ppermute | solution.py:81
  178.2 39.7 %collective-permute-start.28 = (bf16[256,2304]{1,0:T(8,128)(2,1)S(1)}, bf16[256,2304]{1,0:T(8,128)(2,1)S(1)}, u32[]{:S(2)}, u32[]{:S(2)}) collective-permute-start(bf16[256,2304]{1,0:T(8,128)(2,1)S(1)} %collective-permute-done.27.refs_4_), channel_id=1, source_target_pairs={{8,0},{16,8},{24,16},{28,24},{20,28},{12,20},{4,12},{0,4},{9,1},{1... | collective-permute-start | bytes 3538952 | tf_op jit(solution)/shard_map/ppermute | solution.py:84
  178.8 49.4 %collective-permute-start.20 = (bf16[256,1920]{1,0:T(8,128)(2,1)S(1)}, bf16[256,1920]{1,0:T(8,128)(2,1)S(1)}, u32[]{:S(2)}, u32[]{:S(2)}) collective-permute-start(bf16[256,1920]{1,0:T(8,128)(2,1)S(1)} %collective-permute-done.19.refs_4_), channel_id=1, source_target_pairs={{8,0},{16,8},{24,16},{28,24},{20,28},{12,20},{4,12},{0,4},{9,1},{1... | collective-permute-start | bytes 2949128 | tf_op jit(solution)/shard_map/ppermute | solution.py:84
  196.9 79.2 %collective-permute-start.15 = (bf16[512,2048]{1,0:T(8,128)(2,1)S(1)}, bf16[512,2048]{1,0:T(8,128)(2,1)S(1)}, u32[]{:S(2)}, u32[]{:S(2)}) collective-permute-start(bf16[512,2048]{1,0:T(8,128)(2,1)S(1)} %constant_dynamic-update-slice_fusion.2.cot_near_ref.refs_3_.refs_5_.refs_7_), channel_id=1, source_target_pairs={{0,1},{1,0},{2,3},{3,2},{4,5},{5,4},{6,7},{7,6},{8,9},{9,8},{10,11... | collective-permute-start | bytes 6291464 | tf_op jit(solution)/shard_map/ppermute | solution.py:106
  197.4 45.8 %collective-permute-start.26 = (bf16[256,2304]{1,0:T(8,128)(2,1)S(1)}, bf16[256,2304]{1,0:T(8,128)(2,1)S(1)}, u32[]{:S(2)}, u32[]{:S(2)}) collective-permute-start(bf16[256,2304]{1,0:T(8,128)(2,1)S(1)} %collective-permute-done.25.refs_2_), channel_id=1, source_target_pairs={{0,8},{8,16},{16,24},{24,28},{28,20},{20,12},{12,4},{4,0},{1,9},{9... | collective-permute-start | bytes 3538952 | tf_op jit(solution)/shard_map/ppermute | solution.py:81
  218.0 70.1 %collective-permute-start.13 = (bf16[512,2048]{1,0:T(8,128)(2,1)S(1)}, bf16[512,2048]{1,0:T(8,128)(2,1)}, u32[]{:S(2)}, u32[]{:S(2)}) collective-permute-start(bf16[512,2048]{1,0:T(8,128)(2,1)S(1)} %pad_maximum_fusion.1.near_ref.refs_0_.refs_2_), channel_id=1, source_target_pairs={{0,1},{1,0},{2,3},{3,2},{4,5},{5,4},{6,7},{7,6},{8,9},{9,8},{10,11... | collective-permute-start | bytes 6291464 | tf_op jit(solution)/shard_map/ppermute | solution.py:106
  218.0 35.5 %collective-permute-start.29 = (bf16[256,2304]{1,0:T(8,128)(2,1)S(1)}, bf16[256,2304]{1,0:T(8,128)(2,1)S(1)}, u32[]{:S(2)}, u32[]{:S(2)}) collective-permute-start(bf16[256,2304]{1,0:T(8,128)(2,1)S(1)} %collective-permute-done.28.refs_5_), channel_id=1, source_target_pairs={{8,0},{16,8},{24,16},{28,24},{20,28},{12,20},{4,12},{0,4},{9,1},{1... | collective-permute-start | bytes 3538952 | tf_op jit(solution)/shard_map/ppermute | solution.py:84
  228.2 36.1 %collective-permute-start.18 = (bf16[256,1920]{1,0:T(8,128)(2,1)S(1)}, bf16[256,1920]{1,0:T(8,128)(2,1)S(1)}, u32[]{:S(2)}, u32[]{:S(2)}) collective-permute-start(bf16[256,1920]{1,0:T(8,128)(2,1)S(1)} %collective-permute-done.17.refs_2_), channel_id=1, source_target_pairs={{0,8},{8,16},{16,24},{24,28},{28,20},{20,12},{12,4},{4,0},{1,9},{9... | collective-permute-start | bytes 2949128 | tf_op jit(solution)/shard_map/ppermute | solution.py:81
  243.2 31.3 %collective-permute-start.21 = (bf16[256,1920]{1,0:T(8,128)(2,1)S(1)}, bf16[256,1920]{1,0:T(8,128)(2,1)S(1)}, u32[]{:S(2)}, u32[]{:S(2)}) collective-permute-start(bf16[256,1920]{1,0:T(8,128)(2,1)S(1)} %collective-permute-done.20.refs_5_), channel_id=1, source_target_pairs={{8,0},{16,8},{24,16},{28,24},{20,28},{12,20},{4,12},{0,4},{9,1},{1... | collective-permute-start | bytes 2949128 | tf_op jit(solution)/shard_map/ppermute | solution.py:84
  253.5 24.5 %collective-permute-start.30 = (bf16[128,2304]{1,0:T(8,128)(2,1)S(1)}, bf16[128,2304]{1,0:T(8,128)(2,1)S(1)}, u32[]{:S(2)}, u32[]{:S(2)}) collective-permute-start(bf16[128,2304]{1,0:T(8,128)(2,1)S(1)} %slice.163), channel_id=1, source_target_pairs={{0,8},{8,16},{16,24},{24,28},{28,20},{20,12},{12,4},{4,0},{1,9},{9... | collective-permute-start | bytes 1769480 | tf_op jit(solution)/shard_map/ppermute | solution.py:81
  264.3 22.9 %collective-permute-start.31 = (bf16[128,2304]{1,0:T(8,128)(2,1)S(1)}, bf16[128,2304]{1,0:T(8,128)(2,1)S(1)}, u32[]{:S(2)}, u32[]{:S(2)}) collective-permute-start(bf16[128,2304]{1,0:T(8,128)(2,1)S(1)} %slice.164), channel_id=1, source_target_pairs={{8,0},{16,8},{24,16},{28,24},{20,28},{12,20},{4,12},{0,4},{9,1},{1... | collective-permute-start | bytes 1769480 | tf_op jit(solution)/shard_map/ppermute | solution.py:84
  274.6 41.6 %collective-permute-start.22 = (bf16[128,1920]{1,0:T(8,128)(2,1)S(1)}, bf16[128,1920]{1,0:T(8,128)(2,1)}, u32[]{:S(2)}, u32[]{:S(2)}) collective-permute-start(bf16[128,1920]{1,0:T(8,128)(2,1)S(1)} %slice.161), channel_id=1, source_target_pairs={{0,8},{8,16},{16,24},{24,28},{28,20},{20,12},{12,4},{4,0},{1,9},{9... | collective-permute-start | bytes 1474568 | tf_op jit(solution)/shard_map/ppermute | solution.py:81
  277.5 38.6 %collective-permute-start.23 = (bf16[128,1920]{1,0:T(8,128)(2,1)S(1)}, bf16[128,1920]{1,0:T(8,128)(2,1)}, u32[]{:S(2)}, u32[]{:S(2)}) collective-permute-start(bf16[128,1920]{1,0:T(8,128)(2,1)S(1)} %slice.162), channel_id=1, source_target_pairs={{8,0},{16,8},{24,16},{28,24},{20,28},{12,20},{4,12},{0,4},{9,1},{1... | collective-permute-start | bytes 1474568 | tf_op jit(solution)/shard_map/ppermute | solution.py:84
  358.4 26.4 %collective-permute-start.35 = (bf16[256,2048]{1,0:T(8,128)(2,1)}, bf16[256,2048]{1,0:T(8,128)(2,1)}, u32[]{:S(2)}, u32[]{:S(2)}) collective-permute-start(bf16[256,2048]{1,0:T(8,128)(2,1)} %slice.214), channel_id=1, source_target_pairs={{0,2},{1,3},{2,0},{3,1},{4,6},{5,7},{6,4},{7,5},{8,10},{9,11},{10,... | collective-permute-start | bytes 3145736 | tf_op jit(solution)/shard_map/ppermute | solution.py:106
  364.3 41.4 %collective-permute-start.33 = (bf16[256,2048]{1,0:T(8,128)(2,1)}, bf16[256,2048]{1,0:T(8,128)(2,1)}, u32[]{:S(2)}, u32[]{:S(2)}) collective-permute-start(bf16[256,2048]{1,0:T(8,128)(2,1)} %slice.215), channel_id=1, source_target_pairs={{0,2},{1,3},{2,0},{3,1},{4,6},{5,7},{6,4},{7,5},{8,10},{9,11},{10,... | collective-permute-start | bytes 3145736 | tf_op jit(solution)/shard_map/ppermute | solution.py:106
  375.8 43.1 %collective-permute-start.62 = (bf16[256,2304]{1,0:T(8,128)(2,1)}, bf16[256,2304]{1,0:T(8,128)(2,1)}, u32[]{:S(2)}, u32[]{:S(2)}) collective-permute-start(bf16[256,2304]{1,0:T(8,128)(2,1)} %get-tuple-element.126), channel_id=1, source_target_pairs={{0,8},{8,16},{16,24},{24,28},{28,20},{20,12},{12,4},{4,0},{1,9},{9... | collective-permute-start | bytes 3538952 | tf_op jit(solution)/shard_map/ppermute | solution.py:81
  376.8 42.1 %collective-permute-start.63 = (bf16[256,2304]{1,0:T(8,128)(2,1)}, bf16[256,2304]{1,0:T(8,128)(2,1)}, u32[]{:S(2)}, u32[]{:S(2)}) collective-permute-start(bf16[256,2304]{1,0:T(8,128)(2,1)} %get-tuple-element.127), channel_id=1, source_target_pairs={{8,0},{16,8},{24,16},{28,24},{20,28},{12,20},{4,12},{0,4},{9,1},{1... | collective-permute-start | bytes 3538952 | tf_op jit(solution)/shard_map/ppermute | solution.py:84
  410.9 29.6 %collective-permute-start.36 = (bf16[256,2048]{1,0:T(8,128)(2,1)}, bf16[256,2048]{1,0:T(8,128)(2,1)}, u32[]{:S(2)}, u32[]{:S(2)}) collective-permute-start(bf16[256,2048]{1,0:T(8,128)(2,1)} %get-tuple-element.149), channel_id=1, source_target_pairs={{0,2},{1,3},{2,0},{3,1},{4,6},{5,7},{6,4},{7,5},{8,10},{9,11},{10,... | collective-permute-start | bytes 3145736 | tf_op jit(solution)/shard_map/ppermute | solution.py:106
  426.3 29.1 %collective-permute-start.64 = (bf16[256,2304]{1,0:T(8,128)(2,1)}, bf16[256,2304]{1,0:T(8,128)(2,1)S(1)}, u32[]{:S(2)}, u32[]{:S(2)}) collective-permute-start(bf16[256,2304]{1,0:T(8,128)(2,1)} %get-tuple-element.128), channel_id=1, source_target_pairs={{0,8},{8,16},{16,24},{24,28},{28,20},{20,12},{12,4},{4,0},{1,9},{9... | collective-permute-start | bytes 3538952 | tf_op jit(solution)/shard_map/ppermute | solution.py:81
  427.8 29.2 %collective-permute-start.65 = (bf16[256,2304]{1,0:T(8,128)(2,1)}, bf16[256,2304]{1,0:T(8,128)(2,1)}, u32[]{:S(2)}, u32[]{:S(2)}) collective-permute-start(bf16[256,2304]{1,0:T(8,128)(2,1)} %get-tuple-element.129), channel_id=1, source_target_pairs={{8,0},{16,8},{24,16},{28,24},{20,28},{12,20},{4,12},{0,4},{9,1},{1... | collective-permute-start | bytes 3538952 | tf_op jit(solution)/shard_map/ppermute | solution.py:84
  438.3 38.2 %collective-permute-start.72 = (bf16[256,1920]{1,0:T(8,128)(2,1)}, bf16[256,1920]{1,0:T(8,128)(2,1)}, u32[]{:S(2)}, u32[]{:S(2)}) collective-permute-start(bf16[256,1920]{1,0:T(8,128)(2,1)} %get-tuple-element.136), channel_id=1, source_target_pairs={{0,8},{8,16},{16,24},{24,28},{28,20},{20,12},{12,4},{4,0},{1,9},{9... | collective-permute-start | bytes 2949128 | tf_op jit(solution)/shard_map/ppermute | solution.py:81
  439.4 38.7 %collective-permute-start.73 = (bf16[256,1920]{1,0:T(8,128)(2,1)}, bf16[256,1920]{1,0:T(8,128)(2,1)}, u32[]{:S(2)}, u32[]{:S(2)}) collective-permute-start(bf16[256,1920]{1,0:T(8,128)(2,1)} %get-tuple-element.137), channel_id=1, source_target_pairs={{8,0},{16,8},{24,16},{28,24},{20,28},{12,20},{4,12},{0,4},{9,1},{1... | collective-permute-start | bytes 2949128 | tf_op jit(solution)/shard_map/ppermute | solution.py:84
  442.2 96.6 %collective-permute-start.37 = (bf16[512,2048]{1,0:T(8,128)(2,1)S(1)}, bf16[512,2048]{1,0:T(8,128)(2,1)}, u32[]{:S(2)}, u32[]{:S(2)}) collective-permute-start(bf16[512,2048]{1,0:T(8,128)(2,1)S(1)} %pad_maximum_fusion.2.near_ref.refs_0_.refs_2_), channel_id=1, source_target_pairs={{0,1},{1,0},{2,3},{3,2},{4,5},{5,4},{6,7},{7,6},{8,9},{9,8},{10,11... | collective-permute-start | bytes 6291464 | tf_op jit(solution)/shard_map/ppermute | solution.py:106
  464.5 66.7 %collective-permute-start.66 = (bf16[256,2304]{1,0:T(8,128)(2,1)}, bf16[256,2304]{1,0:T(8,128)(2,1)S(1)}, u32[]{:S(2)}, u32[]{:S(2)}) collective-permute-start(bf16[256,2304]{1,0:T(8,128)(2,1)} %get-tuple-element.130), channel_id=1, source_target_pairs={{0,8},{8,16},{16,24},{24,28},{28,20},{20,12},{12,4},{4,0},{1,9},{9... | collective-permute-start | bytes 3538952 | tf_op jit(solution)/shard_map/ppermute | solution.py:81
  465.5 65.7 %collective-permute-start.67 = (bf16[256,2304]{1,0:T(8,128)(2,1)}, bf16[256,2304]{1,0:T(8,128)(2,1)}, u32[]{:S(2)}, u32[]{:S(2)}) collective-permute-start(bf16[256,2304]{1,0:T(8,128)(2,1)} %get-tuple-element.131), channel_id=1, source_target_pairs={{8,0},{16,8},{24,16},{28,24},{20,28},{12,20},{4,12},{0,4},{9,1},{1... | collective-permute-start | bytes 3538952 | tf_op jit(solution)/shard_map/ppermute | solution.py:84
  484.7 36.5 %collective-permute-start.74 = (bf16[256,1920]{1,0:T(8,128)(2,1)}, bf16[256,1920]{1,0:T(8,128)(2,1)}, u32[]{:S(2)}, u32[]{:S(2)}) collective-permute-start(bf16[256,1920]{1,0:T(8,128)(2,1)} %get-tuple-element.138), channel_id=1, source_target_pairs={{0,8},{8,16},{16,24},{24,28},{28,20},{20,12},{12,4},{4,0},{1,9},{9... | collective-permute-start | bytes 2949128 | tf_op jit(solution)/shard_map/ppermute | solution.py:81
  485.8 36.7 %collective-permute-start.75 = (bf16[256,1920]{1,0:T(8,128)(2,1)}, bf16[256,1920]{1,0:T(8,128)(2,1)}, u32[]{:S(2)}, u32[]{:S(2)}) collective-permute-start(bf16[256,1920]{1,0:T(8,128)(2,1)} %get-tuple-element.139), channel_id=1, source_target_pairs={{8,0},{16,8},{24,16},{28,24},{20,28},{12,20},{4,12},{0,4},{9,1},{1... | collective-permute-start | bytes 2949128 | tf_op jit(solution)/shard_map/ppermute | solution.py:84
  529.1 65.4 %collective-permute-start.76 = (bf16[256,1920]{1,0:T(8,128)(2,1)}, bf16[256,1920]{1,0:T(8,128)(2,1)}, u32[]{:S(2)}, u32[]{:S(2)}) collective-permute-start(bf16[256,1920]{1,0:T(8,128)(2,1)} %get-tuple-element.140), channel_id=1, source_target_pairs={{0,8},{8,16},{16,24},{24,28},{28,20},{20,12},{12,4},{4,0},{1,9},{9... | collective-permute-start | bytes 2949128 | tf_op jit(solution)/shard_map/ppermute | solution.py:81
  530.1 65.9 %collective-permute-start.77 = (bf16[256,1920]{1,0:T(8,128)(2,1)}, bf16[256,1920]{1,0:T(8,128)(2,1)}, u32[]{:S(2)}, u32[]{:S(2)}) collective-permute-start(bf16[256,1920]{1,0:T(8,128)(2,1)} %get-tuple-element.141), channel_id=1, source_target_pairs={{8,0},{16,8},{24,16},{28,24},{20,28},{12,20},{4,12},{0,4},{9,1},{1... | collective-permute-start | bytes 2949128 | tf_op jit(solution)/shard_map/ppermute | solution.py:84
  538.0 88.6 %collective-permute-start.68 = (bf16[256,2304]{1,0:T(8,128)(2,1)}, bf16[256,2304]{1,0:T(8,128)(2,1)}, u32[]{:S(2)}, u32[]{:S(2)}) collective-permute-start(bf16[256,2304]{1,0:T(8,128)(2,1)} %ring_terms.34), channel_id=1, source_target_pairs={{0,2},{1,3},{2,0},{3,1},{4,6},{5,7},{6,4},{7,5},{8,10},{9,11},{10,... | collective-permute-start | bytes 3538952 | tf_op jit(solution)/shard_map/ppermute | solution.py:106
  590.8 71.4 %collective-permute-start.38 = (bf16[512,2048]{1,0:T(8,128)(2,1)}, bf16[512,2048]{1,0:T(8,128)(2,1)}, u32[]{:S(2)}, u32[]{:S(2)}) collective-permute-start(bf16[512,2048]{1,0:T(8,128)(2,1)} %slice.136), channel_id=1, source_target_pairs={{0,1},{1,0},{2,3},{3,2},{4,5},{5,4},{6,7},{7,6},{8,9},{9,8},{10,11... | collective-permute-start | bytes 6291464 | tf_op jit(solution)/shard_map/ppermute | solution.py:106
  596.0 17.1 %collective-permute-start.53 = (bf16[256,512]{1,0:T(8,128)(2,1)}, bf16[256,512]{1,0:T(8,128)(2,1)S(1)}, u32[]{:S(2)}, u32[]{:S(2)}) collective-permute-start(bf16[256,512]{1,0:T(8,128)(2,1)} %get-tuple-element.112), channel_id=1, source_target_pairs={{8,0},{16,8},{24,16},{28,24},{20,28},{12,20},{4,12},{0,4},{9,1},{1... | collective-permute-start | bytes 786440 | tf_op jit(solution)/shard_map/ppermute | solution.py:84
  606.8 26.8 %collective-permute-start.78 = (bf16[256,1920]{1,0:T(8,128)(2,1)}, bf16[256,1920]{1,0:T(8,128)(2,1)}, u32[]{:S(2)}, u32[]{:S(2)}) collective-permute-start(bf16[256,1920]{1,0:T(8,128)(2,1)} %ring_terms.39), channel_id=1, source_target_pairs={{0,2},{1,3},{2,0},{3,1},{4,6},{5,7},{6,4},{7,5},{8,10},{9,11},{10,... | collective-permute-start | bytes 2949128 | tf_op jit(solution)/shard_map/ppermute | solution.py:106
  629.4 46.6 %collective-permute-start.69 = (bf16[512,2304]{1,0:T(8,128)(2,1)S(1)}, bf16[512,2304]{1,0:T(8,128)(2,1)}, u32[]{:S(2)}, u32[]{:S(2)}) collective-permute-start(bf16[512,2304]{1,0:T(8,128)(2,1)S(1)} %pad_maximum_fusion.refs_0_), channel_id=1, source_target_pairs={{0,1},{1,0},{2,3},{3,2},{4,5},{5,4},{6,7},{7,6},{8,9},{9,8},{10,11... | collective-permute-start | bytes 7077896 | tf_op jit(solution)/shard_map/ppermute | solution.py:106
  640.8 35.2 %collective-permute-start.79 = (bf16[512,1920]{1,0:T(8,128)(2,1)}, bf16[512,1920]{1,0:T(8,128)(2,1)}, u32[]{:S(2)}, u32[]{:S(2)}) collective-permute-start(bf16[512,1920]{1,0:T(8,128)(2,1)} %pad_maximum_fusion.3.refs_2_), channel_id=1, source_target_pairs={{0,1},{1,0},{2,3},{3,2},{4,5},{5,4},{6,7},{7,6},{8,9},{9,8},{10,11... | collective-permute-start | bytes 5898248 | tf_op jit(solution)/shard_map/ppermute | solution.py:106
  666.5 28.2 %collective-permute-start.39 = (bf16[256,2048]{1,0:T(8,128)(2,1)}, bf16[256,2048]{1,0:T(8,128)(2,1)}, u32[]{:S(2)}, u32[]{:S(2)}) collective-permute-start(bf16[256,2048]{1,0:T(8,128)(2,1)} %slice.213), channel_id=1, source_target_pairs={{0,2},{1,3},{2,0},{3,1},{4,6},{5,7},{6,4},{7,5},{8,10},{9,11},{10,... | collective-permute-start | bytes 3145736 | tf_op jit(solution)/shard_map/ppermute | solution.py:106
  (103 other events, 1367.4 us)

commit v3 on v2

v3 whole, which is shorter than its diff:
```python
import functools

import jax
import jax.numpy as jnp
from jax import lax
from jax.experimental import pallas as pl
from jax.experimental.pallas import tpu as pltpu
from jax.sharding import PartitionSpec as P

HEADS = 32
HD = 64
KVH = 4
EPS = 1e-05
TOP = 16
BF = jnp.bfloat16
F32 = jnp.float32
NEG = -1e30
VMEM_LIMIT = 60 << 20
COST = pl.CostEstimate(flops=1000, transcendentals=0, bytes_accessed=1000)


def dot(left_side, right_side):
    return jnp.dot(left_side, right_side, preferred_element_type=F32)


def cross(left_side, right_side):
    return lax.dot_general(
        left_side, right_side, (((0,), (0,)), ((), ())), preferred_element_type=F32
    )


def against(left_side, right_side):
    return lax.dot_general(
        left_side, right_side, (((1,), (1,)), ((), ())), preferred_element_type=F32
    )


def kernel_call(body, outs, scratch=(), flops=0, moved=0, smem=0, args=(), name=None):
    vmem = pl.BlockSpec(memory_space=pltpu.VMEM)
    return pl.pallas_call(
        body,
        out_shape=tuple(jax.ShapeDtypeStruct(s, d) for s, d in outs),
        in_specs=[pl.BlockSpec(memory_space=pltpu.SMEM)] * smem + [vmem] * (len(args) - smem),
        out_specs=tuple(vmem for _ in outs),
        scratch_shapes=list(scratch),
        compiler_params=pltpu.CompilerParams(vmem_limit_bytes=VMEM_LIMIT),
        cost_estimate=COST,
        name=name,
    )(*args)


class Ring:
    def __init__(self, size):
        self.size = size
        self.half = size // 2
        self.order = list(range(0, size, 2)) + list(range(size - 1, 0, -2))
        place = [0] * size
        for position, device in enumerate(self.order):
            place[device] = position
        self.place = place
        walk = [(self.order[i], self.order[(i + 1) % size]) for i in range(size)]
        self.up = walk
        self.down = [(b, a) for a, b in walk]
        self.steps = (
            [-t for t in range(self.half)] + [t for t in range(1, self.half)] + [self.half]
        )

    def slot_owners(self):
        mine = jnp.asarray(self.place, jnp.int32)[lax.axis_index("dp")]
        wanted = (mine + jnp.asarray(self.steps, jnp.int32)) % self.size
        return jnp.asarray(self.order, jnp.int32)[wanted]

    def owner_slots(self):
        mine = jnp.asarray(self.place, jnp.int32)[lax.axis_index("dp")]
        slot_of_step = [0] * self.size
        for slot, step in enumerate(self.steps):
            slot_of_step[step % self.size] = slot
        step = (jnp.asarray(self.place, jnp.int32) - mine) % self.size
        return jnp.asarray(slot_of_step, jnp.int32)[step]

    def go_up(self, block):
        return lax.ppermute(block, "dp", self.up)

    def go_down(self, block):
        return lax.ppermute(block, "dp", self.down)


class Clock:
    def __init__(self):
        self.last = None

    def tie(self, *arrays):
        if self.last is None:
            out = lax.optimization_barrier(arrays)
        else:
            out = lax.optimization_barrier((*arrays, self.last))[: len(arrays)]
        self.last = out[0]
        return out if len(out) > 1 else out[0]

    def done(self, array):
        self.last = array


class Gather:
    def __init__(self, ring, block, cut):
        self.ring, self.cut = ring, cut
        self.up, self.down = [block], [block]
        self.flying = (ring.go_up(block), ring.go_down(block))
        self.left = ring.half - 1

    def land(self, clock):
        up, down = clock.tie(*self.flying)
        self.flying = None
        self.up.append(up)
        self.down.append(down)

    def go(self, clock):
        up, down = clock.tie(self.up[-1], self.down[-1])
        self.left -= 1
        if self.left == 0:
            up, down = up[: self.cut], down[self.cut :]
        self.flying = (self.ring.go_up(up), self.ring.go_down(down))

    def relay(self, clock):
        if self.left:
            self.land(clock)
            self.go(clock)

    def finish(self, clock):
        while self.left:
            self.relay(clock)
        return self.up + self.down[1:] + list(clock.tie(*self.flying))


class Scatter:
    def __init__(self, ring, terms, cut, tile):
        self.ring, self.terms, self.cut, self.tile = ring, terms, cut, tile
        self.full = terms.shape[0] // ring.size
        begin = (ring.size - 1) * self.full
        self.left = ring.half - 1
        self.flying = (
            ring.go_up(terms[begin : begin + cut]),
            ring.go_down(terms[begin + cut : begin + self.full]),
        )

    def term(self, slot, begin=0, end=None):
        end = self.full if end is None else end
        return self.terms[slot * self.full + begin : slot * self.full + end]

    def relay(self, clock):
        if self.left == 0:
            return
        up, down = clock.tie(*self.flying)
        above, below = self.ring.half - 1 + self.left, self.left
        if up.shape[0] == self.full:
            up, down = plus(self.term(above), up), plus(self.term(below), down)
        else:
            up, down = ring_add(self.terms, (above, below), up, down, self.full, self.cut, self.tile)
        self.left -= 1
        up, down = clock.tie(up, down)
        self.flying = (self.ring.go_up(up), self.ring.go_down(down))

    def finish(self, clock):
        while self.left:
            self.relay(clock)
        up, down = clock.tie(*self.flying)
        out = (self.term(0).astype(F32) + up.astype(F32) + down.astype(F32)).astype(BF)
        return clock.tie(out)


def plus(one, two):
    return (one.astype(F32) + two.astype(F32)).astype(BF)


def swap(block, distance):
    return lax.ppermute(block, "seq", [(i, i ^ distance) for i in range(4)])


def fill_weights(pieces, scratch, top, width, columns):
    begin = 0
    for index, piece in enumerate(pieces):
        skip = top if index < len(pieces) - 1 else 0
        count = piece.shape[0] - skip
        scratch[begin : begin + count, :] = piece[skip:, columns]
        begin += count


def put_features(values, order_ref, target, slots, width):
    for j in range(slots):
        to = pl.ds(pl.multiple_of(order_ref[j] * width, 128), width)
        target[:, to] = values[:, j * width : (j + 1) * width]


def blocks_in_order(array, order, size):
    width = array.shape[1] // size
    return jnp.concatenate(
        [lax.dynamic_slice_in_dim(array, order[i] * width, width, 1) for i in range(size)],
        axis=1,
    )


def permute_features(array, order, size):
    width = array.shape[1] // size
    if width % 128:
        return blocks_in_order(array, order, size)

    def body(order_ref, source, target):
        for j in range(size):
            begin = pl.ds(pl.multiple_of(order_ref[j] * width, 128), width)
            target[:, j * width : (j + 1) * width] = source[:, begin]

    return kernel_call(
        body, [(array.shape, array.dtype)], smem=1, args=[order, array], name="permute_features"
    )[0]


def pack_heads(here, w_query, w_key, w_value, w_out, gain_attn, gain_mlp, seq):
    width = w_query.shape[0]
    q_cols, k_cols = w_query.shape[1] // seq, w_key.shape[1] // seq
    total = 2 * q_cols + 2 * k_cols

    def body(here_ref, query_ref, key_ref, value_ref, out_ref, one_ref, two_ref, block_ref):
        s = here_ref[0]
        block_ref[:TOP, :] = jnp.zeros((TOP, total), BF)
        block_ref[:1, :width] = one_ref[...].reshape(1, width)
        block_ref[:1, width : 2 * width] = two_ref[...].reshape(1, width)
        block_ref[TOP:, :q_cols] = query_ref[...]

        def mine(ref):
            part = jnp.zeros((width, k_cols), F32)
            for place in range(seq):
                piece = ref[:, place * k_cols : (place + 1) * k_cols].astype(F32)
                part = jnp.where(s == place, piece, part)
            return part

        both = jnp.concatenate([mine(key_ref), mine(value_ref)], axis=1)
        block_ref[TOP:, q_cols : q_cols + 2 * k_cols] = both.astype(BF)
        block_ref[TOP:, q_cols + 2 * k_cols :] = out_ref[...].astype(F32).T.astype(BF)

    whole = lambda shape: pl.BlockSpec(shape, lambda i, o: (0, 0))
    return pl.pallas_call(
        body,
        out_shape=jax.ShapeDtypeStruct((TOP + width, total), BF),
        grid_spec=pltpu.PrefetchScalarGridSpec(
            num_scalar_prefetch=1,
            grid=(1,),
            in_specs=[
                pl.BlockSpec((width, q_cols), lambda i, o: (0, o[0])),
                whole(w_key.shape),
                whole(w_value.shape),
                pl.BlockSpec((q_cols, width), lambda i, o: (o[0], 0)),
                pl.BlockSpec((width,), lambda i, o: (0,)),
                pl.BlockSpec((width,), lambda i, o: (0,)),
            ],
            out_specs=whole((TOP + width, total)),
        ),
        name="pack_heads",
    )(here, w_query, w_key, w_value, w_out, gain_attn, gain_mlp)


def pack_mlp(here, w_gate, w_up, w_down, bounds, seq):
    width, ff = w_gate.shape[0], w_gate.shape[1] // seq

    def body(here_ref, gate_ref, up_ref, down_ref, *blocks):
        for (a, b), block in zip(bounds, blocks):
            size = b - a
            block[:, :size] = gate_ref[:, a:b]
            block[:, size : 2 * size] = up_ref[:, a:b]
            block[:, 2 * size :] = down_ref[a:b, :].astype(F32).T.astype(BF)

    columns = pl.BlockSpec((width, ff), lambda i, o: (0, o[0]))
    return pl.pallas_call(
        body,
        out_shape=tuple(jax.ShapeDtypeStruct((width, 3 * (b - a)), BF) for a, b in bounds),
        grid_spec=pltpu.PrefetchScalarGridSpec(
            num_scalar_prefetch=1,
            grid=(1,),
            in_specs=[columns, columns, pl.BlockSpec((ff, width), lambda i, o: (o[0], 0))],
            out_specs=tuple(
                pl.BlockSpec((width, 3 * (b - a)), lambda i, o: (0, 0)) for a, b in bounds
            ),
        ),
        name="pack_mlp",
    )(here, w_gate, w_up, w_down)


def turn(values, cosine, sine_part):
    half_dim = HD // 2
    pieces = []
    for h in range(values.shape[0] // HD):
        first = values[h * HD : h * HD + half_dim]
        second = values[h * HD + half_dim : (h + 1) * HD]
        pieces.append(first * cosine - second * sine_part)
        pieces.append(second * cosine + first * sine_part)
    return jnp.concatenate(pieces, axis=0)


def rounded(values):
    return values.astype(BF).astype(F32)


def pick(refs, place, target):
    for index, ref in enumerate(refs):

        @pl.when(place == index)
        def _():
            target[...] = ref[...]


def write_bias(bias_ref, lengths_ref, live, block, rows):
    keys = (block + 1) * rows
    query = lax.broadcasted_iota(jnp.int32, (1, rows), 1) + block * rows
    low = jnp.zeros((1, rows), jnp.int32)
    start = 0
    for slot in range(lengths_ref.shape[0]):
        low = jnp.where(query >= start, jnp.maximum(low, start), low)
        start = start + lengths_ref[slot]
    high = jnp.minimum(query, live - 1)
    key = lax.broadcasted_iota(jnp.int32, (keys, rows), 0)
    allowed = ((key >= low) & (key <= high)) | (key == query)
    bias_ref[:keys, :] = jnp.where(allowed, 0.0, NEG)


def attention_forward(places, lengths, live, tokens, pieces, cosine, sine_part, q_cols):
    rows, model = tokens[0].shape
    pack_size = 4 * rows
    n_heads = q_cols // HD
    heads_cols = q_cols + 2 * HD
    width = pieces[0].shape[0] - TOP

    def body(places_ref, lengths_ref, live_ref, cos_ref, sin_ref, *refs):
        token_refs, piece_refs, refs = refs[:4], refs[4 : 4 + len(pieces)], refs[4 + len(pieces) :]
        (
            normed_ref, query_ref, kv_ref, kvt_ref, lse_ref, mixed_t_ref, mixed_ref, keep_ref,
            send_ref, gains_ref, w_ref, bias_ref, query_s, mixed_s, tokens_s,
        ) = refs
        live_count = live_ref[0]
        fill_weights(piece_refs, w_ref, TOP, width, slice(None))
        gains_ref[...] = jnp.zeros_like(gains_ref)
        for index, piece in enumerate(piece_refs[:-1]):
            at = slice(index * width, (index + 1) * width)
            gains_ref[0:1, at] = piece[0:1, :width].astype(F32)
            gains_ref[1:2, at] = piece[0:1, width : 2 * width].astype(F32)
        ones = jnp.ones((HD, rows), BF)
        for block in range(4):
            place = places_ref[block]
            at = slice(block * rows, (block + 1) * rows)
            keys = (block + 1) * rows
            to = pl.ds(pl.multiple_of(place * rows, rows), rows)
            pick(token_refs, place, tokens_s)
            inputs = tokens_s[...].astype(F32)
            inverse = lax.rsqrt(jnp.mean(inputs * inputs, axis=1, keepdims=True) + EPS)
            normed = (inputs * inverse * gains_ref[0:1, :]).astype(BF)
            normed_ref[to, :] = normed
            pre = dot(normed, w_ref[:, :heads_cols]).T
            cos_b, sin_b = cos_ref[:, at], sin_ref[:, at]
            query = (rounded(turn(pre[:q_cols], cos_b, sin_b)) * HD**-0.5).astype(BF)
            query_s[...] = query
            query_ref[:, at] = query
            key_t = rounded(turn(pre[q_cols : q_cols + HD], cos_b, sin_b))
            value_t = rounded(pre[q_cols + HD :])
            kv_t = jnp.concatenate([key_t, value_t], axis=0)
            kv_ref[at, :] = kv_t.T.astype(BF)
            kvt_ref[: 2 * HD, at] = kv_t.astype(BF)
            kvt_ref[2 * HD :, at] = ones
            write_bias(bias_ref, lengths_ref, live_count, block, rows)

            def attend(h, _):
                mine = pl.ds(pl.multiple_of(h * HD, HD), HD)
                scores = dot(kv_ref[:keys, :HD], query_s[mine, :]) + bias_ref[:keys, :]
                peak = jnp.max(scores, axis=0, keepdims=True)
                weights = jnp.exp(scores - peak).astype(BF)
                summed = dot(kvt_ref[HD:, :keys], weights)
                total = summed[HD : HD + 1]
                mixed = summed[:HD] * (1.0 / total)
                mixed_s[mine, :] = mixed
                lse_ref[pl.ds(h, 1), at] = peak + jnp.log(total)
                return 0

            lax.fori_loop(0, n_heads, attend, 0, unroll=2)
            mixed_t = mixed_s[...]
            mixed_t_ref[:, at] = mixed_t
            mixed = mixed_t.T.astype(BF)
            mixed_ref[to, :] = mixed
            branch = against(mixed, w_ref[:, heads_cols:]).astype(BF)
            half_to = pl.ds(pl.multiple_of((place % 2) * rows, rows), rows)

            @pl.when(place < 2)
            def _():
                keep_ref[half_to, :] = branch

            @pl.when(place >= 2)
            def _():
                send_ref[half_to, :] = branch

    args = [places, lengths, live, cosine, sine_part, *tokens, *pieces]
    flops = 2 * pack_size * model * (heads_cols + q_cols) + 4 * n_heads * pack_size**2 * HD * 3
    return kernel_call(
        body,
        [
            ((pack_size, model), BF),
            ((q_cols, pack_size), BF),
            ((pack_size, 2 * HD), BF),
            ((3 * HD, pack_size), BF),
            ((n_heads, pack_size), F32),
            ((q_cols, pack_size), F32),
            ((pack_size, q_cols), BF),
            ((pack_size // 2, model), BF),
            ((pack_size // 2, model), BF),
            ((8, model), F32),
        ],
        scratch=[
            pltpu.VMEM((model, heads_cols + q_cols), BF),
            pltpu.VMEM((pack_size, rows), F32),
            pltpu.VMEM((q_cols, rows), BF),
            pltpu.VMEM((q_cols, rows), F32),
            pltpu.VMEM((rows, model), BF),
        ],
        flops=flops,
        moved=30 << 20,
        smem=3,
        args=args,
        name="attention_forward",
    )


def attention_backward(
    places, lengths, live, tokens, pieces, cosine, sine_part, query, kv, kvt, lse, mixed_t
):
    q_cols, pack_size = query.shape
    rows, model = tokens[0].shape
    n_heads = q_cols // HD
    heads_cols = q_cols + 2 * HD
    width = pieces[0].shape[0] - TOP

    def body(
        places_ref, lengths_ref, live_ref, cos_ref, sin_ref,
        query_ref, kv_ref, kvt_ref, lse_ref, mixed_t_ref, *refs
    ):
        token_refs, piece_refs, refs = refs[:4], refs[4 : 4 + len(pieces)], refs[4 + len(pieces) :]
        (
            grad_q_ref, grad_kv_ref, w_ref, bias_ref, grad_s, grad_q_s, key_acc, value_acc, inner_s,
            tokens_s,
        ) = refs
        live_count = live_ref[0]
        fill_weights(piece_refs, w_ref, TOP, width, slice(heads_cols, heads_cols + q_cols))
        key_acc[...] = jnp.zeros_like(key_acc)
        value_acc[...] = jnp.zeros_like(value_acc)
        for block in range(4):
            place = places_ref[block]
            at = slice(block * rows, (block + 1) * rows)
            keys = (block + 1) * rows
            to = pl.ds(pl.multiple_of(place * rows, rows), rows)
            pick(token_refs, place, tokens_s)
            grad_t = rounded(dot(tokens_s[...], w_ref[...]).T)
            grad_s[...] = grad_t.astype(BF)
            product = grad_t * mixed_t_ref[:, at]
            for h in range(n_heads):
                inner_s[h : h + 1, :] = jnp.sum(
                    product[h * HD : (h + 1) * HD], axis=0, keepdims=True
                )
            write_bias(bias_ref, lengths_ref, live_count, block, rows)

            def attend(h, _):
                mine = pl.ds(pl.multiple_of(h * HD, HD), HD)
                query_h = query_ref[mine, at]
                grad_h = grad_s[mine, :]
                scores = dot(kv_ref[:keys, :HD], query_h) + bias_ref[:keys, :]
                probs = jnp.exp(scores - lse_ref[pl.ds(h, 1), at])
                grad_probs = dot(kv_ref[:keys, HD:], grad_h)
                grad_scores = (probs * (grad_probs - inner_s[pl.ds(h, 1), :])).astype(BF)
                grad_q_s[mine, :] = dot(kvt_ref[:HD, :keys], grad_scores) * HD**-0.5
                key_acc[:keys, :] += against(grad_scores, query_h)
                value_acc[:keys, :] += against(probs.astype(BF), grad_h)
                return 0

            lax.fori_loop(0, n_heads, attend, 0, unroll=2)
            turned = turn(rounded(grad_q_s[...]), cos_ref[:, at], -sin_ref[:, at])
            grad_q_ref[to, :] = turned.T.astype(BF)
        for block in range(4):
            at = slice(block * rows, (block + 1) * rows)
            to = pl.ds(pl.multiple_of(places_ref[block] * rows, rows), rows)
            key_t = turn(rounded(key_acc[at, :]).T, cos_ref[:, at], -sin_ref[:, at])
            grad_kv_ref[to, :] = jnp.concatenate([key_t.T, value_acc[at, :]], axis=1).astype(BF)

    args = [
        places, lengths, live, cosine, sine_part, query, kv, kvt, lse, mixed_t, *tokens, *pieces
    ]
    return kernel_call(
        body,
        [((pack_size, q_cols), BF), ((pack_size, 2 * HD), BF)],
        scratch=[
            pltpu.VMEM((model, q_cols), BF),
            pltpu.VMEM((pack_size, rows), F32),
            pltpu.VMEM((q_cols, rows), BF),
            pltpu.VMEM((q_cols, rows), F32),
            pltpu.VMEM((pack_size, HD), F32),
            pltpu.VMEM((pack_size, HD), F32),
            pltpu.VMEM((n_heads, rows), F32),
            pltpu.VMEM((rows, model), BF),
        ],
        flops=2 * pack_size * model * q_cols + 10 * n_heads * pack_size**2 * HD * 3,
        moved=20 << 20,
        smem=3,
        args=args,
        name="attention_backward",
    )


def heads_back(grad_q, grad_kv, tokens, pieces):
    pack_size, q_cols = grad_q.shape
    rows, model = tokens[0].shape
    heads_cols = q_cols + 2 * HD
    width = pieces[0].shape[0] - TOP

    def body(grad_q_ref, grad_kv_ref, *refs):
        token_refs, piece_refs = refs[:4], refs[4 : 4 + len(pieces)]
        keep_ref, send_ref, gain_ref, w_ref, tokens_s = refs[4 + len(pieces) :]
        step = pl.program_id(0)

        @pl.when(step == 0)
        def _():
            fill_weights(piece_refs, w_ref, TOP, width, slice(0, heads_cols))
            gain_ref[...] = jnp.zeros_like(gain_ref)

        pick(token_refs, step, tokens_s)
        inputs = tokens_s[...].astype(F32)
        inverse = lax.rsqrt(jnp.mean(inputs * inputs, axis=1, keepdims=True) + EPS)
        grad = against(grad_q_ref[...], w_ref[:, :q_cols]) + against(
            grad_kv_ref[...], w_ref[:, q_cols:]
        )

        @pl.when(step < 2)
        def _():
            keep_ref[...] = grad.astype(BF)

        @pl.when(step >= 2)
        def _():
            send_ref[...] = grad.astype(BF)

        total = jnp.sum(grad * inputs * inverse, axis=0, keepdims=True)
        gain_ref[...] += jnp.broadcast_to(total, gain_ref.shape)

    first = pl.BlockSpec((rows, model), lambda i: (jnp.minimum(i, 1), 0))
    second = pl.BlockSpec((rows, model), lambda i: (jnp.maximum(i - 2, 0), 0))
    fixed = lambda a: pl.BlockSpec(a.shape, lambda i: (0, 0), pipeline_mode=pl.Buffered(1))
    half = jax.ShapeDtypeStruct((pack_size // 2, model), BF)
    return pl.pallas_call(
        body,
        grid=(4,),
        out_shape=(half, half, jax.ShapeDtypeStruct((8, model), F32)),
        in_specs=[
            pl.BlockSpec((rows, q_cols), lambda i: (i, 0)),
            pl.BlockSpec((rows, 2 * HD), lambda i: (i, 0)),
        ]
        + [fixed(a) for a in (*tokens, *pieces)],
        out_specs=(first, second, pl.BlockSpec((8, model), lambda i: (0, 0))),
        scratch_shapes=[pltpu.VMEM((model, heads_cols), BF), pltpu.VMEM((rows, model), BF)],
        compiler_params=pltpu.CompilerParams(vmem_limit_bytes=VMEM_LIMIT),
        cost_estimate=COST,
        name="heads_back",
    )(grad_q, grad_kv, *tokens, *pieces)


def mlp_half(tokens, cots, pieces, before, size):
    rows, model = tokens[0].shape

    def body(*refs):
        token_refs, cot_refs, refs = refs[:2], refs[2:4], refs[4:]
        piece_refs, refs = refs[: len(pieces)], refs[len(pieces) :]
        before_refs, refs = refs[: len(before)], refs[len(before) :]
        down_ref, grad_ref, both_ref, w_ref, tokens_s, cot_s = refs
        step = pl.program_id(0)

        @pl.when(step == 0)
        def _():
            fill_weights(piece_refs, w_ref, 0, model, slice(None))

        pick(token_refs, step, tokens_s)
        pick(cot_refs, step, cot_s)
        both = dot(tokens_s[...], w_ref[:, : 2 * size])
        grad_act = dot(cot_s[...], w_ref[:, 2 * size :])
        gate_pre, up_pre = both[:, :size], both[:, size:]
        sig = 1.0 / (1.0 + jnp.exp(-gate_pre))
        active = gate_pre * sig
        both_ref[:, 2 * size :] = (active * up_pre).astype(BF)
        both_ref[:, size : 2 * size] = (grad_act * active).astype(BF)
        both_ref[:, :size] = (grad_act * up_pre * (sig + active * (1.0 - sig))).astype(BF)
        down = against(both_ref[:, 2 * size :], w_ref[:, 2 * size :])
        grad = against(both_ref[:, : 2 * size], w_ref[:, : 2 * size])
        if before_refs:
            down = down + before_refs[0][...].astype(F32)
            grad = grad + before_refs[1][...].astype(F32)
        down_ref[...] = down.astype(BF)
        grad_ref[...] = grad.astype(BF)

    by_rows = lambda cols: pl.BlockSpec((rows, cols), lambda i: (i, 0))
    fixed = lambda array: pl.BlockSpec(
        array.shape, lambda i: (0, 0), pipeline_mode=pl.Buffered(1)
    )
    half = jax.ShapeDtypeStruct((2 * rows, model), BF)
    return pl.pallas_call(
        body,
        grid=(2,),
        out_shape=(half, half, jax.ShapeDtypeStruct((2 * rows, 3 * size), BF)),
        in_specs=[fixed(a) for a in (*tokens, *cots, *pieces)] + [by_rows(model)] * len(before),
        out_specs=(by_rows(model), by_rows(model), by_rows(3 * size)),
        scratch_shapes=[
            pltpu.VMEM((model, 3 * size), BF),
            pltpu.VMEM((rows, model), BF),
            pltpu.VMEM((rows, model), BF),
        ],
        compiler_params=pltpu.CompilerParams(vmem_limit_bytes=VMEM_LIMIT),
        cost_estimate=COST,
        name="mlp_half",
    )(*tokens, *cots, *pieces, *before)


def weight_terms(pairs, width, n_slots, group, tops=None):
    tokens = sum(x.shape[0] for x in pairs[0][0])
    total = sum(cols.stop - cols.start for _, _, cols in pairs)
    head = 0 if tops is None else TOP

    def distinct(lists):
        out = []
        for one in lists:
            if not any(one is other for other in out):
                out.append(one)
        return out

    x_lists = distinct(x for x, _, _ in pairs)
    g_lists = distinct(g for _, g, _ in pairs)
    while (width * group) % 128:
        group *= 2
    wide = width * group
    args, specs = [], []
    for x in [x for xs in x_lists for x in xs]:
        args.append(x)
        specs.append(pl.BlockSpec((x.shape[0], wide), lambda i: (0, i)))
    for g in [g for gs in g_lists for g in gs]:
        args.append(g)
        specs.append(pl.BlockSpec(g.shape, lambda i: (0, 0), pipeline_mode=pl.Buffered(1)))
    if head:
        args.append(tops)
        specs.append(pl.BlockSpec((group * TOP, total), lambda i: (i, 0)))

    def body(*refs):
        def take(lists):
            nonlocal refs
            out = []
            for one in lists:
                out.append((one, refs[: len(one)]))
                refs = refs[len(one) :]
            return out

        x_refs, g_refs = take(x_lists), take(g_lists)
        out_ref, x_s = refs[-2:]
        lane = 0
        filled = None
        for xs, gs, cols in pairs:
            parts = next(r for other, r in x_refs if other is xs)
            g_parts = next(r for other, r in g_refs if other is gs)
            if len(parts) > 1 and filled is not xs:
                at = 0
                for part in parts:
                    x_s[at : at + part.shape[0], :] = part[...]
                    at += part.shape[0]
                filled = xs
            product, at = None, 0
            for g in g_parts:
                rows = g.shape[0]
                x = (x_s if len(parts) > 1 else parts[0])[at : at + rows, :]
                at += rows
                more = cross(x, g[:, cols])
                product = more if product is None else product + more
            product = product.astype(BF)
            count = cols.stop - cols.start
            for j in range(group):
                at = j * (head + width) + head
                out_ref[at : at + width, lane : lane + count] = product[
                    j * width : (j + 1) * width
                ]
            lane += count
        if head:
            for j in range(group):
                at = j * (head + width)
                out_ref[at : at + head, :] = refs[0][j * TOP : (j + 1) * TOP, :]

    return pl.pallas_call(
        body,
        grid=(n_slots // group,),
        out_shape=jax.ShapeDtypeStruct((n_slots * (head + width), total), BF),
        in_specs=specs,
        out_specs=pl.BlockSpec((group * (head + width), total), lambda i: (i, 0)),
        scratch_shapes=[pltpu.VMEM((tokens, wide), BF)],
        compiler_params=pltpu.CompilerParams(vmem_limit_bytes=VMEM_LIMIT),
        cost_estimate=COST,
        name="weight_terms",
    )(*args)


def ring_add(terms, slots, up, down, full, cut, tile):
    total = terms.shape[1]

    def body(up_term, down_term, up_ref, down_ref, up_out, down_out):
        if up_ref.shape[0] == full:
            up_out[...] = (up_term[...].astype(F32) + up_ref[...].astype(F32)).astype(BF)
            down_out[...] = (down_term[...].astype(F32) + down_ref[...].astype(F32)).astype(BF)
        else:
            up_out[:cut, :] = (up_term[:cut, :].astype(F32) + up_ref[...].astype(F32)).astype(BF)
            up_out[cut:, :] = up_term[cut:, :]
            down_out[:cut, :] = down_term[:cut, :]
            down_out[cut:, :] = (
                down_term[cut:, :].astype(F32) + down_ref[...].astype(F32)
            ).astype(BF)

    columns = lambda array: pl.BlockSpec((array.shape[0], tile), lambda i: (0, i))
    out = jax.ShapeDtypeStruct((full, total), BF)
    return pl.pallas_call(
        body,
        grid=(total // tile,),
        out_shape=(out, out),
        in_specs=[
            pl.BlockSpec((full, tile), lambda i: (slots[0], i)),
            pl.BlockSpec((full, tile), lambda i: (slots[1], i)),
            columns(up),
            columns(down),
        ],
        out_specs=(columns(out), columns(out)),
        cost_estimate=COST,
        name="ring_add",
    )(terms, terms, up, down)


def row_call(body, outs, row_args, fixed_args, steps, smem=(), name=None):
    rows = outs[0][0][0] if outs[0][2] else row_args[0][0].shape[0]
    tile = rows // steps
    n_smem = len(smem)
    by_rows = lambda cols, at: pl.BlockSpec((tile, cols), lambda i, *_: (i + at, 0))
    return pl.pallas_call(
        body,
        out_shape=tuple(jax.ShapeDtypeStruct(s, d) for s, d, _ in outs),
        grid_spec=pltpu.PrefetchScalarGridSpec(
            num_scalar_prefetch=n_smem,
            grid=(steps,),
            in_specs=[by_rows(a.shape[1], at * steps) for a, at in row_args]
            + [pl.BlockSpec(a.shape, lambda i, *_: (0, 0)) for a in fixed_args],
            out_specs=tuple(
                by_rows(s[1], 0) if split else pl.BlockSpec(s, lambda i, *_: (0, 0))
                for s, _, split in outs
            ),
        ),
        cost_estimate=COST,
        name=name,
    )(*smem, *[a for a, _ in row_args], *fixed_args)


STEPS = 2


def second_norm(inputs, keep, came, last, gains):
    def body(inputs_ref, keep_ref, came_ref, last_ref, gains_ref, hidden_ref, normed_ref):
        branch = keep_ref[...].astype(F32) + came_ref[...].astype(F32) + last_ref[...].astype(F32)
        hidden = inputs_ref[...].astype(F32) + branch
        inverse = lax.rsqrt(jnp.mean(hidden * hidden, axis=1, keepdims=True) + EPS)
        hidden_ref[...] = hidden
        normed_ref[...] = (hidden * inverse * gains_ref[1:2, :]).astype(BF)

    return row_call(
        body,
        [(inputs.shape, F32, True), (inputs.shape, BF, True)],
        [(inputs, 0), (keep, 0), (came, 0), (last, 0)],
        [gains],
        STEPS,
        name="second_norm",
    )


def norm_back(grad, values, gain):
    inverse = lax.rsqrt(jnp.mean(values * values, axis=1, keepdims=True) + EPS)
    scaled = grad * gain
    mean = jnp.mean(scaled * values, axis=1, keepdims=True)
    return inverse, inverse * (scaled - values * (inverse * inverse * mean))


def second_norm_back(cot, hidden, keep, came, last, gains):
    rows, model = hidden.shape

    def body(cot_ref, hidden_ref, keep_ref, came_ref, last_ref, gains_ref, grad_ref, low_ref, gain_ref):
        @pl.when(pl.program_id(0) == 0)
        def _():
            gain_ref[...] = jnp.zeros_like(gain_ref)

        grad = keep_ref[...].astype(F32) + came_ref[...].astype(F32) + last_ref[...].astype(F32)
        hidden_v = hidden_ref[...]
        inverse, back = norm_back(grad, hidden_v, gains_ref[1:2, :])
        total = jnp.sum(grad * hidden_v * inverse, axis=0, keepdims=True)
        gain_ref[...] += jnp.broadcast_to(total, gain_ref.shape)
        out = cot_ref[...].astype(F32) + back
        grad_ref[...] = out
        low_ref[...] = out.astype(BF)

    return row_call(
        body,
        [((rows, model), F32, True), ((rows, model), BF, True), ((8, model), F32, False)],
        [(cot, 0), (hidden, 0), (keep, 0), (came, 0), (last, 0)],
        [gains],
        STEPS,
        name="second_norm_back",
    )


def first_norm_back(grad_hidden, inputs, keep, came, last, gains, order, n_slots):
    width = inputs.shape[1] // n_slots

    def body(order_ref, grad_ref, inputs_ref, keep_ref, came_ref, last_ref, gains_ref, out_ref):
        grad = keep_ref[...].astype(F32) + came_ref[...].astype(F32) + last_ref[...].astype(F32)
        _, back = norm_back(grad, inputs_ref[...].astype(F32), gains_ref[0:1, :])
        out = (grad_ref[...] + back).astype(BF)
        if width % 128:
            out_ref[...] = out
        else:
            put_features(out, order_ref, out_ref, n_slots, width)

    return row_call(
        body,
        [(inputs.shape, BF, True)],
        [(grad_hidden, 0), (inputs, 0), (keep, 0), (came, 0), (last, 0)],
        [gains],
        STEPS,
        smem=(order,),
        name="first_norm_back",
    )[0]


def layer_output(hidden, keep, came, last, order, n_slots):
    width = hidden.shape[1] // n_slots

    def body(order_ref, hidden_ref, keep_ref, came_ref, last_ref, out_ref):
        down = keep_ref[...].astype(F32) + came_ref[...].astype(F32) + last_ref[...].astype(F32)
        out = (hidden_ref[...] + down).astype(BF)
        if width % 128:
            out_ref[...] = out
        else:
            put_features(out, order_ref, out_ref, n_slots, width)

    return row_call(
        body,
        [(hidden.shape, BF, True)],
        [(hidden, 0), (keep, 0), (came, 0), (last, 0)],
        [],
        STEPS,
        smem=(order,),
        name="layer_output",
    )[0]


def unpack_mlp(places, chunks, bounds, width, ff):
    flat = [block for blocks in chunks for block in blocks]

    def body(places_ref, *refs):
        ins = refs[: len(flat)]
        gate_ref, up_ref, down_ref = refs[len(flat) : len(flat) + 3]
        scratches = refs[len(flat) + 3 :]
        place = places_ref[pl.program_id(0)]
        for c, (a, b) in enumerate(bounds):
            size = b - a
            block_s = scratches[c]
            pick(ins[4 * c : 4 * c + 4], place, block_s)
            gate_ref[:, a:b] = block_s[:, :size].astype(F32)
            up_ref[:, a:b] = block_s[:, size : 2 * size].astype(F32)
            down_ref[a:b, :] = block_s[:, 2 * size :].astype(F32).T

    columns = pl.BlockSpec((width, ff), lambda i, p: (0, i))
    return pl.pallas_call(
        body,
        out_shape=(
            jax.ShapeDtypeStruct((width, 4 * ff), F32),
            jax.ShapeDtypeStruct((width, 4 * ff), F32),
            jax.ShapeDtypeStruct((4 * ff, width), F32),
        ),
        grid_spec=pltpu.PrefetchScalarGridSpec(
            num_scalar_prefetch=1,
            grid=(4,),
            in_specs=[
                pl.BlockSpec(h.shape, lambda i, p: (0, 0), pipeline_mode=pl.Buffered(1))
                for h in flat
            ],
            out_specs=(columns, columns, pl.BlockSpec((ff, width), lambda i, p: (i, 0))),
            scratch_shapes=[pltpu.VMEM((width, 3 * (b - a)), BF) for a, b in bounds],
        ),
        compiler_params=pltpu.CompilerParams(vmem_limit_bytes=VMEM_LIMIT),
        cost_estimate=COST,
        name="unpack_mlp",
    )(places, *flat)


def unpack_heads(places, heads, width, q_cols):
    kv = q_cols + 2 * HD

    def body(places_ref, *refs):
        head_refs = refs[:4]
        query_ref, key_ref, value_ref, out_ref, gain_ref, head_s = refs[4:]
        gain = jnp.zeros((8, 2 * width), F32)
        for place in range(4):
            pick(head_refs, places_ref[place], head_s)
            gain = gain + head_s[:TOP, : 2 * width].astype(F32)[:8]
            at = slice(place * q_cols, (place + 1) * q_cols)
            query_ref[:, at] = head_s[TOP:, :q_cols].astype(F32)
            both = head_s[TOP:, q_cols:kv].astype(F32)
            key_ref[:, place * HD : (place + 1) * HD] = both[:, :HD]
            value_ref[:, place * HD : (place + 1) * HD] = both[:, HD:]
            out_ref[at, :] = head_s[TOP:, kv:].astype(F32).T
        gain_ref[...] = gain

    args = [places, *heads]
    return kernel_call(
        body,
        [
            ((width, 4 * q_cols), F32),
            ((width, 4 * HD), F32),
            ((width, 4 * HD), F32),
            ((4 * q_cols, width), F32),
            ((8, 2 * width), F32),
        ],
        scratch=[pltpu.VMEM(heads[0].shape, BF)],
        smem=1,
        args=args,
        name="unpack_heads",
    )


def doc_positions(lengths, pack_size):
    doc_starts = jnp.cumsum(lengths) - lengths
    places = jnp.arange(pack_size, dtype=jnp.int32)
    doc_first = jnp.max(
        jnp.where(places[:, None] >= doc_starts[None, :], doc_starts[None, :], 0), axis=1
    )
    return places - doc_first


def rotary_tables(positions):
    half_dim = HD // 2
    frequency = 10000.0 ** (-2.0 * jnp.arange(half_dim, dtype=F32) / HD)
    angle_table = frequency[:, None] * positions.astype(F32)[None, :]
    return (jnp.cos(angle_table), jnp.sin(angle_table))


def layer(
    hidden_in,
    cotangent,
    gain_attn,
    w_query,
    w_key,
    w_value,
    w_out,
    gain_mlp,
    w_gate,
    w_up,
    w_down,
    doc_lengths,
    valid_count,
):
    seq = lax.axis_size("seq")
    n_dp = lax.axis_size("dp")
    here = lax.axis_index("seq").astype(jnp.int32)
    ring = Ring(n_dp)
    rows, model = hidden_in.shape
    pack_size = rows * seq
    width = gain_attn.shape[0]
    q_cols = w_query.shape[1] // seq
    ff = w_gate.shape[1] // seq
    here_1 = here.reshape(1)
    lengths, live = doc_lengths[0], valid_count[:1]
    middle = width // 2

    offset = here ^ jnp.arange(4, dtype=jnp.int32)
    places = (offset % 2) * 2 + offset // 2

    first = (ff // 2 + 127) // 128 * 128
    bounds = [(0, first), (first, ff)]
    sizes = [b - a for a, b in bounds]

    def other_half(keep, came):
        return plus(keep[rows:], came[rows:])

    def four(block, across, beside):
        return [block, across, beside, swap(across, 1)]

    clock = Clock()
    head_block = pack_heads(here_1, w_query, w_key, w_value, w_out, gain_attn, gain_mlp, seq)
    clock.done(head_block)
    heads = Gather(ring, head_block, TOP + middle)
    hidden_in, cotangent = clock.tie(hidden_in, cotangent)
    mine = permute_features(hidden_in, ring.slot_owners(), n_dp)
    clock.done(mine)
    across, beside = swap(mine, 2), swap(mine, 1)
    w_gate, w_up, w_down, cotangent = clock.tie(w_gate, w_up, w_down, cotangent)
    blocks = pack_mlp(here_1, w_gate, w_up, w_down, bounds, seq)
    clock.done(blocks[0])
    heads.relay(clock)
    cotangent = clock.tie(cotangent)
    my_cot = permute_features(cotangent, ring.slot_owners(), n_dp)
    cosine, sine_part = rotary_tables(doc_positions(lengths, pack_size))
    cosine, sine_part, my_cot = clock.tie(cosine, sine_part, my_cot)
    heads.relay(clock)
    across, my_cot = clock.tie(across, my_cot)
    tokens = four(mine, across, beside)
    cot_across, cot_beside = swap(my_cot, 2), swap(my_cot, 1)
    heads.relay(clock)
    head_pieces = heads.finish(clock)
    tokens = list(clock.tie(*tokens))
    blocks = clock.tie(*blocks)
    chunks = [Gather(ring, block, middle) for block in blocks]
    normed, query, kv, kvt, lse, mixed_t, mixed, keep, send, gains = attention_forward(
        places, lengths, live, tokens, head_pieces, cosine, sine_part, q_cols
    )
    clock.done(lse)
    chunks[0].relay(clock)
    chunks[1].land(clock)
    cot_across, send = clock.tie(cot_across, send)
    came = clock.tie(swap(send, 1))
    last = swap(clock.tie(other_half(keep, came)), 2)
    cots = four(my_cot, cot_across, cot_beside)
    chunks[0].relay(clock)
    last = clock.tie(last)
    hidden, my_normed = second_norm(mine, keep, came, last, gains)
    clock.done(my_normed)
    across, beside = swap(my_normed, 2), swap(my_normed, 1)
    chunks[0].relay(clock)
    across = clock.tie(across)
    seconds = four(my_normed, across, beside)
    pieces = chunks[0].finish(clock)
    chunks[1].go(clock)
    seconds = list(clock.tie(*seconds))
    cots = list(clock.tie(*cots))

    def terms_of(both, size):
        return weight_terms(
            [(seconds, both, slice(0, 2 * size)), (cots, both, slice(2 * size, 3 * size))],
            width,
            n_dp,
            2,
        )

    down_send, grad_send, both_send = mlp_half(seconds[2:], cots[2:], pieces, (), sizes[0])
    clock.done(both_send)
    chunks[1].relay(clock)
    first_two = clock.tie(*seconds[:2])
    down_keep, grad_keep, both_keep = mlp_half(first_two, cots[:2], pieces, (), sizes[0])
    clock.done(both_keep)
    chunks[1].relay(clock)
    both = list(clock.tie(both_keep, both_send))
    terms = terms_of(both, sizes[0])
    clock.done(terms)
    pieces = chunks[1].finish(clock)
    sums = [Scatter(ring, clock.tie(terms), middle, sizes[0])]
    down_send, grad_send, both_send = mlp_half(
        seconds[2:], cots[2:], clock.tie(*pieces), (down_send, grad_send), sizes[1]
    )
    clock.done(both_send)
    sums[0].relay(clock)
    grad_send, down_send = clock.tie(grad_send, down_send)
    came, down_came = swap(grad_send, 1), swap(down_send, 1)
    first_two = clock.tie(*seconds[:2])
    down_keep, grad_keep, both_keep = mlp_half(
        first_two, cots[:2], pieces, (down_keep, grad_keep), sizes[1]
    )
    clock.done(both_keep)
    came, down_came = clock.tie(came, down_came)
    last = swap(clock.tie(other_half(grad_keep, came)), 2)
    sums[0].relay(clock)
    both = list(clock.tie(both_keep, both_send))
    terms = terms_of(both, sizes[1])
    clock.done(terms)
    sums.append(Scatter(ring, clock.tie(terms), middle, sizes[1]))
    last = clock.tie(last)
    grad_hidden, my_branch, gain_two_terms = second_norm_back(
        my_cot, hidden, grad_keep, came, last, gains
    )
    clock.done(my_branch)
    across, beside = swap(my_branch, 2), swap(my_branch, 1)
    down_other = clock.tie(other_half(down_keep, down_came))
    sums[0].relay(clock)
    sums[1].relay(clock)
    across = clock.tie(across)
    branches = four(my_branch, across, beside)
    down_last = swap(clock.tie(down_other), 2)
    branches = list(clock.tie(*branches))
    grad_q, grad_kv = attention_backward(
        places, lengths, live, branches, head_pieces, cosine, sine_part,
        query, kv, kvt, lse, mixed_t
    )
    clock.done(grad_kv)
    sums[1].relay(clock)
    chunk_sum = sums[0].finish(clock)
    down_last = clock.tie(down_last)
    chunk_across, chunk_beside = swap(clock.tie(chunk_sum), 2), swap(chunk_sum, 1)
    tokens = clock.tie(*tokens)
    grad_keep, grad_send, gain_one_terms = heads_back(grad_q, grad_kv, tokens, head_pieces)
    clock.done(gain_one_terms)
    columns = head_block.shape[1]
    tops = jnp.concatenate(
        [
            gain_one_terms[0].reshape(n_dp, width),
            gain_two_terms[0].reshape(n_dp, width),
            jnp.zeros((n_dp, columns - 2 * width), F32),
        ],
        axis=1,
    ).astype(BF)
    tops = jnp.pad(tops[:, None], ((0, 0), (0, TOP - 1), (0, 0))).reshape(n_dp * TOP, -1)
    normed, tops = clock.tie(normed, tops)
    normed = [normed]
    head_terms = weight_terms(
        [
            (normed, [grad_q], slice(0, q_cols)),
            (normed, [grad_kv], slice(0, 2 * HD)),
            (branches, [mixed], slice(0, q_cols)),
        ],
        width,
        n_dp,
        2,
        tops,
    )
    clock.done(head_terms)
    chunk_across = clock.tie(chunk_across)
    firsts = four(chunk_sum, chunk_across, chunk_beside)
    head_ring = Scatter(ring, clock.tie(head_terms), TOP + middle, columns)
    sums[1].relay(clock)
    came = clock.tie(swap(clock.tie(grad_send), 1))
    last = swap(clock.tie(other_half(grad_keep, came)), 2)
    head_ring.relay(clock)
    last = clock.tie(last)
    firsts = list(clock.tie(*firsts))
    grad_input = first_norm_back(
        grad_hidden, mine, grad_keep, came, last, gains, ring.slot_owners(), n_dp
    )
    clock.done(grad_input)
    second_sum = sums[1].finish(clock)
    second_across, second_beside = swap(second_sum, 2), swap(second_sum, 1)
    head_ring.relay(clock)
    down_came = clock.tie(down_came)
    result = layer_output(hidden, down_keep, down_came, down_last, ring.slot_owners(), n_dp)
    clock.done(result)
    head_ring.relay(clock)
    second_across = clock.tie(second_across)
    others = four(second_sum, second_across, second_beside)
    head_sum = head_ring.finish(clock)
    head_across, head_beside = swap(head_sum, 2), swap(head_sum, 1)
    firsts, others = list(clock.tie(*firsts)), list(clock.tie(*others))
    grad_gate, grad_up, grad_down = unpack_mlp(places, [firsts, others], bounds, width, ff)
    clock.done(grad_gate)
    head_across = clock.tie(head_across)
    head_blocks = four(head_sum, head_across, head_beside)
    grad_query, grad_key, grad_value, grad_out, gain_sums = unpack_heads(
        places, list(clock.tie(*head_blocks)), width, q_cols
    )
    if width % 128:
        slots = ring.owner_slots()
        result = blocks_in_order(result, slots, n_dp)
        grad_input = blocks_in_order(grad_input, slots, n_dp)

    return (
        result,
        grad_input,
        gain_sums[0, :width],
        grad_query,
        grad_key,
        grad_value,
        grad_out,
        gain_sums[0, width:],
        grad_gate,
        grad_up,
        grad_down,
    )


def solution(mesh):
    return jax.shard_map(
        layer,
        mesh=mesh,
        in_specs=(
            P(("dp", "seq"), None),
            P(("dp", "seq"), None),
            P("dp"),
            P("dp", None),
            P("dp", None),
            P("dp", None),
            P(None, "dp"),
            P("dp"),
            P("dp", None),
            P("dp", None),
            P(None, "dp"),
            P("dp", None),
            P("dp"),
        ),
        out_specs=(
            P(("dp", "seq"), None),
            P(("dp", "seq"), None),
            P("dp"),
            P("dp", None),
            P("dp", None),
            P("dp", None),
            P(None, "dp"),
            P("dp"),
            P("dp", None),
            P("dp", None),
            P(None, "dp"),
        ),
        check_vma=False,
    )
```

time: 712 us -> 570 us (0.80)
  waiting for transfers between devices: 296 us -> 189 us
  local copies, waits for them, and re-layouts: 40.7 us -> 22.4 us
  Pallas kernels: 255 us -> 240 us
  starting transfers between devices: 76.7 us -> 69.1 us
    ppermute x28 -> x24, waiting for transfers between devices: 188 us -> 122 us  [go_up(): return lax.ppermute(block, 'dp', self.up)]
    ppermute x24 -> x29, waiting for transfers between devices: 51.5 us -> 20.7 us  [swap(): return lax.ppermute(block, 'seq', [(i, i ^ distance) for i in range(4)])]
    convert_element_type x3 -> x13, other arithmetic: 8.51 us -> 36.7 us  [the longest x10 31.1 us: plus(): return (one.astype(F32) + two.astype(F32)).astype(BF)]
    pallas_call x24 -> x15, Pallas kernels: 161 us -> 148 us  [the longest x4 67.5 us: mlp_half(): pl.pallas_call(body, grid=(2,), out_shape=(half, half, jax.ShapeDtypeStru...]
    add x4 -> x0, other arithmetic: 11.7 us -> none  [seq_scatter(): near = terms[:half].astype(F32) + swap(terms[half:], 1).astype(F32)]
    ppermute x28 -> x24, starting transfers between devices: 39.4 us -> 28.8 us  [go_up(): return lax.ppermute(block, 'dp', self.up)]
    ppermute x28 -> x24, waiting for transfers between devices: 56.4 us -> 46.8 us  [go_down(): return lax.ppermute(block, 'dp', self.down)]
    slice x18 -> x12, local copies, waits for them, and re-layouts: 19.5 us -> 11.5 us  [the longest x3 5.63 us: __init__(): terms[begin + cut:begin + self.full]]
  transfers between devices with their start and end apart: 80 -> 77, of which waited for: 34 -> 39; matrix products, arithmetic and copies ran while one was open for 8% -> 8% of each run, Pallas kernels for 26% -> 41%
where the time goes in v3:
time: 570 us; the launch traced here: 562 us
  Pallas kernels  240 us (42%)
  waiting for transfers between devices  189 us (33%)
  starting transfers between devices  69.1 us (12%)
  other arithmetic  39.4 us (7%)
  local copies, waits for them, and re-layouts  22.4 us (4%)
    ppermute x24, waiting for transfers between devices, go_up(): return lax.ppermute(block, 'dp', self.up)  122 us
    pallas_call x5, Pallas kernels, kernel_call(): pl.pallas_call(body, out_shape=tuple((jax.ShapeDtypeStruct(s, d) for s, d...  75.2 us
    pallas_call x4, Pallas kernels, mlp_half(): pl.pallas_call(body, grid=(2,), out_shape=(half, half, jax.ShapeDtypeStru...  67.5 us
    ppermute x24, waiting for transfers between devices, go_down(): return lax.ppermute(block, 'dp', self.down)  46.8 us
    pallas_call x3, Pallas kernels, weight_terms(): pl.pallas_call(body, grid=(n_slots // group,), out_shape=jax.ShapeDtypeSt...  39.8 us
    convert_element_type x10, other arithmetic, plus(): return (one.astype(F32) + two.astype(F32)).astype(BF)  31.1 us
    ppermute x24, starting transfers between devices, go_up(): return lax.ppermute(block, 'dp', self.up)  28.8 us
    ppermute x24, starting transfers between devices, go_down(): return lax.ppermute(block, 'dp', self.down)  22.4 us
  transfers between devices with their start and end apart: 77, of which 39 were waited for; matrix products, arithmetic and copies ran while one was open for 8% of the time, Pallas kernels for 41%

profile of v3, /device:TPU:0, one launch (start us, length us, event | category | flops | bytes accessed | tf_op | source)
XLA Modules:
  0.0 562.2 jit_solution(12806198271624421355)
XLA Ops:
  0.7 2.5 pack_heads.1.refs_4_
  3.2 3.0 collective-permute-start
  13.2 3.2 pack_mlp.1
  16.4 4.1 collective-permute-done.refs_5_
  27.8 9.0 %collective-permute-done.3.refs_6_ = bf16[272,1152]{1,0:T(8,128)(2,1)S(1)} collective-permute-done((bf16[272,1152]{1,0:T(8,128)(2,1)S(1)}, bf16[272,1152]{1,0:T(8,128)(2,1)S(1)}, u32[]{:S(2)}, u32[]{:S(2)}) %collective-permute-start.3) | collective-permute-done | bytes 626720 | tf_op jit(solution)/shard_map/ppermute | solution.py:82
  40.2 14.4 %collective-permute-done.7.refs_7_ = bf16[272,1152]{1,0:T(8,128)(2,1)S(1)} collective-permute-done((bf16[272,1152]{1,0:T(8,128)(2,1)S(1)}, bf16[272,1152]{1,0:T(8,128)(2,1)S(1)}, u32[]{:S(2)}, u32[]{:S(2)}) %collective-permute-start.7) | collective-permute-done | bytes 626720 | tf_op jit(solution)/shard_map/ppermute | solution.py:82
  58.1 7.4 %collective-permute-done.10.refs_12_ = bf16[128,1152]{1,0:T(8,128)(2,1)S(1)} collective-permute-done((bf16[128,1152]{1,0:T(8,128)(2,1)S(1)}, bf16[128,1152]{1,0:T(8,128)(2,1)S(1)}, u32[]{:S(2)}, u32[]{:S(2)}) %collective-permute-start.10) | collective-permute-done | bytes 294944 | tf_op jit(solution)/shard_map/ppermute | solution.py:85
  72.4 35.7 %attention_forward.1 = (bf16[1024,2048]{1,0:T(8,128)(2,1)}, bf16[512,1024]{1,0:T(8,128)(2,1)}, bf16[1024,128]{1,0:T(8,128)(2,1)}, bf16[192,1024]{1,0:T(8,128)(2,...) custom-call(s32[4]{0:T(128)} %fusion.2.places_ref, ...), custom_call_target="tpu_custom_call" | custom-call | flops 1000 | bytes 1000 | tf_op jit(solution)/shard_map/attention_forward/pallas_call | solution.py:40
  108.2 4.8 collective-permute-done.12.refs_5_
  122.4 20.4 %collective-permute-done.18.refs_6_ = bf16[256,2304]{1,0:T(8,128)(2,1)} collective-permute-done((bf16[256,2304]{1,0:T(8,128)(2,1)}, bf16[256,2304]{1,0:T(8,128)(2,1)}, u32[]{:S(2)}, u32[]{:S(2)}) %collective-permute-start.18) | collective-permute-done | bytes 1179680 | tf_op jit(solution)/shard_map/ppermute | solution.py:82
  146.2 3.9 second_norm.1
  151.6 19.3 %collective-permute-done.21.refs_7_ = bf16[256,2304]{1,0:T(8,128)(2,1)} collective-permute-done((bf16[256,2304]{1,0:T(8,128)(2,1)}, bf16[256,2304]{1,0:T(8,128)(2,1)}, u32[]{:S(2)}, u32[]{:S(2)}) %collective-permute-start.21) | collective-permute-done | bytes 1179680 | tf_op jit(solution)/shard_map/ppermute | solution.py:82
  176.2 9.7 %collective-permute-done.25.refs_11_ = bf16[128,2304]{1,0:T(8,128)(2,1)S(1)} collective-permute-done((bf16[128,2304]{1,0:T(8,128)(2,1)S(1)}, bf16[128,2304]{1,0:T(8,128)(2,1)S(1)}, u32[]{:S(2)}, u32[]{:S(2)}) %collective-permute-start.25) | collective-permute-done | bytes 589856 | tf_op jit(solution)/shard_map/ppermute | solution.py:82
  191.6 17.4 %mlp_half.4 = (bf16[512,2048]{1,0:T(8,128)(2,1)}, bf16[512,2048]{1,0:T(8,128)(2,1)}, bf16[512,2304]{1,0:T(8,128)(2,1)}) custom-call(bf16[256,2048]{1,0:T(8,128)(2,1)} %copy-done.4, bf16[256,2048]{1,0:T(8,128)(2,1)} %copy-done.5, bf16[256,2048]{1,0:T(8,128)(2,1)} %copy-done.6, bf16[256,2048]{1,0:T(8,128)(2,1)} %collective-permute-done.28.refs_3_.refs_7_, ...), custom_call_target="tpu_custom_call" | custom-call | flops 1000 | bytes 1000 | tf_op jit(solution)/shard_map/mlp_half/pallas_call | solution.py:602
  213.0 17.3 %mlp_half.5 = (bf16[512,2048]{1,0:T(8,128)(2,1)}, bf16[512,2048]{1,0:T(8,128)(2,1)}, bf16[512,2304]{1,0:T(8,128)(2,1)}) custom-call(bf16[256,2048]{1,0:T(8,128)(2,1)} %get-tuple-element.351.refs_0_, bf16[256,2048]{1,0:T(8,128)(2,1)} %copy-done.3, bf16[256,2048]{1,0:T(8,128)(2,1)} %permute_features.3.refs_2_.refs_4_.cot_ref, bf16[256,2048]{1,0:T(8,128)(2,1)} %copy-done.2, ...), custom_call_target="tpu_custom_call" | custom-call | flops 1000 | bytes 1000 | tf_op jit(solution)/shard_map/mlp_half/pallas_call | solution.py:602
  230.3 2.7 collective-permute-done.31.refs_7_
  236.3 15.4 %weight_terms.3.up_term.down_term = bf16[2048,2304]{1,0:T(8,128)(2,1)} custom-call(bf16[256,2048]{1,0:T(8,128)(2,1)} %get-tuple-element.351.refs_0_, bf16[256,2048]{1,0:T(8,128)(2,1)} %copy-done.3, bf16[256,2048]{1,0:T(8,128)(2,1)} %copy-done.4, bf16[256,2048]{1,0:T(8,128)(2,1)} %copy-done.5, bf16[256,2048]{1,0:T(8,128)(2,1)} %permute_features.3.refs_2_.refs_4_.cot_ref, ...), custom_call_target="tpu_custom_call" | custom-call | flops 1000 | bytes 1000 | tf_op jit(solution)/shard_map/weight_terms/pallas_call | solution.py:689
  256.3 16.4 %mlp_half.6 = (bf16[512,2048]{1,0:T(8,128)(2,1)}, bf16[512,2048]{1,0:T(8,128)(2,1)}, bf16[512,1920]{1,0:T(8,128)(2,1)}) custom-call(bf16[256,2048]{1,0:T(8,128)(2,1)} %copy-done.4, bf16[256,2048]{1,0:T(8,128)(2,1)} %copy-done.5, bf16[256,2048]{1,0:T(8,128)(2,1)} %copy-done.6, bf16[256,2048]{1,0:T(8,128)(2,1)} %collective-permute-done.28.refs_3_.refs_7_, ...), custom_call_target="tpu_custom_call" | custom-call | flops 1000 | bytes 1000 | tf_op jit(solution)/shard_map/mlp_half/pallas_call | solution.py:602
  273.8 4.2 ring_add.3
  280.6 16.4 %mlp_half.7 = (bf16[512,2048]{1,0:T(8,128)(2,1)}, bf16[512,2048]{1,0:T(8,128)(2,1)}, bf16[512,1920]{1,0:T(8,128)(2,1)}) custom-call(bf16[256,2048]{1,0:T(8,128)(2,1)} %get-tuple-element.351.refs_0_, bf16[256,2048]{1,0:T(8,128)(2,1)} %copy-done.3, bf16[256,2048]{1,0:T(8,128)(2,1)} %permute_features.3.refs_2_.refs_4_.cot_ref, bf16[256,2048]{1,0:T(8,128)(2,1)} %copy-done.2, ...), custom_call_target="tpu_custom_call" | custom-call | flops 1000 | bytes 1000 | tf_op jit(solution)/shard_map/mlp_half/pallas_call | solution.py:602
  297.0 3.7 add_convert_fusion.7
  302.2 4.4 collective-permute-done.40
  307.3 4.0 add_convert_fusion.3
  313.3 14.0 %weight_terms.4.up_term.down_term = bf16[2048,1920]{1,0:T(8,128)(2,1)} custom-call(bf16[256,2048]{1,0:T(8,128)(2,1)} %get-tuple-element.351.refs_0_, bf16[256,2048]{1,0:T(8,128)(2,1)} %copy-done.3, bf16[256,2048]{1,0:T(8,128)(2,1)} %copy-done.4, bf16[256,2048]{1,0:T(8,128)(2,1)} %copy-done.5, bf16[256,2048]{1,0:T(8,128)(2,1)} %permute_features.3.refs_2_.refs_4_.cot_ref, ...), custom_call_target="tpu_custom_call" | custom-call | flops 1000 | bytes 1000 | tf_op jit(solution)/shard_map/weight_terms/pallas_call | solution.py:689
  331.5 5.5 second_norm_back.1
  338.6 2.6 add_convert_fusion.6
  341.4 4.3 add_convert_fusion.1
  345.7 3.2 collective-permute-done.43.up_ref
  349.5 4.0 ring_add.4
  353.5 6.8 %collective-permute-done.42.refs_1_.refs_2_ = bf16[256,2048]{1,0:T(8,128)(2,1)} collective-permute-done((bf16[256,2048]{1,0:T(8,128)(2,1)}, bf16[256,2048]{1,0:T(8,128)(2,1)}, u32[]{:S(2)}, u32[]{:S(2)}) %collective-permute-start.42) | collective-permute-done | bytes 1048608 | tf_op jit(solution)/shard_map/ppermute | solution.py:176
  365.8 30.0 %attention_backward.1 = (bf16[1024,512]{1,0:T(8,128)(2,1)}, bf16[1024,128]{1,0:T(8,128)(2,1)}) custom-call(s32[4]{0:T(128)} %fusion.2.places_ref, s32[6]{0:T(128)} %bitcast.14, s32[1]{0:T(128)S(6)} %copy.42.live_ref, f32[32,1024]{1,0:T(8,128)} %get-tuple-element.253.cos_ref, f32[32,1024]{1,0:T(8,128)} %get-tuple-element.254.sin_ref, ...), custom_call_target="tpu_custom_call" | custom-call | flops 1000 | bytes 1000 | tf_op jit(solution)/shard_map/attention_backward/pallas_call | solution.py:40
  395.9 3.9 add_convert_fusion.12
  399.7 10.3 %collective-permute-done.49 = bf16[256,2304]{1,0:T(8,128)(2,1)} collective-permute-done((bf16[256,2304]{1,0:T(8,128)(2,1)}, bf16[256,2304]{1,0:T(8,128)(2,1)}, u32[]{:S(2)}, u32[]{:S(2)}) %collective-permute-start.49) | collective-permute-done | bytes 1179680 | tf_op jit(solution)/shard_map/ppermute | solution.py:82
  417.8 11.6 %heads_back.1 = (bf16[512,2048]{1,0:T(8,128)(2,1)}, bf16[512,2048]{1,0:T(8,128)(2,1)}, f32[8,2048]{1,0:T(8,128)}) custom-call(bf16[1024,512]{1,0:T(8,128)(2,1)} %get-tuple-element.391.grad_q_ref.refs_5_, bf16[1024,128]{1,0:T(8,128)(2,1)} %get-tuple-element.392.grad_kv_ref.refs_6_, bf16[256,2048]{1,0:T(8,128)(2,1)} %permute_features.2.refs_0_.inputs_ref, ...), custom_call_target="tpu_custom_call" | custom-call | flops 1000 | bytes 1000 | tf_op jit(solution)/shard_map/heads_back/pallas_call | solution.py:548
  430.9 10.4 %weight_terms.5.up_term.down_term = bf16[2176,1152]{1,0:T(8,128)(2,1)} custom-call(bf16[1024,2048]{1,0:T(8,128)(2,1)} %get-tuple-element.409.refs_0_, bf16[256,2048]{1,0:T(8,128)(2,1)} %get-tuple-element.387.refs_0_.refs_1_, bf16[256,2048]{1,0:T(8,128)(2,1)} %collective-permute-done.42.refs_1_.refs_2_, bf16[256,2048]{1,0:T(8,128)(2,1)} %copy-done.22, ...), custom_call_target="tpu_custom_call" | custom-call | flops 1000 | bytes 1000 | tf_op jit(solution)/shard_map/weight_terms/pallas_call | solution.py:689
  441.4 4.0 add_convert_fusion.10
  445.3 4.2 collective-permute-done.59.came_ref
  458.0 25.4 %collective-permute-done.56.down_ref = bf16[128,1152]{1,0:T(8,128)(2,1)} collective-permute-done((bf16[128,1152]{1,0:T(8,128)(2,1)S(1)}, bf16[128,1152]{1,0:T(8,128)(2,1)}, u32[]{:S(2)}, u32[]{:S(2)}) %collective-permute-start.56) | collective-permute-done | bytes 294944 | tf_op jit(solution)/shard_map/ppermute | solution.py:85
  483.4 2.6 ring_add.5
  489.1 5.1 first_norm_back.1
  496.0 5.0 collective-permute-done.60
  502.4 2.8 add_convert_fusion.17
  508.6 4.2 layer_output.1
  512.8 6.2 %collective-permute-done.65 = bf16[272,1152]{1,0:T(8,128)(2,1)} collective-permute-done((bf16[272,1152]{1,0:T(8,128)(2,1)}, bf16[272,1152]{1,0:T(8,128)(2,1)}, u32[]{:S(2)}, u32[]{:S(2)}) %collective-permute-start.65) | collective-permute-done | bytes 626720 | tf_op jit(solution)/shard_map/ppermute | solution.py:82
  524.7 3.2 collective-permute-done.69.refs_5_
  527.9 6.8 %collective-permute-done.67 = bf16[272,1152]{1,0:T(8,128)(2,1)S(1)} collective-permute-done((bf16[272,1152]{1,0:T(8,128)(2,1)S(1)}, bf16[272,1152]{1,0:T(8,128)(2,1)S(1)}, u32[]{:S(2)}, u32[]{:S(2)}) %collective-permute-start.67) | collective-permute-done | bytes 626720 | tf_op jit(solution)/shard_map/ppermute | solution.py:82
  540.8 10.7 %unpack_mlp.1 = (f32[256,5632]{1,0:T(8,128)}, f32[256,5632]{1,0:T(8,128)}, f32[5632,256]{1,0:T(8,128)}) custom-call(s32[4]{0:T(128)} %fusion.2.places_ref, bf16[256,2304]{1,0:T(8,128)(2,1)} %copy-done.18, bf16[256,2304]{1,0:T(8,128)(2,1)} %collective-permute-done.54.refs_1_, bf16[256,2304]{1,0:T(8,128)(2,1)} %copy-done.32, bf16[256,2304]{1,0:T(8,128)(2,1)} %copy-done.33, ...), custom_call_target="tpu_custom_call" | custom-call | flops 1000 | bytes 1000 | tf_op jit(solution)/shard_map/unpack_mlp/pallas_call | solution.py:875
  555.9 4.7 unpack_heads.1
  (258 shorter events, 129.4 us)
Async XLA Ops:
  3.2 17.3 %collective-permute-start = (bf16[272,1152]{1,0:T(8,128)(2,1)}, bf16[272,1152]{1,0:T(8,128)(2,1)S(1)}, u32[]{:S(2)}, u32[]{:S(2)}) collective-permute-start(bf16[272,1152]{1,0:T(8,128)(2,1)} %pack_heads.1.refs_4_), channel_id=1, source_target_pairs={{0,8},{8,16},{16,24},{24,28},{28,20},{20,12},{12,4},{4,0},{1,9},{9... | collective-permute-start | bytes 1880072 | tf_op jit(solution)/shard_map/ppermute | solution.py:82
  11.0 27.1 %collective-permute-start.2 = (bf16[256,2048]{1,0:T(8,128)(2,1)}, bf16[256,2048]{1,0:T(8,128)(2,1)}, u32[]{:S(2)}, u32[]{:S(2)}) collective-permute-start(bf16[256,2048]{1,0:T(8,128)(2,1)} %permute_features.2.refs_0_.inputs_ref), channel_id=1, source_target_pairs={{0,2},{1,3},{2,0},{3,1},{4,6},{5,7},{6,4},{7,5},{8,10},{9,11},{10,... | collective-permute-start | bytes 3145736 | tf_op jit(solution)/shard_map/ppermute | solution.py:176
  13.0 52.6 %collective-permute-start.5 = (bf16[256,2048]{1,0:T(8,128)(2,1)}, bf16[256,2048]{1,0:T(8,128)(2,1)}, u32[]{:S(2)}, u32[]{:S(2)}) collective-permute-start(bf16[256,2048]{1,0:T(8,128)(2,1)} %permute_features.2.refs_0_.inputs_ref), channel_id=1, source_target_pairs={{0,1},{1,0},{2,3},{3,2},{4,5},{5,4},{6,7},{7,6},{8,9},{9,8},{10,11... | collective-permute-start | bytes 3145736 | tf_op jit(solution)/shard_map/ppermute | solution.py:176
  38.1 27.5 %collective-permute-start.6 = (bf16[256,2048]{1,0:T(8,128)(2,1)}, bf16[256,2048]{1,0:T(8,128)(2,1)S(1)}, u32[]{:S(2)}, u32[]{:S(2)}) collective-permute-start(bf16[256,2048]{1,0:T(8,128)(2,1)} %collective-permute-done.2.refs_1_), channel_id=1, source_target_pairs={{0,1},{1,0},{2,3},{3,2},{4,5},{5,4},{6,7},{7,6},{8,9},{9,8},{10,11... | collective-permute-start | bytes 3145736 | tf_op jit(solution)/shard_map/ppermute | solution.py:176
  65.6 42.6 %collective-permute-start.14 = (bf16[256,2304]{1,0:T(8,128)(2,1)}, bf16[256,2304]{1,0:T(8,128)(2,1)}, u32[]{:S(2)}, u32[]{:S(2)}) collective-permute-start(bf16[256,2304]{1,0:T(8,128)(2,1)} %get-tuple-element.277.refs_4_), channel_id=1, source_target_pairs={{0,8},{8,16},{16,24},{24,28},{28,20},{20,12},{12,4},{4,0},{1,9},{9... | collective-permute-start | bytes 3538952 | tf_op jit(solution)/shard_map/ppermute | solution.py:82
  66.6 41.6 %collective-permute-start.15 = (bf16[256,2304]{1,0:T(8,128)(2,1)}, bf16[256,2304]{1,0:T(8,128)(2,1)}, u32[]{:S(2)}, u32[]{:S(2)}) collective-permute-start(bf16[256,2304]{1,0:T(8,128)(2,1)} %get-tuple-element.277.refs_4_), channel_id=1, source_target_pairs={{8,0},{16,8},{24,16},{28,24},{20,28},{12,20},{4,12},{0,4},{9,1},{1... | collective-permute-start | bytes 3538952 | tf_op jit(solution)/shard_map/ppermute | solution.py:85
  67.7 46.4 %collective-permute-start.11 = (bf16[256,2048]{1,0:T(8,128)(2,1)}, bf16[256,2048]{1,0:T(8,128)(2,1)S(1)}, u32[]{:S(2)}, u32[]{:S(2)}) collective-permute-start(bf16[256,2048]{1,0:T(8,128)(2,1)} %permute_features.3.refs_2_.refs_4_.cot_ref), channel_id=1, source_target_pairs={{0,2},{1,3},{2,0},{3,1},{4,6},{5,7},{6,4},{7,5},{8,10},{9,11},{10,... | collective-permute-start | bytes 3145736 | tf_op jit(solution)/shard_map/ppermute | solution.py:176
  69.3 43.8 %collective-permute-start.12 = (bf16[256,1920]{1,0:T(8,128)(2,1)}, bf16[256,1920]{1,0:T(8,128)(2,1)}, u32[]{:S(2)}, u32[]{:S(2)}) collective-permute-start(bf16[256,1920]{1,0:T(8,128)(2,1)} %get-tuple-element.331.refs_4_), channel_id=1, source_target_pairs={{0,8},{8,16},{16,24},{24,28},{28,20},{20,12},{12,4},{4,0},{1,9},{9... | collective-permute-start | bytes 2949128 | tf_op jit(solution)/shard_map/ppermute | solution.py:82
  70.2 43.8 %collective-permute-start.13 = (bf16[256,1920]{1,0:T(8,128)(2,1)}, bf16[256,1920]{1,0:T(8,128)(2,1)}, u32[]{:S(2)}, u32[]{:S(2)}) collective-permute-start(bf16[256,1920]{1,0:T(8,128)(2,1)} %get-tuple-element.331.refs_4_), channel_id=1, source_target_pairs={{8,0},{16,8},{24,16},{28,24},{20,28},{12,20},{4,12},{0,4},{9,1},{1... | collective-permute-start | bytes 2949128 | tf_op jit(solution)/shard_map/ppermute | solution.py:85
  114.1 28.7 %collective-permute-start.18 = (bf16[256,2304]{1,0:T(8,128)(2,1)}, bf16[256,2304]{1,0:T(8,128)(2,1)}, u32[]{:S(2)}, u32[]{:S(2)}) collective-permute-start(bf16[256,2304]{1,0:T(8,128)(2,1)} %collective-permute-done.14.refs_5_), channel_id=1, source_target_pairs={{0,8},{8,16},{16,24},{24,28},{28,20},{20,12},{12,4},{4,0},{1,9},{9... | collective-permute-start | bytes 3538952 | tf_op jit(solution)/shard_map/ppermute | solution.py:82
  115.0 28.4 %collective-permute-start.19 = (bf16[256,2304]{1,0:T(8,128)(2,1)}, bf16[256,2304]{1,0:T(8,128)(2,1)}, u32[]{:S(2)}, u32[]{:S(2)}) collective-permute-start(bf16[256,2304]{1,0:T(8,128)(2,1)} %collective-permute-done.15.refs_8_), channel_id=1, source_target_pairs={{8,0},{16,8},{24,16},{28,24},{20,28},{12,20},{4,12},{0,4},{9,1},{1... | collective-permute-start | bytes 3538952 | tf_op jit(solution)/shard_map/ppermute | solution.py:85
  120.8 25.4 %collective-permute-start.17 = (bf16[256,2048]{1,0:T(8,128)(2,1)S(1)}, bf16[256,2048]{1,0:T(8,128)(2,1)}, u32[]{:S(2)}, u32[]{:S(2)}) collective-permute-start(bf16[256,2048]{1,0:T(8,128)(2,1)S(1)} %add_convert_fusion.8), channel_id=1, source_target_pairs={{0,2},{1,3},{2,0},{3,1},{4,6},{5,7},{6,4},{7,5},{8,10},{9,11},{10,... | collective-permute-start | bytes 3145736 | tf_op jit(solution)/shard_map/ppermute | solution.py:176
  143.4 27.5 %collective-permute-start.21 = (bf16[256,2304]{1,0:T(8,128)(2,1)}, bf16[256,2304]{1,0:T(8,128)(2,1)}, u32[]{:S(2)}, u32[]{:S(2)}) collective-permute-start(bf16[256,2304]{1,0:T(8,128)(2,1)} %collective-permute-done.18.refs_6_), channel_id=1, source_target_pairs={{0,8},{8,16},{16,24},{24,28},{28,20},{20,12},{12,4},{4,0},{1,9},{9... | collective-permute-start | bytes 3538952 | tf_op jit(solution)/shard_map/ppermute | solution.py:82
  144.1 27.3 %collective-permute-start.22 = (bf16[256,2304]{1,0:T(8,128)(2,1)}, bf16[256,2304]{1,0:T(8,128)(2,1)}, u32[]{:S(2)}, u32[]{:S(2)}) collective-permute-start(bf16[256,2304]{1,0:T(8,128)(2,1)} %collective-permute-done.19.refs_9_), channel_id=1, source_target_pairs={{8,0},{16,8},{24,16},{28,24},{20,28},{12,20},{4,12},{0,4},{9,1},{1... | collective-permute-start | bytes 3538952 | tf_op jit(solution)/shard_map/ppermute | solution.py:85
  150.1 25.6 %collective-permute-start.20 = (bf16[256,2048]{1,0:T(8,128)(2,1)}, bf16[256,2048]{1,0:T(8,128)(2,1)S(1)}, u32[]{:S(2)}, u32[]{:S(2)}) collective-permute-start(bf16[256,2048]{1,0:T(8,128)(2,1)} %get-tuple-element.351.refs_0_), channel_id=1, source_target_pairs={{0,2},{1,3},{2,0},{3,1},{4,6},{5,7},{6,4},{7,5},{8,10},{9,11},{10,... | collective-permute-start | bytes 3145736 | tf_op jit(solution)/shard_map/ppermute | solution.py:176
  151.6 36.5 %collective-permute-start.23 = (bf16[256,2048]{1,0:T(8,128)(2,1)}, bf16[256,2048]{1,0:T(8,128)(2,1)S(1)}, u32[]{:S(2)}, u32[]{:S(2)}) collective-permute-start(bf16[256,2048]{1,0:T(8,128)(2,1)} %get-tuple-element.351.refs_0_), channel_id=1, source_target_pairs={{0,1},{1,0},{2,3},{3,2},{4,5},{5,4},{6,7},{7,6},{8,9},{9,8},{10,11... | collective-permute-start | bytes 3145736 | tf_op jit(solution)/shard_map/ppermute | solution.py:176
  187.4 22.9 %collective-permute-start.29 = (bf16[256,1920]{1,0:T(8,128)(2,1)}, bf16[256,1920]{1,0:T(8,128)(2,1)}, u32[]{:S(2)}, u32[]{:S(2)}) collective-permute-start(bf16[256,1920]{1,0:T(8,128)(2,1)} %collective-permute-done.12.refs_5_), channel_id=1, source_target_pairs={{0,8},{8,16},{16,24},{24,28},{28,20},{20,12},{12,4},{4,0},{1,9},{9... | collective-permute-start | bytes 2949128 | tf_op jit(solution)/shard_map/ppermute | solution.py:82
  188.1 22.8 %collective-permute-start.30 = (bf16[256,1920]{1,0:T(8,128)(2,1)}, bf16[256,1920]{1,0:T(8,128)(2,1)}, u32[]{:S(2)}, u32[]{:S(2)}) collective-permute-start(bf16[256,1920]{1,0:T(8,128)(2,1)} %collective-permute-done.13.refs_8_), channel_id=1, source_target_pairs={{8,0},{16,8},{24,16},{28,24},{20,28},{12,20},{4,12},{0,4},{9,1},{1... | collective-permute-start | bytes 2949128 | tf_op jit(solution)/shard_map/ppermute | solution.py:85
  211.0 22.0 %collective-permute-start.31 = (bf16[256,1920]{1,0:T(8,128)(2,1)}, bf16[256,1920]{1,0:T(8,128)(2,1)S(1)}, u32[]{:S(2)}, u32[]{:S(2)}) collective-permute-start(bf16[256,1920]{1,0:T(8,128)(2,1)} %collective-permute-done.29.refs_6_), channel_id=1, source_target_pairs={{0,8},{8,16},{16,24},{24,28},{28,20},{20,12},{12,4},{4,0},{1,9},{9... | collective-permute-start | bytes 2949128 | tf_op jit(solution)/shard_map/ppermute | solution.py:82
  211.7 21.3 %collective-permute-start.32 = (bf16[256,1920]{1,0:T(8,128)(2,1)}, bf16[256,1920]{1,0:T(8,128)(2,1)S(1)}, u32[]{:S(2)}, u32[]{:S(2)}) collective-permute-start(bf16[256,1920]{1,0:T(8,128)(2,1)} %collective-permute-done.30.refs_9_), channel_id=1, source_target_pairs={{8,0},{16,8},{24,16},{28,24},{20,28},{12,20},{4,12},{0,4},{9,1},{1... | collective-permute-start | bytes 2949128 | tf_op jit(solution)/shard_map/ppermute | solution.py:85
  233.0 18.8 %collective-permute-start.33 = (bf16[128,1920]{1,0:T(8,128)(2,1)S(1)}, bf16[128,1920]{1,0:T(8,128)(2,1)S(1)}, u32[]{:S(2)}, u32[]{:S(2)}) collective-permute-start(bf16[128,1920]{1,0:T(8,128)(2,1)S(1)} %slice.125), channel_id=1, source_target_pairs={{0,8},{8,16},{16,24},{24,28},{28,20},{20,12},{12,4},{4,0},{1,9},{9... | collective-permute-start | bytes 1474568 | tf_op jit(solution)/shard_map/ppermute | solution.py:82
  254.3 18.5 %collective-permute-start.35 = (bf16[128,2304]{1,0:T(8,128)(2,1)}, bf16[128,2304]{1,0:T(8,128)(2,1)S(1)}, u32[]{:S(2)}, u32[]{:S(2)}) collective-permute-start(bf16[128,2304]{1,0:T(8,128)(2,1)} %get-tuple-element.478), channel_id=1, source_target_pairs={{0,8},{8,16},{16,24},{24,28},{28,20},{20,12},{12,4},{4,0},{1,9},{9... | collective-permute-start | bytes 1769480 | tf_op jit(solution)/shard_map/ppermute | solution.py:82
  255.0 17.8 %collective-permute-start.36 = (bf16[128,2304]{1,0:T(8,128)(2,1)S(1)}, bf16[128,2304]{1,0:T(8,128)(2,1)S(1)}, u32[]{:S(2)}, u32[]{:S(2)}) collective-permute-start(bf16[128,2304]{1,0:T(8,128)(2,1)S(1)} %get-tuple-element.477), channel_id=1, source_target_pairs={{8,0},{16,8},{24,16},{28,24},{20,28},{12,20},{4,12},{0,4},{9,1},{1... | collective-permute-start | bytes 1769480 | tf_op jit(solution)/shard_map/ppermute | solution.py:85
  277.9 19.1 %collective-permute-start.37 = (bf16[512,2048]{1,0:T(8,128)(2,1)}, bf16[512,2048]{1,0:T(8,128)(2,1)}, u32[]{:S(2)}, u32[]{:S(2)}) collective-permute-start(bf16[512,2048]{1,0:T(8,128)(2,1)} %get-tuple-element.350), channel_id=1, source_target_pairs={{0,1},{1,0},{2,3},{3,2},{4,5},{5,4},{6,7},{7,6},{8,9},{9,8},{10,11... | collective-permute-start | bytes 6291464 | tf_op jit(solution)/shard_map/ppermute | solution.py:176
  277.9 19.1 %collective-permute-start.38 = (bf16[512,2048]{1,0:T(8,128)(2,1)}, bf16[512,2048]{1,0:T(8,128)(2,1)S(1)}, u32[]{:S(2)}, u32[]{:S(2)}) collective-permute-start(bf16[512,2048]{1,0:T(8,128)(2,1)} %get-tuple-element.356), channel_id=1, source_target_pairs={{0,1},{1,0},{2,3},{3,2},{4,5},{5,4},{6,7},{7,6},{8,9},{9,8},{10,11... | collective-permute-start | bytes 6291464 | tf_op jit(solution)/shard_map/ppermute | solution.py:176
  278.5 28.1 %collective-permute-start.40 = (bf16[256,2304]{1,0:T(8,128)(2,1)}, bf16[256,2304]{1,0:T(8,128)(2,1)S(1)}, u32[]{:S(2)}, u32[]{:S(2)}) collective-permute-start(bf16[256,2304]{1,0:T(8,128)(2,1)} %get-tuple-element.349), channel_id=1, source_target_pairs={{0,8},{8,16},{16,24},{24,28},{28,20},{20,12},{12,4},{4,0},{1,9},{9... | collective-permute-start | bytes 3538952 | tf_op jit(solution)/shard_map/ppermute | solution.py:82
  279.2 28.1 %collective-permute-start.41 = (bf16[256,2304]{1,0:T(8,128)(2,1)}, bf16[256,2304]{1,0:T(8,128)(2,1)}, u32[]{:S(2)}, u32[]{:S(2)}) collective-permute-start(bf16[256,2304]{1,0:T(8,128)(2,1)} %get-tuple-element.367), channel_id=1, source_target_pairs={{8,0},{16,8},{24,16},{28,24},{20,28},{12,20},{4,12},{0,4},{9,1},{1... | collective-permute-start | bytes 3538952 | tf_op jit(solution)/shard_map/ppermute | solution.py:85
  300.7 30.7 %collective-permute-start.39 = (bf16[256,2048]{1,0:T(8,128)(2,1)}, bf16[256,2048]{1,0:T(8,128)(2,1)}, u32[]{:S(2)}, u32[]{:S(2)}) collective-permute-start(bf16[256,2048]{1,0:T(8,128)(2,1)} %add_convert_fusion.7), channel_id=1, source_target_pairs={{0,2},{1,3},{2,0},{3,1},{4,6},{5,7},{6,4},{7,5},{8,10},{9,11},{10,... | collective-permute-start | bytes 3145736 | tf_op jit(solution)/shard_map/ppermute | solution.py:176
  311.2 30.0 %collective-permute-start.45 = (bf16[256,2304]{1,0:T(8,128)(2,1)}, bf16[256,2304]{1,0:T(8,128)(2,1)}, u32[]{:S(2)}, u32[]{:S(2)}) collective-permute-start(bf16[256,2304]{1,0:T(8,128)(2,1)} %get-tuple-element.370), channel_id=1, source_target_pairs={{0,8},{8,16},{16,24},{24,28},{28,20},{20,12},{12,4},{4,0},{1,9},{9... | collective-permute-start | bytes 3538952 | tf_op jit(solution)/shard_map/ppermute | solution.py:82
  312.2 29.2 %collective-permute-start.46 = (bf16[256,2304]{1,0:T(8,128)(2,1)}, bf16[256,2304]{1,0:T(8,128)(2,1)}, u32[]{:S(2)}, u32[]{:S(2)}) collective-permute-start(bf16[256,2304]{1,0:T(8,128)(2,1)} %get-tuple-element.375), channel_id=1, source_target_pairs={{8,0},{16,8},{24,16},{28,24},{20,28},{12,20},{4,12},{0,4},{9,1},{1... | collective-permute-start | bytes 3538952 | tf_op jit(solution)/shard_map/ppermute | solution.py:85
  329.4 19.4 %collective-permute-start.43 = (bf16[128,1920]{1,0:T(8,128)(2,1)}, bf16[128,1920]{1,0:T(8,128)(2,1)}, u32[]{:S(2)}, u32[]{:S(2)}) collective-permute-start(bf16[128,1920]{1,0:T(8,128)(2,1)} %get-tuple-element.484), channel_id=1, source_target_pairs={{0,8},{8,16},{16,24},{24,28},{28,20},{20,12},{12,4},{4,0},{1,9},{9... | collective-permute-start | bytes 1474568 | tf_op jit(solution)/shard_map/ppermute | solution.py:82
  330.4 19.1 %collective-permute-start.44 = (bf16[128,1920]{1,0:T(8,128)(2,1)}, bf16[128,1920]{1,0:T(8,128)(2,1)}, u32[]{:S(2)}, u32[]{:S(2)}) collective-permute-start(bf16[128,1920]{1,0:T(8,128)(2,1)} %get-tuple-element.483), channel_id=1, source_target_pairs={{8,0},{16,8},{24,16},{28,24},{20,28},{12,20},{4,12},{0,4},{9,1},{1... | collective-permute-start | bytes 1474568 | tf_op jit(solution)/shard_map/ppermute | solution.py:85
  337.0 23.2 %collective-permute-start.42 = (bf16[256,2048]{1,0:T(8,128)(2,1)}, bf16[256,2048]{1,0:T(8,128)(2,1)}, u32[]{:S(2)}, u32[]{:S(2)}) collective-permute-start(bf16[256,2048]{1,0:T(8,128)(2,1)} %get-tuple-element.387.refs_0_.refs_1_), channel_id=1, source_target_pairs={{0,2},{1,3},{2,0},{3,1},{4,6},{5,7},{6,4},{7,5},{8,10},{9,11},{10,... | collective-permute-start | bytes 3145736 | tf_op jit(solution)/shard_map/ppermute | solution.py:176
  341.2 22.0 %collective-permute-start.47 = (bf16[256,2048]{1,0:T(8,128)(2,1)S(1)}, bf16[256,2048]{1,0:T(8,128)(2,1)S(1)}, u32[]{:S(2)}, u32[]{:S(2)}) collective-permute-start(bf16[256,2048]{1,0:T(8,128)(2,1)S(1)} %copy-done.21), channel_id=1, source_target_pairs={{0,1},{1,0},{2,3},{3,2},{4,5},{5,4},{6,7},{7,6},{8,9},{9,8},{10,11... | collective-permute-start | bytes 3145736 | tf_op jit(solution)/shard_map/ppermute | solution.py:176
  360.2 35.6 %collective-permute-start.51 = (bf16[256,1920]{1,0:T(8,128)(2,1)}, bf16[256,1920]{1,0:T(8,128)(2,1)}, u32[]{:S(2)}, u32[]{:S(2)}) collective-permute-start(bf16[256,1920]{1,0:T(8,128)(2,1)} %get-tuple-element.384), channel_id=1, source_target_pairs={{0,8},{8,16},{16,24},{24,28},{28,20},{20,12},{12,4},{4,0},{1,9},{9... | collective-permute-start | bytes 2949128 | tf_op jit(solution)/shard_map/ppermute | solution.py:82
  361.2 34.7 %collective-permute-start.52 = (bf16[256,1920]{1,0:T(8,128)(2,1)}, bf16[256,1920]{1,0:T(8,128)(2,1)}, u32[]{:S(2)}, u32[]{:S(2)}) collective-permute-start(bf16[256,1920]{1,0:T(8,128)(2,1)} %get-tuple-element.394), channel_id=1, source_target_pairs={{8,0},{16,8},{24,16},{28,24},{20,28},{12,20},{4,12},{0,4},{9,1},{1... | collective-permute-start | bytes 2949128 | tf_op jit(solution)/shard_map/ppermute | solution.py:85
  362.3 47.7 %collective-permute-start.49 = (bf16[256,2304]{1,0:T(8,128)(2,1)}, bf16[256,2304]{1,0:T(8,128)(2,1)}, u32[]{:S(2)}, u32[]{:S(2)}) collective-permute-start(bf16[256,2304]{1,0:T(8,128)(2,1)} %get-tuple-element.379), channel_id=1, source_target_pairs={{0,8},{8,16},{16,24},{24,28},{28,20},{20,12},{12,4},{4,0},{1,9},{9... | collective-permute-start | bytes 3538952 | tf_op jit(solution)/shard_map/ppermute | solution.py:82
  363.2 47.5 %collective-permute-start.50 = (bf16[256,2304]{1,0:T(8,128)(2,1)}, bf16[256,2304]{1,0:T(8,128)(2,1)}, u32[]{:S(2)}, u32[]{:S(2)}) collective-permute-start(bf16[256,2304]{1,0:T(8,128)(2,1)} %get-tuple-element.393), channel_id=1, source_target_pairs={{8,0},{16,8},{24,16},{28,24},{20,28},{12,20},{4,12},{0,4},{9,1},{1... | collective-permute-start | bytes 3538952 | tf_op jit(solution)/shard_map/ppermute | solution.py:85
  364.3 48.8 %collective-permute-start.53 = (bf16[256,2048]{1,0:T(8,128)(2,1)}, bf16[256,2048]{1,0:T(8,128)(2,1)}, u32[]{:S(2)}, u32[]{:S(2)}) collective-permute-start(bf16[256,2048]{1,0:T(8,128)(2,1)} %add_convert_fusion.6), channel_id=1, source_target_pairs={{0,2},{1,3},{2,0},{3,1},{4,6},{5,7},{6,4},{7,5},{8,10},{9,11},{10,... | collective-permute-start | bytes 3145736 | tf_op jit(solution)/shard_map/ppermute | solution.py:176
  413.1 28.3 %collective-permute-start.54 = (bf16[256,2304]{1,0:T(8,128)(2,1)S(1)}, bf16[256,2304]{1,0:T(8,128)(2,1)}, u32[]{:S(2)}, u32[]{:S(2)}) collective-permute-start(bf16[256,2304]{1,0:T(8,128)(2,1)S(1)} %add_convert_fusion.refs_0_), channel_id=1, source_target_pairs={{0,2},{1,3},{2,0},{3,1},{4,6},{5,7},{6,4},{7,5},{8,10},{9,11},{10,... | collective-permute-start | bytes 3538952 | tf_op jit(solution)/shard_map/ppermute | solution.py:176
  414.6 26.7 %collective-permute-start.57 = (bf16[256,1920]{1,0:T(8,128)(2,1)}, bf16[256,1920]{1,0:T(8,128)(2,1)}, u32[]{:S(2)}, u32[]{:S(2)}) collective-permute-start(bf16[256,1920]{1,0:T(8,128)(2,1)} %get-tuple-element.397), channel_id=1, source_target_pairs={{0,8},{8,16},{16,24},{24,28},{28,20},{20,12},{12,4},{4,0},{1,9},{9... | collective-permute-start | bytes 2949128 | tf_op jit(solution)/shard_map/ppermute | solution.py:82
  416.4 25.0 %collective-permute-start.58 = (bf16[256,1920]{1,0:T(8,128)(2,1)}, bf16[256,1920]{1,0:T(8,128)(2,1)}, u32[]{:S(2)}, u32[]{:S(2)}) collective-permute-start(bf16[256,1920]{1,0:T(8,128)(2,1)} %get-tuple-element.416), channel_id=1, source_target_pairs={{8,0},{16,8},{24,16},{28,24},{20,28},{12,20},{4,12},{0,4},{9,1},{1... | collective-permute-start | bytes 2949128 | tf_op jit(solution)/shard_map/ppermute | solution.py:85
  451.2 37.0 %collective-permute-start.64 = (bf16[256,2048]{1,0:T(8,128)(2,1)}, bf16[256,2048]{1,0:T(8,128)(2,1)S(1)}, u32[]{:S(2)}, u32[]{:S(2)}) collective-permute-start(bf16[256,2048]{1,0:T(8,128)(2,1)} %add_convert_fusion.5), channel_id=1, source_target_pairs={{0,2},{1,3},{2,0},{3,1},{4,6},{5,7},{6,4},{7,5},{8,10},{9,11},{10,... | collective-permute-start | bytes 3145736 | tf_op jit(solution)/shard_map/ppermute | solution.py:176
  451.8 42.3 %collective-permute-start.62 = (bf16[256,1920]{1,0:T(8,128)(2,1)}, bf16[256,1920]{1,0:T(8,128)(2,1)S(1)}, u32[]{:S(2)}, u32[]{:S(2)}) collective-permute-start(bf16[256,1920]{1,0:T(8,128)(2,1)} %get-tuple-element.419), channel_id=1, source_target_pairs={{0,8},{8,16},{16,24},{24,28},{28,20},{20,12},{12,4},{4,0},{1,9},{9... | collective-permute-start | bytes 2949128 | tf_op jit(solution)/shard_map/ppermute | solution.py:82
  453.6 40.6 %collective-permute-start.63 = (bf16[256,1920]{1,0:T(8,128)(2,1)}, bf16[256,1920]{1,0:T(8,128)(2,1)}, u32[]{:S(2)}, u32[]{:S(2)}) collective-permute-start(bf16[256,1920]{1,0:T(8,128)(2,1)} %get-tuple-element.429), channel_id=1, source_target_pairs={{8,0},{16,8},{24,16},{28,24},{20,28},{12,20},{4,12},{0,4},{9,1},{1... | collective-permute-start | bytes 2949128 | tf_op jit(solution)/shard_map/ppermute | solution.py:85
  454.9 28.6 %collective-permute-start.55 = (bf16[144,1152]{1,0:T(8,128)(2,1)S(1)}, bf16[144,1152]{1,0:T(8,128)(2,1)}, u32[]{:S(2)}, u32[]{:S(2)}) collective-permute-start(bf16[144,1152]{1,0:T(8,128)(2,1)S(1)} %slice.145), channel_id=1, source_target_pairs={{0,8},{8,16},{16,24},{24,28},{28,20},{20,12},{12,4},{4,0},{1,9},{9... | collective-permute-start | bytes 995336 | tf_op jit(solution)/shard_map/ppermute | solution.py:82
  457.6 25.8 %collective-permute-start.56 = (bf16[128,1152]{1,0:T(8,128)(2,1)S(1)}, bf16[128,1152]{1,0:T(8,128)(2,1)}, u32[]{:S(2)}, u32[]{:S(2)}) collective-permute-start(bf16[128,1152]{1,0:T(8,128)(2,1)S(1)} %slice.146), channel_id=1, source_target_pairs={{8,0},{16,8},{24,16},{28,24},{20,28},{12,20},{4,12},{0,4},{9,1},{1... | collective-permute-start | bytes 884744 | tf_op jit(solution)/shard_map/ppermute | solution.py:85
  507.2 20.7 %collective-permute-start.69 = (bf16[256,1920]{1,0:T(8,128)(2,1)S(1)}, bf16[256,1920]{1,0:T(8,128)(2,1)}, u32[]{:S(2)}, u32[]{:S(2)}) collective-permute-start(bf16[256,1920]{1,0:T(8,128)(2,1)S(1)} %add_convert_fusion.9.refs_4_), channel_id=1, source_target_pairs={{0,2},{1,3},{2,0},{3,1},{4,6},{5,7},{6,4},{7,5},{8,10},{9,11},{10,... | collective-permute-start | bytes 2949128 | tf_op jit(solution)/shard_map/ppermute | solution.py:176
  (73 other events, 1031.4 us)

commit v4 on v3

--- a/solution.py
+++ b/solution.py
@@ -15,7 +15,25 @@
 BF = jnp.bfloat16
 F32 = jnp.float32
 NEG = -1e30
-VMEM_LIMIT = 60 << 20
+LIMITS = {
+    "attention_forward": 20,
+    "attention_backward": 16,
+    "heads_back": 14,
+    "mlp_half": 26,
+    "mlp_half_far": 44,
+    "weight_terms": 14,
+    "unpack_mlp": 28,
+    "unpack_heads": 12,
+    "permute_features": 56,
+    "pack_heads": 56,
+    "pack_mlp": 56,
+}
+
+
+def limits(name):
+    return pltpu.CompilerParams(vmem_limit_bytes=LIMITS.get(name, 12) << 20)
+
+
 COST = pl.CostEstimate(flops=1000, transcendentals=0, bytes_accessed=1000)
 
 
@@ -43,7 +61,7 @@
         in_specs=[pl.BlockSpec(memory_space=pltpu.SMEM)] * smem + [vmem] * (len(args) - smem),
         out_specs=tuple(vmem for _ in outs),
         scratch_shapes=list(scratch),
-        compiler_params=pltpu.CompilerParams(vmem_limit_bytes=VMEM_LIMIT),
+        compiler_params=limits(name),
         cost_estimate=COST,
         name=name,
     )(*args)
@@ -134,14 +152,11 @@
 
 class Scatter:
     def __init__(self, ring, terms, cut, tile):
-        self.ring, self.terms, self.cut, self.tile = ring, terms, cut, tile
-        self.full = terms.shape[0] // ring.size
-        begin = (ring.size - 1) * self.full
+        self.ring, self.cut, self.tile = ring, cut, tile
+        self.terms, up, down = terms
+        self.full = self.terms.shape[0] // ring.size
         self.left = ring.half - 1
-        self.flying = (
-            ring.go_up(terms[begin : begin + cut]),
-            ring.go_down(terms[begin + cut : begin + self.full]),
-        )
+        self.flying = (ring.go_up(up), ring.go_down(down))
 
     def term(self, slot, begin=0, end=None):
         end = self.full if end is None else end
@@ -254,6 +269,7 @@
             ],
             out_specs=whole((TOP + width, total)),
         ),
+        compiler_params=limits("pack_heads"),
         name="pack_heads",
     )(here, w_query, w_key, w_value, w_out, gain_attn, gain_mlp)
 
@@ -280,6 +296,7 @@
                 pl.BlockSpec((width, 3 * (b - a)), lambda i, o: (0, 0)) for a, b in bounds
             ),
         ),
+        compiler_params=limits("pack_mlp"),
         name="pack_mlp",
     )(here, w_gate, w_up, w_down)
 
@@ -474,7 +491,7 @@
                 value_acc[:keys, :] += against(probs.astype(BF), grad_h)
                 return 0
 
-            lax.fori_loop(0, n_heads, attend, 0, unroll=2)
+            lax.fori_loop(0, n_heads, attend, 0, unroll=8)
             turned = turn(rounded(grad_q_s[...]), cos_ref[:, at], -sin_ref[:, at])
             grad_q_ref[to, :] = turned.T.astype(BF)
         for block in range(4):
@@ -543,7 +560,7 @@
 
     first = pl.BlockSpec((rows, model), lambda i: (jnp.minimum(i, 1), 0))
     second = pl.BlockSpec((rows, model), lambda i: (jnp.maximum(i - 2, 0), 0))
-    fixed = lambda a: pl.BlockSpec(a.shape, lambda i: (0, 0), pipeline_mode=pl.Buffered(1))
+    fixed = lambda a: pl.BlockSpec(memory_space=pltpu.VMEM)
     half = jax.ShapeDtypeStruct((pack_size // 2, model), BF)
     return pl.pallas_call(
         body,
@@ -556,13 +573,13 @@
         + [fixed(a) for a in (*tokens, *pieces)],
         out_specs=(first, second, pl.BlockSpec((8, model), lambda i: (0, 0))),
         scratch_shapes=[pltpu.VMEM((model, heads_cols), BF), pltpu.VMEM((rows, model), BF)],
-        compiler_params=pltpu.CompilerParams(vmem_limit_bytes=VMEM_LIMIT),
+        compiler_params=limits("heads_back"),
         cost_estimate=COST,
         name="heads_back",
     )(grad_q, grad_kv, *tokens, *pieces)
 
 
-def mlp_half(tokens, cots, pieces, before, size):
+def mlp_half(tokens, cots, pieces, before, size, room="mlp_half"):
     rows, model = tokens[0].shape
 
     def body(*refs):
@@ -595,9 +612,7 @@
         grad_ref[...] = grad.astype(BF)
 
     by_rows = lambda cols: pl.BlockSpec((rows, cols), lambda i: (i, 0))
-    fixed = lambda array: pl.BlockSpec(
-        array.shape, lambda i: (0, 0), pipeline_mode=pl.Buffered(1)
-    )
+    fixed = lambda array: pl.BlockSpec(memory_space=pltpu.VMEM)
     half = jax.ShapeDtypeStruct((2 * rows, model), BF)
     return pl.pallas_call(
         body,
@@ -610,13 +625,13 @@
             pltpu.VMEM((rows, model), BF),
             pltpu.VMEM((rows, model), BF),
         ],
-        compiler_params=pltpu.CompilerParams(vmem_limit_bytes=VMEM_LIMIT),
+        compiler_params=limits(room),
         cost_estimate=COST,
         name="mlp_half",
     )(*tokens, *cots, *pieces, *before)
 
 
-def weight_terms(pairs, width, n_slots, group, tops=None):
+def weight_terms(pairs, width, n_slots, group, cut, tops=None):
     tokens = sum(x.shape[0] for x in pairs[0][0])
     total = sum(cols.stop - cols.start for _, _, cols in pairs)
     head = 0 if tops is None else TOP
@@ -639,7 +654,7 @@
         specs.append(pl.BlockSpec((x.shape[0], wide), lambda i: (0, i)))
     for g in [g for gs in g_lists for g in gs]:
         args.append(g)
-        specs.append(pl.BlockSpec(g.shape, lambda i: (0, 0), pipeline_mode=pl.Buffered(1)))
+        specs.append(pl.BlockSpec(memory_space=pltpu.VMEM))
     if head:
         args.append(tops)
         specs.append(pl.BlockSpec((group * TOP, total), lambda i: (i, 0)))
@@ -654,7 +669,7 @@
             return out
 
         x_refs, g_refs = take(x_lists), take(g_lists)
-        out_ref, x_s = refs[-2:]
+        out_ref, up_ref, down_ref, x_s = refs[-4:]
         lane = 0
         filled = None
         for xs, gs, cols in pairs:
@@ -686,14 +701,27 @@
                 at = j * (head + width)
                 out_ref[at : at + head, :] = refs[0][j * TOP : (j + 1) * TOP, :]
 
+        @pl.when(pl.program_id(0) == n_slots // group - 1)
+        def _():
+            begin = (group - 1) * (head + width)
+            up_ref[...] = out_ref[begin : begin + cut, :]
+            down_ref[...] = out_ref[begin + cut : begin + head + width, :]
+
+    far = [(cut, total), (head + width - cut, total)]
     return pl.pallas_call(
         body,
         grid=(n_slots // group,),
-        out_shape=jax.ShapeDtypeStruct((n_slots * (head + width), total), BF),
+        out_shape=(
+            jax.ShapeDtypeStruct((n_slots * (head + width), total), BF),
+            *[jax.ShapeDtypeStruct(shape, BF) for shape in far],
+        ),
         in_specs=specs,
-        out_specs=pl.BlockSpec((group * (head + width), total), lambda i: (i, 0)),
+        out_specs=(
+            pl.BlockSpec((group * (head + width), total), lambda i: (i, 0)),
+            *[pl.BlockSpec(shape, lambda i: (0, 0)) for shape in far],
+        ),
         scratch_shapes=[pltpu.VMEM((tokens, wide), BF)],
-        compiler_params=pltpu.CompilerParams(vmem_limit_bytes=VMEM_LIMIT),
+        compiler_params=limits("weight_terms"),
         cost_estimate=COST,
         name="weight_terms",
     )(*args)
@@ -727,6 +755,7 @@
             columns(down),
         ],
         out_specs=(columns(out), columns(out)),
+        compiler_params=limits("ring_add"),
         cost_estimate=COST,
         name="ring_add",
     )(terms, terms, up, down)
@@ -750,6 +779,7 @@
                 for s, _, split in outs
             ),
         ),
+        compiler_params=limits(name),
         cost_estimate=COST,
         name=name,
     )(*smem, *[a for a, _ in row_args], *fixed_args)
@@ -889,7 +919,7 @@
             out_specs=(columns, columns, pl.BlockSpec((ff, width), lambda i, p: (i, 0))),
             scratch_shapes=[pltpu.VMEM((width, 3 * (b - a)), BF) for a, b in bounds],
         ),
-        compiler_params=pltpu.CompilerParams(vmem_limit_bytes=VMEM_LIMIT),
+        compiler_params=limits("unpack_mlp"),
         cost_estimate=COST,
         name="unpack_mlp",
     )(places, *flat)
@@ -984,6 +1014,9 @@
     def other_half(keep, came):
         return plus(keep[rows:], came[rows:])
 
+    def far_memory(*arrays):
+        return [pltpu.with_memory_space_constraint(a, pltpu.HBM) for a in arrays]
+
     def four(block, across, beside):
         return [block, across, beside, swap(across, 1)]
 
@@ -1015,6 +1048,7 @@
     normed, query, kv, kvt, lse, mixed_t, mixed, keep, send, gains = attention_forward(
         places, lengths, live, tokens, head_pieces, cosine, sine_part, q_cols
     )
+    normed, query, kv, kvt, mixed_t, mixed = far_memory(normed, query, kv, kvt, mixed_t, mixed)
     clock.done(lse)
     chunks[0].relay(clock)
     chunks[1].land(clock)
@@ -1027,6 +1061,7 @@
     hidden, my_normed = second_norm(mine, keep, came, last, gains)
     clock.done(my_normed)
     across, beside = swap(my_normed, 2), swap(my_normed, 1)
+    beside = clock.tie(beside)
     chunks[0].relay(clock)
     across = clock.tie(across)
     seconds = four(my_normed, across, beside)
@@ -1041,39 +1076,46 @@
             width,
             n_dp,
             2,
+            middle,
         )
 
-    down_send, grad_send, both_send = mlp_half(seconds[2:], cots[2:], pieces, (), sizes[0])
+    down_send, grad_send, both_send = far_memory(
+        *mlp_half(seconds[2:], cots[2:], pieces, (), sizes[0])
+    )
     clock.done(both_send)
-    chunks[1].relay(clock)
     first_two = clock.tie(*seconds[:2])
-    down_keep, grad_keep, both_keep = mlp_half(first_two, cots[:2], pieces, (), sizes[0])
+    down_keep, grad_keep, both_keep = far_memory(
+        *mlp_half(first_two, cots[:2], pieces, (), sizes[0])
+    )
     clock.done(both_keep)
     chunks[1].relay(clock)
     both = list(clock.tie(both_keep, both_send))
     terms = terms_of(both, sizes[0])
-    clock.done(terms)
-    pieces = chunks[1].finish(clock)
-    sums = [Scatter(ring, clock.tie(terms), middle, sizes[0])]
+    clock.done(terms[0])
+    chunks[1].relay(clock)
+    pieces = far_memory(*chunks[1].finish(clock))
+    sums = [Scatter(ring, clock.tie(*terms), middle, sizes[0])]
     down_send, grad_send, both_send = mlp_half(
-        seconds[2:], cots[2:], clock.tie(*pieces), (down_send, grad_send), sizes[1]
+        seconds[2:], cots[2:], clock.tie(*pieces), (down_send, grad_send), sizes[1], "mlp_half_far"
     )
     clock.done(both_send)
+    both_send = far_memory(both_send)[0]
     sums[0].relay(clock)
     grad_send, down_send = clock.tie(grad_send, down_send)
     came, down_came = swap(grad_send, 1), swap(down_send, 1)
     first_two = clock.tie(*seconds[:2])
     down_keep, grad_keep, both_keep = mlp_half(
-        first_two, cots[:2], pieces, (down_keep, grad_keep), sizes[1]
-    )
+        first_two, cots[:2], pieces, (down_keep, grad_keep), sizes[1], "mlp_half_far"
+    )
+    both_keep = far_memory(both_keep)[0]
     clock.done(both_keep)
     came, down_came = clock.tie(came, down_came)
     last = swap(clock.tie(other_half(grad_keep, came)), 2)
     sums[0].relay(clock)
     both = list(clock.tie(both_keep, both_send))
     terms = terms_of(both, sizes[1])
-    clock.done(terms)
-    sums.append(Scatter(ring, clock.tie(terms), middle, sizes[1]))
+    clock.done(terms[0])
+    sums.append(Scatter(ring, clock.tie(*terms), middle, sizes[1]))
     last = clock.tie(last)
     grad_hidden, my_branch, gain_two_terms = second_norm_back(
         my_cot, hidden, grad_keep, came, last, gains
@@ -1081,22 +1123,19 @@
     clock.done(my_branch)
     across, beside = swap(my_branch, 2), swap(my_branch, 1)
     down_other = clock.tie(other_half(down_keep, down_came))
+    beside = clock.tie(beside)
     sums[0].relay(clock)
     sums[1].relay(clock)
     across = clock.tie(across)
     branches = four(my_branch, across, beside)
+    branches = list(clock.tie(*branches))
     down_last = swap(clock.tie(down_other), 2)
-    branches = list(clock.tie(*branches))
     grad_q, grad_kv = attention_backward(
         places, lengths, live, branches, head_pieces, cosine, sine_part,
         query, kv, kvt, lse, mixed_t
     )
     clock.done(grad_kv)
-    sums[1].relay(clock)
-    chunk_sum = sums[0].finish(clock)
-    down_last = clock.tie(down_last)
-    chunk_across, chunk_beside = swap(clock.tie(chunk_sum), 2), swap(chunk_sum, 1)
-    tokens = clock.tie(*tokens)
+    down_last, *tokens = clock.tie(down_last, *tokens)
     grad_keep, grad_send, gain_one_terms = heads_back(grad_q, grad_kv, tokens, head_pieces)
     clock.done(gain_one_terms)
     columns = head_block.shape[1]
@@ -1120,34 +1159,40 @@
         width,
         n_dp,
         2,
+        TOP + middle,
         tops,
     )
-    clock.done(head_terms)
+    clock.done(head_terms[0])
+    head_ring = Scatter(ring, head_terms, TOP + middle, columns)
+    sums[1].relay(clock)
+    chunk_sum = sums[0].finish(clock)
+    chunk_across, chunk_beside = swap(chunk_sum, 2), swap(chunk_sum, 1)
+    head_ring.relay(clock)
+    came = clock.tie(swap(clock.tie(grad_send), 1))
+    last = swap(clock.tie(other_half(grad_keep, came)), 2)
+    chunk_beside = clock.tie(chunk_beside)
+    sums[1].relay(clock)
     chunk_across = clock.tie(chunk_across)
     firsts = four(chunk_sum, chunk_across, chunk_beside)
-    head_ring = Scatter(ring, clock.tie(head_terms), TOP + middle, columns)
-    sums[1].relay(clock)
-    came = clock.tie(swap(clock.tie(grad_send), 1))
-    last = swap(clock.tie(other_half(grad_keep, came)), 2)
     head_ring.relay(clock)
+    firsts = list(clock.tie(*firsts))
     last = clock.tie(last)
-    firsts = list(clock.tie(*firsts))
     grad_input = first_norm_back(
         grad_hidden, mine, grad_keep, came, last, gains, ring.slot_owners(), n_dp
     )
     clock.done(grad_input)
-    second_sum = sums[1].finish(clock)
-    second_across, second_beside = swap(second_sum, 2), swap(second_sum, 1)
-    head_ring.relay(clock)
     down_came = clock.tie(down_came)
     result = layer_output(hidden, down_keep, down_came, down_last, ring.slot_owners(), n_dp)
     clock.done(result)
+    second_sum = sums[1].finish(clock)
+    second_across, second_beside = swap(second_sum, 2), swap(second_sum, 1)
+    second_beside = clock.tie(second_beside)
     head_ring.relay(clock)
+    head_sum = head_ring.finish(clock)
+    head_across, head_beside = swap(head_sum, 2), swap(head_sum, 1)
     second_across = clock.tie(second_across)
     others = four(second_sum, second_across, second_beside)
-    head_sum = head_ring.finish(clock)
-    head_across, head_beside = swap(head_sum, 2), swap(head_sum, 1)
-    firsts, others = list(clock.tie(*firsts)), list(clock.tie(*others))
+    others = list(clock.tie(*others))
     grad_gate, grad_up, grad_down = unpack_mlp(places, [firsts, others], bounds, width, ff)
     clock.done(grad_gate)
     head_across = clock.tie(head_across)

time: 570 us -> 550 us (0.965)
  waiting for transfers between devices: 189 us -> 254 us
  Pallas kernels: 240 us -> 181 us
  other arithmetic: 39.4 us -> 19.8 us
    ppermute x24, waiting for transfers between devices: 122 us -> 174 us  [go_up(): return lax.ppermute(block, 'dp', self.up)]
    ppermute x29, waiting for transfers between devices: 20.7 us -> 52.5 us  [swap(): return lax.ppermute(block, 'seq', [(i, i ^ distance) for i in range(4)])]
    ppermute x24, waiting for transfers between devices: 46.8 us -> 27.2 us  [go_down(): return lax.ppermute(block, 'dp', self.down)]
    pallas_call x4, Pallas kernels: 67.5 us -> 50.9 us  [mlp_half(): pl.pallas_call(body, grid=(2,), out_shape=(half, half, jax.ShapeDtypeStru...]
    convert_element_type x10, other arithmetic: 31.1 us -> 15 us  [plus(): return (one.astype(F32) + two.astype(F32)).astype(BF)]
    pallas_call x5, Pallas kernels: 75.2 us -> 59.2 us  [kernel_call(): pl.pallas_call(body, out_shape=tuple((jax.ShapeDtypeStruct(s, d) for s, d...]
    pallas_call x4, Pallas kernels: 18.7 us -> 10 us  [row_call(): pl.pallas_call(body, out_shape=tuple((jax.ShapeDtypeStruct(s, d) for s, d...]
    unnamed x88 -> x192, local copies, waits for them, and re-layouts: 7.12 us -> 15.7 us
  transfers between devices with their start and end apart: 77 -> 77, of which waited for: 39 -> 48; matrix products, arithmetic and copies ran while one was open for 8% -> 4% of each run, Pallas kernels for 41% -> 31%
where the time goes in v4:
time: 550 us; the launch traced here: 542 us
  waiting for transfers between devices  254 us (46%)
  Pallas kernels  181 us (33%)
  starting transfers between devices  66.3 us (12%)
  other arithmetic  19.8 us (4%)
  local copies, waits for them, and re-layouts  18.3 us (3%)
    ppermute x24, waiting for transfers between devices, go_up(): return lax.ppermute(block, 'dp', self.up)  174 us
    pallas_call x5, Pallas kernels, kernel_call(): pl.pallas_call(body, out_shape=tuple((jax.ShapeDtypeStruct(s, d) for s, d...  59.2 us
    ppermute x29, waiting for transfers between devices, swap(): return lax.ppermute(block, 'seq', [(i, i ^ distance) for i in range(4)])  52.5 us
    pallas_call x4, Pallas kernels, mlp_half(): pl.pallas_call(body, grid=(2,), out_shape=(half, half, jax.ShapeDtypeStru...  50.9 us
    pallas_call x3, Pallas kernels, weight_terms(): pl.pallas_call(body, grid=(n_slots // group,), out_shape=(jax.ShapeDtypeS...  35.7 us
    ppermute x24, starting transfers between devices, go_up(): return lax.ppermute(block, 'dp', self.up)  29.5 us
    ppermute x24, waiting for transfers between devices, go_down(): return lax.ppermute(block, 'dp', self.down)  27.2 us
    ppermute x24, starting transfers between devices, go_down(): return lax.ppermute(block, 'dp', self.down)  21.5 us
  transfers between devices with their start and end apart: 77, of which 48 were waited for; matrix products, arithmetic and copies ran while one was open for 4% of the time, Pallas kernels for 31%

profile of v4, /device:TPU:0, one launch (start us, length us, event | category | flops | bytes accessed | tf_op | source)
XLA Modules:
  0.0 542.1 jit_solution(8436717047656569229)
XLA Ops:
  0.7 2.6 pack_heads.1.refs_4_
  3.3 3.0 collective-permute-start
  8.7 2.4 permute_features.2.refs_0_.inputs_ref
  13.3 3.1 pack_mlp.1
  16.4 4.1 collective-permute-done.refs_5_
  25.4 2.4 permute_features.3.refs_2_.refs_4_.cot_ref
  27.9 8.9 %collective-permute-done.3.refs_6_ = bf16[272,1152]{1,0:T(8,128)(2,1)S(1)} collective-permute-done((bf16[272,1152]{1,0:T(8,128)(2,1)S(1)}, bf16[272,1152]{1,0:T(8,128)(2,1)S(1)}, u32[]{:S(2)}, u32[]{:S(2)}) %collective-permute-start.3) | collective-permute-done | bytes 626720 | tf_op jit(solution)/shard_map/ppermute | solution.py:100
  40.2 14.4 %collective-permute-done.7.refs_7_ = bf16[272,1152]{1,0:T(8,128)(2,1)S(1)} collective-permute-done((bf16[272,1152]{1,0:T(8,128)(2,1)S(1)}, bf16[272,1152]{1,0:T(8,128)(2,1)S(1)}, u32[]{:S(2)}, u32[]{:S(2)}) %collective-permute-start.7) | collective-permute-done | bytes 626720 | tf_op jit(solution)/shard_map/ppermute | solution.py:100
  58.1 7.4 %collective-permute-done.10.refs_12_ = bf16[128,1152]{1,0:T(8,128)(2,1)S(1)} collective-permute-done((bf16[128,1152]{1,0:T(8,128)(2,1)S(1)}, bf16[128,1152]{1,0:T(8,128)(2,1)S(1)}, u32[]{:S(2)}, u32[]{:S(2)}) %collective-permute-start.10) | collective-permute-done | bytes 294944 | tf_op jit(solution)/shard_map/ppermute | solution.py:103
  72.9 28.1 %attention_forward.1 = (bf16[1024,2048]{1,0:T(8,128)(2,1)S(1)}, bf16[512,1024]{1,0:T(8,128)(2,1)S(1)}, bf16[1024,128]{1,0:T(8,128)(2,1)S(1)}, bf16[192,1024]{1,0...) custom-call(s32[4]{0:T(128)S(1)} %fusion.2.places_ref, ...), custom_call_target="tpu_custom_call" | custom-call | flops 1000 | bytes 1000 | tf_op jit(solution)/shard_map/attention_forward/pallas_call | solution.py:58
  102.9 9.9 %collective-permute-done.12.refs_5_ = bf16[256,1920]{1,0:T(8,128)(2,1)S(1)} collective-permute-done((bf16[256,1920]{1,0:T(8,128)(2,1)}, bf16[256,1920]{1,0:T(8,128)(2,1)S(1)}, u32[]{:S(2)}, u32[]{:S(2)}) %collective-permute-start.12) | collective-permute-done | bytes 983072 | tf_op jit(solution)/shard_map/ppermute | solution.py:100
  119.9 22.2 %collective-permute-done.18.refs_6_ = bf16[256,2304]{1,0:T(8,128)(2,1)S(1)} collective-permute-done((bf16[256,2304]{1,0:T(8,128)(2,1)S(1)}, bf16[256,2304]{1,0:T(8,128)(2,1)S(1)}, u32[]{:S(2)}, u32[]{:S(2)}) %collective-permute-start.18) | collective-permute-done | bytes 1179680 | tf_op jit(solution)/shard_map/ppermute | solution.py:100
  149.7 20.1 %collective-permute-done.21.refs_7_ = bf16[256,2304]{1,0:T(8,128)(2,1)S(1)} collective-permute-done((bf16[256,2304]{1,0:T(8,128)(2,1)S(1)}, bf16[256,2304]{1,0:T(8,128)(2,1)S(1)}, u32[]{:S(2)}, u32[]{:S(2)}) %collective-permute-start.21) | collective-permute-done | bytes 1179680 | tf_op jit(solution)/shard_map/ppermute | solution.py:100
  173.2 10.5 %collective-permute-done.25.refs_11_ = bf16[128,2304]{1,0:T(8,128)(2,1)S(1)} collective-permute-done((bf16[128,2304]{1,0:T(8,128)(2,1)S(1)}, bf16[128,2304]{1,0:T(8,128)(2,1)S(1)}, u32[]{:S(2)}, u32[]{:S(2)}) %collective-permute-start.25) | collective-permute-done | bytes 589856 | tf_op jit(solution)/shard_map/ppermute | solution.py:100
  186.5 11.1 %mlp_half.4 = (bf16[512,2048]{1,0:T(8,128)(2,1)S(1)}, bf16[512,2048]{1,0:T(8,128)(2,1)S(1)}, bf16[512,2304]{1,0:T(8,128)(2,1)S(1)}) custom-call(bf16[256,2048]{1,0:T(8,128)(2,1)S(1)} %collective-permute-done.23.refs_0_.refs_2_, bf16[256,2048]{1,0:T(8,128)(2,1)S(1)} %collective-permute-done.24.refs_1_.refs_3_, ...), custom_call_target="tpu_custom_call" | custom-call | flops 1000 | bytes 1000 | tf_op jit(solution)/shard_map/mlp_half/pallas_call | solution.py:617
  201.7 11.1 %mlp_half.5 = (bf16[512,2048]{1,0:T(8,128)(2,1)S(1)}, bf16[512,2048]{1,0:T(8,128)(2,1)S(1)}, bf16[512,2304]{1,0:T(8,128)(2,1)S(1)}) custom-call(bf16[256,2048]{1,0:T(8,128)(2,1)S(1)} %get-tuple-element.366.refs_0_, bf16[256,2048]{1,0:T(8,128)(2,1)S(1)} %collective-permute-done.20.refs_1_, bf16[256,2048]{1,0:T(8,128)(2,1)S(1)} %copy-done, ...), custom_call_target="tpu_custom_call" | custom-call | flops 1000 | bytes 1000 | tf_op jit(solution)/shard_map/mlp_half/pallas_call | solution.py:617
  216.5 14.6 %weight_terms.3 = (bf16[2048,2304]{1,0:T(8,128)(2,1)S(1)}, bf16[128,2304]{1,0:T(8,128)(2,1)}, bf16[128,2304]{1,0:T(8,128)(2,1)}) custom-call(bf16[256,2048]{1,0:T(8,128)(2,1)S(1)} %get-tuple-element.366.refs_0_, bf16[256,2048]{1,0:T(8,128)(2,1)S(1)} %collective-permute-done.20.refs_1_, bf16[256,2048]{1,0:T(8,128)(2,1)S(1)} %collective-permute-done.23.refs_0_.refs_2_, ...), custom_call_target="tpu_custom_call" | custom-call | flops 1000 | bytes 1000 | tf_op jit(solution)/shard_map/weight_terms/pallas_call | solution.py:711
  231.2 4.5 collective-permute-done.31.refs_7_
  238.7 8.9 %collective-permute-done.33.refs_11_ = bf16[128,1920]{1,0:T(8,128)(2,1)S(1)} collective-permute-done((bf16[128,1920]{1,0:T(8,128)(2,1)S(1)}, bf16[128,1920]{1,0:T(8,128)(2,1)S(1)}, u32[]{:S(2)}, u32[]{:S(2)}) %collective-permute-start.33) | collective-permute-done | bytes 491552 | tf_op jit(solution)/shard_map/ppermute | solution.py:100
  253.8 14.9 %mlp_half.6 = (bf16[512,2048]{1,0:T(8,128)(2,1)}, bf16[512,2048]{1,0:T(8,128)(2,1)}, bf16[512,1920]{1,0:T(8,128)(2,1)S(1)}) custom-call(bf16[256,2048]{1,0:T(8,128)(2,1)S(1)} %copy-done.8, bf16[256,2048]{1,0:T(8,128)(2,1)S(1)} %copy-done.13, bf16[256,2048]{1,0:T(8,128)(2,1)S(1)} %copy-done.16, bf16[256,2048]{1,0:T(8,128)(2,1)S(1)} %copy-done.19, ...), custom_call_target="tpu_custom_call" | custom-call | flops 1000 | bytes 1000 | tf_op jit(solution)/shard_map/mlp_half/pallas_call | solution.py:617
  268.7 4.5 ring_add.3
  276.1 13.9 %mlp_half.7 = (bf16[512,2048]{1,0:T(8,128)(2,1)S(1)}, bf16[512,2048]{1,0:T(8,128)(2,1)S(1)}, bf16[512,1920]{1,0:T(8,128)(2,1)S(1)}) custom-call(bf16[256,2048]{1,0:T(8,128)(2,1)S(1)} %copy-done.6, bf16[256,2048]{1,0:T(8,128)(2,1)S(1)} %copy-done.11, bf16[256,2048]{1,0:T(8,128)(2,1)S(1)} %copy-done, bf16[256,2048]{1,0:T(8,128)(2,1)S(1)} %copy-done.4, ...), custom_call_target="tpu_custom_call" | custom-call | flops 1000 | bytes 1000 | tf_op jit(solution)/shard_map/mlp_half/pallas_call | solution.py:617
  290.1 2.4 add_convert_fusion.7
  294.1 8.1 %collective-permute-done.40 = bf16[256,2304]{1,0:T(8,128)(2,1)} collective-permute-done((bf16[256,2304]{1,0:T(8,128)(2,1)}, bf16[256,2304]{1,0:T(8,128)(2,1)}, u32[]{:S(2)}, u32[]{:S(2)}) %collective-permute-start.40) | collective-permute-done | bytes 1179680 | tf_op jit(solution)/shard_map/ppermute | solution.py:100
  304.0 3.6 add_convert_fusion.3
  309.7 12.3 %weight_terms.4 = (bf16[2048,1920]{1,0:T(8,128)(2,1)S(1)}, bf16[128,1920]{1,0:T(8,128)(2,1)S(1)}, bf16[128,1920]{1,0:T(8,128)(2,1)S(1)}) custom-call(bf16[256,2048]{1,0:T(8,128)(2,1)S(1)} %copy-done.6, bf16[256,2048]{1,0:T(8,128)(2,1)S(1)} %copy-done.11, bf16[256,2048]{1,0:T(8,128)(2,1)S(1)} %copy-done.9, bf16[256,2048]{1,0:T(8,128)(2,1)S(1)} %copy-done.14, ...), custom_call_target="tpu_custom_call" | custom-call | flops 1000 | bytes 1000 | tf_op jit(solution)/shard_map/weight_terms/pallas_call | solution.py:711
  322.0 3.2 second_norm_back.1
  331.7 5.1 collective-permute-done.45
  338.9 3.6 add_convert_fusion.1
  342.6 2.9 collective-permute-done.43.up_ref
  348.0 5.8 %collective-permute-done.42.refs_1_.refs_2_ = bf16[256,2048]{1,0:T(8,128)(2,1)S(1)} collective-permute-done((bf16[256,2048]{1,0:T(8,128)(2,1)S(1)}, bf16[256,2048]{1,0:T(8,128)(2,1)S(1)}, u32[]{:S(2)}, u32[]{:S(2)}) %collective-permute-start.42) | collective-permute-done | bytes 1048608 | tf_op jit(solution)/shard_map/ppermute | solution.py:191
  353.8 2.7 collective-permute-done.48.refs_3_.refs_4_
  362.3 22.8 %attention_backward.1 = (bf16[1024,512]{1,0:T(8,128)(2,1)S(1)}, bf16[1024,128]{1,0:T(8,128)(2,1)S(1)}) custom-call(s32[4]{0:T(128)S(1)} %copy-done.79, s32[6]{0:T(128)S(1)} %bitcast.12, s32[1]{0:T(128)S(6)} %copy.42.live_ref, f32[32,1024]{1,0:T(8,128)S(1)} %copy-done.68, f32[32,1024]{1,0:T(8,128)S(1)} %copy-done.66, bf16[512,1024]{1,0:T(8,128)(2,1)} %copy-done.72, ...), custom_call_target="tpu_custom_call" | custom-call | flops 1000 | bytes 1000 | tf_op jit(solution)/shard_map/attention_backward/pallas_call | solution.py:58
  385.1 6.6 %heads_back.1 = (bf16[512,2048]{1,0:T(8,128)(2,1)S(1)}, bf16[512,2048]{1,0:T(8,128)(2,1)S(1)}, f32[8,2048]{1,0:T(8,128)S(1)}) custom-call(bf16[1024,512]{1,0:T(8,128)(2,1)S(1)} %get-tuple-element.409.grad_q_ref.refs_5_, bf16[1024,128]{1,0:T(8,128)(2,1)S(1)} %get-tuple-element.410.grad_kv_ref.refs_6_, bf16[256,2048]{1,0:T(8,128)(2,1)S(1)} %copy-done.2, ...), custom_call_target="tpu_custom_call" | custom-call | flops 1000 | bytes 1000 | tf_op jit(solution)/shard_map/heads_back/pallas_call | solution.py:565
  391.9 8.8 %weight_terms.5 = (bf16[2176,1152]{1,0:T(8,128)(2,1)S(1)}, bf16[144,1152]{1,0:T(8,128)(2,1)S(1)}, bf16[128,1152]{1,0:T(8,128)(2,1)S(1)}) custom-call(bf16[1024,2048]{1,0:T(8,128)(2,1)} %copy-done.47, bf16[256,2048]{1,0:T(8,128)(2,1)S(1)} %get-tuple-element.405.refs_0_.refs_1_, bf16[256,2048]{1,0:T(8,128)(2,1)S(1)} %copy-done.49, ...), custom_call_target="tpu_custom_call" | custom-call | flops 1000 | bytes 1000 | tf_op jit(solution)/shard_map/weight_terms/pallas_call | solution.py:711
  411.9 2.7 collective-permute-done.51.down_ref
  421.5 18.5 %collective-permute-done.59 = bf16[256,1920]{1,0:T(8,128)(2,1)S(1)} collective-permute-done((bf16[256,1920]{1,0:T(8,128)(2,1)S(1)}, bf16[256,1920]{1,0:T(8,128)(2,1)S(1)}, u32[]{:S(2)}, u32[]{:S(2)}) %collective-permute-start.59) | collective-permute-done | bytes 983072 | tf_op jit(solution)/shard_map/ppermute | solution.py:100
  441.8 3.2 collective-permute-done.58.refs_1_
  446.6 6.8 %collective-permute-done.63 = bf16[272,1152]{1,0:T(8,128)(2,1)S(1)} collective-permute-done((bf16[272,1152]{1,0:T(8,128)(2,1)S(1)}, bf16[272,1152]{1,0:T(8,128)(2,1)S(1)}, u32[]{:S(2)}, u32[]{:S(2)}) %collective-permute-start.63) | collective-permute-done | bytes 626720 | tf_op jit(solution)/shard_map/ppermute | solution.py:100
  454.0 16.5 %collective-permute-done.57.last_ref = bf16[256,2048]{1,0:T(8,128)(2,1)S(1)} collective-permute-done((bf16[256,2048]{1,0:T(8,128)(2,1)S(1)}, bf16[256,2048]{1,0:T(8,128)(2,1)S(1)}, u32[]{:S(2)}, u32[]{:S(2)}) %collective-permute-start.57) | collective-permute-done | bytes 1048608 | tf_op jit(solution)/shard_map/ppermute | solution.py:191
  470.6 2.9 first_norm_back.1
  473.5 2.9 layer_output.1
  479.4 14.0 %collective-permute-done.65 = bf16[272,1152]{1,0:T(8,128)(2,1)S(1)} collective-permute-done((bf16[272,1152]{1,0:T(8,128)(2,1)S(1)}, bf16[272,1152]{1,0:T(8,128)(2,1)S(1)}, u32[]{:S(2)}, u32[]{:S(2)}) %collective-permute-start.65) | collective-permute-done | bytes 626720 | tf_op jit(solution)/shard_map/ppermute | solution.py:100
  497.0 12.8 %collective-permute-done.70 = bf16[272,1152]{1,0:T(8,128)(2,1)S(1)} collective-permute-done((bf16[272,1152]{1,0:T(8,128)(2,1)S(1)}, bf16[272,1152]{1,0:T(8,128)(2,1)S(1)}, u32[]{:S(2)}, u32[]{:S(2)}) %collective-permute-start.70) | collective-permute-done | bytes 626720 | tf_op jit(solution)/shard_map/ppermute | solution.py:100
  510.4 8.5 %collective-permute-done.73.refs_5_ = bf16[256,1920]{1,0:T(8,128)(2,1)S(1)} collective-permute-done((bf16[256,1920]{1,0:T(8,128)(2,1)S(1)}, bf16[256,1920]{1,0:T(8,128)(2,1)S(1)}, u32[]{:S(2)}, u32[]{:S(2)}) %collective-permute-start.73) | collective-permute-done | bytes 983072 | tf_op jit(solution)/shard_map/ppermute | solution.py:191
  521.5 7.1 %unpack_mlp.1 = (f32[256,5632]{1,0:T(8,128)}, f32[256,5632]{1,0:T(8,128)}, f32[5632,256]{1,0:T(8,128)}) custom-call(s32[4]{0:T(128)S(1)} %copy-done.79, bf16[256,2304]{1,0:T(8,128)(2,1)S(1)} %add_convert_fusion.refs_0_, bf16[256,2304]{1,0:T(8,128)(2,1)S(1)} %collective-permute-done.58.refs_1_, bf16[256,2304]{1,0:T(8,128)(2,1)S(1)} %collective-permute-done.61.refs_2_, ...), custom_call_target="tpu_custom_call" | custom-call | flops 1000 | bytes 1000 | tf_op jit(solution)/shard_map/unpack_mlp/pallas_call | solution.py:905
  528.7 6.8 %collective-permute-done.72.refs_1_ = bf16[272,1152]{1,0:T(8,128)(2,1)S(1)} collective-permute-done((bf16[272,1152]{1,0:T(8,128)(2,1)S(1)}, bf16[272,1152]{1,0:T(8,128)(2,1)S(1)}, u32[]{:S(2)}, u32[]{:S(2)}) %collective-permute-start.72) | collective-permute-done | bytes 626720 | tf_op jit(solution)/shard_map/ppermute | solution.py:191
  537.6 3.6 unpack_heads.1
  (358 shorter events, 122.1 us)
Async XLA Ops:
  3.3 17.3 %collective-permute-start = (bf16[272,1152]{1,0:T(8,128)(2,1)}, bf16[272,1152]{1,0:T(8,128)(2,1)S(1)}, u32[]{:S(2)}, u32[]{:S(2)}) collective-permute-start(bf16[272,1152]{1,0:T(8,128)(2,1)} %pack_heads.1.refs_4_), channel_id=1, source_target_pairs={{0,8},{8,16},{16,24},{24,28},{28,20},{20,12},{12,4},{4,0},{1,9},{9... | collective-permute-start | bytes 1880072 | tf_op jit(solution)/shard_map/ppermute | solution.py:100
  11.1 26.9 %collective-permute-start.2 = (bf16[256,2048]{1,0:T(8,128)(2,1)}, bf16[256,2048]{1,0:T(8,128)(2,1)S(1)}, u32[]{:S(2)}, u32[]{:S(2)}) collective-permute-start(bf16[256,2048]{1,0:T(8,128)(2,1)} %permute_features.2.refs_0_.inputs_ref), channel_id=1, source_target_pairs={{0,2},{1,3},{2,0},{3,1},{4,6},{5,7},{6,4},{7,5},{8,10},{9,11},{10,... | collective-permute-start | bytes 3145736 | tf_op jit(solution)/shard_map/ppermute | solution.py:191
  13.1 52.5 %collective-permute-start.5 = (bf16[256,2048]{1,0:T(8,128)(2,1)}, bf16[256,2048]{1,0:T(8,128)(2,1)S(1)}, u32[]{:S(2)}, u32[]{:S(2)}) collective-permute-start(bf16[256,2048]{1,0:T(8,128)(2,1)} %permute_features.2.refs_0_.inputs_ref), channel_id=1, source_target_pairs={{0,1},{1,0},{2,3},{3,2},{4,5},{5,4},{6,7},{7,6},{8,9},{9,8},{10,11... | collective-permute-start | bytes 3145736 | tf_op jit(solution)/shard_map/ppermute | solution.py:191
  38.1 27.5 %collective-permute-start.6 = (bf16[256,2048]{1,0:T(8,128)(2,1)S(1)}, bf16[256,2048]{1,0:T(8,128)(2,1)S(1)}, u32[]{:S(2)}, u32[]{:S(2)}) collective-permute-start(bf16[256,2048]{1,0:T(8,128)(2,1)S(1)} %collective-permute-done.2.refs_1_), channel_id=1, source_target_pairs={{0,1},{1,0},{2,3},{3,2},{4,5},{5,4},{6,7},{7,6},{8,9},{9,8},{10,11... | collective-permute-start | bytes 3145736 | tf_op jit(solution)/shard_map/ppermute | solution.py:191
  38.1 16.5 %collective-permute-start.7 = (bf16[272,1152]{1,0:T(8,128)(2,1)S(1)}, bf16[272,1152]{1,0:T(8,128)(2,1)S(1)}, u32[]{:S(2)}, u32[]{:S(2)}) collective-permute-start(bf16[272,1152]{1,0:T(8,128)(2,1)S(1)} %collective-permute-done.3.refs_6_), channel_id=1, source_target_pairs={{0,8},{8,16},{16,24},{24,28},{28,20},{20,12},{12,4},{4,0},{1,9},{9... | collective-permute-start | bytes 1880072 | tf_op jit(solution)/shard_map/ppermute | solution.py:100
  39.8 16.2 %collective-permute-start.8 = (bf16[272,1152]{1,0:T(8,128)(2,1)S(1)}, bf16[272,1152]{1,0:T(8,128)(2,1)S(1)}, u32[]{:S(2)}, u32[]{:S(2)}) collective-permute-start(bf16[272,1152]{1,0:T(8,128)(2,1)S(1)} %collective-permute-done.4.refs_9_), channel_id=1, source_target_pairs={{8,0},{16,8},{24,16},{28,24},{20,28},{12,20},{4,12},{0,4},{9,1},{1... | collective-permute-start | bytes 1880072 | tf_op jit(solution)/shard_map/ppermute | solution.py:103
  65.6 37.2 %collective-permute-start.14 = (bf16[256,2304]{1,0:T(8,128)(2,1)S(1)}, bf16[256,2304]{1,0:T(8,128)(2,1)S(1)}, u32[]{:S(2)}, u32[]{:S(2)}) collective-permute-start(bf16[256,2304]{1,0:T(8,128)(2,1)S(1)} %copy-done.40), channel_id=1, source_target_pairs={{0,8},{8,16},{16,24},{24,28},{28,20},{20,12},{12,4},{4,0},{1,9},{9... | collective-permute-start | bytes 3538952 | tf_op jit(solution)/shard_map/ppermute | solution.py:100
  66.7 36.2 %collective-permute-start.15 = (bf16[256,2304]{1,0:T(8,128)(2,1)S(1)}, bf16[256,2304]{1,0:T(8,128)(2,1)S(1)}, u32[]{:S(2)}, u32[]{:S(2)}) collective-permute-start(bf16[256,2304]{1,0:T(8,128)(2,1)S(1)} %copy-done.40), channel_id=1, source_target_pairs={{8,0},{16,8},{24,16},{28,24},{20,28},{12,20},{4,12},{0,4},{9,1},{1... | collective-permute-start | bytes 3538952 | tf_op jit(solution)/shard_map/ppermute | solution.py:103
  67.7 46.0 %collective-permute-start.11 = (bf16[256,2048]{1,0:T(8,128)(2,1)}, bf16[256,2048]{1,0:T(8,128)(2,1)S(1)}, u32[]{:S(2)}, u32[]{:S(2)}) collective-permute-start(bf16[256,2048]{1,0:T(8,128)(2,1)} %permute_features.3.refs_2_.refs_4_.cot_ref), channel_id=1, source_target_pairs={{0,2},{1,3},{2,0},{3,1},{4,6},{5,7},{6,4},{7,5},{8,10},{9,11},{10,... | collective-permute-start | bytes 3145736 | tf_op jit(solution)/shard_map/ppermute | solution.py:191
  69.2 43.5 %collective-permute-start.12 = (bf16[256,1920]{1,0:T(8,128)(2,1)}, bf16[256,1920]{1,0:T(8,128)(2,1)S(1)}, u32[]{:S(2)}, u32[]{:S(2)}) collective-permute-start(bf16[256,1920]{1,0:T(8,128)(2,1)} %get-tuple-element.344.refs_4_), channel_id=1, source_target_pairs={{0,8},{8,16},{16,24},{24,28},{28,20},{20,12},{12,4},{4,0},{1,9},{9... | collective-permute-start | bytes 2949128 | tf_op jit(solution)/shard_map/ppermute | solution.py:100
  70.2 43.5 %collective-permute-start.13 = (bf16[256,1920]{1,0:T(8,128)(2,1)}, bf16[256,1920]{1,0:T(8,128)(2,1)S(1)}, u32[]{:S(2)}, u32[]{:S(2)}) collective-permute-start(bf16[256,1920]{1,0:T(8,128)(2,1)} %get-tuple-element.344.refs_4_), channel_id=1, source_target_pairs={{8,0},{16,8},{24,16},{28,24},{20,28},{12,20},{4,12},{0,4},{9,1},{1... | collective-permute-start | bytes 2949128 | tf_op jit(solution)/shard_map/ppermute | solution.py:103
  113.8 28.4 %collective-permute-start.18 = (bf16[256,2304]{1,0:T(8,128)(2,1)S(1)}, bf16[256,2304]{1,0:T(8,128)(2,1)S(1)}, u32[]{:S(2)}, u32[]{:S(2)}) collective-permute-start(bf16[256,2304]{1,0:T(8,128)(2,1)S(1)} %collective-permute-done.14.refs_5_), channel_id=1, source_target_pairs={{0,8},{8,16},{16,24},{24,28},{28,20},{20,12},{12,4},{4,0},{1,9},{9... | collective-permute-start | bytes 3538952 | tf_op jit(solution)/shard_map/ppermute | solution.py:100
  114.5 28.0 %collective-permute-start.19 = (bf16[256,2304]{1,0:T(8,128)(2,1)S(1)}, bf16[256,2304]{1,0:T(8,128)(2,1)S(1)}, u32[]{:S(2)}, u32[]{:S(2)}) collective-permute-start(bf16[256,2304]{1,0:T(8,128)(2,1)S(1)} %collective-permute-done.15.refs_8_), channel_id=1, source_target_pairs={{8,0},{16,8},{24,16},{28,24},{20,28},{12,20},{4,12},{0,4},{9,1},{1... | collective-permute-start | bytes 3538952 | tf_op jit(solution)/shard_map/ppermute | solution.py:103
  118.4 26.2 %collective-permute-start.17 = (bf16[256,2048]{1,0:T(8,128)(2,1)S(1)}, bf16[256,2048]{1,0:T(8,128)(2,1)S(1)}, u32[]{:S(2)}, u32[]{:S(2)}) collective-permute-start(bf16[256,2048]{1,0:T(8,128)(2,1)S(1)} %add_convert_fusion.8), channel_id=1, source_target_pairs={{0,2},{1,3},{2,0},{3,1},{4,6},{5,7},{6,4},{7,5},{8,10},{9,11},{10,... | collective-permute-start | bytes 3145736 | tf_op jit(solution)/shard_map/ppermute | solution.py:191
  142.6 27.2 %collective-permute-start.21 = (bf16[256,2304]{1,0:T(8,128)(2,1)S(1)}, bf16[256,2304]{1,0:T(8,128)(2,1)S(1)}, u32[]{:S(2)}, u32[]{:S(2)}) collective-permute-start(bf16[256,2304]{1,0:T(8,128)(2,1)S(1)} %collective-permute-done.18.refs_6_), channel_id=1, source_target_pairs={{0,8},{8,16},{16,24},{24,28},{28,20},{20,12},{12,4},{4,0},{1,9},{9... | collective-permute-start | bytes 3538952 | tf_op jit(solution)/shard_map/ppermute | solution.py:100
  143.3 26.9 %collective-permute-start.22 = (bf16[256,2304]{1,0:T(8,128)(2,1)S(1)}, bf16[256,2304]{1,0:T(8,128)(2,1)S(1)}, u32[]{:S(2)}, u32[]{:S(2)}) collective-permute-start(bf16[256,2304]{1,0:T(8,128)(2,1)S(1)} %collective-permute-done.19.refs_9_), channel_id=1, source_target_pairs={{8,0},{16,8},{24,16},{28,24},{20,28},{12,20},{4,12},{0,4},{9,1},{1... | collective-permute-start | bytes 3538952 | tf_op jit(solution)/shard_map/ppermute | solution.py:103
  147.0 25.6 %collective-permute-start.20 = (bf16[256,2048]{1,0:T(8,128)(2,1)S(1)}, bf16[256,2048]{1,0:T(8,128)(2,1)S(1)}, u32[]{:S(2)}, u32[]{:S(2)}) collective-permute-start(bf16[256,2048]{1,0:T(8,128)(2,1)S(1)} %get-tuple-element.366.refs_0_), channel_id=1, source_target_pairs={{0,2},{1,3},{2,0},{3,1},{4,6},{5,7},{6,4},{7,5},{8,10},{9,11},{10,... | collective-permute-start | bytes 3145736 | tf_op jit(solution)/shard_map/ppermute | solution.py:191
  184.3 29.9 %collective-permute-start.29 = (bf16[256,1920]{1,0:T(8,128)(2,1)S(1)}, bf16[256,1920]{1,0:T(8,128)(2,1)S(1)}, u32[]{:S(2)}, u32[]{:S(2)}) collective-permute-start(bf16[256,1920]{1,0:T(8,128)(2,1)S(1)} %collective-permute-done.12.refs_5_), channel_id=1, source_target_pairs={{0,8},{8,16},{16,24},{24,28},{28,20},{20,12},{12,4},{4,0},{1,9},{9... | collective-permute-start | bytes 2949128 | tf_op jit(solution)/shard_map/ppermute | solution.py:100
  184.9 29.3 %collective-permute-start.30 = (bf16[256,1920]{1,0:T(8,128)(2,1)S(1)}, bf16[256,1920]{1,0:T(8,128)(2,1)S(1)}, u32[]{:S(2)}, u32[]{:S(2)}) collective-permute-start(bf16[256,1920]{1,0:T(8,128)(2,1)S(1)} %collective-permute-done.13.refs_8_), channel_id=1, source_target_pairs={{8,0},{16,8},{24,16},{28,24},{20,28},{12,20},{4,12},{0,4},{9,1},{1... | collective-permute-start | bytes 2949128 | tf_op jit(solution)/shard_map/ppermute | solution.py:103
  214.2 21.5 %collective-permute-start.31 = (bf16[256,1920]{1,0:T(8,128)(2,1)S(1)}, bf16[256,1920]{1,0:T(8,128)(2,1)S(1)}, u32[]{:S(2)}, u32[]{:S(2)}) collective-permute-start(bf16[256,1920]{1,0:T(8,128)(2,1)S(1)} %collective-permute-done.29.refs_6_), channel_id=1, source_target_pairs={{0,8},{8,16},{16,24},{24,28},{28,20},{20,12},{12,4},{4,0},{1,9},{9... | collective-permute-start | bytes 2949128 | tf_op jit(solution)/shard_map/ppermute | solution.py:100
  214.8 21.7 %collective-permute-start.32 = (bf16[256,1920]{1,0:T(8,128)(2,1)S(1)}, bf16[256,1920]{1,0:T(8,128)(2,1)S(1)}, u32[]{:S(2)}, u32[]{:S(2)}) collective-permute-start(bf16[256,1920]{1,0:T(8,128)(2,1)S(1)} %collective-permute-done.30.refs_9_), channel_id=1, source_target_pairs={{8,0},{16,8},{24,16},{28,24},{20,28},{12,20},{4,12},{0,4},{9,1},{1... | collective-permute-start | bytes 2949128 | tf_op jit(solution)/shard_map/ppermute | solution.py:103
  247.6 21.1 %collective-permute-start.35 = (bf16[128,2304]{1,0:T(8,128)(2,1)}, bf16[128,2304]{1,0:T(8,128)(2,1)}, u32[]{:S(2)}, u32[]{:S(2)}) collective-permute-start(bf16[128,2304]{1,0:T(8,128)(2,1)} %get-tuple-element.357), channel_id=1, source_target_pairs={{0,8},{8,16},{16,24},{24,28},{28,20},{20,12},{12,4},{4,0},{1,9},{9... | collective-permute-start | bytes 1769480 | tf_op jit(solution)/shard_map/ppermute | solution.py:100
  249.0 19.7 %collective-permute-start.36 = (bf16[128,2304]{1,0:T(8,128)(2,1)}, bf16[128,2304]{1,0:T(8,128)(2,1)}, u32[]{:S(2)}, u32[]{:S(2)}) collective-permute-start(bf16[128,2304]{1,0:T(8,128)(2,1)} %get-tuple-element.358), channel_id=1, source_target_pairs={{8,0},{16,8},{24,16},{28,24},{20,28},{12,20},{4,12},{0,4},{9,1},{1... | collective-permute-start | bytes 1769480 | tf_op jit(solution)/shard_map/ppermute | solution.py:103
  273.2 16.8 %collective-permute-start.37 = (bf16[512,2048]{1,0:T(8,128)(2,1)}, bf16[512,2048]{1,0:T(8,128)(2,1)}, u32[]{:S(2)}, u32[]{:S(2)}) collective-permute-start(bf16[512,2048]{1,0:T(8,128)(2,1)} %get-tuple-element.365), channel_id=1, source_target_pairs={{0,1},{1,0},{2,3},{3,2},{4,5},{5,4},{6,7},{7,6},{8,9},{9,8},{10,11... | collective-permute-start | bytes 6291464 | tf_op jit(solution)/shard_map/ppermute | solution.py:191
  273.2 16.8 %collective-permute-start.38 = (bf16[512,2048]{1,0:T(8,128)(2,1)}, bf16[512,2048]{1,0:T(8,128)(2,1)}, u32[]{:S(2)}, u32[]{:S(2)}) collective-permute-start(bf16[512,2048]{1,0:T(8,128)(2,1)} %get-tuple-element.371), channel_id=1, source_target_pairs={{0,1},{1,0},{2,3},{3,2},{4,5},{5,4},{6,7},{7,6},{8,9},{9,8},{10,11... | collective-permute-start | bytes 6291464 | tf_op jit(solution)/shard_map/ppermute | solution.py:191
  273.7 28.5 %collective-permute-start.40 = (bf16[256,2304]{1,0:T(8,128)(2,1)}, bf16[256,2304]{1,0:T(8,128)(2,1)}, u32[]{:S(2)}, u32[]{:S(2)}) collective-permute-start(bf16[256,2304]{1,0:T(8,128)(2,1)} %get-tuple-element.364), channel_id=1, source_target_pairs={{0,8},{8,16},{16,24},{24,28},{28,20},{20,12},{12,4},{4,0},{1,9},{9... | collective-permute-start | bytes 3538952 | tf_op jit(solution)/shard_map/ppermute | solution.py:100
  274.7 29.3 %collective-permute-start.41 = (bf16[256,2304]{1,0:T(8,128)(2,1)}, bf16[256,2304]{1,0:T(8,128)(2,1)}, u32[]{:S(2)}, u32[]{:S(2)}) collective-permute-start(bf16[256,2304]{1,0:T(8,128)(2,1)} %get-tuple-element.377), channel_id=1, source_target_pairs={{8,0},{16,8},{24,16},{28,24},{20,28},{12,20},{4,12},{0,4},{9,1},{1... | collective-permute-start | bytes 3538952 | tf_op jit(solution)/shard_map/ppermute | solution.py:103
  292.5 29.5 %collective-permute-start.39 = (bf16[256,2048]{1,0:T(8,128)(2,1)S(1)}, bf16[256,2048]{1,0:T(8,128)(2,1)S(1)}, u32[]{:S(2)}, u32[]{:S(2)}) collective-permute-start(bf16[256,2048]{1,0:T(8,128)(2,1)S(1)} %add_convert_fusion.7), channel_id=1, source_target_pairs={{0,2},{1,3},{2,0},{3,1},{4,6},{5,7},{6,4},{7,5},{8,10},{9,11},{10,... | collective-permute-start | bytes 3145736 | tf_op jit(solution)/shard_map/ppermute | solution.py:191
  307.6 29.3 %collective-permute-start.45 = (bf16[256,2304]{1,0:T(8,128)(2,1)}, bf16[256,2304]{1,0:T(8,128)(2,1)}, u32[]{:S(2)}, u32[]{:S(2)}) collective-permute-start(bf16[256,2304]{1,0:T(8,128)(2,1)} %get-tuple-element.380), channel_id=1, source_target_pairs={{0,8},{8,16},{16,24},{24,28},{28,20},{20,12},{12,4},{4,0},{1,9},{9... | collective-permute-start | bytes 3538952 | tf_op jit(solution)/shard_map/ppermute | solution.py:100
  309.7 29.2 %collective-permute-start.46 = (bf16[256,2304]{1,0:T(8,128)(2,1)}, bf16[256,2304]{1,0:T(8,128)(2,1)}, u32[]{:S(2)}, u32[]{:S(2)}) collective-permute-start(bf16[256,2304]{1,0:T(8,128)(2,1)} %get-tuple-element.393), channel_id=1, source_target_pairs={{8,0},{16,8},{24,16},{28,24},{20,28},{12,20},{4,12},{0,4},{9,1},{1... | collective-permute-start | bytes 3538952 | tf_op jit(solution)/shard_map/ppermute | solution.py:103
  326.5 19.0 %collective-permute-start.43 = (bf16[128,1920]{1,0:T(8,128)(2,1)S(1)}, bf16[128,1920]{1,0:T(8,128)(2,1)S(1)}, u32[]{:S(2)}, u32[]{:S(2)}) collective-permute-start(bf16[128,1920]{1,0:T(8,128)(2,1)S(1)} %get-tuple-element.391), channel_id=1, source_target_pairs={{0,8},{8,16},{16,24},{24,28},{28,20},{20,12},{12,4},{4,0},{1,9},{9... | collective-permute-start | bytes 1474568 | tf_op jit(solution)/shard_map/ppermute | solution.py:100
  328.5 25.3 %collective-permute-start.42 = (bf16[256,2048]{1,0:T(8,128)(2,1)S(1)}, bf16[256,2048]{1,0:T(8,128)(2,1)S(1)}, u32[]{:S(2)}, u32[]{:S(2)}) collective-permute-start(bf16[256,2048]{1,0:T(8,128)(2,1)S(1)} %get-tuple-element.405.refs_0_.refs_1_), channel_id=1, source_target_pairs={{0,2},{1,3},{2,0},{3,1},{4,6},{5,7},{6,4},{7,5},{8,10},{9,11},{10,... | collective-permute-start | bytes 3145736 | tf_op jit(solution)/shard_map/ppermute | solution.py:191
  356.5 28.6 %collective-permute-start.49 = (bf16[256,2048]{1,0:T(8,128)(2,1)S(1)}, bf16[256,2048]{1,0:T(8,128)(2,1)S(1)}, u32[]{:S(2)}, u32[]{:S(2)}) collective-permute-start(bf16[256,2048]{1,0:T(8,128)(2,1)S(1)} %add_convert_fusion.6), channel_id=1, source_target_pairs={{0,2},{1,3},{2,0},{3,1},{4,6},{5,7},{6,4},{7,5},{8,10},{9,11},{10,... | collective-permute-start | bytes 3145736 | tf_op jit(solution)/shard_map/ppermute | solution.py:191
  358.0 44.5 %collective-permute-start.54 = (bf16[256,1920]{1,0:T(8,128)(2,1)S(1)}, bf16[256,1920]{1,0:T(8,128)(2,1)}, u32[]{:S(2)}, u32[]{:S(2)}) collective-permute-start(bf16[256,1920]{1,0:T(8,128)(2,1)S(1)} %get-tuple-element.403), channel_id=1, source_target_pairs={{0,8},{8,16},{16,24},{24,28},{28,20},{20,12},{12,4},{4,0},{1,9},{9... | collective-permute-start | bytes 2949128 | tf_op jit(solution)/shard_map/ppermute | solution.py:100
  359.7 43.1 %collective-permute-start.55 = (bf16[256,1920]{1,0:T(8,128)(2,1)S(1)}, bf16[256,1920]{1,0:T(8,128)(2,1)S(1)}, u32[]{:S(2)}, u32[]{:S(2)}) collective-permute-start(bf16[256,1920]{1,0:T(8,128)(2,1)S(1)} %get-tuple-element.428), channel_id=1, source_target_pairs={{8,0},{16,8},{24,16},{28,24},{20,28},{12,20},{4,12},{0,4},{9,1},{1... | collective-permute-start | bytes 2949128 | tf_op jit(solution)/shard_map/ppermute | solution.py:103
  360.0 48.0 %collective-permute-start.52 = (bf16[256,2304]{1,0:T(8,128)(2,1)}, bf16[256,2304]{1,0:T(8,128)(2,1)}, u32[]{:S(2)}, u32[]{:S(2)}) collective-permute-start(bf16[256,2304]{1,0:T(8,128)(2,1)} %get-tuple-element.398), channel_id=1, source_target_pairs={{0,8},{8,16},{16,24},{24,28},{28,20},{20,12},{12,4},{4,0},{1,9},{9... | collective-permute-start | bytes 3538952 | tf_op jit(solution)/shard_map/ppermute | solution.py:100
  361.8 48.0 %collective-permute-start.53 = (bf16[256,2304]{1,0:T(8,128)(2,1)}, bf16[256,2304]{1,0:T(8,128)(2,1)}, u32[]{:S(2)}, u32[]{:S(2)}) collective-permute-start(bf16[256,2304]{1,0:T(8,128)(2,1)} %get-tuple-element.427), channel_id=1, source_target_pairs={{8,0},{16,8},{24,16},{28,24},{20,28},{12,20},{4,12},{0,4},{9,1},{1... | collective-permute-start | bytes 3538952 | tf_op jit(solution)/shard_map/ppermute | solution.py:103
  415.3 24.6 %collective-permute-start.59 = (bf16[256,1920]{1,0:T(8,128)(2,1)S(1)}, bf16[256,1920]{1,0:T(8,128)(2,1)S(1)}, u32[]{:S(2)}, u32[]{:S(2)}) collective-permute-start(bf16[256,1920]{1,0:T(8,128)(2,1)S(1)} %get-tuple-element.431), channel_id=1, source_target_pairs={{0,8},{8,16},{16,24},{24,28},{28,20},{20,12},{12,4},{4,0},{1,9},{9... | collective-permute-start | bytes 2949128 | tf_op jit(solution)/shard_map/ppermute | solution.py:100
  416.4 24.9 %collective-permute-start.60 = (bf16[256,1920]{1,0:T(8,128)(2,1)S(1)}, bf16[256,1920]{1,0:T(8,128)(2,1)S(1)}, u32[]{:S(2)}, u32[]{:S(2)}) collective-permute-start(bf16[256,1920]{1,0:T(8,128)(2,1)S(1)} %get-tuple-element.443), channel_id=1, source_target_pairs={{8,0},{16,8},{24,16},{28,24},{20,28},{12,20},{4,12},{0,4},{9,1},{1... | collective-permute-start | bytes 2949128 | tf_op jit(solution)/shard_map/ppermute | solution.py:103
  417.6 27.4 %collective-permute-start.58 = (bf16[256,2304]{1,0:T(8,128)(2,1)S(1)}, bf16[256,2304]{1,0:T(8,128)(2,1)S(1)}, u32[]{:S(2)}, u32[]{:S(2)}) collective-permute-start(bf16[256,2304]{1,0:T(8,128)(2,1)S(1)} %add_convert_fusion.refs_0_), channel_id=1, source_target_pairs={{0,2},{1,3},{2,0},{3,1},{4,6},{5,7},{6,4},{7,5},{8,10},{9,11},{10,... | collective-permute-start | bytes 3538952 | tf_op jit(solution)/shard_map/ppermute | solution.py:191
  419.0 34.4 %collective-permute-start.63 = (bf16[272,1152]{1,0:T(8,128)(2,1)S(1)}, bf16[272,1152]{1,0:T(8,128)(2,1)S(1)}, u32[]{:S(2)}, u32[]{:S(2)}) collective-permute-start(bf16[272,1152]{1,0:T(8,128)(2,1)S(1)} %get-tuple-element.439), channel_id=1, source_target_pairs={{0,8},{8,16},{16,24},{24,28},{28,20},{20,12},{12,4},{4,0},{1,9},{9... | collective-permute-start | bytes 1880072 | tf_op jit(solution)/shard_map/ppermute | solution.py:100
  420.7 33.0 %collective-permute-start.64 = (bf16[272,1152]{1,0:T(8,128)(2,1)S(1)}, bf16[272,1152]{1,0:T(8,128)(2,1)S(1)}, u32[]{:S(2)}, u32[]{:S(2)}) collective-permute-start(bf16[272,1152]{1,0:T(8,128)(2,1)S(1)} %get-tuple-element.449), channel_id=1, source_target_pairs={{8,0},{16,8},{24,16},{28,24},{20,28},{12,20},{4,12},{0,4},{9,1},{1... | collective-permute-start | bytes 1880072 | tf_op jit(solution)/shard_map/ppermute | solution.py:103
  445.0 25.6 %collective-permute-start.57 = (bf16[256,2048]{1,0:T(8,128)(2,1)S(1)}, bf16[256,2048]{1,0:T(8,128)(2,1)S(1)}, u32[]{:S(2)}, u32[]{:S(2)}) collective-permute-start(bf16[256,2048]{1,0:T(8,128)(2,1)S(1)} %add_convert_fusion.5), channel_id=1, source_target_pairs={{0,2},{1,3},{2,0},{3,1},{4,6},{5,7},{6,4},{7,5},{8,10},{9,11},{10,... | collective-permute-start | bytes 3145736 | tf_op jit(solution)/shard_map/ppermute | solution.py:191
  445.5 30.9 %collective-permute-start.67 = (bf16[256,1920]{1,0:T(8,128)(2,1)S(1)}, bf16[256,1920]{1,0:T(8,128)(2,1)S(1)}, u32[]{:S(2)}, u32[]{:S(2)}) collective-permute-start(bf16[256,1920]{1,0:T(8,128)(2,1)S(1)} %get-tuple-element.447), channel_id=1, source_target_pairs={{0,8},{8,16},{16,24},{24,28},{28,20},{20,12},{12,4},{4,0},{1,9},{9... | collective-permute-start | bytes 2949128 | tf_op jit(solution)/shard_map/ppermute | solution.py:100
  453.4 23.0 %collective-permute-start.68 = (bf16[256,1920]{1,0:T(8,128)(2,1)S(1)}, bf16[256,1920]{1,0:T(8,128)(2,1)S(1)}, u32[]{:S(2)}, u32[]{:S(2)}) collective-permute-start(bf16[256,1920]{1,0:T(8,128)(2,1)S(1)} %get-tuple-element.458), channel_id=1, source_target_pairs={{8,0},{16,8},{24,16},{28,24},{20,28},{12,20},{4,12},{0,4},{9,1},{1... | collective-permute-start | bytes 2949128 | tf_op jit(solution)/shard_map/ppermute | solution.py:103
  476.8 16.5 %collective-permute-start.65 = (bf16[272,1152]{1,0:T(8,128)(2,1)S(1)}, bf16[272,1152]{1,0:T(8,128)(2,1)S(1)}, u32[]{:S(2)}, u32[]{:S(2)}) collective-permute-start(bf16[272,1152]{1,0:T(8,128)(2,1)S(1)} %get-tuple-element.452), channel_id=1, source_target_pairs={{0,8},{8,16},{16,24},{24,28},{28,20},{20,12},{12,4},{4,0},{1,9},{9... | collective-permute-start | bytes 1880072 | tf_op jit(solution)/shard_map/ppermute | solution.py:100
  496.5 22.4 %collective-permute-start.73 = (bf16[256,1920]{1,0:T(8,128)(2,1)S(1)}, bf16[256,1920]{1,0:T(8,128)(2,1)S(1)}, u32[]{:S(2)}, u32[]{:S(2)}) collective-permute-start(bf16[256,1920]{1,0:T(8,128)(2,1)S(1)} %add_convert_fusion.9.refs_4_), channel_id=1, source_target_pairs={{0,2},{1,3},{2,0},{3,1},{4,6},{5,7},{6,4},{7,5},{8,10},{9,11},{10,... | collective-permute-start | bytes 2949128 | tf_op jit(solution)/shard_map/ppermute | solution.py:191
  519.0 16.5 %collective-permute-start.72 = (bf16[272,1152]{1,0:T(8,128)(2,1)S(1)}, bf16[272,1152]{1,0:T(8,128)(2,1)S(1)}, u32[]{:S(2)}, u32[]{:S(2)}) collective-permute-start(bf16[272,1152]{1,0:T(8,128)(2,1)S(1)} %add_convert_fusion.14.refs_0_), channel_id=1, source_target_pairs={{0,2},{1,3},{2,0},{3,1},{4,6},{5,7},{6,4},{7,5},{8,10},{9,11},{10,... | collective-permute-start | bytes 1880072 | tf_op jit(solution)/shard_map/ppermute | solution.py:191
  (125 other events, 2744.7 us)

commit v5 on v4

--- a/solution.py
+++ b/solution.py
@@ -19,8 +19,8 @@
     "attention_forward": 20,
     "attention_backward": 16,
     "heads_back": 14,
-    "mlp_half": 26,
-    "mlp_half_far": 44,
+    "mlp_chunk": 26,
+    "mlp_chunk_far": 44,
     "weight_terms": 14,
     "unpack_mlp": 28,
     "unpack_heads": 12,
@@ -579,14 +579,15 @@
     )(grad_q, grad_kv, *tokens, *pieces)
 
 
-def mlp_half(tokens, cots, pieces, before, size, room="mlp_half"):
+def mlp_chunk(tokens, cots, pieces, before, size, room):
     rows, model = tokens[0].shape
+    pack_size = 4 * rows
 
     def body(*refs):
-        token_refs, cot_refs, refs = refs[:2], refs[2:4], refs[4:]
+        token_refs, cot_refs, refs = refs[:4], refs[4:8], refs[8:]
         piece_refs, refs = refs[: len(pieces)], refs[len(pieces) :]
         before_refs, refs = refs[: len(before)], refs[len(before) :]
-        down_ref, grad_ref, both_ref, w_ref, tokens_s, cot_s = refs
+        down_keep, down_send, grad_keep, grad_send, both_ref, w_ref, tokens_s, cot_s = refs
         step = pl.program_id(0)
 
         @pl.when(step == 0)
@@ -605,21 +606,32 @@
         both_ref[:, :size] = (grad_act * up_pre * (sig + active * (1.0 - sig))).astype(BF)
         down = against(both_ref[:, 2 * size :], w_ref[:, 2 * size :])
         grad = against(both_ref[:, : 2 * size], w_ref[:, : 2 * size])
-        if before_refs:
-            down = down + before_refs[0][...].astype(F32)
-            grad = grad + before_refs[1][...].astype(F32)
-        down_ref[...] = down.astype(BF)
-        grad_ref[...] = grad.astype(BF)
-
-    by_rows = lambda cols: pl.BlockSpec((rows, cols), lambda i: (i, 0))
-    fixed = lambda array: pl.BlockSpec(memory_space=pltpu.VMEM)
-    half = jax.ShapeDtypeStruct((2 * rows, model), BF)
+
+        def put(keep, send, value, keep_before, send_before):
+            @pl.when(step < 2)
+            def _():
+                extra = 0.0 if keep_before is None else keep_before[...].astype(F32)
+                keep[...] = (value + extra).astype(BF)
+
+            @pl.when(step >= 2)
+            def _():
+                extra = 0.0 if send_before is None else send_before[...].astype(F32)
+                send[...] = (value + extra).astype(BF)
+
+        old = before_refs or [None] * 4
+        put(down_keep, down_send, down, old[0], old[1])
+        put(grad_keep, grad_send, grad, old[2], old[3])
+
+    first = pl.BlockSpec((rows, model), lambda i: (jnp.minimum(i, 1), 0))
+    second = pl.BlockSpec((rows, model), lambda i: (jnp.maximum(i - 2, 0), 0))
+    fixed = pl.BlockSpec(memory_space=pltpu.VMEM)
+    half = jax.ShapeDtypeStruct((pack_size // 2, model), BF)
     return pl.pallas_call(
         body,
-        grid=(2,),
-        out_shape=(half, half, jax.ShapeDtypeStruct((2 * rows, 3 * size), BF)),
-        in_specs=[fixed(a) for a in (*tokens, *cots, *pieces)] + [by_rows(model)] * len(before),
-        out_specs=(by_rows(model), by_rows(model), by_rows(3 * size)),
+        grid=(4,),
+        out_shape=(half, half, half, half, jax.ShapeDtypeStruct((pack_size, 3 * size), BF)),
+        in_specs=[fixed] * (8 + len(pieces)) + [first, second] * (len(before) // 2),
+        out_specs=(first, second, first, second, pl.BlockSpec((rows, 3 * size), lambda i: (i, 0))),
         scratch_shapes=[
             pltpu.VMEM((model, 3 * size), BF),
             pltpu.VMEM((rows, model), BF),
@@ -627,7 +639,7 @@
         ],
         compiler_params=limits(room),
         cost_estimate=COST,
-        name="mlp_half",
+        name="mlp_chunk",
     )(*tokens, *cots, *pieces, *before)
 
 
@@ -1072,50 +1084,38 @@
 
     def terms_of(both, size):
         return weight_terms(
-            [(seconds, both, slice(0, 2 * size)), (cots, both, slice(2 * size, 3 * size))],
+            [(seconds, [both], slice(0, 2 * size)), (cots, [both], slice(2 * size, 3 * size))],
             width,
             n_dp,
             2,
             middle,
         )
 
-    down_send, grad_send, both_send = far_memory(
-        *mlp_half(seconds[2:], cots[2:], pieces, (), sizes[0])
-    )
-    clock.done(both_send)
-    first_two = clock.tie(*seconds[:2])
-    down_keep, grad_keep, both_keep = far_memory(
-        *mlp_half(first_two, cots[:2], pieces, (), sizes[0])
-    )
-    clock.done(both_keep)
+    *before, both = far_memory(*mlp_chunk(seconds, cots, pieces, (), sizes[0], "mlp_chunk"))
+    clock.done(both)
     chunks[1].relay(clock)
-    both = list(clock.tie(both_keep, both_send))
-    terms = terms_of(both, sizes[0])
+    terms = terms_of(clock.tie(both), sizes[0])
     clock.done(terms[0])
+    sums = [Scatter(ring, terms, middle, sizes[0])]
     chunks[1].relay(clock)
     pieces = far_memory(*chunks[1].finish(clock))
-    sums = [Scatter(ring, clock.tie(*terms), middle, sizes[0])]
-    down_send, grad_send, both_send = mlp_half(
-        seconds[2:], cots[2:], clock.tie(*pieces), (down_send, grad_send), sizes[1], "mlp_half_far"
-    )
-    clock.done(both_send)
-    both_send = far_memory(both_send)[0]
+    sums[0].relay(clock)
+    down_keep, down_send, grad_keep, grad_send, both = mlp_chunk(
+        seconds, cots, clock.tie(*pieces), before, sizes[1], "mlp_chunk_far"
+    )
+    both = far_memory(both)[0]
+    clock.done(both)
     sums[0].relay(clock)
     grad_send, down_send = clock.tie(grad_send, down_send)
     came, down_came = swap(grad_send, 1), swap(down_send, 1)
-    first_two = clock.tie(*seconds[:2])
-    down_keep, grad_keep, both_keep = mlp_half(
-        first_two, cots[:2], pieces, (down_keep, grad_keep), sizes[1], "mlp_half_far"
-    )
-    both_keep = far_memory(both_keep)[0]
-    clock.done(both_keep)
-    came, down_came = clock.tie(came, down_came)
+    came = clock.tie(came)
     last = swap(clock.tie(other_half(grad_keep, came)), 2)
+    terms = terms_of(clock.tie(both), sizes[1])
+    clock.done(terms[0])
+    sums.append(Scatter(ring, terms, middle, sizes[1]))
+    down_came = clock.tie(down_came)
     sums[0].relay(clock)
-    both = list(clock.tie(both_keep, both_send))
-    terms = terms_of(both, sizes[1])
-    clock.done(terms[0])
-    sums.append(Scatter(ring, clock.tie(*terms), middle, sizes[1]))
+    sums[1].relay(clock)
     last = clock.tie(last)
     grad_hidden, my_branch, gain_two_terms = second_norm_back(
         my_cot, hidden, grad_keep, came, last, gains
@@ -1124,18 +1124,21 @@
     across, beside = swap(my_branch, 2), swap(my_branch, 1)
     down_other = clock.tie(other_half(down_keep, down_came))
     beside = clock.tie(beside)
-    sums[0].relay(clock)
-    sums[1].relay(clock)
+    chunk_sum = sums[0].finish(clock)
+    chunk_across, chunk_beside = swap(chunk_sum, 2), swap(chunk_sum, 1)
     across = clock.tie(across)
     branches = four(my_branch, across, beside)
     branches = list(clock.tie(*branches))
-    down_last = swap(clock.tie(down_other), 2)
     grad_q, grad_kv = attention_backward(
         places, lengths, live, branches, head_pieces, cosine, sine_part,
         query, kv, kvt, lse, mixed_t
     )
     clock.done(grad_kv)
-    down_last, *tokens = clock.tie(down_last, *tokens)
+    sums[1].relay(clock)
+    chunk_across, chunk_beside = clock.tie(chunk_across, chunk_beside)
+    firsts = four(chunk_sum, chunk_across, chunk_beside)
+    down_last = swap(clock.tie(down_other), 2)
+    tokens = clock.tie(*tokens)
     grad_keep, grad_send, gain_one_terms = heads_back(grad_q, grad_kv, tokens, head_pieces)
     clock.done(gain_one_terms)
     columns = head_block.shape[1]
@@ -1165,33 +1168,27 @@
     clock.done(head_terms[0])
     head_ring = Scatter(ring, head_terms, TOP + middle, columns)
     sums[1].relay(clock)
-    chunk_sum = sums[0].finish(clock)
-    chunk_across, chunk_beside = swap(chunk_sum, 2), swap(chunk_sum, 1)
+    firsts = list(clock.tie(*firsts))
     head_ring.relay(clock)
+    down_last = clock.tie(down_last)
     came = clock.tie(swap(clock.tie(grad_send), 1))
     last = swap(clock.tie(other_half(grad_keep, came)), 2)
-    chunk_beside = clock.tie(chunk_beside)
-    sums[1].relay(clock)
-    chunk_across = clock.tie(chunk_across)
-    firsts = four(chunk_sum, chunk_across, chunk_beside)
+    second_sum = sums[1].finish(clock)
+    second_across, second_beside = swap(second_sum, 2), swap(second_sum, 1)
     head_ring.relay(clock)
-    firsts = list(clock.tie(*firsts))
-    last = clock.tie(last)
-    grad_input = first_norm_back(
-        grad_hidden, mine, grad_keep, came, last, gains, ring.slot_owners(), n_dp
-    )
-    clock.done(grad_input)
     down_came = clock.tie(down_came)
     result = layer_output(hidden, down_keep, down_came, down_last, ring.slot_owners(), n_dp)
     clock.done(result)
-    second_sum = sums[1].finish(clock)
-    second_across, second_beside = swap(second_sum, 2), swap(second_sum, 1)
-    second_beside = clock.tie(second_beside)
+    last, second_beside = clock.tie(last, second_beside)
+    grad_input = first_norm_back(
+        grad_hidden, mine, grad_keep, came, last, gains, ring.slot_owners(), n_dp
+    )
+    clock.done(grad_input)
     head_ring.relay(clock)
+    second_across = clock.tie(second_across)
+    others = four(second_sum, second_across, second_beside)
     head_sum = head_ring.finish(clock)
     head_across, head_beside = swap(head_sum, 2), swap(head_sum, 1)
-    second_across = clock.tie(second_across)
-    others = four(second_sum, second_across, second_beside)
     others = list(clock.tie(*others))
     grad_gate, grad_up, grad_down = unpack_mlp(places, [firsts, others], bounds, width, ff)
     clock.done(grad_gate)

time: 550 us -> 523 us (0.951)
  waiting for transfers between devices: 254 us -> 238 us
  other arithmetic: 19.8 us -> 11.1 us
    ppermute x29, waiting for transfers between devices: 52.5 us -> 25.2 us  [swap(): return lax.ppermute(block, 'seq', [(i, i ^ distance) for i in range(4)])]
    ppermute x24, waiting for transfers between devices: 174 us -> 184 us  [go_up(): return lax.ppermute(block, 'dp', self.up)]
    convert_element_type x10, other arithmetic: 15 us -> 8.54 us  [plus(): return (one.astype(F32) + two.astype(F32)).astype(BF)]
    unnamed x192 -> x122, local copies, waits for them, and re-layouts: 15.7 us -> 11.7 us
    pallas_call x4 -> x2, Pallas kernels: 50.9 us -> 51.5 us  [mlp_chunk(): pl.pallas_call(body, grid=(4,), out_shape=(half, half, half, half, jax.Sh...]
  transfers between devices with their start and end apart: 77 -> 77, of which waited for: 48 -> 44; matrix products, arithmetic and copies ran while one was open for 4% -> 2% of each run, Pallas kernels for 31% -> 34%
where the time goes in v5:
time: 523 us; the launch traced here: 515 us
  waiting for transfers between devices  238 us (46%)
  Pallas kernels  181 us (35%)
  starting transfers between devices  67.7 us (13%)
  local copies, waits for them, and re-layouts  14.3 us (3%)
  other arithmetic  11.1 us (2%)
    ppermute x24, waiting for transfers between devices, go_up(): return lax.ppermute(block, 'dp', self.up)  184 us
    pallas_call x5, Pallas kernels, kernel_call(): pl.pallas_call(body, out_shape=tuple((jax.ShapeDtypeStruct(s, d) for s, d...  59.6 us
    pallas_call x2, Pallas kernels, mlp_chunk(): pl.pallas_call(body, grid=(4,), out_shape=(half, half, half, half, jax.Sh...  51.5 us
    pallas_call x3, Pallas kernels, weight_terms(): pl.pallas_call(body, grid=(n_slots // group,), out_shape=(jax.ShapeDtypeS...  36.7 us
    ppermute x24, starting transfers between devices, go_up(): return lax.ppermute(block, 'dp', self.up)  29.8 us
    ppermute x24, waiting for transfers between devices, go_down(): return lax.ppermute(block, 'dp', self.down)  28.9 us
    ppermute x29, waiting for transfers between devices, swap(): return lax.ppermute(block, 'seq', [(i, i ^ distance) for i in range(4)])  25.2 us
    ppermute x24, starting transfers between devices, go_down(): return lax.ppermute(block, 'dp', self.down)  22.7 us
  transfers between devices with their start and end apart: 77, of which 44 were waited for; matrix products, arithmetic and copies ran while one was open for 2% of the time, Pallas kernels for 34%

profile of v5, /device:TPU:0, one launch (start us, length us, event | category | flops | bytes accessed | tf_op | source)
XLA Modules:
  0.0 515.2 jit_solution(14045908151343935301)
XLA Ops:
  0.7 2.5 pack_heads.1.refs_4_
  3.2 3.0 collective-permute-start
  8.7 2.4 permute_features.2.refs_0_.inputs_ref
  11.0 2.0 collective-permute-start.2
  13.2 3.1 pack_mlp.1
  16.3 4.1 collective-permute-done.refs_5_
  24.7 2.4 permute_features.3.refs_4_.cot_ref
  27.1 9.6 %collective-permute-done.3.refs_6_ = bf16[272,1152]{1,0:T(8,128)(2,1)S(1)} collective-permute-done((bf16[272,1152]{1,0:T(8,128)(2,1)S(1)}, bf16[272,1152]{1,0:T(8,128)(2,1)S(1)}, u32[]{:S(2)}, u32[]{:S(2)}) %collective-permute-start.3) | collective-permute-done | bytes 626720 | tf_op jit(solution)/shard_map/ppermute | solution.py:100
  40.3 14.4 %collective-permute-done.7.refs_7_ = bf16[272,1152]{1,0:T(8,128)(2,1)S(1)} collective-permute-done((bf16[272,1152]{1,0:T(8,128)(2,1)S(1)}, bf16[272,1152]{1,0:T(8,128)(2,1)S(1)}, u32[]{:S(2)}, u32[]{:S(2)}) %collective-permute-start.7) | collective-permute-done | bytes 626720 | tf_op jit(solution)/shard_map/ppermute | solution.py:100
  58.2 7.4 %collective-permute-done.10.refs_12_ = bf16[128,1152]{1,0:T(8,128)(2,1)S(1)} collective-permute-done((bf16[128,1152]{1,0:T(8,128)(2,1)S(1)}, bf16[128,1152]{1,0:T(8,128)(2,1)S(1)}, u32[]{:S(2)}, u32[]{:S(2)}) %collective-permute-start.10) | collective-permute-done | bytes 294944 | tf_op jit(solution)/shard_map/ppermute | solution.py:103
  74.1 28.8 %attention_forward.1 = (bf16[1024,2048]{1,0:T(8,128)(2,1)S(1)}, bf16[512,1024]{1,0:T(8,128)(2,1)S(1)}, bf16[1024,128]{1,0:T(8,128)(2,1)S(1)}, bf16[192,1024]{1,0...) custom-call(s32[4]{0:T(128)S(1)} %fusion.2.places_ref, ...), custom_call_target="tpu_custom_call" | custom-call | flops 1000 | bytes 1000 | tf_op jit(solution)/shard_map/attention_forward/pallas_call | solution.py:58
  106.3 6.5 %collective-permute-done.12.refs_9_ = bf16[256,1920]{1,0:T(8,128)(2,1)S(1)} collective-permute-done((bf16[256,1920]{1,0:T(8,128)(2,1)}, bf16[256,1920]{1,0:T(8,128)(2,1)S(1)}, u32[]{:S(2)}, u32[]{:S(2)}) %collective-permute-start.12) | collective-permute-done | bytes 983072 | tf_op jit(solution)/shard_map/ppermute | solution.py:100
  115.8 2.1 collective-permute-done.16.came_ref
  119.9 22.2 %collective-permute-done.18.refs_10_ = bf16[256,2304]{1,0:T(8,128)(2,1)S(1)} collective-permute-done((bf16[256,2304]{1,0:T(8,128)(2,1)S(1)}, bf16[256,2304]{1,0:T(8,128)(2,1)S(1)}, u32[]{:S(2)}, u32[]{:S(2)}) %collective-permute-start.18) | collective-permute-done | bytes 1179680 | tf_op jit(solution)/shard_map/ppermute | solution.py:100
  148.4 21.3 %collective-permute-done.21.refs_11_ = bf16[256,2304]{1,0:T(8,128)(2,1)S(1)} collective-permute-done((bf16[256,2304]{1,0:T(8,128)(2,1)S(1)}, bf16[256,2304]{1,0:T(8,128)(2,1)S(1)}, u32[]{:S(2)}, u32[]{:S(2)}) %collective-permute-start.21) | collective-permute-done | bytes 1179680 | tf_op jit(solution)/shard_map/ppermute | solution.py:100
  173.0 10.7 %collective-permute-done.25.refs_15_ = bf16[128,2304]{1,0:T(8,128)(2,1)S(1)} collective-permute-done((bf16[128,2304]{1,0:T(8,128)(2,1)S(1)}, bf16[128,2304]{1,0:T(8,128)(2,1)S(1)}, u32[]{:S(2)}, u32[]{:S(2)}) %collective-permute-start.25) | collective-permute-done | bytes 589856 | tf_op jit(solution)/shard_map/ppermute | solution.py:100
  184.8 1.8 collective-permute-start.30
  186.7 23.6 %mlp_chunk.2 = (bf16[512,2048]{1,0:T(8,128)(2,1)S(1)}, bf16[512,2048]{1,0:T(8,128)(2,1)S(1)}, bf16[512,2048]{1,0:T(8,128)(2,1)S(1)}, bf16[512,2048]{1,0:T(8,128)(2,1)S(1)}, bf16[1024,2304]{1,0:T(8,128)(2,1)}) custom-call(bf16[256,2048]{1,0:T(8,128)(2,1)S(1)} %get-tuple-element.303.refs_0_, bf16[256,2048]{1,0:T(8,128)(2,1)S(1)} %collective-permute-done.20.refs_1_, ...), custom_call_target="tpu_custom_call" | custom-call | flops 1000 | bytes 1000 | tf_op jit(solution)/shard_map/mlp_chunk/pallas_call | solution.py:629
  217.7 15.0 %weight_terms.3 = (bf16[2048,2304]{1,0:T(8,128)(2,1)S(1)}, bf16[128,2304]{1,0:T(8,128)(2,1)S(1)}, bf16[128,2304]{1,0:T(8,128)(2,1)S(1)}) custom-call(bf16[256,2048]{1,0:T(8,128)(2,1)S(1)} %get-tuple-element.303.refs_0_, bf16[256,2048]{1,0:T(8,128)(2,1)S(1)} %collective-permute-done.20.refs_1_, bf16[256,2048]{1,0:T(8,128)(2,1)S(1)} %collective-permute-done.23.refs_2_, ...), custom_call_target="tpu_custom_call" | custom-call | flops 1000 | bytes 1000 | tf_op jit(solution)/shard_map/weight_terms/pallas_call | solution.py:723
  234.8 5.4 %collective-permute-done.31.refs_11_ = bf16[256,1920]{1,0:T(8,128)(2,1)S(1)} collective-permute-done((bf16[256,1920]{1,0:T(8,128)(2,1)S(1)}, bf16[256,1920]{1,0:T(8,128)(2,1)S(1)}, u32[]{:S(2)}, u32[]{:S(2)}) %collective-permute-start.31) | collective-permute-done | bytes 983072 | tf_op jit(solution)/shard_map/ppermute | solution.py:100
  242.9 16.2 %collective-permute-done.33.refs_15_ = bf16[128,1920]{1,0:T(8,128)(2,1)S(1)} collective-permute-done((bf16[128,1920]{1,0:T(8,128)(2,1)S(1)}, bf16[128,1920]{1,0:T(8,128)(2,1)S(1)}, u32[]{:S(2)}, u32[]{:S(2)}) %collective-permute-start.33) | collective-permute-done | bytes 491552 | tf_op jit(solution)/shard_map/ppermute | solution.py:100
  260.2 2.2 ring_add.3
  264.7 28.0 %mlp_chunk.3 = (bf16[512,2048]{1,0:T(8,128)(2,1)}, bf16[512,2048]{1,0:T(8,128)(2,1)}, bf16[512,2048]{1,0:T(8,128)(2,1)}, bf16[512,2048]{1,0:T(8,128)(2,1)}, bf16[1024,1920]{1,0:T(8,128)(2,1)}) custom-call(bf16[256,2048]{1,0:T(8,128)(2,1)S(1)} %get-tuple-element.303.refs_0_, bf16[256,2048]{1,0:T(8,128)(2,1)S(1)} %collective-permute-done.20.refs_1_, ...), custom_call_target="tpu_custom_call" | custom-call | flops 1000 | bytes 1000 | tf_op jit(solution)/shard_map/mlp_chunk/pallas_call | solution.py:629
  292.7 2.3 add_convert_fusion.3
  297.7 3.8 collective-permute-done.40.came_ref
  301.5 1.7 add_convert_fusion.7
  304.7 13.4 %weight_terms.4 = (bf16[2048,1920]{1,0:T(8,128)(2,1)S(1)}, bf16[128,1920]{1,0:T(8,128)(2,1)S(1)}, bf16[128,1920]{1,0:T(8,128)(2,1)S(1)}) custom-call(bf16[256,2048]{1,0:T(8,128)(2,1)S(1)} %get-tuple-element.303.refs_0_, bf16[256,2048]{1,0:T(8,128)(2,1)S(1)} %collective-permute-done.20.refs_1_, bf16[256,2048]{1,0:T(8,128)(2,1)S(1)} %collective-permute-done.23.refs_2_, ...), custom_call_target="tpu_custom_call" | custom-call | flops 1000 | bytes 1000 | tf_op jit(solution)/shard_map/weight_terms/pallas_call | solution.py:723
  320.2 4.3 collective-permute-done.44
  328.4 6.6 %collective-permute-done.42.up_ref = bf16[128,1920]{1,0:T(8,128)(2,1)S(1)} collective-permute-done((bf16[128,1920]{1,0:T(8,128)(2,1)S(1)}, bf16[128,1920]{1,0:T(8,128)(2,1)S(1)}, u32[]{:S(2)}, u32[]{:S(2)}) %collective-permute-start.42) | collective-permute-done | bytes 491552 | tf_op jit(solution)/shard_map/ppermute | solution.py:100
  336.7 2.1 second_norm_back.1
  342.2 17.2 %collective-permute-done.47 = bf16[256,2304]{1,0:T(8,128)(2,1)S(1)} collective-permute-done((bf16[256,2304]{1,0:T(8,128)(2,1)S(1)}, bf16[256,2304]{1,0:T(8,128)(2,1)S(1)}, u32[]{:S(2)}, u32[]{:S(2)}) %collective-permute-start.47) | collective-permute-done | bytes 1179680 | tf_op jit(solution)/shard_map/ppermute | solution.py:100
  360.3 4.1 collective-permute-done.46.refs_1_.refs_2_
  368.1 22.4 %attention_backward.1 = (bf16[1024,512]{1,0:T(8,128)(2,1)S(1)}, bf16[1024,128]{1,0:T(8,128)(2,1)S(1)}) custom-call(s32[4]{0:T(128)S(1)} %fusion.2.places_ref, s32[6]{0:T(128)S(1)} %bitcast.12, s32[1]{0:T(128)S(6)} %copy.42.live_ref, f32[32,1024]{1,0:T(8,128)S(1)} %copy-done.36, f32[32,1024]{1,0:T(8,128)S(1)} %get-tuple-element.252.sin_ref, ...), custom_call_target="tpu_custom_call" | custom-call | flops 1000 | bytes 1000 | tf_op jit(solution)/shard_map/attention_backward/pallas_call | solution.py:58
  395.9 8.2 %heads_back.1 = (bf16[512,2048]{1,0:T(8,128)(2,1)S(1)}, bf16[512,2048]{1,0:T(8,128)(2,1)S(1)}, f32[8,2048]{1,0:T(8,128)S(1)}) custom-call(bf16[1024,512]{1,0:T(8,128)(2,1)S(1)} %get-tuple-element.391.grad_q_ref.refs_5_, bf16[1024,128]{1,0:T(8,128)(2,1)S(1)} %get-tuple-element.392.grad_kv_ref.refs_6_, bf16[256,2048]{1,0:T(8,128)(2,1)S(1)} %copy-done.1, ...), custom_call_target="tpu_custom_call" | custom-call | flops 1000 | bytes 1000 | tf_op jit(solution)/shard_map/heads_back/pallas_call | solution.py:565
  404.1 8.3 %weight_terms.5 = (bf16[2176,1152]{1,0:T(8,128)(2,1)S(1)}, bf16[144,1152]{1,0:T(8,128)(2,1)S(1)}, bf16[128,1152]{1,0:T(8,128)(2,1)S(1)}) custom-call(bf16[1024,2048]{1,0:T(8,128)(2,1)} %copy-done.23, bf16[256,2048]{1,0:T(8,128)(2,1)S(1)} %get-tuple-element.387.refs_0_.refs_1_, bf16[256,2048]{1,0:T(8,128)(2,1)S(1)} %collective-permute-done.46.refs_1_.refs_2_, ...), custom_call_target="tpu_custom_call" | custom-call | flops 1000 | bytes 1000 | tf_op jit(solution)/shard_map/weight_terms/pallas_call | solution.py:723
  417.0 6.8 %collective-permute-done.56.down_ref = bf16[128,1152]{1,0:T(8,128)(2,1)S(1)} collective-permute-done((bf16[128,1152]{1,0:T(8,128)(2,1)S(1)}, bf16[128,1152]{1,0:T(8,128)(2,1)S(1)}, u32[]{:S(2)}, u32[]{:S(2)}) %collective-permute-start.56) | collective-permute-done | bytes 294944 | tf_op jit(solution)/shard_map/ppermute | solution.py:103
  426.2 1.8 collective-permute-start.60
  429.1 19.7 %collective-permute-done.62 = bf16[256,1920]{1,0:T(8,128)(2,1)S(1)} collective-permute-done((bf16[256,1920]{1,0:T(8,128)(2,1)S(1)}, bf16[256,1920]{1,0:T(8,128)(2,1)S(1)}, u32[]{:S(2)}, u32[]{:S(2)}) %collective-permute-start.62) | collective-permute-done | bytes 983072 | tf_op jit(solution)/shard_map/ppermute | solution.py:100
  450.8 10.9 %collective-permute-done.60 = bf16[272,1152]{1,0:T(8,128)(2,1)S(1)} collective-permute-done((bf16[272,1152]{1,0:T(8,128)(2,1)S(1)}, bf16[272,1152]{1,0:T(8,128)(2,1)S(1)}, u32[]{:S(2)}, u32[]{:S(2)}) %collective-permute-start.60) | collective-permute-done | bytes 626720 | tf_op jit(solution)/shard_map/ppermute | solution.py:100
  465.7 2.9 layer_output.1
  468.7 3.0 first_norm_back.1
  471.6 7.2 %collective-permute-done.68 = bf16[272,1152]{1,0:T(8,128)(2,1)S(1)} collective-permute-done((bf16[272,1152]{1,0:T(8,128)(2,1)S(1)}, bf16[272,1152]{1,0:T(8,128)(2,1)S(1)}, u32[]{:S(2)}, u32[]{:S(2)}) %collective-permute-start.68) | collective-permute-done | bytes 626720 | tf_op jit(solution)/shard_map/ppermute | solution.py:100
  482.4 5.5 %collective-permute-done.72.refs_5_ = bf16[256,1920]{1,0:T(8,128)(2,1)S(1)} collective-permute-done((bf16[256,1920]{1,0:T(8,128)(2,1)S(1)}, bf16[256,1920]{1,0:T(8,128)(2,1)S(1)}, u32[]{:S(2)}, u32[]{:S(2)}) %collective-permute-start.72) | collective-permute-done | bytes 983072 | tf_op jit(solution)/shard_map/ppermute | solution.py:191
  487.9 6.6 %collective-permute-done.70 = bf16[272,1152]{1,0:T(8,128)(2,1)S(1)} collective-permute-done((bf16[272,1152]{1,0:T(8,128)(2,1)S(1)}, bf16[272,1152]{1,0:T(8,128)(2,1)S(1)}, u32[]{:S(2)}, u32[]{:S(2)}) %collective-permute-start.70) | collective-permute-done | bytes 626720 | tf_op jit(solution)/shard_map/ppermute | solution.py:100
  496.3 7.1 %unpack_mlp.1 = (f32[256,5632]{1,0:T(8,128)}, f32[256,5632]{1,0:T(8,128)}, f32[5632,256]{1,0:T(8,128)}) custom-call(s32[4]{0:T(128)S(1)} %fusion.2.places_ref, bf16[256,2304]{1,0:T(8,128)(2,1)S(1)} %add_convert_fusion.refs_0_, bf16[256,2304]{1,0:T(8,128)(2,1)S(1)} %collective-permute-done.51.refs_1_, bf16[256,2304]{1,0:T(8,128)(2,1)S(1)} %collective-permute-done.52.refs_2_, ...), custom_call_target="tpu_custom_call" | custom-call | flops 1000 | bytes 1000 | tf_op jit(solution)/shard_map/unpack_mlp/pallas_call | solution.py:917
  503.4 5.4 %collective-permute-done.73.refs_1_ = bf16[272,1152]{1,0:T(8,128)(2,1)S(1)} collective-permute-done((bf16[272,1152]{1,0:T(8,128)(2,1)S(1)}, bf16[272,1152]{1,0:T(8,128)(2,1)S(1)}, u32[]{:S(2)}, u32[]{:S(2)}) %collective-permute-start.73) | collective-permute-done | bytes 626720 | tf_op jit(solution)/shard_map/ppermute | solution.py:191
  508.8 2.1 collective-permute-done.76.refs_3_
  510.9 3.6 unpack_heads.1
  (286 shorter events, 100.7 us)
Async XLA Ops:
  3.2 17.3 %collective-permute-start = (bf16[272,1152]{1,0:T(8,128)(2,1)}, bf16[272,1152]{1,0:T(8,128)(2,1)S(1)}, u32[]{:S(2)}, u32[]{:S(2)}) collective-permute-start(bf16[272,1152]{1,0:T(8,128)(2,1)} %pack_heads.1.refs_4_), channel_id=1, source_target_pairs={{0,8},{8,16},{16,24},{24,28},{28,20},{20,12},{12,4},{4,0},{1,9},{9... | collective-permute-start | bytes 1880072 | tf_op jit(solution)/shard_map/ppermute | solution.py:100
  11.0 27.1 %collective-permute-start.2 = (bf16[256,2048]{1,0:T(8,128)(2,1)}, bf16[256,2048]{1,0:T(8,128)(2,1)}, u32[]{:S(2)}, u32[]{:S(2)}) collective-permute-start(bf16[256,2048]{1,0:T(8,128)(2,1)} %permute_features.2.refs_0_.inputs_ref), channel_id=1, source_target_pairs={{0,2},{1,3},{2,0},{3,1},{4,6},{5,7},{6,4},{7,5},{8,10},{9,11},{10,... | collective-permute-start | bytes 3145736 | tf_op jit(solution)/shard_map/ppermute | solution.py:191
  13.0 52.6 %collective-permute-start.5 = (bf16[256,2048]{1,0:T(8,128)(2,1)}, bf16[256,2048]{1,0:T(8,128)(2,1)}, u32[]{:S(2)}, u32[]{:S(2)}) collective-permute-start(bf16[256,2048]{1,0:T(8,128)(2,1)} %permute_features.2.refs_0_.inputs_ref), channel_id=1, source_target_pairs={{0,1},{1,0},{2,3},{3,2},{4,5},{5,4},{6,7},{7,6},{8,9},{9,8},{10,11... | collective-permute-start | bytes 3145736 | tf_op jit(solution)/shard_map/ppermute | solution.py:191
  38.1 27.5 %collective-permute-start.6 = (bf16[256,2048]{1,0:T(8,128)(2,1)}, bf16[256,2048]{1,0:T(8,128)(2,1)S(1)}, u32[]{:S(2)}, u32[]{:S(2)}) collective-permute-start(bf16[256,2048]{1,0:T(8,128)(2,1)} %collective-permute-done.2.refs_1_), channel_id=1, source_target_pairs={{0,1},{1,0},{2,3},{3,2},{4,5},{5,4},{6,7},{7,6},{8,9},{9,8},{10,11... | collective-permute-start | bytes 3145736 | tf_op jit(solution)/shard_map/ppermute | solution.py:191
  65.7 40.6 %collective-permute-start.14 = (bf16[256,2304]{1,0:T(8,128)(2,1)S(1)}, bf16[256,2304]{1,0:T(8,128)(2,1)S(1)}, u32[]{:S(2)}, u32[]{:S(2)}) collective-permute-start(bf16[256,2304]{1,0:T(8,128)(2,1)S(1)} %copy-done.37), channel_id=1, source_target_pairs={{0,8},{8,16},{16,24},{24,28},{28,20},{20,12},{12,4},{4,0},{1,9},{9... | collective-permute-start | bytes 3538952 | tf_op jit(solution)/shard_map/ppermute | solution.py:100
  66.7 39.6 %collective-permute-start.15 = (bf16[256,2304]{1,0:T(8,128)(2,1)S(1)}, bf16[256,2304]{1,0:T(8,128)(2,1)S(1)}, u32[]{:S(2)}, u32[]{:S(2)}) collective-permute-start(bf16[256,2304]{1,0:T(8,128)(2,1)S(1)} %copy-done.37), channel_id=1, source_target_pairs={{8,0},{16,8},{24,16},{28,24},{20,28},{12,20},{4,12},{0,4},{9,1},{1... | collective-permute-start | bytes 3538952 | tf_op jit(solution)/shard_map/ppermute | solution.py:103
  67.7 46.0 %collective-permute-start.11 = (bf16[256,2048]{1,0:T(8,128)(2,1)}, bf16[256,2048]{1,0:T(8,128)(2,1)S(1)}, u32[]{:S(2)}, u32[]{:S(2)}) collective-permute-start(bf16[256,2048]{1,0:T(8,128)(2,1)} %permute_features.3.refs_4_.cot_ref), channel_id=1, source_target_pairs={{0,2},{1,3},{2,0},{3,1},{4,6},{5,7},{6,4},{7,5},{8,10},{9,11},{10,... | collective-permute-start | bytes 3145736 | tf_op jit(solution)/shard_map/ppermute | solution.py:191
  69.2 43.5 %collective-permute-start.12 = (bf16[256,1920]{1,0:T(8,128)(2,1)}, bf16[256,1920]{1,0:T(8,128)(2,1)S(1)}, u32[]{:S(2)}, u32[]{:S(2)}) collective-permute-start(bf16[256,1920]{1,0:T(8,128)(2,1)} %get-tuple-element.333.refs_8_), channel_id=1, source_target_pairs={{0,8},{8,16},{16,24},{24,28},{28,20},{20,12},{12,4},{4,0},{1,9},{9... | collective-permute-start | bytes 2949128 | tf_op jit(solution)/shard_map/ppermute | solution.py:100
  70.2 43.5 %collective-permute-start.13 = (bf16[256,1920]{1,0:T(8,128)(2,1)}, bf16[256,1920]{1,0:T(8,128)(2,1)S(1)}, u32[]{:S(2)}, u32[]{:S(2)}) collective-permute-start(bf16[256,1920]{1,0:T(8,128)(2,1)} %get-tuple-element.333.refs_8_), channel_id=1, source_target_pairs={{8,0},{16,8},{24,16},{28,24},{20,28},{12,20},{4,12},{0,4},{9,1},{1... | collective-permute-start | bytes 2949128 | tf_op jit(solution)/shard_map/ppermute | solution.py:103
  113.8 28.4 %collective-permute-start.18 = (bf16[256,2304]{1,0:T(8,128)(2,1)S(1)}, bf16[256,2304]{1,0:T(8,128)(2,1)S(1)}, u32[]{:S(2)}, u32[]{:S(2)}) collective-permute-start(bf16[256,2304]{1,0:T(8,128)(2,1)S(1)} %collective-permute-done.14.refs_9_), channel_id=1, source_target_pairs={{0,8},{8,16},{16,24},{24,28},{28,20},{20,12},{12,4},{4,0},{1,9},{9... | collective-permute-start | bytes 3538952 | tf_op jit(solution)/shard_map/ppermute | solution.py:100
  114.5 28.0 %collective-permute-start.19 = (bf16[256,2304]{1,0:T(8,128)(2,1)S(1)}, bf16[256,2304]{1,0:T(8,128)(2,1)S(1)}, u32[]{:S(2)}, u32[]{:S(2)}) collective-permute-start(bf16[256,2304]{1,0:T(8,128)(2,1)S(1)} %collective-permute-done.15.refs_12_), channel_id=1, source_target_pairs={{8,0},{16,8},{24,16},{28,24},{20,28},{12,20},{4,12},{0,4},{9,1},{1... | collective-permute-start | bytes 3538952 | tf_op jit(solution)/shard_map/ppermute | solution.py:103
  118.3 26.2 %collective-permute-start.17 = (bf16[256,2048]{1,0:T(8,128)(2,1)S(1)}, bf16[256,2048]{1,0:T(8,128)(2,1)S(1)}, u32[]{:S(2)}, u32[]{:S(2)}) collective-permute-start(bf16[256,2048]{1,0:T(8,128)(2,1)S(1)} %add_convert_fusion.8), channel_id=1, source_target_pairs={{0,2},{1,3},{2,0},{3,1},{4,6},{5,7},{6,4},{7,5},{8,10},{9,11},{10,... | collective-permute-start | bytes 3145736 | tf_op jit(solution)/shard_map/ppermute | solution.py:191
  142.5 27.2 %collective-permute-start.21 = (bf16[256,2304]{1,0:T(8,128)(2,1)S(1)}, bf16[256,2304]{1,0:T(8,128)(2,1)S(1)}, u32[]{:S(2)}, u32[]{:S(2)}) collective-permute-start(bf16[256,2304]{1,0:T(8,128)(2,1)S(1)} %collective-permute-done.18.refs_10_), channel_id=1, source_target_pairs={{0,8},{8,16},{16,24},{24,28},{28,20},{20,12},{12,4},{4,0},{1,9},{9... | collective-permute-start | bytes 3538952 | tf_op jit(solution)/shard_map/ppermute | solution.py:100
  143.3 26.9 %collective-permute-start.22 = (bf16[256,2304]{1,0:T(8,128)(2,1)S(1)}, bf16[256,2304]{1,0:T(8,128)(2,1)S(1)}, u32[]{:S(2)}, u32[]{:S(2)}) collective-permute-start(bf16[256,2304]{1,0:T(8,128)(2,1)S(1)} %collective-permute-done.19.refs_13_), channel_id=1, source_target_pairs={{8,0},{16,8},{24,16},{28,24},{20,28},{12,20},{4,12},{0,4},{9,1},{1... | collective-permute-start | bytes 3538952 | tf_op jit(solution)/shard_map/ppermute | solution.py:103
  145.8 26.6 %collective-permute-start.20 = (bf16[256,2048]{1,0:T(8,128)(2,1)S(1)}, bf16[256,2048]{1,0:T(8,128)(2,1)S(1)}, u32[]{:S(2)}, u32[]{:S(2)}) collective-permute-start(bf16[256,2048]{1,0:T(8,128)(2,1)S(1)} %get-tuple-element.303.refs_0_), channel_id=1, source_target_pairs={{0,2},{1,3},{2,0},{3,1},{4,6},{5,7},{6,4},{7,5},{8,10},{9,11},{10,... | collective-permute-start | bytes 3145736 | tf_op jit(solution)/shard_map/ppermute | solution.py:191
  184.2 31.4 %collective-permute-start.29 = (bf16[256,1920]{1,0:T(8,128)(2,1)S(1)}, bf16[256,1920]{1,0:T(8,128)(2,1)S(1)}, u32[]{:S(2)}, u32[]{:S(2)}) collective-permute-start(bf16[256,1920]{1,0:T(8,128)(2,1)S(1)} %collective-permute-done.12.refs_9_), channel_id=1, source_target_pairs={{0,8},{8,16},{16,24},{24,28},{28,20},{20,12},{12,4},{4,0},{1,9},{9... | collective-permute-start | bytes 2949128 | tf_op jit(solution)/shard_map/ppermute | solution.py:100
  184.8 30.8 %collective-permute-start.30 = (bf16[256,1920]{1,0:T(8,128)(2,1)S(1)}, bf16[256,1920]{1,0:T(8,128)(2,1)S(1)}, u32[]{:S(2)}, u32[]{:S(2)}) collective-permute-start(bf16[256,1920]{1,0:T(8,128)(2,1)S(1)} %collective-permute-done.13.refs_12_), channel_id=1, source_target_pairs={{8,0},{16,8},{24,16},{28,24},{20,28},{12,20},{4,12},{0,4},{9,1},{1... | collective-permute-start | bytes 2949128 | tf_op jit(solution)/shard_map/ppermute | solution.py:103
  215.6 24.7 %collective-permute-start.31 = (bf16[256,1920]{1,0:T(8,128)(2,1)S(1)}, bf16[256,1920]{1,0:T(8,128)(2,1)S(1)}, u32[]{:S(2)}, u32[]{:S(2)}) collective-permute-start(bf16[256,1920]{1,0:T(8,128)(2,1)S(1)} %collective-permute-done.29.refs_10_), channel_id=1, source_target_pairs={{0,8},{8,16},{16,24},{24,28},{28,20},{20,12},{12,4},{4,0},{1,9},{9... | collective-permute-start | bytes 2949128 | tf_op jit(solution)/shard_map/ppermute | solution.py:100
  216.2 24.4 %collective-permute-start.32 = (bf16[256,1920]{1,0:T(8,128)(2,1)S(1)}, bf16[256,1920]{1,0:T(8,128)(2,1)S(1)}, u32[]{:S(2)}, u32[]{:S(2)}) collective-permute-start(bf16[256,1920]{1,0:T(8,128)(2,1)S(1)} %collective-permute-done.30.refs_13_), channel_id=1, source_target_pairs={{8,0},{16,8},{24,16},{28,24},{20,28},{12,20},{4,12},{0,4},{9,1},{1... | collective-permute-start | bytes 2949128 | tf_op jit(solution)/shard_map/ppermute | solution.py:103
  232.8 26.7 %collective-permute-start.35 = (bf16[128,2304]{1,0:T(8,128)(2,1)S(1)}, bf16[128,2304]{1,0:T(8,128)(2,1)S(1)}, u32[]{:S(2)}, u32[]{:S(2)}) collective-permute-start(bf16[128,2304]{1,0:T(8,128)(2,1)S(1)} %get-tuple-element.326), channel_id=1, source_target_pairs={{0,8},{8,16},{16,24},{24,28},{28,20},{20,12},{12,4},{4,0},{1,9},{9... | collective-permute-start | bytes 1769480 | tf_op jit(solution)/shard_map/ppermute | solution.py:100
  233.4 26.8 %collective-permute-start.36 = (bf16[128,2304]{1,0:T(8,128)(2,1)S(1)}, bf16[128,2304]{1,0:T(8,128)(2,1)S(1)}, u32[]{:S(2)}, u32[]{:S(2)}) collective-permute-start(bf16[128,2304]{1,0:T(8,128)(2,1)S(1)} %get-tuple-element.327), channel_id=1, source_target_pairs={{8,0},{16,8},{24,16},{28,24},{20,28},{12,20},{4,12},{0,4},{9,1},{1... | collective-permute-start | bytes 1769480 | tf_op jit(solution)/shard_map/ppermute | solution.py:103
  240.7 18.3 %collective-permute-start.33 = (bf16[128,1920]{1,0:T(8,128)(2,1)S(1)}, bf16[128,1920]{1,0:T(8,128)(2,1)S(1)}, u32[]{:S(2)}, u32[]{:S(2)}) collective-permute-start(bf16[128,1920]{1,0:T(8,128)(2,1)S(1)} %slice.107), channel_id=1, source_target_pairs={{0,8},{8,16},{16,24},{24,28},{28,20},{20,12},{12,4},{4,0},{1,9},{9... | collective-permute-start | bytes 1474568 | tf_op jit(solution)/shard_map/ppermute | solution.py:100
  241.6 17.8 %collective-permute-start.34 = (bf16[128,1920]{1,0:T(8,128)(2,1)S(1)}, bf16[128,1920]{1,0:T(8,128)(2,1)S(1)}, u32[]{:S(2)}, u32[]{:S(2)}) collective-permute-start(bf16[128,1920]{1,0:T(8,128)(2,1)S(1)} %slice.108), channel_id=1, source_target_pairs={{8,0},{16,8},{24,16},{28,24},{20,28},{12,20},{4,12},{0,4},{9,1},{1... | collective-permute-start | bytes 1474568 | tf_op jit(solution)/shard_map/ppermute | solution.py:103
  262.5 30.2 %collective-permute-start.37 = (bf16[256,2304]{1,0:T(8,128)(2,1)}, bf16[256,2304]{1,0:T(8,128)(2,1)}, u32[]{:S(2)}, u32[]{:S(2)}) collective-permute-start(bf16[256,2304]{1,0:T(8,128)(2,1)} %get-tuple-element.332), channel_id=1, source_target_pairs={{0,8},{8,16},{16,24},{24,28},{28,20},{20,12},{12,4},{4,0},{1,9},{9... | collective-permute-start | bytes 3538952 | tf_op jit(solution)/shard_map/ppermute | solution.py:100
  263.3 29.4 %collective-permute-start.38 = (bf16[256,2304]{1,0:T(8,128)(2,1)}, bf16[256,2304]{1,0:T(8,128)(2,1)}, u32[]{:S(2)}, u32[]{:S(2)}) collective-permute-start(bf16[256,2304]{1,0:T(8,128)(2,1)} %get-tuple-element.349), channel_id=1, source_target_pairs={{8,0},{16,8},{24,16},{28,24},{20,28},{12,20},{4,12},{0,4},{9,1},{1... | collective-permute-start | bytes 3538952 | tf_op jit(solution)/shard_map/ppermute | solution.py:103
  295.1 23.0 %collective-permute-start.39 = (bf16[512,2048]{1,0:T(8,128)(2,1)}, bf16[512,2048]{1,0:T(8,128)(2,1)}, u32[]{:S(2)}, u32[]{:S(2)}) collective-permute-start(bf16[512,2048]{1,0:T(8,128)(2,1)} %get-tuple-element.354), channel_id=1, source_target_pairs={{0,1},{1,0},{2,3},{3,2},{4,5},{5,4},{6,7},{7,6},{8,9},{9,8},{10,11... | collective-permute-start | bytes 6291464 | tf_op jit(solution)/shard_map/ppermute | solution.py:191
  295.6 28.8 %collective-permute-start.44 = (bf16[256,2304]{1,0:T(8,128)(2,1)S(1)}, bf16[256,2304]{1,0:T(8,128)(2,1)S(1)}, u32[]{:S(2)}, u32[]{:S(2)}) collective-permute-start(bf16[256,2304]{1,0:T(8,128)(2,1)S(1)} %get-tuple-element.353), channel_id=1, source_target_pairs={{0,8},{8,16},{16,24},{24,28},{28,20},{20,12},{12,4},{4,0},{1,9},{9... | collective-permute-start | bytes 3538952 | tf_op jit(solution)/shard_map/ppermute | solution.py:100
  296.4 28.9 %collective-permute-start.45 = (bf16[256,2304]{1,0:T(8,128)(2,1)S(1)}, bf16[256,2304]{1,0:T(8,128)(2,1)S(1)}, u32[]{:S(2)}, u32[]{:S(2)}) collective-permute-start(bf16[256,2304]{1,0:T(8,128)(2,1)S(1)} %get-tuple-element.369), channel_id=1, source_target_pairs={{8,0},{16,8},{24,16},{28,24},{20,28},{12,20},{4,12},{0,4},{9,1},{1... | collective-permute-start | bytes 3538952 | tf_op jit(solution)/shard_map/ppermute | solution.py:103
  303.1 33.4 %collective-permute-start.41 = (bf16[256,2048]{1,0:T(8,128)(2,1)}, bf16[256,2048]{1,0:T(8,128)(2,1)S(1)}, u32[]{:S(2)}, u32[]{:S(2)}) collective-permute-start(bf16[256,2048]{1,0:T(8,128)(2,1)} %add_convert_fusion.7), channel_id=1, source_target_pairs={{0,2},{1,3},{2,0},{3,1},{4,6},{5,7},{6,4},{7,5},{8,10},{9,11},{10,... | collective-permute-start | bytes 3145736 | tf_op jit(solution)/shard_map/ppermute | solution.py:191
  318.1 16.9 %collective-permute-start.42 = (bf16[128,1920]{1,0:T(8,128)(2,1)S(1)}, bf16[128,1920]{1,0:T(8,128)(2,1)S(1)}, u32[]{:S(2)}, u32[]{:S(2)}) collective-permute-start(bf16[128,1920]{1,0:T(8,128)(2,1)S(1)} %get-tuple-element.367), channel_id=1, source_target_pairs={{0,8},{8,16},{16,24},{24,28},{28,20},{20,12},{12,4},{4,0},{1,9},{9... | collective-permute-start | bytes 1474568 | tf_op jit(solution)/shard_map/ppermute | solution.py:100
  325.9 33.5 %collective-permute-start.47 = (bf16[256,2304]{1,0:T(8,128)(2,1)S(1)}, bf16[256,2304]{1,0:T(8,128)(2,1)S(1)}, u32[]{:S(2)}, u32[]{:S(2)}) collective-permute-start(bf16[256,2304]{1,0:T(8,128)(2,1)S(1)} %get-tuple-element.372), channel_id=1, source_target_pairs={{0,8},{8,16},{16,24},{24,28},{28,20},{20,12},{12,4},{4,0},{1,9},{9... | collective-permute-start | bytes 3538952 | tf_op jit(solution)/shard_map/ppermute | solution.py:100
  327.5 32.4 %collective-permute-start.48 = (bf16[256,2304]{1,0:T(8,128)(2,1)S(1)}, bf16[256,2304]{1,0:T(8,128)(2,1)S(1)}, u32[]{:S(2)}, u32[]{:S(2)}) collective-permute-start(bf16[256,2304]{1,0:T(8,128)(2,1)S(1)} %get-tuple-element.380), channel_id=1, source_target_pairs={{8,0},{16,8},{24,16},{28,24},{20,28},{12,20},{4,12},{0,4},{9,1},{1... | collective-permute-start | bytes 3538952 | tf_op jit(solution)/shard_map/ppermute | solution.py:103
  338.9 25.6 %collective-permute-start.46 = (bf16[256,2048]{1,0:T(8,128)(2,1)S(1)}, bf16[256,2048]{1,0:T(8,128)(2,1)S(1)}, u32[]{:S(2)}, u32[]{:S(2)}) collective-permute-start(bf16[256,2048]{1,0:T(8,128)(2,1)S(1)} %get-tuple-element.387.refs_0_.refs_1_), channel_id=1, source_target_pairs={{0,2},{1,3},{2,0},{3,1},{4,6},{5,7},{6,4},{7,5},{8,10},{9,11},{10,... | collective-permute-start | bytes 3145736 | tf_op jit(solution)/shard_map/ppermute | solution.py:191
  364.4 26.1 %collective-permute-start.53 = (bf16[256,1920]{1,0:T(8,128)(2,1)S(1)}, bf16[256,1920]{1,0:T(8,128)(2,1)S(1)}, u32[]{:S(2)}, u32[]{:S(2)}) collective-permute-start(bf16[256,1920]{1,0:T(8,128)(2,1)S(1)} %get-tuple-element.377), channel_id=1, source_target_pairs={{0,8},{8,16},{16,24},{24,28},{28,20},{20,12},{12,4},{4,0},{1,9},{9... | collective-permute-start | bytes 2949128 | tf_op jit(solution)/shard_map/ppermute | solution.py:100
  366.0 24.5 %collective-permute-start.54 = (bf16[256,1920]{1,0:T(8,128)(2,1)S(1)}, bf16[256,1920]{1,0:T(8,128)(2,1)S(1)}, u32[]{:S(2)}, u32[]{:S(2)}) collective-permute-start(bf16[256,1920]{1,0:T(8,128)(2,1)S(1)} %get-tuple-element.393), channel_id=1, source_target_pairs={{8,0},{16,8},{24,16},{28,24},{20,28},{12,20},{4,12},{0,4},{9,1},{1... | collective-permute-start | bytes 2949128 | tf_op jit(solution)/shard_map/ppermute | solution.py:103
  366.5 27.8 %collective-permute-start.51 = (bf16[256,2304]{1,0:T(8,128)(2,1)S(1)}, bf16[256,2304]{1,0:T(8,128)(2,1)S(1)}, u32[]{:S(2)}, u32[]{:S(2)}) collective-permute-start(bf16[256,2304]{1,0:T(8,128)(2,1)S(1)} %add_convert_fusion.refs_0_), channel_id=1, source_target_pairs={{0,2},{1,3},{2,0},{3,1},{4,6},{5,7},{6,4},{7,5},{8,10},{9,11},{10,... | collective-permute-start | bytes 3538952 | tf_op jit(solution)/shard_map/ppermute | solution.py:191
  368.0 26.3 %collective-permute-start.52 = (bf16[256,2304]{1,0:T(8,128)(2,1)S(1)}, bf16[256,2304]{1,0:T(8,128)(2,1)S(1)}, u32[]{:S(2)}, u32[]{:S(2)}) collective-permute-start(bf16[256,2304]{1,0:T(8,128)(2,1)S(1)} %add_convert_fusion.refs_0_), channel_id=1, source_target_pairs={{0,1},{1,0},{2,3},{3,2},{4,5},{5,4},{6,7},{7,6},{8,9},{9,8},{10,11... | collective-permute-start | bytes 3538952 | tf_op jit(solution)/shard_map/ppermute | solution.py:191
  391.0 24.2 %collective-permute-start.58 = (bf16[256,1920]{1,0:T(8,128)(2,1)S(1)}, bf16[256,1920]{1,0:T(8,128)(2,1)S(1)}, u32[]{:S(2)}, u32[]{:S(2)}) collective-permute-start(bf16[256,1920]{1,0:T(8,128)(2,1)S(1)} %get-tuple-element.396), channel_id=1, source_target_pairs={{0,8},{8,16},{16,24},{24,28},{28,20},{20,12},{12,4},{4,0},{1,9},{9... | collective-permute-start | bytes 2949128 | tf_op jit(solution)/shard_map/ppermute | solution.py:100
  392.7 23.9 %collective-permute-start.59 = (bf16[256,1920]{1,0:T(8,128)(2,1)S(1)}, bf16[256,1920]{1,0:T(8,128)(2,1)S(1)}, u32[]{:S(2)}, u32[]{:S(2)}) collective-permute-start(bf16[256,1920]{1,0:T(8,128)(2,1)S(1)} %get-tuple-element.412), channel_id=1, source_target_pairs={{8,0},{16,8},{24,16},{28,24},{20,28},{12,20},{4,12},{0,4},{9,1},{1... | collective-permute-start | bytes 2949128 | tf_op jit(solution)/shard_map/ppermute | solution.py:103
  394.3 22.7 %collective-permute-start.57 = (bf16[256,2304]{1,0:T(8,128)(2,1)S(1)}, bf16[256,2304]{1,0:T(8,128)(2,1)S(1)}, u32[]{:S(2)}, u32[]{:S(2)}) collective-permute-start(bf16[256,2304]{1,0:T(8,128)(2,1)S(1)} %collective-permute-done.51.refs_1_), channel_id=1, source_target_pairs={{0,1},{1,0},{2,3},{3,2},{4,5},{5,4},{6,7},{7,6},{8,9},{9,8},{10,11... | collective-permute-start | bytes 3538952 | tf_op jit(solution)/shard_map/ppermute | solution.py:191
  394.3 29.8 %collective-permute-start.64 = (bf16[256,2048]{1,0:T(8,128)(2,1)S(1)}, bf16[256,2048]{1,0:T(8,128)(2,1)S(1)}, u32[]{:S(2)}, u32[]{:S(2)}) collective-permute-start(bf16[256,2048]{1,0:T(8,128)(2,1)S(1)} %add_convert_fusion.6), channel_id=1, source_target_pairs={{0,2},{1,3},{2,0},{3,1},{4,6},{5,7},{6,4},{7,5},{8,10},{9,11},{10,... | collective-permute-start | bytes 3145736 | tf_op jit(solution)/shard_map/ppermute | solution.py:191
  424.2 24.6 %collective-permute-start.62 = (bf16[256,1920]{1,0:T(8,128)(2,1)S(1)}, bf16[256,1920]{1,0:T(8,128)(2,1)S(1)}, u32[]{:S(2)}, u32[]{:S(2)}) collective-permute-start(bf16[256,1920]{1,0:T(8,128)(2,1)S(1)} %get-tuple-element.415), channel_id=1, source_target_pairs={{0,8},{8,16},{16,24},{24,28},{28,20},{20,12},{12,4},{4,0},{1,9},{9... | collective-permute-start | bytes 2949128 | tf_op jit(solution)/shard_map/ppermute | solution.py:100
  425.8 24.6 %collective-permute-start.63 = (bf16[256,1920]{1,0:T(8,128)(2,1)S(1)}, bf16[256,1920]{1,0:T(8,128)(2,1)S(1)}, u32[]{:S(2)}, u32[]{:S(2)}) collective-permute-start(bf16[256,1920]{1,0:T(8,128)(2,1)S(1)} %get-tuple-element.423), channel_id=1, source_target_pairs={{8,0},{16,8},{24,16},{28,24},{20,28},{12,20},{4,12},{0,4},{9,1},{1... | collective-permute-start | bytes 2949128 | tf_op jit(solution)/shard_map/ppermute | solution.py:103
  426.2 35.5 %collective-permute-start.60 = (bf16[272,1152]{1,0:T(8,128)(2,1)S(1)}, bf16[272,1152]{1,0:T(8,128)(2,1)S(1)}, u32[]{:S(2)}, u32[]{:S(2)}) collective-permute-start(bf16[272,1152]{1,0:T(8,128)(2,1)S(1)} %get-tuple-element.421), channel_id=1, source_target_pairs={{0,8},{8,16},{16,24},{24,28},{28,20},{20,12},{12,4},{4,0},{1,9},{9... | collective-permute-start | bytes 1880072 | tf_op jit(solution)/shard_map/ppermute | solution.py:100
  428.0 35.0 %collective-permute-start.61 = (bf16[272,1152]{1,0:T(8,128)(2,1)S(1)}, bf16[272,1152]{1,0:T(8,128)(2,1)S(1)}, u32[]{:S(2)}, u32[]{:S(2)}) collective-permute-start(bf16[272,1152]{1,0:T(8,128)(2,1)S(1)} %get-tuple-element.422), channel_id=1, source_target_pairs={{8,0},{16,8},{24,16},{28,24},{20,28},{12,20},{4,12},{0,4},{9,1},{1... | collective-permute-start | bytes 1880072 | tf_op jit(solution)/shard_map/ppermute | solution.py:103
  428.9 39.7 %collective-permute-start.66 = (bf16[256,2048]{1,0:T(8,128)(2,1)S(1)}, bf16[256,2048]{1,0:T(8,128)(2,1)S(1)}, u32[]{:S(2)}, u32[]{:S(2)}) collective-permute-start(bf16[256,2048]{1,0:T(8,128)(2,1)S(1)} %add_convert_fusion.5), channel_id=1, source_target_pairs={{0,2},{1,3},{2,0},{3,1},{4,6},{5,7},{6,4},{7,5},{8,10},{9,11},{10,... | collective-permute-start | bytes 3145736 | tf_op jit(solution)/shard_map/ppermute | solution.py:191
  450.8 17.9 %collective-permute-start.67 = (bf16[256,1920]{1,0:T(8,128)(2,1)S(1)}, bf16[256,1920]{1,0:T(8,128)(2,1)S(1)}, u32[]{:S(2)}, u32[]{:S(2)}) collective-permute-start(bf16[256,1920]{1,0:T(8,128)(2,1)S(1)} %add_convert_fusion.9.refs_4_), channel_id=1, source_target_pairs={{0,1},{1,0},{2,3},{3,2},{4,5},{5,4},{6,7},{7,6},{8,9},{9,8},{10,11... | collective-permute-start | bytes 2949128 | tf_op jit(solution)/shard_map/ppermute | solution.py:191
  465.5 22.4 %collective-permute-start.72 = (bf16[256,1920]{1,0:T(8,128)(2,1)S(1)}, bf16[256,1920]{1,0:T(8,128)(2,1)S(1)}, u32[]{:S(2)}, u32[]{:S(2)}) collective-permute-start(bf16[256,1920]{1,0:T(8,128)(2,1)S(1)} %add_convert_fusion.9.refs_4_), channel_id=1, source_target_pairs={{0,2},{1,3},{2,0},{3,1},{4,6},{5,7},{6,4},{7,5},{8,10},{9,11},{10,... | collective-permute-start | bytes 2949128 | tf_op jit(solution)/shard_map/ppermute | solution.py:191
  (90 other events, 1713.1 us)

commit v6 on v5

--- a/solution.py
+++ b/solution.py
@@ -16,12 +16,12 @@
 F32 = jnp.float32
 NEG = -1e30
 LIMITS = {
-    "attention_forward": 20,
-    "attention_backward": 16,
-    "heads_back": 14,
-    "mlp_chunk": 26,
+    "attention_forward": 23,
+    "attention_backward": 18,
+    "heads_back": 15,
+    "mlp_chunk": 29,
     "mlp_chunk_far": 44,
-    "weight_terms": 14,
+    "weight_terms": 15,
     "unpack_mlp": 28,
     "unpack_heads": 12,
     "permute_features": 56,
@@ -140,9 +140,15 @@
         self.flying = (self.ring.go_up(up), self.ring.go_down(down))
 
     def relay(self, clock):
-        if self.left:
-            self.land(clock)
-            self.go(clock)
+        if self.left == 0:
+            return
+        self.left -= 1
+        up = clock.tie(self.flying[0])
+        self.up.append(up)
+        up = self.ring.go_up(up if self.left else up[: self.cut])
+        down = clock.tie(self.flying[1])
+        self.down.append(down)
+        self.flying = (up, self.ring.go_down(down if self.left else down[self.cut :]))
 
     def finish(self, clock):
         while self.left:
@@ -162,25 +168,62 @@
         end = self.full if end is None else end
         return self.terms[slot * self.full + begin : slot * self.full + end]
 
-    def relay(self, clock):
+    def land(self, clock):
+        self.relay(clock, hold=True)
+
+    def go(self, clock):
+        up, down = clock.tie(*self.held)
+        self.flying = (self.ring.go_up(up), self.ring.go_down(down))
+
+    def relay(self, clock, hold=False):
         if self.left == 0:
             return
-        up, down = clock.tie(*self.flying)
         above, below = self.ring.half - 1 + self.left, self.left
-        if up.shape[0] == self.full:
-            up, down = plus(self.term(above), up), plus(self.term(below), down)
-        else:
-            up, down = ring_add(self.terms, (above, below), up, down, self.full, self.cut, self.tile)
         self.left -= 1
-        up, down = clock.tie(up, down)
-        self.flying = (self.ring.go_up(up), self.ring.go_down(down))
+        up, down = self.flying
+        if up.shape[0] < self.full:
+            up, down = clock.tie(up, down)
+            self.held = ring_add(
+                self.terms, (above, below), up, down, self.full, self.cut, self.tile
+            )
+            if not hold:
+                self.go(clock)
+            return
+        up = self.ring.go_up(clock.tie(plus(self.term(above), clock.tie(up))))
+        down = self.ring.go_down(clock.tie(plus(self.term(below), clock.tie(down))))
+        self.flying = (up, down)
 
     def finish(self, clock):
         while self.left:
             self.relay(clock)
         up, down = clock.tie(*self.flying)
-        out = (self.term(0).astype(F32) + up.astype(F32) + down.astype(F32)).astype(BF)
-        return clock.tie(out)
+        return clock.tie(self.last(0, self.full, up, down))
+
+    def last(self, begin, end, up, down):
+        return (self.term(0, begin, end).astype(F32) + up.astype(F32) + down.astype(F32)).astype(BF)
+
+    def fork(self, clock):
+        while self.left > 2:
+            self.relay(clock)
+        up, down = clock.tie(*self.flying)
+        self.rows = [(0, self.cut), (self.cut, self.full)]
+        self.parts = []
+        for begin, end in self.rows:
+            self.parts.append(self.pass_on(2, begin, end, up[begin:end], down[begin:end], clock))
+
+    def pass_on(self, left, begin, end, up, down, clock):
+        up = plus(self.term(self.ring.half - 1 + left, begin, end), up)
+        down = plus(self.term(left, begin, end), down)
+        up, down = clock.tie(up, down)
+        return self.ring.go_up(up), self.ring.go_down(down)
+
+    def relay_part(self, part, clock):
+        up, down = clock.tie(*self.parts[part])
+        self.parts[part] = self.pass_on(1, *self.rows[part], up, down, clock)
+
+    def finish_part(self, part, clock):
+        up, down = clock.tie(*self.parts[part])
+        return clock.tie(self.last(*self.rows[part], up, down))
 
 
 def plus(one, two):
@@ -317,11 +360,15 @@
 
 
 def pick(refs, place, target):
-    for index, ref in enumerate(refs):
+    rows = target.shape[0]
+    at = 0
+    for ref in refs:
+        index, begin, count = at // rows, at % rows, ref.shape[0]
+        at += count
 
         @pl.when(place == index)
         def _():
-            target[...] = ref[...]
+            target[begin : begin + count, :] = ref[...]
 
 
 def write_bias(bias_ref, lengths_ref, live, block, rows):
@@ -625,11 +672,11 @@
     first = pl.BlockSpec((rows, model), lambda i: (jnp.minimum(i, 1), 0))
     second = pl.BlockSpec((rows, model), lambda i: (jnp.maximum(i - 2, 0), 0))
     fixed = pl.BlockSpec(memory_space=pltpu.VMEM)
-    half = jax.ShapeDtypeStruct((pack_size // 2, model), BF)
+    half = pltpu.HBM((pack_size // 2, model), BF)
     return pl.pallas_call(
         body,
         grid=(4,),
-        out_shape=(half, half, half, half, jax.ShapeDtypeStruct((pack_size, 3 * size), BF)),
+        out_shape=(half, half, half, half, pltpu.HBM((pack_size, 3 * size), BF)),
         in_specs=[fixed] * (8 + len(pieces)) + [first, second] * (len(before) // 2),
         out_specs=(first, second, first, second, pl.BlockSpec((rows, 3 * size), lambda i: (i, 0))),
         scratch_shapes=[
@@ -941,8 +988,8 @@
     kv = q_cols + 2 * HD
 
     def body(places_ref, *refs):
-        head_refs = refs[:4]
-        query_ref, key_ref, value_ref, out_ref, gain_ref, head_s = refs[4:]
+        head_refs = refs[: len(heads)]
+        query_ref, key_ref, value_ref, out_ref, gain_ref, head_s = refs[len(heads) :]
         gain = jnp.zeros((8, 2 * width), F32)
         for place in range(4):
             pick(head_refs, places_ref[place], head_s)
@@ -965,7 +1012,7 @@
             ((4 * q_cols, width), F32),
             ((8, 2 * width), F32),
         ],
-        scratch=[pltpu.VMEM(heads[0].shape, BF)],
+        scratch=[pltpu.VMEM((TOP + width, heads[0].shape[1]), BF)],
         smem=1,
         args=args,
         name="unpack_heads",
@@ -1091,19 +1138,19 @@
             middle,
         )
 
-    *before, both = far_memory(*mlp_chunk(seconds, cots, pieces, (), sizes[0], "mlp_chunk"))
+    *before, both = mlp_chunk(seconds, cots, pieces, (), sizes[0], "mlp_chunk")
     clock.done(both)
     chunks[1].relay(clock)
     terms = terms_of(clock.tie(both), sizes[0])
     clock.done(terms[0])
     sums = [Scatter(ring, terms, middle, sizes[0])]
     chunks[1].relay(clock)
+    sums[0].land(clock)
     pieces = far_memory(*chunks[1].finish(clock))
-    sums[0].relay(clock)
+    sums[0].go(clock)
     down_keep, down_send, grad_keep, grad_send, both = mlp_chunk(
         seconds, cots, clock.tie(*pieces), before, sizes[1], "mlp_chunk_far"
     )
-    both = far_memory(both)[0]
     clock.done(both)
     sums[0].relay(clock)
     grad_send, down_send = clock.tie(grad_send, down_send)
@@ -1175,7 +1222,7 @@
     last = swap(clock.tie(other_half(grad_keep, came)), 2)
     second_sum = sums[1].finish(clock)
     second_across, second_beside = swap(second_sum, 2), swap(second_sum, 1)
-    head_ring.relay(clock)
+    head_ring.fork(clock)
     down_came = clock.tie(down_came)
     result = layer_output(hidden, down_keep, down_came, down_last, ring.slot_owners(), n_dp)
     clock.done(result)
@@ -1184,16 +1231,22 @@
         grad_hidden, mine, grad_keep, came, last, gains, ring.slot_owners(), n_dp
     )
     clock.done(grad_input)
-    head_ring.relay(clock)
+    head_ring.relay_part(0, clock)
+    head_ring.relay_part(1, clock)
+    head_sums = [head_ring.finish_part(0, clock)]
+    head_across = [swap(head_sums[0], 2)]
     second_across = clock.tie(second_across)
     others = four(second_sum, second_across, second_beside)
-    head_sum = head_ring.finish(clock)
-    head_across, head_beside = swap(head_sum, 2), swap(head_sum, 1)
+    head_sums.append(head_ring.finish_part(1, clock))
+    head_across.append(swap(head_sums[1], 2))
     others = list(clock.tie(*others))
     grad_gate, grad_up, grad_down = unpack_mlp(places, [firsts, others], bounds, width, ff)
     clock.done(grad_gate)
-    head_across = clock.tie(head_across)
-    head_blocks = four(head_sum, head_across, head_beside)
+    head_beside = [swap(part, 1) for part in head_sums]
+    head_across = clock.tie(*head_across)
+    head_blocks = [
+        *head_sums, *head_across, *head_beside, *[swap(part, 1) for part in head_across]
+    ]
     grad_query, grad_key, grad_value, grad_out, gain_sums = unpack_heads(
         places, list(clock.tie(*head_blocks)), width, q_cols
     )

time: 523 us -> 519 us (level)
    pallas_call x3, Pallas kernels: 36.7 us -> 29.8 us  [weight_terms(): pl.pallas_call(body, grid=(n_slots // group,), out_shape=(jax.ShapeDtypeS...]
    ppermute x29 -> x32, waiting for transfers between devices: 25.2 us -> 22.1 us  [swap(): return lax.ppermute(block, 'seq', [(i, i ^ distance) for i in range(4)])]
    unnamed x122 -> x104, local copies, waits for them, and re-layouts: 11.7 us -> 9.12 us
    ppermute x24 -> x26, starting transfers between devices: 22.7 us -> 24.7 us  [go_down(): return lax.ppermute(block, 'dp', self.down)]
    ppermute x24 -> x26, waiting for transfers between devices: 28.9 us -> 30.5 us  [go_down(): return lax.ppermute(block, 'dp', self.down)]
    ppermute x29 -> x32, starting transfers between devices: 15.2 us -> 16.6 us  [swap(): return lax.ppermute(block, 'seq', [(i, i ^ distance) for i in range(4)])]
    ppermute x24 -> x26, starting transfers between devices: 29.8 us -> 31 us  [go_up(): return lax.ppermute(block, 'dp', self.up)]
    ppermute x24 -> x26, waiting for transfers between devices: 184 us -> 185 us  [go_up(): return lax.ppermute(block, 'dp', self.up)]
  transfers between devices with their start and end apart: 77 -> 84, of which waited for: 44 -> 47; matrix products, arithmetic and copies ran while one was open for 2% -> 2% of each run, Pallas kernels for 34% -> 33%
where the time goes in v6:
time: 519 us; the launch traced here: 512 us
  waiting for transfers between devices  237 us (46%)
  Pallas kernels  176 us (34%)
  starting transfers between devices  72.3 us (14%)
  other arithmetic  12.4 us (2%)
  local copies, waits for them, and re-layouts  11.7 us (2%)
    ppermute x26, waiting for transfers between devices, go_up(): return lax.ppermute(block, 'dp', self.up)  185 us
    pallas_call x5, Pallas kernels, kernel_call(): pl.pallas_call(body, out_shape=tuple((jax.ShapeDtypeStruct(s, d) for s, d...  59.6 us
    pallas_call x2, Pallas kernels, mlp_chunk(): pl.pallas_call(body, grid=(4,), out_shape=(half, half, half, half, pltpu....  54.3 us
    ppermute x26, starting transfers between devices, go_up(): return lax.ppermute(block, 'dp', self.up)  31 us
    ppermute x26, waiting for transfers between devices, go_down(): return lax.ppermute(block, 'dp', self.down)  30.5 us
    pallas_call x3, Pallas kernels, weight_terms(): pl.pallas_call(body, grid=(n_slots // group,), out_shape=(jax.ShapeDtypeS...  29.8 us
    ppermute x26, starting transfers between devices, go_down(): return lax.ppermute(block, 'dp', self.down)  24.7 us
    ppermute x32, waiting for transfers between devices, swap(): return lax.ppermute(block, 'seq', [(i, i ^ distance) for i in range(4)])  22.1 us
  transfers between devices with their start and end apart: 84, of which 47 were waited for; matrix products, arithmetic and copies ran while one was open for 2% of the time, Pallas kernels for 33%

profile of v6, /device:TPU:0, one launch (start us, length us, event | category | flops | bytes accessed | tf_op | source)
XLA Modules:
  0.0 511.9 jit_solution(17628325496782100089)
XLA Ops:
  0.7 2.5 pack_heads.1.refs_4_
  3.2 2.9 collective-permute-start
  8.7 2.4 permute_features.2.refs_0_.inputs_ref
  11.0 2.0 collective-permute-start.2
  13.2 3.2 pack_mlp.1
  16.4 5.5 %collective-permute-done.1.refs_5_ = bf16[272,1152]{1,0:T(8,128)(2,1)S(1)} collective-permute-done((bf16[272,1152]{1,0:T(8,128)(2,1)}, bf16[272,1152]{1,0:T(8,128)(2,1)S(1)}, u32[]{:S(2)}, u32[]{:S(2)}) %collective-permute-start.1) | collective-permute-done | bytes 626720 | tf_op jit(solution)/shard_map/ppermute | solution.py:100
  24.6 2.4 permute_features.3.refs_4_.cot_ref
  27.1 9.6 %collective-permute-done.4.refs_6_ = bf16[272,1152]{1,0:T(8,128)(2,1)S(1)} collective-permute-done((bf16[272,1152]{1,0:T(8,128)(2,1)S(1)}, bf16[272,1152]{1,0:T(8,128)(2,1)S(1)}, u32[]{:S(2)}, u32[]{:S(2)}) %collective-permute-start.4) | collective-permute-done | bytes 626720 | tf_op jit(solution)/shard_map/ppermute | solution.py:100
  39.2 14.4 %collective-permute-done.7.refs_7_ = bf16[272,1152]{1,0:T(8,128)(2,1)S(1)} collective-permute-done((bf16[272,1152]{1,0:T(8,128)(2,1)S(1)}, bf16[272,1152]{1,0:T(8,128)(2,1)S(1)}, u32[]{:S(2)}, u32[]{:S(2)}) %collective-permute-start.7) | collective-permute-done | bytes 626720 | tf_op jit(solution)/shard_map/ppermute | solution.py:100
  55.8 7.7 %collective-permute-done.10.refs_12_ = bf16[128,1152]{1,0:T(8,128)(2,1)S(1)} collective-permute-done((bf16[128,1152]{1,0:T(8,128)(2,1)S(1)}, bf16[128,1152]{1,0:T(8,128)(2,1)S(1)}, u32[]{:S(2)}, u32[]{:S(2)}) %collective-permute-start.10) | collective-permute-done | bytes 294944 | tf_op jit(solution)/shard_map/ppermute | solution.py:103
  69.9 28.8 %attention_forward.1 = (bf16[1024,2048]{1,0:T(8,128)(2,1)S(1)}, bf16[512,1024]{1,0:T(8,128)(2,1)S(1)}, bf16[1024,128]{1,0:T(8,128)(2,1)S(1)}, bf16[192,1024]{1,0...) custom-call(s32[4]{0:T(128)S(1)} %fusion.2.places_ref, ...), custom_call_target="tpu_custom_call" | custom-call | flops 1000 | bytes 1000 | tf_op jit(solution)/shard_map/attention_forward/pallas_call | solution.py:58
  98.8 2.0 copy-done.19
  102.5 8.8 %collective-permute-done.12.refs_9_ = bf16[256,1920]{1,0:T(8,128)(2,1)S(1)} collective-permute-done((bf16[256,1920]{1,0:T(8,128)(2,1)}, bf16[256,1920]{1,0:T(8,128)(2,1)S(1)}, u32[]{:S(2)}, u32[]{:S(2)}) %collective-permute-start.12) | collective-permute-done | bytes 983072 | tf_op jit(solution)/shard_map/ppermute | solution.py:100
  114.6 2.1 collective-permute-done.16.came_ref
  118.7 22.4 %collective-permute-done.19.refs_10_ = bf16[256,2304]{1,0:T(8,128)(2,1)S(1)} collective-permute-done((bf16[256,2304]{1,0:T(8,128)(2,1)S(1)}, bf16[256,2304]{1,0:T(8,128)(2,1)S(1)}, u32[]{:S(2)}, u32[]{:S(2)}) %collective-permute-start.19) | collective-permute-done | bytes 1179680 | tf_op jit(solution)/shard_map/ppermute | solution.py:100
  147.0 21.3 %collective-permute-done.22.refs_11_ = bf16[256,2304]{1,0:T(8,128)(2,1)S(1)} collective-permute-done((bf16[256,2304]{1,0:T(8,128)(2,1)S(1)}, bf16[256,2304]{1,0:T(8,128)(2,1)S(1)}, u32[]{:S(2)}, u32[]{:S(2)}) %collective-permute-start.22) | collective-permute-done | bytes 1179680 | tf_op jit(solution)/shard_map/ppermute | solution.py:100
  172.3 10.7 %collective-permute-done.25.refs_15_ = bf16[128,2304]{1,0:T(8,128)(2,1)S(1)} collective-permute-done((bf16[128,2304]{1,0:T(8,128)(2,1)S(1)}, bf16[128,2304]{1,0:T(8,128)(2,1)S(1)}, u32[]{:S(2)}, u32[]{:S(2)}) %collective-permute-start.25) | collective-permute-done | bytes 589856 | tf_op jit(solution)/shard_map/ppermute | solution.py:100
  186.8 26.3 %mlp_chunk.2 = (bf16[512,2048]{1,0:T(8,128)(2,1)}, bf16[512,2048]{1,0:T(8,128)(2,1)}, bf16[512,2048]{1,0:T(8,128)(2,1)}, bf16[512,2048]{1,0:T(8,128)(2,1)}, bf16[1024,2304]{1,0:T(8,128)(2,1)}) custom-call(bf16[256,2048]{1,0:T(8,128)(2,1)S(1)} %get-tuple-element.289.refs_0_, bf16[256,2048]{1,0:T(8,128)(2,1)S(1)} %collective-permute-done.20.refs_1_, ...), custom_call_target="tpu_custom_call" | custom-call | flops 1000 | bytes 1000 | tf_op jit(solution)/shard_map/mlp_chunk/pallas_call | solution.py:676
  215.3 2.3 copy-done.2
  217.6 11.4 %weight_terms.3 = (bf16[2048,2304]{1,0:T(8,128)(2,1)S(1)}, bf16[128,2304]{1,0:T(8,128)(2,1)S(1)}, bf16[128,2304]{1,0:T(8,128)(2,1)S(1)}) custom-call(bf16[256,2048]{1,0:T(8,128)(2,1)S(1)} %get-tuple-element.289.refs_0_, bf16[256,2048]{1,0:T(8,128)(2,1)S(1)} %collective-permute-done.20.refs_1_, bf16[256,2048]{1,0:T(8,128)(2,1)S(1)} %collective-permute-done.23.refs_2_, ...), custom_call_target="tpu_custom_call" | custom-call | flops 1000 | bytes 1000 | tf_op jit(solution)/shard_map/weight_terms/pallas_call | solution.py:770
  231.1 6.8 %collective-permute-done.30.refs_11_ = bf16[256,1920]{1,0:T(8,128)(2,1)S(1)} collective-permute-done((bf16[256,1920]{1,0:T(8,128)(2,1)S(1)}, bf16[256,1920]{1,0:T(8,128)(2,1)S(1)}, u32[]{:S(2)}, u32[]{:S(2)}) %collective-permute-start.30) | collective-permute-done | bytes 983072 | tf_op jit(solution)/shard_map/ppermute | solution.py:100
  241.6 9.0 %collective-permute-done.35.up_ref = bf16[128,2304]{1,0:T(8,128)(2,1)S(1)} collective-permute-done((bf16[128,2304]{1,0:T(8,128)(2,1)S(1)}, bf16[128,2304]{1,0:T(8,128)(2,1)S(1)}, u32[]{:S(2)}, u32[]{:S(2)}) %collective-permute-start.35) | collective-permute-done | bytes 589856 | tf_op jit(solution)/shard_map/ppermute | solution.py:100
  252.1 2.2 ring_add.3
  254.3 2.2 collective-permute-done.33.refs_15_
  260.7 28.0 %mlp_chunk.3 = (bf16[512,2048]{1,0:T(8,128)(2,1)}, bf16[512,2048]{1,0:T(8,128)(2,1)}, bf16[512,2048]{1,0:T(8,128)(2,1)}, bf16[512,2048]{1,0:T(8,128)(2,1)}, bf16[1024,1920]{1,0:T(8,128)(2,1)}) custom-call(bf16[256,2048]{1,0:T(8,128)(2,1)S(1)} %get-tuple-element.289.refs_0_, bf16[256,2048]{1,0:T(8,128)(2,1)S(1)} %collective-permute-done.20.refs_1_, ...), custom_call_target="tpu_custom_call" | custom-call | flops 1000 | bytes 1000 | tf_op jit(solution)/shard_map/mlp_chunk/pallas_call | solution.py:676
  290.4 1.7 add_convert_fusion.3
  294.7 3.8 collective-permute-done.40.came_ref
  300.5 10.3 %weight_terms.4 = (bf16[2048,1920]{1,0:T(8,128)(2,1)S(1)}, bf16[128,1920]{1,0:T(8,128)(2,1)S(1)}, bf16[128,1920]{1,0:T(8,128)(2,1)S(1)}) custom-call(bf16[256,2048]{1,0:T(8,128)(2,1)S(1)} %get-tuple-element.289.refs_0_, bf16[256,2048]{1,0:T(8,128)(2,1)S(1)} %collective-permute-done.20.refs_1_, bf16[256,2048]{1,0:T(8,128)(2,1)S(1)} %collective-permute-done.23.refs_2_, ...), custom_call_target="tpu_custom_call" | custom-call | flops 1000 | bytes 1000 | tf_op jit(solution)/shard_map/weight_terms/pallas_call | solution.py:770
  312.9 8.6 %collective-permute-done.45 = bf16[256,2304]{1,0:T(8,128)(2,1)S(1)} collective-permute-done((bf16[256,2304]{1,0:T(8,128)(2,1)S(1)}, bf16[256,2304]{1,0:T(8,128)(2,1)S(1)}, u32[]{:S(2)}, u32[]{:S(2)}) %collective-permute-start.45) | collective-permute-done | bytes 1179680 | tf_op jit(solution)/shard_map/ppermute | solution.py:100
  324.7 7.3 %collective-permute-done.42.up_ref = bf16[128,1920]{1,0:T(8,128)(2,1)S(1)} collective-permute-done((bf16[128,1920]{1,0:T(8,128)(2,1)S(1)}, bf16[128,1920]{1,0:T(8,128)(2,1)S(1)}, u32[]{:S(2)}, u32[]{:S(2)}) %collective-permute-start.42) | collective-permute-done | bytes 491552 | tf_op jit(solution)/shard_map/ppermute | solution.py:100
  334.2 2.0 second_norm_back.1
  340.4 16.1 %collective-permute-done.47 = bf16[256,2304]{1,0:T(8,128)(2,1)} collective-permute-done((bf16[256,2304]{1,0:T(8,128)(2,1)S(1)}, bf16[256,2304]{1,0:T(8,128)(2,1)}, u32[]{:S(2)}, u32[]{:S(2)}) %collective-permute-start.47) | collective-permute-done | bytes 1179680 | tf_op jit(solution)/shard_map/ppermute | solution.py:100
  357.6 2.0 add_convert_fusion.refs_0_
  359.6 3.5 collective-permute-done.46.refs_1_.refs_2_
  366.7 22.4 %attention_backward.1 = (bf16[1024,512]{1,0:T(8,128)(2,1)S(1)}, bf16[1024,128]{1,0:T(8,128)(2,1)S(1)}) custom-call(s32[4]{0:T(128)S(1)} %fusion.2.places_ref, s32[6]{0:T(128)S(1)} %bitcast.12, s32[1]{0:T(128)S(6)} %copy.42.live_ref, f32[32,1024]{1,0:T(8,128)S(1)} %copy-done.28, f32[32,1024]{1,0:T(8,128)S(1)} %get-tuple-element.249.sin_ref, ...), custom_call_target="tpu_custom_call" | custom-call | flops 1000 | bytes 1000 | tf_op jit(solution)/shard_map/attention_backward/pallas_call | solution.py:58
  394.4 8.0 %heads_back.1 = (bf16[512,2048]{1,0:T(8,128)(2,1)S(1)}, bf16[512,2048]{1,0:T(8,128)(2,1)S(1)}, f32[8,2048]{1,0:T(8,128)S(1)}) custom-call(bf16[1024,512]{1,0:T(8,128)(2,1)S(1)} %get-tuple-element.373.grad_q_ref.refs_5_, bf16[1024,128]{1,0:T(8,128)(2,1)S(1)} %get-tuple-element.374.grad_kv_ref.refs_6_, bf16[256,2048]{1,0:T(8,128)(2,1)S(1)} %copy-done.1, ...), custom_call_target="tpu_custom_call" | custom-call | flops 1000 | bytes 1000 | tf_op jit(solution)/shard_map/heads_back/pallas_call | solution.py:612
  402.6 8.1 %weight_terms.5 = (bf16[2176,1152]{1,0:T(8,128)(2,1)S(1)}, bf16[144,1152]{1,0:T(8,128)(2,1)S(1)}, bf16[128,1152]{1,0:T(8,128)(2,1)S(1)}) custom-call(bf16[1024,2048]{1,0:T(8,128)(2,1)} %copy-done.19, bf16[256,2048]{1,0:T(8,128)(2,1)S(1)} %get-tuple-element.369.refs_0_.refs_1_, bf16[256,2048]{1,0:T(8,128)(2,1)S(1)} %collective-permute-done.46.refs_1_.refs_2_, ...), custom_call_target="tpu_custom_call" | custom-call | flops 1000 | bytes 1000 | tf_op jit(solution)/shard_map/weight_terms/pallas_call | solution.py:770
  415.0 7.2 %collective-permute-done.56.down_ref = bf16[128,1152]{1,0:T(8,128)(2,1)S(1)} collective-permute-done((bf16[128,1152]{1,0:T(8,128)(2,1)S(1)}, bf16[128,1152]{1,0:T(8,128)(2,1)S(1)}, u32[]{:S(2)}, u32[]{:S(2)}) %collective-permute-start.56) | collective-permute-done | bytes 294944 | tf_op jit(solution)/shard_map/ppermute | solution.py:103
  427.7 19.4 %collective-permute-done.62 = bf16[256,1920]{1,0:T(8,128)(2,1)S(1)} collective-permute-done((bf16[256,1920]{1,0:T(8,128)(2,1)S(1)}, bf16[256,1920]{1,0:T(8,128)(2,1)S(1)}, u32[]{:S(2)}, u32[]{:S(2)}) %collective-permute-start.62) | collective-permute-done | bytes 983072 | tf_op jit(solution)/shard_map/ppermute | solution.py:100
  448.9 11.2 %collective-permute-done.60 = bf16[272,1152]{1,0:T(8,128)(2,1)S(1)} collective-permute-done((bf16[272,1152]{1,0:T(8,128)(2,1)S(1)}, bf16[272,1152]{1,0:T(8,128)(2,1)S(1)}, u32[]{:S(2)}, u32[]{:S(2)}) %collective-permute-start.60) | collective-permute-done | bytes 626720 | tf_op jit(solution)/shard_map/ppermute | solution.py:100
  464.4 1.9 layer_output.1
  468.0 2.9 first_norm_back.1
  475.2 3.2 collective-permute-done.72
  481.5 4.1 collective-permute-done.70
  486.5 2.0 collective-permute-done.76.refs_5_
  491.3 7.1 %unpack_mlp.1 = (f32[256,5632]{1,0:T(8,128)}, f32[256,5632]{1,0:T(8,128)}, f32[5632,256]{1,0:T(8,128)}) custom-call(s32[4]{0:T(128)S(1)} %fusion.2.places_ref, bf16[256,2304]{1,0:T(8,128)(2,1)S(1)} %add_convert_fusion.refs_0_, bf16[256,2304]{1,0:T(8,128)(2,1)S(1)} %collective-permute-done.51.refs_1_, bf16[256,2304]{1,0:T(8,128)(2,1)S(1)} %collective-permute-done.52.refs_2_, ...), custom_call_target="tpu_custom_call" | custom-call | flops 1000 | bytes 1000 | tf_op jit(solution)/shard_map/unpack_mlp/pallas_call | solution.py:964
  498.5 6.6 %collective-permute-done.78.refs_3_ = bf16[128,1152]{1,0:T(8,128)(2,1)S(1)} collective-permute-done((bf16[128,1152]{1,0:T(8,128)(2,1)S(1)}, bf16[128,1152]{1,0:T(8,128)(2,1)S(1)}, u32[]{:S(2)}, u32[]{:S(2)}) %collective-permute-start.78) | collective-permute-done | bytes 294944 | tf_op jit(solution)/shard_map/ppermute | solution.py:234
  507.5 3.6 unpack_heads.1
  (289 shorter events, 109.3 us)
Async XLA Ops:
  3.2 19.1 %collective-permute-start = (bf16[272,1152]{1,0:T(8,128)(2,1)}, bf16[272,1152]{1,0:T(8,128)(2,1)S(1)}, u32[]{:S(2)}, u32[]{:S(2)}) collective-permute-start(bf16[272,1152]{1,0:T(8,128)(2,1)} %pack_heads.1.refs_4_), channel_id=1, source_target_pairs={{8,0},{16,8},{24,16},{28,24},{20,28},{12,20},{4,12},{0,4},{9,1},{1... | collective-permute-start | bytes 1880072 | tf_op jit(solution)/shard_map/ppermute | solution.py:103
  11.0 26.1 %collective-permute-start.2 = (bf16[256,2048]{1,0:T(8,128)(2,1)}, bf16[256,2048]{1,0:T(8,128)(2,1)}, u32[]{:S(2)}, u32[]{:S(2)}) collective-permute-start(bf16[256,2048]{1,0:T(8,128)(2,1)} %permute_features.2.refs_0_.inputs_ref), channel_id=1, source_target_pairs={{0,2},{1,3},{2,0},{3,1},{4,6},{5,7},{6,4},{7,5},{8,10},{9,11},{10,... | collective-permute-start | bytes 3145736 | tf_op jit(solution)/shard_map/ppermute | solution.py:234
  13.0 50.6 %collective-permute-start.5 = (bf16[256,2048]{1,0:T(8,128)(2,1)}, bf16[256,2048]{1,0:T(8,128)(2,1)}, u32[]{:S(2)}, u32[]{:S(2)}) collective-permute-start(bf16[256,2048]{1,0:T(8,128)(2,1)} %permute_features.2.refs_0_.inputs_ref), channel_id=1, source_target_pairs={{0,1},{1,0},{2,3},{3,2},{4,5},{5,4},{6,7},{7,6},{8,9},{9,8},{10,11... | collective-permute-start | bytes 3145736 | tf_op jit(solution)/shard_map/ppermute | solution.py:234
  37.1 26.4 %collective-permute-start.6 = (bf16[256,2048]{1,0:T(8,128)(2,1)}, bf16[256,2048]{1,0:T(8,128)(2,1)S(1)}, u32[]{:S(2)}, u32[]{:S(2)}) collective-permute-start(bf16[256,2048]{1,0:T(8,128)(2,1)} %collective-permute-done.2.refs_1_), channel_id=1, source_target_pairs={{0,1},{1,0},{2,3},{3,2},{4,5},{5,4},{6,7},{7,6},{8,9},{9,8},{10,11... | collective-permute-start | bytes 3145736 | tf_op jit(solution)/shard_map/ppermute | solution.py:234
  63.6 38.9 %collective-permute-start.15 = (bf16[256,2304]{1,0:T(8,128)(2,1)}, bf16[256,2304]{1,0:T(8,128)(2,1)S(1)}, u32[]{:S(2)}, u32[]{:S(2)}) collective-permute-start(bf16[256,2304]{1,0:T(8,128)(2,1)} %get-tuple-element.267.refs_8_), channel_id=1, source_target_pairs={{0,8},{8,16},{16,24},{24,28},{28,20},{20,12},{12,4},{4,0},{1,9},{9... | collective-permute-start | bytes 3538952 | tf_op jit(solution)/shard_map/ppermute | solution.py:100
  65.2 37.3 %collective-permute-start.14 = (bf16[256,2304]{1,0:T(8,128)(2,1)}, bf16[256,2304]{1,0:T(8,128)(2,1)S(1)}, u32[]{:S(2)}, u32[]{:S(2)}) collective-permute-start(bf16[256,2304]{1,0:T(8,128)(2,1)} %get-tuple-element.267.refs_8_), channel_id=1, source_target_pairs={{8,0},{16,8},{24,16},{28,24},{20,28},{12,20},{4,12},{0,4},{9,1},{1... | collective-permute-start | bytes 3538952 | tf_op jit(solution)/shard_map/ppermute | solution.py:103
  65.7 46.9 %collective-permute-start.11 = (bf16[256,2048]{1,0:T(8,128)(2,1)}, bf16[256,2048]{1,0:T(8,128)(2,1)S(1)}, u32[]{:S(2)}, u32[]{:S(2)}) collective-permute-start(bf16[256,2048]{1,0:T(8,128)(2,1)} %permute_features.3.refs_4_.cot_ref), channel_id=1, source_target_pairs={{0,2},{1,3},{2,0},{3,1},{4,6},{5,7},{6,4},{7,5},{8,10},{9,11},{10,... | collective-permute-start | bytes 3145736 | tf_op jit(solution)/shard_map/ppermute | solution.py:234
  67.2 44.1 %collective-permute-start.12 = (bf16[256,1920]{1,0:T(8,128)(2,1)}, bf16[256,1920]{1,0:T(8,128)(2,1)S(1)}, u32[]{:S(2)}, u32[]{:S(2)}) collective-permute-start(bf16[256,1920]{1,0:T(8,128)(2,1)} %get-tuple-element.315.refs_8_), channel_id=1, source_target_pairs={{0,8},{8,16},{16,24},{24,28},{28,20},{20,12},{12,4},{4,0},{1,9},{9... | collective-permute-start | bytes 2949128 | tf_op jit(solution)/shard_map/ppermute | solution.py:100
  68.8 43.8 %collective-permute-start.13 = (bf16[256,1920]{1,0:T(8,128)(2,1)}, bf16[256,1920]{1,0:T(8,128)(2,1)S(1)}, u32[]{:S(2)}, u32[]{:S(2)}) collective-permute-start(bf16[256,1920]{1,0:T(8,128)(2,1)} %get-tuple-element.315.refs_8_), channel_id=1, source_target_pairs={{8,0},{16,8},{24,16},{28,24},{20,28},{12,20},{4,12},{0,4},{9,1},{1... | collective-permute-start | bytes 2949128 | tf_op jit(solution)/shard_map/ppermute | solution.py:103
  112.6 30.1 %collective-permute-start.18 = (bf16[256,2304]{1,0:T(8,128)(2,1)S(1)}, bf16[256,2304]{1,0:T(8,128)(2,1)S(1)}, u32[]{:S(2)}, u32[]{:S(2)}) collective-permute-start(bf16[256,2304]{1,0:T(8,128)(2,1)S(1)} %collective-permute-done.14.refs_12_), channel_id=1, source_target_pairs={{8,0},{16,8},{24,16},{28,24},{20,28},{12,20},{4,12},{0,4},{9,1},{1... | collective-permute-start | bytes 3538952 | tf_op jit(solution)/shard_map/ppermute | solution.py:103
  113.1 28.0 %collective-permute-start.19 = (bf16[256,2304]{1,0:T(8,128)(2,1)S(1)}, bf16[256,2304]{1,0:T(8,128)(2,1)S(1)}, u32[]{:S(2)}, u32[]{:S(2)}) collective-permute-start(bf16[256,2304]{1,0:T(8,128)(2,1)S(1)} %collective-permute-done.15.refs_9_), channel_id=1, source_target_pairs={{0,8},{8,16},{16,24},{24,28},{28,20},{20,12},{12,4},{4,0},{1,9},{9... | collective-permute-start | bytes 3538952 | tf_op jit(solution)/shard_map/ppermute | solution.py:100
  117.1 26.0 %collective-permute-start.17 = (bf16[256,2048]{1,0:T(8,128)(2,1)S(1)}, bf16[256,2048]{1,0:T(8,128)(2,1)S(1)}, u32[]{:S(2)}, u32[]{:S(2)}) collective-permute-start(bf16[256,2048]{1,0:T(8,128)(2,1)S(1)} %add_convert_fusion.8), channel_id=1, source_target_pairs={{0,2},{1,3},{2,0},{3,1},{4,6},{5,7},{6,4},{7,5},{8,10},{9,11},{10,... | collective-permute-start | bytes 3145736 | tf_op jit(solution)/shard_map/ppermute | solution.py:234
  141.1 27.2 %collective-permute-start.22 = (bf16[256,2304]{1,0:T(8,128)(2,1)S(1)}, bf16[256,2304]{1,0:T(8,128)(2,1)S(1)}, u32[]{:S(2)}, u32[]{:S(2)}) collective-permute-start(bf16[256,2304]{1,0:T(8,128)(2,1)S(1)} %collective-permute-done.19.refs_10_), channel_id=1, source_target_pairs={{0,8},{8,16},{16,24},{24,28},{28,20},{20,12},{12,4},{4,0},{1,9},{9... | collective-permute-start | bytes 3538952 | tf_op jit(solution)/shard_map/ppermute | solution.py:100
  142.7 26.9 %collective-permute-start.21 = (bf16[256,2304]{1,0:T(8,128)(2,1)S(1)}, bf16[256,2304]{1,0:T(8,128)(2,1)S(1)}, u32[]{:S(2)}, u32[]{:S(2)}) collective-permute-start(bf16[256,2304]{1,0:T(8,128)(2,1)S(1)} %collective-permute-done.18.refs_13_), channel_id=1, source_target_pairs={{8,0},{16,8},{24,16},{28,24},{20,28},{12,20},{4,12},{0,4},{9,1},{1... | collective-permute-start | bytes 3538952 | tf_op jit(solution)/shard_map/ppermute | solution.py:103
  144.4 27.4 %collective-permute-start.20 = (bf16[256,2048]{1,0:T(8,128)(2,1)S(1)}, bf16[256,2048]{1,0:T(8,128)(2,1)S(1)}, u32[]{:S(2)}, u32[]{:S(2)}) collective-permute-start(bf16[256,2048]{1,0:T(8,128)(2,1)S(1)} %get-tuple-element.289.refs_0_), channel_id=1, source_target_pairs={{0,2},{1,3},{2,0},{3,1},{4,6},{5,7},{6,4},{7,5},{8,10},{9,11},{10,... | collective-permute-start | bytes 3145736 | tf_op jit(solution)/shard_map/ppermute | solution.py:234
  184.4 28.8 %collective-permute-start.29 = (bf16[256,1920]{1,0:T(8,128)(2,1)S(1)}, bf16[256,1920]{1,0:T(8,128)(2,1)S(1)}, u32[]{:S(2)}, u32[]{:S(2)}) collective-permute-start(bf16[256,1920]{1,0:T(8,128)(2,1)S(1)} %collective-permute-done.12.refs_9_), channel_id=1, source_target_pairs={{0,8},{8,16},{16,24},{24,28},{28,20},{20,12},{12,4},{4,0},{1,9},{9... | collective-permute-start | bytes 2949128 | tf_op jit(solution)/shard_map/ppermute | solution.py:100
  185.9 28.8 %collective-permute-start.31 = (bf16[256,1920]{1,0:T(8,128)(2,1)S(1)}, bf16[256,1920]{1,0:T(8,128)(2,1)S(1)}, u32[]{:S(2)}, u32[]{:S(2)}) collective-permute-start(bf16[256,1920]{1,0:T(8,128)(2,1)S(1)} %collective-permute-done.13.refs_12_), channel_id=1, source_target_pairs={{8,0},{16,8},{24,16},{28,24},{20,28},{12,20},{4,12},{0,4},{9,1},{1... | collective-permute-start | bytes 2949128 | tf_op jit(solution)/shard_map/ppermute | solution.py:103
  213.2 24.7 %collective-permute-start.30 = (bf16[256,1920]{1,0:T(8,128)(2,1)S(1)}, bf16[256,1920]{1,0:T(8,128)(2,1)S(1)}, u32[]{:S(2)}, u32[]{:S(2)}) collective-permute-start(bf16[256,1920]{1,0:T(8,128)(2,1)S(1)} %collective-permute-done.29.refs_10_), channel_id=1, source_target_pairs={{0,8},{8,16},{16,24},{24,28},{28,20},{20,12},{12,4},{4,0},{1,9},{9... | collective-permute-start | bytes 2949128 | tf_op jit(solution)/shard_map/ppermute | solution.py:100
  214.7 24.7 %collective-permute-start.32 = (bf16[256,1920]{1,0:T(8,128)(2,1)S(1)}, bf16[256,1920]{1,0:T(8,128)(2,1)S(1)}, u32[]{:S(2)}, u32[]{:S(2)}) collective-permute-start(bf16[256,1920]{1,0:T(8,128)(2,1)S(1)} %collective-permute-done.31.refs_13_), channel_id=1, source_target_pairs={{8,0},{16,8},{24,16},{28,24},{20,28},{12,20},{4,12},{0,4},{9,1},{1... | collective-permute-start | bytes 2949128 | tf_op jit(solution)/shard_map/ppermute | solution.py:103
  229.0 21.5 %collective-permute-start.35 = (bf16[128,2304]{1,0:T(8,128)(2,1)S(1)}, bf16[128,2304]{1,0:T(8,128)(2,1)S(1)}, u32[]{:S(2)}, u32[]{:S(2)}) collective-permute-start(bf16[128,2304]{1,0:T(8,128)(2,1)S(1)} %get-tuple-element.306), channel_id=1, source_target_pairs={{0,8},{8,16},{16,24},{24,28},{28,20},{20,12},{12,4},{4,0},{1,9},{9... | collective-permute-start | bytes 1769480 | tf_op jit(solution)/shard_map/ppermute | solution.py:100
  230.6 21.5 %collective-permute-start.36 = (bf16[128,2304]{1,0:T(8,128)(2,1)S(1)}, bf16[128,2304]{1,0:T(8,128)(2,1)S(1)}, u32[]{:S(2)}, u32[]{:S(2)}) collective-permute-start(bf16[128,2304]{1,0:T(8,128)(2,1)S(1)} %get-tuple-element.307), channel_id=1, source_target_pairs={{8,0},{16,8},{24,16},{28,24},{20,28},{12,20},{4,12},{0,4},{9,1},{1... | collective-permute-start | bytes 1769480 | tf_op jit(solution)/shard_map/ppermute | solution.py:103
  239.4 17.0 %collective-permute-start.33 = (bf16[128,1920]{1,0:T(8,128)(2,1)S(1)}, bf16[128,1920]{1,0:T(8,128)(2,1)S(1)}, u32[]{:S(2)}, u32[]{:S(2)}) collective-permute-start(bf16[128,1920]{1,0:T(8,128)(2,1)S(1)} %slice.134), channel_id=1, source_target_pairs={{0,8},{8,16},{16,24},{24,28},{28,20},{20,12},{12,4},{4,0},{1,9},{9... | collective-permute-start | bytes 1474568 | tf_op jit(solution)/shard_map/ppermute | solution.py:100
  258.5 30.2 %collective-permute-start.38 = (bf16[256,2304]{1,0:T(8,128)(2,1)}, bf16[256,2304]{1,0:T(8,128)(2,1)}, u32[]{:S(2)}, u32[]{:S(2)}) collective-permute-start(bf16[256,2304]{1,0:T(8,128)(2,1)} %get-tuple-element.314), channel_id=1, source_target_pairs={{0,8},{8,16},{16,24},{24,28},{28,20},{20,12},{12,4},{4,0},{1,9},{9... | collective-permute-start | bytes 3538952 | tf_op jit(solution)/shard_map/ppermute | solution.py:100
  259.8 30.6 %collective-permute-start.37 = (bf16[256,2304]{1,0:T(8,128)(2,1)}, bf16[256,2304]{1,0:T(8,128)(2,1)}, u32[]{:S(2)}, u32[]{:S(2)}) collective-permute-start(bf16[256,2304]{1,0:T(8,128)(2,1)} %get-tuple-element.331), channel_id=1, source_target_pairs={{8,0},{16,8},{24,16},{28,24},{20,28},{12,20},{4,12},{0,4},{9,1},{1... | collective-permute-start | bytes 3538952 | tf_op jit(solution)/shard_map/ppermute | solution.py:103
  292.2 18.6 %collective-permute-start.39 = (bf16[512,2048]{1,0:T(8,128)(2,1)}, bf16[512,2048]{1,0:T(8,128)(2,1)S(1)}, u32[]{:S(2)}, u32[]{:S(2)}) collective-permute-start(bf16[512,2048]{1,0:T(8,128)(2,1)} %get-tuple-element.337), channel_id=1, source_target_pairs={{0,1},{1,0},{2,3},{3,2},{4,5},{5,4},{6,7},{7,6},{8,9},{9,8},{10,11... | collective-permute-start | bytes 6291464 | tf_op jit(solution)/shard_map/ppermute | solution.py:234
  292.7 28.8 %collective-permute-start.45 = (bf16[256,2304]{1,0:T(8,128)(2,1)S(1)}, bf16[256,2304]{1,0:T(8,128)(2,1)S(1)}, u32[]{:S(2)}, u32[]{:S(2)}) collective-permute-start(bf16[256,2304]{1,0:T(8,128)(2,1)S(1)} %add_convert_fusion.4), channel_id=1, source_target_pairs={{0,8},{8,16},{16,24},{24,28},{28,20},{20,12},{12,4},{4,0},{1,9},{9... | collective-permute-start | bytes 3538952 | tf_op jit(solution)/shard_map/ppermute | solution.py:100
  294.0 29.2 %collective-permute-start.44 = (bf16[256,2304]{1,0:T(8,128)(2,1)S(1)}, bf16[256,2304]{1,0:T(8,128)(2,1)S(1)}, u32[]{:S(2)}, u32[]{:S(2)}) collective-permute-start(bf16[256,2304]{1,0:T(8,128)(2,1)S(1)} %add_convert_fusion.3), channel_id=1, source_target_pairs={{8,0},{16,8},{24,16},{28,24},{20,28},{12,20},{4,12},{0,4},{9,1},{1... | collective-permute-start | bytes 3538952 | tf_op jit(solution)/shard_map/ppermute | solution.py:103
  299.0 35.2 %collective-permute-start.41 = (bf16[256,2048]{1,0:T(8,128)(2,1)S(1)}, bf16[256,2048]{1,0:T(8,128)(2,1)S(1)}, u32[]{:S(2)}, u32[]{:S(2)}) collective-permute-start(bf16[256,2048]{1,0:T(8,128)(2,1)S(1)} %add_convert_fusion.7), channel_id=1, source_target_pairs={{0,2},{1,3},{2,0},{3,1},{4,6},{5,7},{6,4},{7,5},{8,10},{9,11},{10,... | collective-permute-start | bytes 3145736 | tf_op jit(solution)/shard_map/ppermute | solution.py:234
  310.8 21.2 %collective-permute-start.42 = (bf16[128,1920]{1,0:T(8,128)(2,1)S(1)}, bf16[128,1920]{1,0:T(8,128)(2,1)S(1)}, u32[]{:S(2)}, u32[]{:S(2)}) collective-permute-start(bf16[128,1920]{1,0:T(8,128)(2,1)S(1)} %get-tuple-element.350), channel_id=1, source_target_pairs={{0,8},{8,16},{16,24},{24,28},{28,20},{20,12},{12,4},{4,0},{1,9},{9... | collective-permute-start | bytes 1474568 | tf_op jit(solution)/shard_map/ppermute | solution.py:100
  312.2 21.2 %collective-permute-start.43 = (bf16[128,1920]{1,0:T(8,128)(2,1)S(1)}, bf16[128,1920]{1,0:T(8,128)(2,1)S(1)}, u32[]{:S(2)}, u32[]{:S(2)}) collective-permute-start(bf16[128,1920]{1,0:T(8,128)(2,1)S(1)} %get-tuple-element.351), channel_id=1, source_target_pairs={{8,0},{16,8},{24,16},{28,24},{20,28},{12,20},{4,12},{0,4},{9,1},{1... | collective-permute-start | bytes 1474568 | tf_op jit(solution)/shard_map/ppermute | solution.py:103
  321.8 34.7 %collective-permute-start.47 = (bf16[256,2304]{1,0:T(8,128)(2,1)S(1)}, bf16[256,2304]{1,0:T(8,128)(2,1)}, u32[]{:S(2)}, u32[]{:S(2)}) collective-permute-start(bf16[256,2304]{1,0:T(8,128)(2,1)S(1)} %add_convert_fusion.2), channel_id=1, source_target_pairs={{0,8},{8,16},{16,24},{24,28},{28,20},{20,12},{12,4},{4,0},{1,9},{9... | collective-permute-start | bytes 3538952 | tf_op jit(solution)/shard_map/ppermute | solution.py:100
  323.5 34.1 %collective-permute-start.48 = (bf16[256,2304]{1,0:T(8,128)(2,1)S(1)}, bf16[256,2304]{1,0:T(8,128)(2,1)}, u32[]{:S(2)}, u32[]{:S(2)}) collective-permute-start(bf16[256,2304]{1,0:T(8,128)(2,1)S(1)} %add_convert_fusion.1), channel_id=1, source_target_pairs={{8,0},{16,8},{24,16},{28,24},{20,28},{12,20},{4,12},{0,4},{9,1},{1... | collective-permute-start | bytes 3538952 | tf_op jit(solution)/shard_map/ppermute | solution.py:103
  337.5 25.6 %collective-permute-start.46 = (bf16[256,2048]{1,0:T(8,128)(2,1)S(1)}, bf16[256,2048]{1,0:T(8,128)(2,1)S(1)}, u32[]{:S(2)}, u32[]{:S(2)}) collective-permute-start(bf16[256,2048]{1,0:T(8,128)(2,1)S(1)} %get-tuple-element.369.refs_0_.refs_1_), channel_id=1, source_target_pairs={{0,2},{1,3},{2,0},{3,1},{4,6},{5,7},{6,4},{7,5},{8,10},{9,11},{10,... | collective-permute-start | bytes 3145736 | tf_op jit(solution)/shard_map/ppermute | solution.py:234
  363.1 26.1 %collective-permute-start.54 = (bf16[256,1920]{1,0:T(8,128)(2,1)S(1)}, bf16[256,1920]{1,0:T(8,128)(2,1)S(1)}, u32[]{:S(2)}, u32[]{:S(2)}) collective-permute-start(bf16[256,1920]{1,0:T(8,128)(2,1)S(1)} %get-tuple-element.360), channel_id=1, source_target_pairs={{0,8},{8,16},{16,24},{24,28},{28,20},{20,12},{12,4},{4,0},{1,9},{9... | collective-permute-start | bytes 2949128 | tf_op jit(solution)/shard_map/ppermute | solution.py:100
  364.2 26.4 %collective-permute-start.53 = (bf16[256,1920]{1,0:T(8,128)(2,1)S(1)}, bf16[256,1920]{1,0:T(8,128)(2,1)S(1)}, u32[]{:S(2)}, u32[]{:S(2)}) collective-permute-start(bf16[256,1920]{1,0:T(8,128)(2,1)S(1)} %get-tuple-element.375), channel_id=1, source_target_pairs={{8,0},{16,8},{24,16},{28,24},{20,28},{12,20},{4,12},{0,4},{9,1},{1... | collective-permute-start | bytes 2949128 | tf_op jit(solution)/shard_map/ppermute | solution.py:103
  365.1 27.8 %collective-permute-start.51 = (bf16[256,2304]{1,0:T(8,128)(2,1)S(1)}, bf16[256,2304]{1,0:T(8,128)(2,1)S(1)}, u32[]{:S(2)}, u32[]{:S(2)}) collective-permute-start(bf16[256,2304]{1,0:T(8,128)(2,1)S(1)} %add_convert_fusion.refs_0_), channel_id=1, source_target_pairs={{0,2},{1,3},{2,0},{3,1},{4,6},{5,7},{6,4},{7,5},{8,10},{9,11},{10,... | collective-permute-start | bytes 3538952 | tf_op jit(solution)/shard_map/ppermute | solution.py:234
  366.6 26.3 %collective-permute-start.52 = (bf16[256,2304]{1,0:T(8,128)(2,1)S(1)}, bf16[256,2304]{1,0:T(8,128)(2,1)S(1)}, u32[]{:S(2)}, u32[]{:S(2)}) collective-permute-start(bf16[256,2304]{1,0:T(8,128)(2,1)S(1)} %add_convert_fusion.refs_0_), channel_id=1, source_target_pairs={{0,1},{1,0},{2,3},{3,2},{4,5},{5,4},{6,7},{7,6},{8,9},{9,8},{10,11... | collective-permute-start | bytes 3538952 | tf_op jit(solution)/shard_map/ppermute | solution.py:234
  389.4 24.2 %collective-permute-start.59 = (bf16[256,1920]{1,0:T(8,128)(2,1)S(1)}, bf16[256,1920]{1,0:T(8,128)(2,1)S(1)}, u32[]{:S(2)}, u32[]{:S(2)}) collective-permute-start(bf16[256,1920]{1,0:T(8,128)(2,1)S(1)} %add_convert_fusion.13), channel_id=1, source_target_pairs={{0,8},{8,16},{16,24},{24,28},{28,20},{20,12},{12,4},{4,0},{1,9},{9... | collective-permute-start | bytes 2949128 | tf_op jit(solution)/shard_map/ppermute | solution.py:100
  390.8 23.9 %collective-permute-start.58 = (bf16[256,1920]{1,0:T(8,128)(2,1)S(1)}, bf16[256,1920]{1,0:T(8,128)(2,1)S(1)}, u32[]{:S(2)}, u32[]{:S(2)}) collective-permute-start(bf16[256,1920]{1,0:T(8,128)(2,1)S(1)} %add_convert_fusion.12), channel_id=1, source_target_pairs={{8,0},{16,8},{24,16},{28,24},{20,28},{12,20},{4,12},{0,4},{9,1},{1... | collective-permute-start | bytes 2949128 | tf_op jit(solution)/shard_map/ppermute | solution.py:103
  392.9 22.1 %collective-permute-start.57 = (bf16[256,2304]{1,0:T(8,128)(2,1)S(1)}, bf16[256,2304]{1,0:T(8,128)(2,1)S(1)}, u32[]{:S(2)}, u32[]{:S(2)}) collective-permute-start(bf16[256,2304]{1,0:T(8,128)(2,1)S(1)} %collective-permute-done.51.refs_1_), channel_id=1, source_target_pairs={{0,1},{1,0},{2,3},{3,2},{4,5},{5,4},{6,7},{7,6},{8,9},{9,8},{10,11... | collective-permute-start | bytes 3538952 | tf_op jit(solution)/shard_map/ppermute | solution.py:234
  392.9 29.5 %collective-permute-start.64 = (bf16[256,2048]{1,0:T(8,128)(2,1)}, bf16[256,2048]{1,0:T(8,128)(2,1)S(1)}, u32[]{:S(2)}, u32[]{:S(2)}) collective-permute-start(bf16[256,2048]{1,0:T(8,128)(2,1)} %add_convert_fusion.6), channel_id=1, source_target_pairs={{0,2},{1,3},{2,0},{3,1},{4,6},{5,7},{6,4},{7,5},{8,10},{9,11},{10,... | collective-permute-start | bytes 3145736 | tf_op jit(solution)/shard_map/ppermute | solution.py:234
  422.5 24.6 %collective-permute-start.62 = (bf16[256,1920]{1,0:T(8,128)(2,1)S(1)}, bf16[256,1920]{1,0:T(8,128)(2,1)S(1)}, u32[]{:S(2)}, u32[]{:S(2)}) collective-permute-start(bf16[256,1920]{1,0:T(8,128)(2,1)S(1)} %add_convert_fusion.11), channel_id=1, source_target_pairs={{0,8},{8,16},{16,24},{24,28},{28,20},{20,12},{12,4},{4,0},{1,9},{9... | collective-permute-start | bytes 2949128 | tf_op jit(solution)/shard_map/ppermute | solution.py:100
  423.7 24.8 %collective-permute-start.63 = (bf16[256,1920]{1,0:T(8,128)(2,1)S(1)}, bf16[256,1920]{1,0:T(8,128)(2,1)S(1)}, u32[]{:S(2)}, u32[]{:S(2)}) collective-permute-start(bf16[256,1920]{1,0:T(8,128)(2,1)S(1)} %add_convert_fusion.10), channel_id=1, source_target_pairs={{8,0},{16,8},{24,16},{28,24},{20,28},{12,20},{4,12},{0,4},{9,1},{1... | collective-permute-start | bytes 2949128 | tf_op jit(solution)/shard_map/ppermute | solution.py:103
  424.8 35.3 %collective-permute-start.60 = (bf16[272,1152]{1,0:T(8,128)(2,1)S(1)}, bf16[272,1152]{1,0:T(8,128)(2,1)S(1)}, u32[]{:S(2)}, u32[]{:S(2)}) collective-permute-start(bf16[272,1152]{1,0:T(8,128)(2,1)S(1)} %get-tuple-element.404), channel_id=1, source_target_pairs={{0,8},{8,16},{16,24},{24,28},{28,20},{20,12},{12,4},{4,0},{1,9},{9... | collective-permute-start | bytes 1880072 | tf_op jit(solution)/shard_map/ppermute | solution.py:100
  425.9 35.2 %collective-permute-start.61 = (bf16[272,1152]{1,0:T(8,128)(2,1)S(1)}, bf16[272,1152]{1,0:T(8,128)(2,1)S(1)}, u32[]{:S(2)}, u32[]{:S(2)}) collective-permute-start(bf16[272,1152]{1,0:T(8,128)(2,1)S(1)} %get-tuple-element.405), channel_id=1, source_target_pairs={{8,0},{16,8},{24,16},{28,24},{20,28},{12,20},{4,12},{0,4},{9,1},{1... | collective-permute-start | bytes 1880072 | tf_op jit(solution)/shard_map/ppermute | solution.py:103
  427.2 39.6 %collective-permute-start.66 = (bf16[256,2048]{1,0:T(8,128)(2,1)S(1)}, bf16[256,2048]{1,0:T(8,128)(2,1)S(1)}, u32[]{:S(2)}, u32[]{:S(2)}) collective-permute-start(bf16[256,2048]{1,0:T(8,128)(2,1)S(1)} %add_convert_fusion.5), channel_id=1, source_target_pairs={{0,2},{1,3},{2,0},{3,1},{4,6},{5,7},{6,4},{7,5},{8,10},{9,11},{10,... | collective-permute-start | bytes 3145736 | tf_op jit(solution)/shard_map/ppermute | solution.py:234
  448.8 17.5 %collective-permute-start.67 = (bf16[256,1920]{1,0:T(8,128)(2,1)S(1)}, bf16[256,1920]{1,0:T(8,128)(2,1)S(1)}, u32[]{:S(2)}, u32[]{:S(2)}) collective-permute-start(bf16[256,1920]{1,0:T(8,128)(2,1)S(1)} %add_convert_fusion.9.refs_4_), channel_id=1, source_target_pairs={{0,1},{1,0},{2,3},{3,2},{4,5},{5,4},{6,7},{7,6},{8,9},{9,8},{10,11... | collective-permute-start | bytes 2949128 | tf_op jit(solution)/shard_map/ppermute | solution.py:234
  466.3 22.2 %collective-permute-start.76 = (bf16[256,1920]{1,0:T(8,128)(2,1)S(1)}, bf16[256,1920]{1,0:T(8,128)(2,1)S(1)}, u32[]{:S(2)}, u32[]{:S(2)}) collective-permute-start(bf16[256,1920]{1,0:T(8,128)(2,1)S(1)} %add_convert_fusion.9.refs_4_), channel_id=1, source_target_pairs={{0,2},{1,3},{2,0},{3,1},{4,6},{5,7},{6,4},{7,5},{8,10},{9,11},{10,... | collective-permute-start | bytes 2949128 | tf_op jit(solution)/shard_map/ppermute | solution.py:234
  (88 other events, 1757.1 us)

commit v7 on v6

--- a/solution.py
+++ b/solution.py
@@ -11,7 +11,7 @@
 HD = 64
 KVH = 4
 EPS = 1e-05
-TOP = 16
+TOP = 8
 BF = jnp.bfloat16
 F32 = jnp.float32
 NEG = -1e30

time: 519 us -> 514 us (level)
  transfers between devices with their start and end apart: 84 -> 84, of which waited for: 47 -> 47; matrix products, arithmetic and copies ran while one was open for 2% -> 3% of each run, Pallas kernels for 33% -> 33%
where the time goes in v7:
time: 514 us; the launch traced here: 507 us
  waiting for transfers between devices  235 us (46%)
  Pallas kernels  174 us (34%)
  starting transfers between devices  72.5 us (14%)
  other arithmetic  12.8 us (2%)
  local copies, waits for them, and re-layouts  9.85 us (2%)
    ppermute x26, waiting for transfers between devices, go_up(): return lax.ppermute(block, 'dp', self.up)  182 us
    pallas_call x5, Pallas kernels, kernel_call(): pl.pallas_call(body, out_shape=tuple((jax.ShapeDtypeStruct(s, d) for s, d...  59.5 us
    pallas_call x2, Pallas kernels, mlp_chunk(): pl.pallas_call(body, grid=(4,), out_shape=(half, half, half, half, pltpu....  53 us
    pallas_call x3, Pallas kernels, weight_terms(): pl.pallas_call(body, grid=(n_slots // group,), out_shape=(jax.ShapeDtypeS...  29.8 us
    ppermute x26, waiting for transfers between devices, go_down(): return lax.ppermute(block, 'dp', self.down)  29.2 us
    ppermute x26, starting transfers between devices, go_up(): return lax.ppermute(block, 'dp', self.up)  28.9 us
    ppermute x26, starting transfers between devices, go_down(): return lax.ppermute(block, 'dp', self.down)  26.7 us
    ppermute x32, waiting for transfers between devices, swap(): return lax.ppermute(block, 'seq', [(i, i ^ distance) for i in range(4)])  23.7 us
  transfers between devices with their start and end apart: 84, of which 47 were waited for; matrix products, arithmetic and copies ran while one was open for 3% of the time, Pallas kernels for 33%

profile of v7, /device:TPU:0, one launch (start us, length us, event | category | flops | bytes accessed | tf_op | source)
XLA Modules:
  0.0 506.6 jit_solution(13181441385783628764)
XLA Ops:
  0.7 2.5 pack_heads.1.refs_4_
  3.2 2.9 collective-permute-start
  8.6 2.4 permute_features.2.refs_0_.inputs_ref
  11.0 2.0 collective-permute-start.2
  13.2 3.1 pack_mlp.1
  16.3 5.2 %collective-permute-done.1.refs_5_ = bf16[264,1152]{1,0:T(8,128)(2,1)S(1)} collective-permute-done((bf16[264,1152]{1,0:T(8,128)(2,1)}, bf16[264,1152]{1,0:T(8,128)(2,1)S(1)}, u32[]{:S(2)}, u32[]{:S(2)}) %collective-permute-start.1) | collective-permute-done | bytes 608288 | tf_op jit(solution)/shard_map/ppermute | solution.py:100
  24.2 2.4 permute_features.3.refs_4_.cot_ref
  26.7 9.2 %collective-permute-done.4.refs_6_ = bf16[264,1152]{1,0:T(8,128)(2,1)S(1)} collective-permute-done((bf16[264,1152]{1,0:T(8,128)(2,1)S(1)}, bf16[264,1152]{1,0:T(8,128)(2,1)S(1)}, u32[]{:S(2)}, u32[]{:S(2)}) %collective-permute-start.4) | collective-permute-done | bytes 608288 | tf_op jit(solution)/shard_map/ppermute | solution.py:100
  38.5 14.0 %collective-permute-done.7.refs_7_ = bf16[264,1152]{1,0:T(8,128)(2,1)S(1)} collective-permute-done((bf16[264,1152]{1,0:T(8,128)(2,1)S(1)}, bf16[264,1152]{1,0:T(8,128)(2,1)S(1)}, u32[]{:S(2)}, u32[]{:S(2)}) %collective-permute-start.7) | collective-permute-done | bytes 608288 | tf_op jit(solution)/shard_map/ppermute | solution.py:100
  54.7 7.7 %collective-permute-done.10.refs_12_ = bf16[128,1152]{1,0:T(8,128)(2,1)S(1)} collective-permute-done((bf16[128,1152]{1,0:T(8,128)(2,1)S(1)}, bf16[128,1152]{1,0:T(8,128)(2,1)S(1)}, u32[]{:S(2)}, u32[]{:S(2)}) %collective-permute-start.10) | collective-permute-done | bytes 294944 | tf_op jit(solution)/shard_map/ppermute | solution.py:103
  70.9 28.7 %attention_forward.1 = (bf16[1024,2048]{1,0:T(8,128)(2,1)S(1)}, bf16[512,1024]{1,0:T(8,128)(2,1)S(1)}, bf16[1024,128]{1,0:T(8,128)(2,1)S(1)}, bf16[192,1024]{1,0...) custom-call(s32[4]{0:T(128)S(1)} %fusion.2.places_ref, ...), custom_call_target="tpu_custom_call" | custom-call | flops 1000 | bytes 1000 | tf_op jit(solution)/shard_map/attention_forward/pallas_call | solution.py:58
  100.8 9.1 %collective-permute-done.12.refs_9_ = bf16[256,1920]{1,0:T(8,128)(2,1)S(1)} collective-permute-done((bf16[256,1920]{1,0:T(8,128)(2,1)}, bf16[256,1920]{1,0:T(8,128)(2,1)S(1)}, u32[]{:S(2)}, u32[]{:S(2)}) %collective-permute-start.12) | collective-permute-done | bytes 983072 | tf_op jit(solution)/shard_map/ppermute | solution.py:100
  113.3 2.1 collective-permute-done.16.came_ref
  117.3 22.4 %collective-permute-done.19.refs_10_ = bf16[256,2304]{1,0:T(8,128)(2,1)S(1)} collective-permute-done((bf16[256,2304]{1,0:T(8,128)(2,1)S(1)}, bf16[256,2304]{1,0:T(8,128)(2,1)S(1)}, u32[]{:S(2)}, u32[]{:S(2)}) %collective-permute-start.19) | collective-permute-done | bytes 1179680 | tf_op jit(solution)/shard_map/ppermute | solution.py:100
  145.7 21.3 %collective-permute-done.22.refs_11_ = bf16[256,2304]{1,0:T(8,128)(2,1)S(1)} collective-permute-done((bf16[256,2304]{1,0:T(8,128)(2,1)S(1)}, bf16[256,2304]{1,0:T(8,128)(2,1)S(1)}, u32[]{:S(2)}, u32[]{:S(2)}) %collective-permute-start.22) | collective-permute-done | bytes 1179680 | tf_op jit(solution)/shard_map/ppermute | solution.py:100
  171.0 10.7 %collective-permute-done.25.refs_15_ = bf16[128,2304]{1,0:T(8,128)(2,1)S(1)} collective-permute-done((bf16[128,2304]{1,0:T(8,128)(2,1)S(1)}, bf16[128,2304]{1,0:T(8,128)(2,1)S(1)}, u32[]{:S(2)}, u32[]{:S(2)}) %collective-permute-start.25) | collective-permute-done | bytes 589856 | tf_op jit(solution)/shard_map/ppermute | solution.py:100
  185.5 25.1 %mlp_chunk.2 = (bf16[512,2048]{1,0:T(8,128)(2,1)}, bf16[512,2048]{1,0:T(8,128)(2,1)}, bf16[512,2048]{1,0:T(8,128)(2,1)}, bf16[512,2048]{1,0:T(8,128)(2,1)}, bf16[1024,2304]{1,0:T(8,128)(2,1)}) custom-call(bf16[256,2048]{1,0:T(8,128)(2,1)S(1)} %get-tuple-element.289.refs_0_, bf16[256,2048]{1,0:T(8,128)(2,1)S(1)} %collective-permute-done.20.refs_1_, ...), custom_call_target="tpu_custom_call" | custom-call | flops 1000 | bytes 1000 | tf_op jit(solution)/shard_map/mlp_chunk/pallas_call | solution.py:676
  212.7 2.3 copy-done.2
  215.0 11.4 %weight_terms.3 = (bf16[2048,2304]{1,0:T(8,128)(2,1)S(1)}, bf16[128,2304]{1,0:T(8,128)(2,1)S(1)}, bf16[128,2304]{1,0:T(8,128)(2,1)S(1)}) custom-call(bf16[256,2048]{1,0:T(8,128)(2,1)S(1)} %get-tuple-element.289.refs_0_, bf16[256,2048]{1,0:T(8,128)(2,1)S(1)} %collective-permute-done.20.refs_1_, bf16[256,2048]{1,0:T(8,128)(2,1)S(1)} %collective-permute-done.23.refs_2_, ...), custom_call_target="tpu_custom_call" | custom-call | flops 1000 | bytes 1000 | tf_op jit(solution)/shard_map/weight_terms/pallas_call | solution.py:770
  228.5 6.8 %collective-permute-done.30.refs_11_ = bf16[256,1920]{1,0:T(8,128)(2,1)S(1)} collective-permute-done((bf16[256,1920]{1,0:T(8,128)(2,1)S(1)}, bf16[256,1920]{1,0:T(8,128)(2,1)S(1)}, u32[]{:S(2)}, u32[]{:S(2)}) %collective-permute-start.30) | collective-permute-done | bytes 983072 | tf_op jit(solution)/shard_map/ppermute | solution.py:100
  238.9 9.0 %collective-permute-done.35.up_ref = bf16[128,2304]{1,0:T(8,128)(2,1)S(1)} collective-permute-done((bf16[128,2304]{1,0:T(8,128)(2,1)S(1)}, bf16[128,2304]{1,0:T(8,128)(2,1)S(1)}, u32[]{:S(2)}, u32[]{:S(2)}) %collective-permute-start.35) | collective-permute-done | bytes 589856 | tf_op jit(solution)/shard_map/ppermute | solution.py:100
  249.4 2.2 ring_add.3
  251.6 2.2 collective-permute-done.33.refs_15_
  258.0 28.0 %mlp_chunk.3 = (bf16[512,2048]{1,0:T(8,128)(2,1)}, bf16[512,2048]{1,0:T(8,128)(2,1)}, bf16[512,2048]{1,0:T(8,128)(2,1)}, bf16[512,2048]{1,0:T(8,128)(2,1)}, bf16[1024,1920]{1,0:T(8,128)(2,1)}) custom-call(bf16[256,2048]{1,0:T(8,128)(2,1)S(1)} %get-tuple-element.289.refs_0_, bf16[256,2048]{1,0:T(8,128)(2,1)S(1)} %collective-permute-done.20.refs_1_, ...), custom_call_target="tpu_custom_call" | custom-call | flops 1000 | bytes 1000 | tf_op jit(solution)/shard_map/mlp_chunk/pallas_call | solution.py:676
  286.0 1.7 add_convert_fusion.4
  287.8 1.7 add_convert_fusion.3
  292.1 3.8 collective-permute-done.40.came_ref
  298.8 10.3 %weight_terms.4 = (bf16[2048,1920]{1,0:T(8,128)(2,1)S(1)}, bf16[128,1920]{1,0:T(8,128)(2,1)S(1)}, bf16[128,1920]{1,0:T(8,128)(2,1)S(1)}) custom-call(bf16[256,2048]{1,0:T(8,128)(2,1)S(1)} %get-tuple-element.289.refs_0_, bf16[256,2048]{1,0:T(8,128)(2,1)S(1)} %collective-permute-done.20.refs_1_, bf16[256,2048]{1,0:T(8,128)(2,1)S(1)} %collective-permute-done.23.refs_2_, ...), custom_call_target="tpu_custom_call" | custom-call | flops 1000 | bytes 1000 | tf_op jit(solution)/shard_map/weight_terms/pallas_call | solution.py:770
  311.1 7.8 %collective-permute-done.45 = bf16[256,2304]{1,0:T(8,128)(2,1)} collective-permute-done((bf16[256,2304]{1,0:T(8,128)(2,1)S(1)}, bf16[256,2304]{1,0:T(8,128)(2,1)}, u32[]{:S(2)}, u32[]{:S(2)}) %collective-permute-start.45) | collective-permute-done | bytes 1179680 | tf_op jit(solution)/shard_map/ppermute | solution.py:100
  323.3 6.0 %collective-permute-done.42.up_ref = bf16[128,1920]{1,0:T(8,128)(2,1)S(1)} collective-permute-done((bf16[128,1920]{1,0:T(8,128)(2,1)S(1)}, bf16[128,1920]{1,0:T(8,128)(2,1)S(1)}, u32[]{:S(2)}, u32[]{:S(2)}) %collective-permute-start.42) | collective-permute-done | bytes 491552 | tf_op jit(solution)/shard_map/ppermute | solution.py:100
  331.4 2.1 second_norm_back.1
  336.6 17.2 %collective-permute-done.47 = bf16[256,2304]{1,0:T(8,128)(2,1)S(1)} collective-permute-done((bf16[256,2304]{1,0:T(8,128)(2,1)S(1)}, bf16[256,2304]{1,0:T(8,128)(2,1)S(1)}, u32[]{:S(2)}, u32[]{:S(2)}) %collective-permute-start.47) | collective-permute-done | bytes 1179680 | tf_op jit(solution)/shard_map/ppermute | solution.py:100
  355.1 4.1 collective-permute-done.46.refs_1_.refs_2_
  362.9 22.4 %attention_backward.1 = (bf16[1024,512]{1,0:T(8,128)(2,1)S(1)}, bf16[1024,128]{1,0:T(8,128)(2,1)S(1)}) custom-call(s32[4]{0:T(128)S(1)} %fusion.2.places_ref, s32[6]{0:T(128)S(1)} %bitcast.12, s32[1]{0:T(128)S(6)} %copy.42.live_ref, f32[32,1024]{1,0:T(8,128)S(1)} %copy-done.30, f32[32,1024]{1,0:T(8,128)S(1)} %get-tuple-element.249.sin_ref, ...), custom_call_target="tpu_custom_call" | custom-call | flops 1000 | bytes 1000 | tf_op jit(solution)/shard_map/attention_backward/pallas_call | solution.py:58
  390.6 8.0 %heads_back.1 = (bf16[512,2048]{1,0:T(8,128)(2,1)S(1)}, bf16[512,2048]{1,0:T(8,128)(2,1)S(1)}, f32[8,2048]{1,0:T(8,128)S(1)}) custom-call(bf16[1024,512]{1,0:T(8,128)(2,1)S(1)} %get-tuple-element.373.grad_q_ref.refs_5_, bf16[1024,128]{1,0:T(8,128)(2,1)S(1)} %get-tuple-element.374.grad_kv_ref.refs_6_, bf16[256,2048]{1,0:T(8,128)(2,1)S(1)} %copy-done.1, ...), custom_call_target="tpu_custom_call" | custom-call | flops 1000 | bytes 1000 | tf_op jit(solution)/shard_map/heads_back/pallas_call | solution.py:612
  398.7 8.1 %weight_terms.5 = (bf16[2112,1152]{1,0:T(8,128)(2,1)S(1)}, bf16[136,1152]{1,0:T(8,128)(2,1)S(1)}, bf16[128,1152]{1,0:T(8,128)(2,1)S(1)}) custom-call(bf16[1024,2048]{1,0:T(8,128)(2,1)} %copy-done.21, bf16[256,2048]{1,0:T(8,128)(2,1)S(1)} %get-tuple-element.369.refs_0_.refs_1_, bf16[256,2048]{1,0:T(8,128)(2,1)S(1)} %collective-permute-done.46.refs_1_.refs_2_, ...), custom_call_target="tpu_custom_call" | custom-call | flops 1000 | bytes 1000 | tf_op jit(solution)/shard_map/weight_terms/pallas_call | solution.py:770
  407.8 2.0 collective-permute-done.59
  411.1 7.2 %collective-permute-done.56.down_ref = bf16[128,1152]{1,0:T(8,128)(2,1)S(1)} collective-permute-done((bf16[128,1152]{1,0:T(8,128)(2,1)S(1)}, bf16[128,1152]{1,0:T(8,128)(2,1)S(1)}, u32[]{:S(2)}, u32[]{:S(2)}) %collective-permute-start.56) | collective-permute-done | bytes 294944 | tf_op jit(solution)/shard_map/ppermute | solution.py:103
  423.9 19.4 %collective-permute-done.62 = bf16[256,1920]{1,0:T(8,128)(2,1)S(1)} collective-permute-done((bf16[256,1920]{1,0:T(8,128)(2,1)S(1)}, bf16[256,1920]{1,0:T(8,128)(2,1)S(1)}, u32[]{:S(2)}, u32[]{:S(2)}) %collective-permute-start.62) | collective-permute-done | bytes 983072 | tf_op jit(solution)/shard_map/ppermute | solution.py:100
  444.6 11.2 %collective-permute-done.60 = bf16[264,1152]{1,0:T(8,128)(2,1)S(1)} collective-permute-done((bf16[264,1152]{1,0:T(8,128)(2,1)S(1)}, bf16[264,1152]{1,0:T(8,128)(2,1)S(1)}, u32[]{:S(2)}, u32[]{:S(2)}) %collective-permute-start.60) | collective-permute-done | bytes 608288 | tf_op jit(solution)/shard_map/ppermute | solution.py:100
  459.7 1.8 layer_output.1
  463.2 2.9 first_norm_back.1
  470.1 3.2 collective-permute-done.72
  476.3 3.7 collective-permute-done.70
  481.0 2.7 collective-permute-done.76.refs_5_
  486.3 7.1 %unpack_mlp.1 = (f32[256,5632]{1,0:T(8,128)}, f32[256,5632]{1,0:T(8,128)}, f32[5632,256]{1,0:T(8,128)}) custom-call(s32[4]{0:T(128)S(1)} %fusion.2.places_ref, bf16[256,2304]{1,0:T(8,128)(2,1)S(1)} %add_convert_fusion.refs_0_, bf16[256,2304]{1,0:T(8,128)(2,1)S(1)} %collective-permute-done.51.refs_1_, bf16[256,2304]{1,0:T(8,128)(2,1)S(1)} %collective-permute-done.52.refs_2_, ...), custom_call_target="tpu_custom_call" | custom-call | flops 1000 | bytes 1000 | tf_op jit(solution)/shard_map/unpack_mlp/pallas_call | solution.py:964
  493.4 6.4 %collective-permute-done.78.refs_3_ = bf16[128,1152]{1,0:T(8,128)(2,1)S(1)} collective-permute-done((bf16[128,1152]{1,0:T(8,128)(2,1)S(1)}, bf16[128,1152]{1,0:T(8,128)(2,1)S(1)}, u32[]{:S(2)}, u32[]{:S(2)}) %collective-permute-start.78) | collective-permute-done | bytes 294944 | tf_op jit(solution)/shard_map/ppermute | solution.py:234
  502.3 3.6 unpack_heads.1
  (293 shorter events, 106.7 us)
Async XLA Ops:
  3.2 18.7 %collective-permute-start = (bf16[264,1152]{1,0:T(8,128)(2,1)}, bf16[264,1152]{1,0:T(8,128)(2,1)S(1)}, u32[]{:S(2)}, u32[]{:S(2)}) collective-permute-start(bf16[264,1152]{1,0:T(8,128)(2,1)} %pack_heads.1.refs_4_), channel_id=1, source_target_pairs={{8,0},{16,8},{24,16},{28,24},{20,28},{12,20},{4,12},{0,4},{9,1},{1... | collective-permute-start | bytes 1824776 | tf_op jit(solution)/shard_map/ppermute | solution.py:103
  11.0 25.3 %collective-permute-start.2 = (bf16[256,2048]{1,0:T(8,128)(2,1)}, bf16[256,2048]{1,0:T(8,128)(2,1)}, u32[]{:S(2)}, u32[]{:S(2)}) collective-permute-start(bf16[256,2048]{1,0:T(8,128)(2,1)} %permute_features.2.refs_0_.inputs_ref), channel_id=1, source_target_pairs={{0,2},{1,3},{2,0},{3,1},{4,6},{5,7},{6,4},{7,5},{8,10},{9,11},{10,... | collective-permute-start | bytes 3145736 | tf_op jit(solution)/shard_map/ppermute | solution.py:234
  13.0 49.4 %collective-permute-start.5 = (bf16[256,2048]{1,0:T(8,128)(2,1)}, bf16[256,2048]{1,0:T(8,128)(2,1)}, u32[]{:S(2)}, u32[]{:S(2)}) collective-permute-start(bf16[256,2048]{1,0:T(8,128)(2,1)} %permute_features.2.refs_0_.inputs_ref), channel_id=1, source_target_pairs={{0,1},{1,0},{2,3},{3,2},{4,5},{5,4},{6,7},{7,6},{8,9},{9,8},{10,11... | collective-permute-start | bytes 3145736 | tf_op jit(solution)/shard_map/ppermute | solution.py:234
  36.3 26.1 %collective-permute-start.6 = (bf16[256,2048]{1,0:T(8,128)(2,1)}, bf16[256,2048]{1,0:T(8,128)(2,1)S(1)}, u32[]{:S(2)}, u32[]{:S(2)}) collective-permute-start(bf16[256,2048]{1,0:T(8,128)(2,1)} %collective-permute-done.2.refs_1_), channel_id=1, source_target_pairs={{0,1},{1,0},{2,3},{3,2},{4,5},{5,4},{6,7},{7,6},{8,9},{9,8},{10,11... | collective-permute-start | bytes 3145736 | tf_op jit(solution)/shard_map/ppermute | solution.py:234
  62.5 38.3 %collective-permute-start.15 = (bf16[256,2304]{1,0:T(8,128)(2,1)S(1)}, bf16[256,2304]{1,0:T(8,128)(2,1)S(1)}, u32[]{:S(2)}, u32[]{:S(2)}) collective-permute-start(bf16[256,2304]{1,0:T(8,128)(2,1)S(1)} %copy-done.31), channel_id=1, source_target_pairs={{0,8},{8,16},{16,24},{24,28},{28,20},{20,12},{12,4},{4,0},{1,9},{9... | collective-permute-start | bytes 3538952 | tf_op jit(solution)/shard_map/ppermute | solution.py:100
  64.1 36.7 %collective-permute-start.14 = (bf16[256,2304]{1,0:T(8,128)(2,1)S(1)}, bf16[256,2304]{1,0:T(8,128)(2,1)S(1)}, u32[]{:S(2)}, u32[]{:S(2)}) collective-permute-start(bf16[256,2304]{1,0:T(8,128)(2,1)S(1)} %copy-done.31), channel_id=1, source_target_pairs={{8,0},{16,8},{24,16},{28,24},{20,28},{12,20},{4,12},{0,4},{9,1},{1... | collective-permute-start | bytes 3538952 | tf_op jit(solution)/shard_map/ppermute | solution.py:103
  64.5 46.7 %collective-permute-start.11 = (bf16[256,2048]{1,0:T(8,128)(2,1)}, bf16[256,2048]{1,0:T(8,128)(2,1)S(1)}, u32[]{:S(2)}, u32[]{:S(2)}) collective-permute-start(bf16[256,2048]{1,0:T(8,128)(2,1)} %permute_features.3.refs_4_.cot_ref), channel_id=1, source_target_pairs={{0,2},{1,3},{2,0},{3,1},{4,6},{5,7},{6,4},{7,5},{8,10},{9,11},{10,... | collective-permute-start | bytes 3145736 | tf_op jit(solution)/shard_map/ppermute | solution.py:234
  66.1 43.8 %collective-permute-start.12 = (bf16[256,1920]{1,0:T(8,128)(2,1)}, bf16[256,1920]{1,0:T(8,128)(2,1)S(1)}, u32[]{:S(2)}, u32[]{:S(2)}) collective-permute-start(bf16[256,1920]{1,0:T(8,128)(2,1)} %get-tuple-element.315.refs_8_), channel_id=1, source_target_pairs={{0,8},{8,16},{16,24},{24,28},{28,20},{20,12},{12,4},{4,0},{1,9},{9... | collective-permute-start | bytes 2949128 | tf_op jit(solution)/shard_map/ppermute | solution.py:100
  67.6 43.6 %collective-permute-start.13 = (bf16[256,1920]{1,0:T(8,128)(2,1)}, bf16[256,1920]{1,0:T(8,128)(2,1)S(1)}, u32[]{:S(2)}, u32[]{:S(2)}) collective-permute-start(bf16[256,1920]{1,0:T(8,128)(2,1)} %get-tuple-element.315.refs_8_), channel_id=1, source_target_pairs={{8,0},{16,8},{24,16},{28,24},{20,28},{12,20},{4,12},{0,4},{9,1},{1... | collective-permute-start | bytes 2949128 | tf_op jit(solution)/shard_map/ppermute | solution.py:103
  111.2 30.1 %collective-permute-start.18 = (bf16[256,2304]{1,0:T(8,128)(2,1)S(1)}, bf16[256,2304]{1,0:T(8,128)(2,1)S(1)}, u32[]{:S(2)}, u32[]{:S(2)}) collective-permute-start(bf16[256,2304]{1,0:T(8,128)(2,1)S(1)} %collective-permute-done.14.refs_12_), channel_id=1, source_target_pairs={{8,0},{16,8},{24,16},{28,24},{20,28},{12,20},{4,12},{0,4},{9,1},{1... | collective-permute-start | bytes 3538952 | tf_op jit(solution)/shard_map/ppermute | solution.py:103
  111.7 28.0 %collective-permute-start.19 = (bf16[256,2304]{1,0:T(8,128)(2,1)S(1)}, bf16[256,2304]{1,0:T(8,128)(2,1)S(1)}, u32[]{:S(2)}, u32[]{:S(2)}) collective-permute-start(bf16[256,2304]{1,0:T(8,128)(2,1)S(1)} %collective-permute-done.15.refs_9_), channel_id=1, source_target_pairs={{0,8},{8,16},{16,24},{24,28},{28,20},{20,12},{12,4},{4,0},{1,9},{9... | collective-permute-start | bytes 3538952 | tf_op jit(solution)/shard_map/ppermute | solution.py:100
  115.7 26.0 %collective-permute-start.17 = (bf16[256,2048]{1,0:T(8,128)(2,1)S(1)}, bf16[256,2048]{1,0:T(8,128)(2,1)S(1)}, u32[]{:S(2)}, u32[]{:S(2)}) collective-permute-start(bf16[256,2048]{1,0:T(8,128)(2,1)S(1)} %add_convert_fusion.8), channel_id=1, source_target_pairs={{0,2},{1,3},{2,0},{3,1},{4,6},{5,7},{6,4},{7,5},{8,10},{9,11},{10,... | collective-permute-start | bytes 3145736 | tf_op jit(solution)/shard_map/ppermute | solution.py:234
  139.8 27.2 %collective-permute-start.22 = (bf16[256,2304]{1,0:T(8,128)(2,1)S(1)}, bf16[256,2304]{1,0:T(8,128)(2,1)S(1)}, u32[]{:S(2)}, u32[]{:S(2)}) collective-permute-start(bf16[256,2304]{1,0:T(8,128)(2,1)S(1)} %collective-permute-done.19.refs_10_), channel_id=1, source_target_pairs={{0,8},{8,16},{16,24},{24,28},{28,20},{20,12},{12,4},{4,0},{1,9},{9... | collective-permute-start | bytes 3538952 | tf_op jit(solution)/shard_map/ppermute | solution.py:100
  141.3 26.9 %collective-permute-start.21 = (bf16[256,2304]{1,0:T(8,128)(2,1)S(1)}, bf16[256,2304]{1,0:T(8,128)(2,1)S(1)}, u32[]{:S(2)}, u32[]{:S(2)}) collective-permute-start(bf16[256,2304]{1,0:T(8,128)(2,1)S(1)} %collective-permute-done.18.refs_13_), channel_id=1, source_target_pairs={{8,0},{16,8},{24,16},{28,24},{20,28},{12,20},{4,12},{0,4},{9,1},{1... | collective-permute-start | bytes 3538952 | tf_op jit(solution)/shard_map/ppermute | solution.py:103
  143.0 27.3 %collective-permute-start.20 = (bf16[256,2048]{1,0:T(8,128)(2,1)S(1)}, bf16[256,2048]{1,0:T(8,128)(2,1)S(1)}, u32[]{:S(2)}, u32[]{:S(2)}) collective-permute-start(bf16[256,2048]{1,0:T(8,128)(2,1)S(1)} %get-tuple-element.289.refs_0_), channel_id=1, source_target_pairs={{0,2},{1,3},{2,0},{3,1},{4,6},{5,7},{6,4},{7,5},{8,10},{9,11},{10,... | collective-permute-start | bytes 3145736 | tf_op jit(solution)/shard_map/ppermute | solution.py:234
  183.0 27.5 %collective-permute-start.29 = (bf16[256,1920]{1,0:T(8,128)(2,1)S(1)}, bf16[256,1920]{1,0:T(8,128)(2,1)S(1)}, u32[]{:S(2)}, u32[]{:S(2)}) collective-permute-start(bf16[256,1920]{1,0:T(8,128)(2,1)S(1)} %collective-permute-done.12.refs_9_), channel_id=1, source_target_pairs={{0,8},{8,16},{16,24},{24,28},{28,20},{20,12},{12,4},{4,0},{1,9},{9... | collective-permute-start | bytes 2949128 | tf_op jit(solution)/shard_map/ppermute | solution.py:100
  184.5 27.6 %collective-permute-start.31 = (bf16[256,1920]{1,0:T(8,128)(2,1)S(1)}, bf16[256,1920]{1,0:T(8,128)(2,1)S(1)}, u32[]{:S(2)}, u32[]{:S(2)}) collective-permute-start(bf16[256,1920]{1,0:T(8,128)(2,1)S(1)} %collective-permute-done.13.refs_12_), channel_id=1, source_target_pairs={{8,0},{16,8},{24,16},{28,24},{20,28},{12,20},{4,12},{0,4},{9,1},{1... | collective-permute-start | bytes 2949128 | tf_op jit(solution)/shard_map/ppermute | solution.py:103
  210.6 24.7 %collective-permute-start.30 = (bf16[256,1920]{1,0:T(8,128)(2,1)S(1)}, bf16[256,1920]{1,0:T(8,128)(2,1)S(1)}, u32[]{:S(2)}, u32[]{:S(2)}) collective-permute-start(bf16[256,1920]{1,0:T(8,128)(2,1)S(1)} %collective-permute-done.29.refs_10_), channel_id=1, source_target_pairs={{0,8},{8,16},{16,24},{24,28},{28,20},{20,12},{12,4},{4,0},{1,9},{9... | collective-permute-start | bytes 2949128 | tf_op jit(solution)/shard_map/ppermute | solution.py:100
  212.1 24.7 %collective-permute-start.32 = (bf16[256,1920]{1,0:T(8,128)(2,1)S(1)}, bf16[256,1920]{1,0:T(8,128)(2,1)S(1)}, u32[]{:S(2)}, u32[]{:S(2)}) collective-permute-start(bf16[256,1920]{1,0:T(8,128)(2,1)S(1)} %collective-permute-done.31.refs_13_), channel_id=1, source_target_pairs={{8,0},{16,8},{24,16},{28,24},{20,28},{12,20},{4,12},{0,4},{9,1},{1... | collective-permute-start | bytes 2949128 | tf_op jit(solution)/shard_map/ppermute | solution.py:103
  226.4 21.5 %collective-permute-start.35 = (bf16[128,2304]{1,0:T(8,128)(2,1)S(1)}, bf16[128,2304]{1,0:T(8,128)(2,1)S(1)}, u32[]{:S(2)}, u32[]{:S(2)}) collective-permute-start(bf16[128,2304]{1,0:T(8,128)(2,1)S(1)} %get-tuple-element.306), channel_id=1, source_target_pairs={{0,8},{8,16},{16,24},{24,28},{28,20},{20,12},{12,4},{4,0},{1,9},{9... | collective-permute-start | bytes 1769480 | tf_op jit(solution)/shard_map/ppermute | solution.py:100
  227.9 21.5 %collective-permute-start.36 = (bf16[128,2304]{1,0:T(8,128)(2,1)S(1)}, bf16[128,2304]{1,0:T(8,128)(2,1)S(1)}, u32[]{:S(2)}, u32[]{:S(2)}) collective-permute-start(bf16[128,2304]{1,0:T(8,128)(2,1)S(1)} %get-tuple-element.307), channel_id=1, source_target_pairs={{8,0},{16,8},{24,16},{28,24},{20,28},{12,20},{4,12},{0,4},{9,1},{1... | collective-permute-start | bytes 1769480 | tf_op jit(solution)/shard_map/ppermute | solution.py:103
  236.8 17.0 %collective-permute-start.33 = (bf16[128,1920]{1,0:T(8,128)(2,1)S(1)}, bf16[128,1920]{1,0:T(8,128)(2,1)S(1)}, u32[]{:S(2)}, u32[]{:S(2)}) collective-permute-start(bf16[128,1920]{1,0:T(8,128)(2,1)S(1)} %slice.134), channel_id=1, source_target_pairs={{0,8},{8,16},{16,24},{24,28},{28,20},{20,12},{12,4},{4,0},{1,9},{9... | collective-permute-start | bytes 1474568 | tf_op jit(solution)/shard_map/ppermute | solution.py:100
  237.7 17.3 %collective-permute-start.34 = (bf16[128,1920]{1,0:T(8,128)(2,1)S(1)}, bf16[128,1920]{1,0:T(8,128)(2,1)S(1)}, u32[]{:S(2)}, u32[]{:S(2)}) collective-permute-start(bf16[128,1920]{1,0:T(8,128)(2,1)S(1)} %slice.135), channel_id=1, source_target_pairs={{8,0},{16,8},{24,16},{28,24},{20,28},{12,20},{4,12},{0,4},{9,1},{1... | collective-permute-start | bytes 1474568 | tf_op jit(solution)/shard_map/ppermute | solution.py:103
  255.9 30.2 %collective-permute-start.38 = (bf16[256,2304]{1,0:T(8,128)(2,1)}, bf16[256,2304]{1,0:T(8,128)(2,1)}, u32[]{:S(2)}, u32[]{:S(2)}) collective-permute-start(bf16[256,2304]{1,0:T(8,128)(2,1)} %get-tuple-element.314), channel_id=1, source_target_pairs={{0,8},{8,16},{16,24},{24,28},{28,20},{20,12},{12,4},{4,0},{1,9},{9... | collective-permute-start | bytes 3538952 | tf_op jit(solution)/shard_map/ppermute | solution.py:100
  257.0 30.8 %collective-permute-start.37 = (bf16[256,2304]{1,0:T(8,128)(2,1)}, bf16[256,2304]{1,0:T(8,128)(2,1)}, u32[]{:S(2)}, u32[]{:S(2)}) collective-permute-start(bf16[256,2304]{1,0:T(8,128)(2,1)} %get-tuple-element.331), channel_id=1, source_target_pairs={{8,0},{16,8},{24,16},{28,24},{20,28},{12,20},{4,12},{0,4},{9,1},{1... | collective-permute-start | bytes 3538952 | tf_op jit(solution)/shard_map/ppermute | solution.py:103
  289.5 19.5 %collective-permute-start.39 = (bf16[512,2048]{1,0:T(8,128)(2,1)}, bf16[512,2048]{1,0:T(8,128)(2,1)S(1)}, u32[]{:S(2)}, u32[]{:S(2)}) collective-permute-start(bf16[512,2048]{1,0:T(8,128)(2,1)} %get-tuple-element.337), channel_id=1, source_target_pairs={{0,1},{1,0},{2,3},{3,2},{4,5},{5,4},{6,7},{7,6},{8,9},{9,8},{10,11... | collective-permute-start | bytes 6291464 | tf_op jit(solution)/shard_map/ppermute | solution.py:234
  290.0 28.9 %collective-permute-start.45 = (bf16[256,2304]{1,0:T(8,128)(2,1)S(1)}, bf16[256,2304]{1,0:T(8,128)(2,1)}, u32[]{:S(2)}, u32[]{:S(2)}) collective-permute-start(bf16[256,2304]{1,0:T(8,128)(2,1)S(1)} %add_convert_fusion.4), channel_id=1, source_target_pairs={{0,8},{8,16},{16,24},{24,28},{28,20},{20,12},{12,4},{4,0},{1,9},{9... | collective-permute-start | bytes 3538952 | tf_op jit(solution)/shard_map/ppermute | solution.py:100
  291.2 30.5 %collective-permute-start.44 = (bf16[256,2304]{1,0:T(8,128)(2,1)S(1)}, bf16[256,2304]{1,0:T(8,128)(2,1)S(1)}, u32[]{:S(2)}, u32[]{:S(2)}) collective-permute-start(bf16[256,2304]{1,0:T(8,128)(2,1)S(1)} %add_convert_fusion.3), channel_id=1, source_target_pairs={{8,0},{16,8},{24,16},{28,24},{20,28},{12,20},{4,12},{0,4},{9,1},{1... | collective-permute-start | bytes 3538952 | tf_op jit(solution)/shard_map/ppermute | solution.py:103
  297.3 34.1 %collective-permute-start.41 = (bf16[256,2048]{1,0:T(8,128)(2,1)}, bf16[256,2048]{1,0:T(8,128)(2,1)S(1)}, u32[]{:S(2)}, u32[]{:S(2)}) collective-permute-start(bf16[256,2048]{1,0:T(8,128)(2,1)} %add_convert_fusion.7), channel_id=1, source_target_pairs={{0,2},{1,3},{2,0},{3,1},{4,6},{5,7},{6,4},{7,5},{8,10},{9,11},{10,... | collective-permute-start | bytes 3145736 | tf_op jit(solution)/shard_map/ppermute | solution.py:234
  309.1 20.3 %collective-permute-start.42 = (bf16[128,1920]{1,0:T(8,128)(2,1)S(1)}, bf16[128,1920]{1,0:T(8,128)(2,1)S(1)}, u32[]{:S(2)}, u32[]{:S(2)}) collective-permute-start(bf16[128,1920]{1,0:T(8,128)(2,1)S(1)} %get-tuple-element.350), channel_id=1, source_target_pairs={{0,8},{8,16},{16,24},{24,28},{28,20},{20,12},{12,4},{4,0},{1,9},{9... | collective-permute-start | bytes 1474568 | tf_op jit(solution)/shard_map/ppermute | solution.py:100
  310.2 20.3 %collective-permute-start.43 = (bf16[128,1920]{1,0:T(8,128)(2,1)S(1)}, bf16[128,1920]{1,0:T(8,128)(2,1)S(1)}, u32[]{:S(2)}, u32[]{:S(2)}) collective-permute-start(bf16[128,1920]{1,0:T(8,128)(2,1)S(1)} %get-tuple-element.351), channel_id=1, source_target_pairs={{8,0},{16,8},{24,16},{28,24},{20,28},{12,20},{4,12},{0,4},{9,1},{1... | collective-permute-start | bytes 1474568 | tf_op jit(solution)/shard_map/ppermute | solution.py:103
  320.5 33.3 %collective-permute-start.47 = (bf16[256,2304]{1,0:T(8,128)(2,1)S(1)}, bf16[256,2304]{1,0:T(8,128)(2,1)S(1)}, u32[]{:S(2)}, u32[]{:S(2)}) collective-permute-start(bf16[256,2304]{1,0:T(8,128)(2,1)S(1)} %add_convert_fusion.2), channel_id=1, source_target_pairs={{0,8},{8,16},{16,24},{24,28},{28,20},{20,12},{12,4},{4,0},{1,9},{9... | collective-permute-start | bytes 3538952 | tf_op jit(solution)/shard_map/ppermute | solution.py:100
  322.0 32.7 %collective-permute-start.48 = (bf16[256,2304]{1,0:T(8,128)(2,1)S(1)}, bf16[256,2304]{1,0:T(8,128)(2,1)S(1)}, u32[]{:S(2)}, u32[]{:S(2)}) collective-permute-start(bf16[256,2304]{1,0:T(8,128)(2,1)S(1)} %add_convert_fusion.1), channel_id=1, source_target_pairs={{8,0},{16,8},{24,16},{28,24},{20,28},{12,20},{4,12},{0,4},{9,1},{1... | collective-permute-start | bytes 3538952 | tf_op jit(solution)/shard_map/ppermute | solution.py:103
  333.6 25.6 %collective-permute-start.46 = (bf16[256,2048]{1,0:T(8,128)(2,1)S(1)}, bf16[256,2048]{1,0:T(8,128)(2,1)S(1)}, u32[]{:S(2)}, u32[]{:S(2)}) collective-permute-start(bf16[256,2048]{1,0:T(8,128)(2,1)S(1)} %get-tuple-element.369.refs_0_.refs_1_), channel_id=1, source_target_pairs={{0,2},{1,3},{2,0},{3,1},{4,6},{5,7},{6,4},{7,5},{8,10},{9,11},{10,... | collective-permute-start | bytes 3145736 | tf_op jit(solution)/shard_map/ppermute | solution.py:234
  359.2 26.1 %collective-permute-start.54 = (bf16[256,1920]{1,0:T(8,128)(2,1)S(1)}, bf16[256,1920]{1,0:T(8,128)(2,1)S(1)}, u32[]{:S(2)}, u32[]{:S(2)}) collective-permute-start(bf16[256,1920]{1,0:T(8,128)(2,1)S(1)} %get-tuple-element.360), channel_id=1, source_target_pairs={{0,8},{8,16},{16,24},{24,28},{28,20},{20,12},{12,4},{4,0},{1,9},{9... | collective-permute-start | bytes 2949128 | tf_op jit(solution)/shard_map/ppermute | solution.py:100
  360.1 26.4 %collective-permute-start.53 = (bf16[256,1920]{1,0:T(8,128)(2,1)S(1)}, bf16[256,1920]{1,0:T(8,128)(2,1)S(1)}, u32[]{:S(2)}, u32[]{:S(2)}) collective-permute-start(bf16[256,1920]{1,0:T(8,128)(2,1)S(1)} %get-tuple-element.375), channel_id=1, source_target_pairs={{8,0},{16,8},{24,16},{28,24},{20,28},{12,20},{4,12},{0,4},{9,1},{1... | collective-permute-start | bytes 2949128 | tf_op jit(solution)/shard_map/ppermute | solution.py:103
  361.2 27.8 %collective-permute-start.51 = (bf16[256,2304]{1,0:T(8,128)(2,1)S(1)}, bf16[256,2304]{1,0:T(8,128)(2,1)S(1)}, u32[]{:S(2)}, u32[]{:S(2)}) collective-permute-start(bf16[256,2304]{1,0:T(8,128)(2,1)S(1)} %add_convert_fusion.refs_0_), channel_id=1, source_target_pairs={{0,2},{1,3},{2,0},{3,1},{4,6},{5,7},{6,4},{7,5},{8,10},{9,11},{10,... | collective-permute-start | bytes 3538952 | tf_op jit(solution)/shard_map/ppermute | solution.py:234
  362.7 26.3 %collective-permute-start.52 = (bf16[256,2304]{1,0:T(8,128)(2,1)S(1)}, bf16[256,2304]{1,0:T(8,128)(2,1)S(1)}, u32[]{:S(2)}, u32[]{:S(2)}) collective-permute-start(bf16[256,2304]{1,0:T(8,128)(2,1)S(1)} %add_convert_fusion.refs_0_), channel_id=1, source_target_pairs={{0,1},{1,0},{2,3},{3,2},{4,5},{5,4},{6,7},{7,6},{8,9},{9,8},{10,11... | collective-permute-start | bytes 3538952 | tf_op jit(solution)/shard_map/ppermute | solution.py:234
  385.5 24.2 %collective-permute-start.59 = (bf16[256,1920]{1,0:T(8,128)(2,1)S(1)}, bf16[256,1920]{1,0:T(8,128)(2,1)S(1)}, u32[]{:S(2)}, u32[]{:S(2)}) collective-permute-start(bf16[256,1920]{1,0:T(8,128)(2,1)S(1)} %add_convert_fusion.13), channel_id=1, source_target_pairs={{0,8},{8,16},{16,24},{24,28},{28,20},{20,12},{12,4},{4,0},{1,9},{9... | collective-permute-start | bytes 2949128 | tf_op jit(solution)/shard_map/ppermute | solution.py:100
  386.7 24.2 %collective-permute-start.58 = (bf16[256,1920]{1,0:T(8,128)(2,1)S(1)}, bf16[256,1920]{1,0:T(8,128)(2,1)S(1)}, u32[]{:S(2)}, u32[]{:S(2)}) collective-permute-start(bf16[256,1920]{1,0:T(8,128)(2,1)S(1)} %add_convert_fusion.12), channel_id=1, source_target_pairs={{8,0},{16,8},{24,16},{28,24},{20,28},{12,20},{4,12},{0,4},{9,1},{1... | collective-permute-start | bytes 2949128 | tf_op jit(solution)/shard_map/ppermute | solution.py:103
  389.0 22.1 %collective-permute-start.57 = (bf16[256,2304]{1,0:T(8,128)(2,1)S(1)}, bf16[256,2304]{1,0:T(8,128)(2,1)S(1)}, u32[]{:S(2)}, u32[]{:S(2)}) collective-permute-start(bf16[256,2304]{1,0:T(8,128)(2,1)S(1)} %collective-permute-done.51.refs_1_), channel_id=1, source_target_pairs={{0,1},{1,0},{2,3},{3,2},{4,5},{5,4},{6,7},{7,6},{8,9},{9,8},{10,11... | collective-permute-start | bytes 3538952 | tf_op jit(solution)/shard_map/ppermute | solution.py:234
  389.0 29.5 %collective-permute-start.64 = (bf16[256,2048]{1,0:T(8,128)(2,1)}, bf16[256,2048]{1,0:T(8,128)(2,1)S(1)}, u32[]{:S(2)}, u32[]{:S(2)}) collective-permute-start(bf16[256,2048]{1,0:T(8,128)(2,1)} %add_convert_fusion.6), channel_id=1, source_target_pairs={{0,2},{1,3},{2,0},{3,1},{4,6},{5,7},{6,4},{7,5},{8,10},{9,11},{10,... | collective-permute-start | bytes 3145736 | tf_op jit(solution)/shard_map/ppermute | solution.py:234
  418.6 24.6 %collective-permute-start.62 = (bf16[256,1920]{1,0:T(8,128)(2,1)S(1)}, bf16[256,1920]{1,0:T(8,128)(2,1)S(1)}, u32[]{:S(2)}, u32[]{:S(2)}) collective-permute-start(bf16[256,1920]{1,0:T(8,128)(2,1)S(1)} %add_convert_fusion.11), channel_id=1, source_target_pairs={{0,8},{8,16},{16,24},{24,28},{28,20},{20,12},{12,4},{4,0},{1,9},{9... | collective-permute-start | bytes 2949128 | tf_op jit(solution)/shard_map/ppermute | solution.py:100
  419.6 24.6 %collective-permute-start.63 = (bf16[256,1920]{1,0:T(8,128)(2,1)S(1)}, bf16[256,1920]{1,0:T(8,128)(2,1)S(1)}, u32[]{:S(2)}, u32[]{:S(2)}) collective-permute-start(bf16[256,1920]{1,0:T(8,128)(2,1)S(1)} %add_convert_fusion.10), channel_id=1, source_target_pairs={{8,0},{16,8},{24,16},{28,24},{20,28},{12,20},{4,12},{0,4},{9,1},{1... | collective-permute-start | bytes 2949128 | tf_op jit(solution)/shard_map/ppermute | solution.py:103
  420.7 35.1 %collective-permute-start.60 = (bf16[264,1152]{1,0:T(8,128)(2,1)S(1)}, bf16[264,1152]{1,0:T(8,128)(2,1)S(1)}, u32[]{:S(2)}, u32[]{:S(2)}) collective-permute-start(bf16[264,1152]{1,0:T(8,128)(2,1)S(1)} %get-tuple-element.404), channel_id=1, source_target_pairs={{0,8},{8,16},{16,24},{24,28},{28,20},{20,12},{12,4},{4,0},{1,9},{9... | collective-permute-start | bytes 1824776 | tf_op jit(solution)/shard_map/ppermute | solution.py:100
  421.8 34.6 %collective-permute-start.61 = (bf16[264,1152]{1,0:T(8,128)(2,1)S(1)}, bf16[264,1152]{1,0:T(8,128)(2,1)S(1)}, u32[]{:S(2)}, u32[]{:S(2)}) collective-permute-start(bf16[264,1152]{1,0:T(8,128)(2,1)S(1)} %get-tuple-element.405), channel_id=1, source_target_pairs={{8,0},{16,8},{24,16},{28,24},{20,28},{12,20},{4,12},{0,4},{9,1},{1... | collective-permute-start | bytes 1824776 | tf_op jit(solution)/shard_map/ppermute | solution.py:103
  423.4 38.6 %collective-permute-start.66 = (bf16[256,2048]{1,0:T(8,128)(2,1)S(1)}, bf16[256,2048]{1,0:T(8,128)(2,1)S(1)}, u32[]{:S(2)}, u32[]{:S(2)}) collective-permute-start(bf16[256,2048]{1,0:T(8,128)(2,1)S(1)} %add_convert_fusion.5), channel_id=1, source_target_pairs={{0,2},{1,3},{2,0},{3,1},{4,6},{5,7},{6,4},{7,5},{8,10},{9,11},{10,... | collective-permute-start | bytes 3145736 | tf_op jit(solution)/shard_map/ppermute | solution.py:234
  461.5 22.2 %collective-permute-start.76 = (bf16[256,1920]{1,0:T(8,128)(2,1)S(1)}, bf16[256,1920]{1,0:T(8,128)(2,1)S(1)}, u32[]{:S(2)}, u32[]{:S(2)}) collective-permute-start(bf16[256,1920]{1,0:T(8,128)(2,1)S(1)} %add_convert_fusion.9.refs_4_), channel_id=1, source_target_pairs={{0,2},{1,3},{2,0},{3,1},{4,6},{5,7},{6,4},{7,5},{8,10},{9,11},{10,... | collective-permute-start | bytes 2949128 | tf_op jit(solution)/shard_map/ppermute | solution.py:234
  (90 other events, 1825.6 us)

commit v8 on v7

--- a/solution.py
+++ b/solution.py
@@ -1222,10 +1222,10 @@
     last = swap(clock.tie(other_half(grad_keep, came)), 2)
     second_sum = sums[1].finish(clock)
     second_across, second_beside = swap(second_sum, 2), swap(second_sum, 1)
-    head_ring.fork(clock)
     down_came = clock.tie(down_came)
     result = layer_output(hidden, down_keep, down_came, down_last, ring.slot_owners(), n_dp)
     clock.done(result)
+    head_ring.fork(clock)
     last, second_beside = clock.tie(last, second_beside)
     grad_input = first_norm_back(
         grad_hidden, mine, grad_keep, came, last, gains, ring.slot_owners(), n_dp

time: 514 us -> 512 us (level)
    ppermute x32, waiting for transfers between devices: 23.7 us -> 18.4 us  [swap(): return lax.ppermute(block, 'seq', [(i, i ^ distance) for i in range(4)])]
  transfers between devices with their start and end apart: 84 -> 84, of which waited for: 47 -> 45; matrix products, arithmetic and copies ran while one was open for 3% -> 3% of each run, Pallas kernels for 33% -> 33%
where the time goes in v8:
time: 512 us; the launch traced here: 504 us
  waiting for transfers between devices  232 us (45%)
  Pallas kernels  174 us (34%)
  starting transfers between devices  72.7 us (14%)
  other arithmetic  12.7 us (2%)
  local copies, waits for them, and re-layouts  9.85 us (2%)
    ppermute x26, waiting for transfers between devices, go_up(): return lax.ppermute(block, 'dp', self.up)  184 us
    pallas_call x5, Pallas kernels, kernel_call(): pl.pallas_call(body, out_shape=tuple((jax.ShapeDtypeStruct(s, d) for s, d...  59.5 us
    pallas_call x2, Pallas kernels, mlp_chunk(): pl.pallas_call(body, grid=(4,), out_shape=(half, half, half, half, pltpu....  53 us
    pallas_call x3, Pallas kernels, weight_terms(): pl.pallas_call(body, grid=(n_slots // group,), out_shape=(jax.ShapeDtypeS...  29.8 us
    ppermute x26, waiting for transfers between devices, go_down(): return lax.ppermute(block, 'dp', self.down)  29.2 us
    ppermute x26, starting transfers between devices, go_up(): return lax.ppermute(block, 'dp', self.up)  28.9 us
    ppermute x26, starting transfers between devices, go_down(): return lax.ppermute(block, 'dp', self.down)  26.7 us
    ppermute x32, waiting for transfers between devices, swap(): return lax.ppermute(block, 'seq', [(i, i ^ distance) for i in range(4)])  18.4 us
  transfers between devices with their start and end apart: 84, of which 45 were waited for; matrix products, arithmetic and copies ran while one was open for 3% of the time, Pallas kernels for 33%

profile of v8, /device:TPU:0, one launch (start us, length us, event | category | flops | bytes accessed | tf_op | source)
XLA Modules:
  0.0 504.0 jit_solution(5947226971333810870)
XLA Ops:
  0.7 2.5 pack_heads.1.refs_4_
  3.2 2.9 collective-permute-start
  8.6 2.4 permute_features.2.refs_0_.inputs_ref
  11.0 2.0 collective-permute-start.2
  13.2 3.1 pack_mlp.1
  16.3 5.2 %collective-permute-done.1.refs_5_ = bf16[264,1152]{1,0:T(8,128)(2,1)S(1)} collective-permute-done((bf16[264,1152]{1,0:T(8,128)(2,1)}, bf16[264,1152]{1,0:T(8,128)(2,1)S(1)}, u32[]{:S(2)}, u32[]{:S(2)}) %collective-permute-start.1) | collective-permute-done | bytes 608288 | tf_op jit(solution)/shard_map/ppermute | solution.py:100
  24.2 2.4 permute_features.3.refs_4_.cot_ref
  26.7 9.2 %collective-permute-done.4.refs_6_ = bf16[264,1152]{1,0:T(8,128)(2,1)S(1)} collective-permute-done((bf16[264,1152]{1,0:T(8,128)(2,1)S(1)}, bf16[264,1152]{1,0:T(8,128)(2,1)S(1)}, u32[]{:S(2)}, u32[]{:S(2)}) %collective-permute-start.4) | collective-permute-done | bytes 608288 | tf_op jit(solution)/shard_map/ppermute | solution.py:100
  38.5 14.0 %collective-permute-done.7.refs_7_ = bf16[264,1152]{1,0:T(8,128)(2,1)S(1)} collective-permute-done((bf16[264,1152]{1,0:T(8,128)(2,1)S(1)}, bf16[264,1152]{1,0:T(8,128)(2,1)S(1)}, u32[]{:S(2)}, u32[]{:S(2)}) %collective-permute-start.7) | collective-permute-done | bytes 608288 | tf_op jit(solution)/shard_map/ppermute | solution.py:100
  54.7 7.7 %collective-permute-done.10.refs_12_ = bf16[128,1152]{1,0:T(8,128)(2,1)S(1)} collective-permute-done((bf16[128,1152]{1,0:T(8,128)(2,1)S(1)}, bf16[128,1152]{1,0:T(8,128)(2,1)S(1)}, u32[]{:S(2)}, u32[]{:S(2)}) %collective-permute-start.10) | collective-permute-done | bytes 294944 | tf_op jit(solution)/shard_map/ppermute | solution.py:103
  70.9 28.7 %attention_forward.1 = (bf16[1024,2048]{1,0:T(8,128)(2,1)S(1)}, bf16[512,1024]{1,0:T(8,128)(2,1)S(1)}, bf16[1024,128]{1,0:T(8,128)(2,1)S(1)}, bf16[192,1024]{1,0...) custom-call(s32[4]{0:T(128)S(1)} %fusion.2.places_ref, ...), custom_call_target="tpu_custom_call" | custom-call | flops 1000 | bytes 1000 | tf_op jit(solution)/shard_map/attention_forward/pallas_call | solution.py:58
  100.8 9.1 %collective-permute-done.12.refs_9_ = bf16[256,1920]{1,0:T(8,128)(2,1)S(1)} collective-permute-done((bf16[256,1920]{1,0:T(8,128)(2,1)}, bf16[256,1920]{1,0:T(8,128)(2,1)S(1)}, u32[]{:S(2)}, u32[]{:S(2)}) %collective-permute-start.12) | collective-permute-done | bytes 983072 | tf_op jit(solution)/shard_map/ppermute | solution.py:100
  113.3 2.1 collective-permute-done.16.came_ref
  117.3 22.4 %collective-permute-done.19.refs_10_ = bf16[256,2304]{1,0:T(8,128)(2,1)S(1)} collective-permute-done((bf16[256,2304]{1,0:T(8,128)(2,1)S(1)}, bf16[256,2304]{1,0:T(8,128)(2,1)S(1)}, u32[]{:S(2)}, u32[]{:S(2)}) %collective-permute-start.19) | collective-permute-done | bytes 1179680 | tf_op jit(solution)/shard_map/ppermute | solution.py:100
  145.7 21.3 %collective-permute-done.22.refs_11_ = bf16[256,2304]{1,0:T(8,128)(2,1)S(1)} collective-permute-done((bf16[256,2304]{1,0:T(8,128)(2,1)S(1)}, bf16[256,2304]{1,0:T(8,128)(2,1)S(1)}, u32[]{:S(2)}, u32[]{:S(2)}) %collective-permute-start.22) | collective-permute-done | bytes 1179680 | tf_op jit(solution)/shard_map/ppermute | solution.py:100
  171.0 10.7 %collective-permute-done.25.refs_15_ = bf16[128,2304]{1,0:T(8,128)(2,1)S(1)} collective-permute-done((bf16[128,2304]{1,0:T(8,128)(2,1)S(1)}, bf16[128,2304]{1,0:T(8,128)(2,1)S(1)}, u32[]{:S(2)}, u32[]{:S(2)}) %collective-permute-start.25) | collective-permute-done | bytes 589856 | tf_op jit(solution)/shard_map/ppermute | solution.py:100
  185.5 25.1 %mlp_chunk.2 = (bf16[512,2048]{1,0:T(8,128)(2,1)}, bf16[512,2048]{1,0:T(8,128)(2,1)}, bf16[512,2048]{1,0:T(8,128)(2,1)}, bf16[512,2048]{1,0:T(8,128)(2,1)}, bf16[1024,2304]{1,0:T(8,128)(2,1)}) custom-call(bf16[256,2048]{1,0:T(8,128)(2,1)S(1)} %get-tuple-element.289.refs_0_, bf16[256,2048]{1,0:T(8,128)(2,1)S(1)} %collective-permute-done.20.refs_1_, ...), custom_call_target="tpu_custom_call" | custom-call | flops 1000 | bytes 1000 | tf_op jit(solution)/shard_map/mlp_chunk/pallas_call | solution.py:676
  212.7 2.3 copy-done.2
  215.0 11.4 %weight_terms.3 = (bf16[2048,2304]{1,0:T(8,128)(2,1)S(1)}, bf16[128,2304]{1,0:T(8,128)(2,1)S(1)}, bf16[128,2304]{1,0:T(8,128)(2,1)S(1)}) custom-call(bf16[256,2048]{1,0:T(8,128)(2,1)S(1)} %get-tuple-element.289.refs_0_, bf16[256,2048]{1,0:T(8,128)(2,1)S(1)} %collective-permute-done.20.refs_1_, bf16[256,2048]{1,0:T(8,128)(2,1)S(1)} %collective-permute-done.23.refs_2_, ...), custom_call_target="tpu_custom_call" | custom-call | flops 1000 | bytes 1000 | tf_op jit(solution)/shard_map/weight_terms/pallas_call | solution.py:770
  228.5 6.8 %collective-permute-done.30.refs_11_ = bf16[256,1920]{1,0:T(8,128)(2,1)S(1)} collective-permute-done((bf16[256,1920]{1,0:T(8,128)(2,1)S(1)}, bf16[256,1920]{1,0:T(8,128)(2,1)S(1)}, u32[]{:S(2)}, u32[]{:S(2)}) %collective-permute-start.30) | collective-permute-done | bytes 983072 | tf_op jit(solution)/shard_map/ppermute | solution.py:100
  238.9 9.0 %collective-permute-done.35.up_ref = bf16[128,2304]{1,0:T(8,128)(2,1)S(1)} collective-permute-done((bf16[128,2304]{1,0:T(8,128)(2,1)S(1)}, bf16[128,2304]{1,0:T(8,128)(2,1)S(1)}, u32[]{:S(2)}, u32[]{:S(2)}) %collective-permute-start.35) | collective-permute-done | bytes 589856 | tf_op jit(solution)/shard_map/ppermute | solution.py:100
  249.4 2.2 ring_add.3
  251.6 2.2 collective-permute-done.33.refs_15_
  258.0 28.0 %mlp_chunk.3 = (bf16[512,2048]{1,0:T(8,128)(2,1)}, bf16[512,2048]{1,0:T(8,128)(2,1)}, bf16[512,2048]{1,0:T(8,128)(2,1)}, bf16[512,2048]{1,0:T(8,128)(2,1)}, bf16[1024,1920]{1,0:T(8,128)(2,1)}) custom-call(bf16[256,2048]{1,0:T(8,128)(2,1)S(1)} %get-tuple-element.289.refs_0_, bf16[256,2048]{1,0:T(8,128)(2,1)S(1)} %collective-permute-done.20.refs_1_, ...), custom_call_target="tpu_custom_call" | custom-call | flops 1000 | bytes 1000 | tf_op jit(solution)/shard_map/mlp_chunk/pallas_call | solution.py:676
  287.8 1.7 add_convert_fusion.3
  292.1 3.8 collective-permute-done.40.came_ref
  298.8 10.3 %weight_terms.4 = (bf16[2048,1920]{1,0:T(8,128)(2,1)S(1)}, bf16[128,1920]{1,0:T(8,128)(2,1)S(1)}, bf16[128,1920]{1,0:T(8,128)(2,1)S(1)}) custom-call(bf16[256,2048]{1,0:T(8,128)(2,1)S(1)} %get-tuple-element.289.refs_0_, bf16[256,2048]{1,0:T(8,128)(2,1)S(1)} %collective-permute-done.20.refs_1_, bf16[256,2048]{1,0:T(8,128)(2,1)S(1)} %collective-permute-done.23.refs_2_, ...), custom_call_target="tpu_custom_call" | custom-call | flops 1000 | bytes 1000 | tf_op jit(solution)/shard_map/weight_terms/pallas_call | solution.py:770
  311.1 7.8 %collective-permute-done.44 = bf16[256,2304]{1,0:T(8,128)(2,1)} collective-permute-done((bf16[256,2304]{1,0:T(8,128)(2,1)S(1)}, bf16[256,2304]{1,0:T(8,128)(2,1)}, u32[]{:S(2)}, u32[]{:S(2)}) %collective-permute-start.44) | collective-permute-done | bytes 1179680 | tf_op jit(solution)/shard_map/ppermute | solution.py:100
  323.3 6.0 %collective-permute-done.41.up_ref = bf16[128,1920]{1,0:T(8,128)(2,1)S(1)} collective-permute-done((bf16[128,1920]{1,0:T(8,128)(2,1)S(1)}, bf16[128,1920]{1,0:T(8,128)(2,1)S(1)}, u32[]{:S(2)}, u32[]{:S(2)}) %collective-permute-start.41) | collective-permute-done | bytes 491552 | tf_op jit(solution)/shard_map/ppermute | solution.py:100
  331.4 2.1 second_norm_back.1
  336.6 17.2 %collective-permute-done.48 = bf16[256,2304]{1,0:T(8,128)(2,1)S(1)} collective-permute-done((bf16[256,2304]{1,0:T(8,128)(2,1)S(1)}, bf16[256,2304]{1,0:T(8,128)(2,1)S(1)}, u32[]{:S(2)}, u32[]{:S(2)}) %collective-permute-start.48) | collective-permute-done | bytes 1179680 | tf_op jit(solution)/shard_map/ppermute | solution.py:100
  355.1 4.1 collective-permute-done.47.refs_1_.refs_2_
  362.9 22.4 %attention_backward.1 = (bf16[1024,512]{1,0:T(8,128)(2,1)S(1)}, bf16[1024,128]{1,0:T(8,128)(2,1)S(1)}) custom-call(s32[4]{0:T(128)S(1)} %fusion.2.places_ref, s32[6]{0:T(128)S(1)} %bitcast.12, s32[1]{0:T(128)S(6)} %copy.42.live_ref, f32[32,1024]{1,0:T(8,128)S(1)} %copy-done.30, f32[32,1024]{1,0:T(8,128)S(1)} %get-tuple-element.249.sin_ref, ...), custom_call_target="tpu_custom_call" | custom-call | flops 1000 | bytes 1000 | tf_op jit(solution)/shard_map/attention_backward/pallas_call | solution.py:58
  390.6 8.0 %heads_back.1 = (bf16[512,2048]{1,0:T(8,128)(2,1)S(1)}, bf16[512,2048]{1,0:T(8,128)(2,1)S(1)}, f32[8,2048]{1,0:T(8,128)S(1)}) custom-call(bf16[1024,512]{1,0:T(8,128)(2,1)S(1)} %get-tuple-element.376.grad_q_ref.refs_5_, bf16[1024,128]{1,0:T(8,128)(2,1)S(1)} %get-tuple-element.372.grad_kv_ref.refs_6_, bf16[256,2048]{1,0:T(8,128)(2,1)S(1)} %copy-done.1, ...), custom_call_target="tpu_custom_call" | custom-call | flops 1000 | bytes 1000 | tf_op jit(solution)/shard_map/heads_back/pallas_call | solution.py:612
  398.7 8.1 %weight_terms.5 = (bf16[2112,1152]{1,0:T(8,128)(2,1)S(1)}, bf16[136,1152]{1,0:T(8,128)(2,1)S(1)}, bf16[128,1152]{1,0:T(8,128)(2,1)S(1)}) custom-call(bf16[1024,2048]{1,0:T(8,128)(2,1)} %copy-done.21, bf16[256,2048]{1,0:T(8,128)(2,1)S(1)} %get-tuple-element.368.refs_0_.refs_1_, bf16[256,2048]{1,0:T(8,128)(2,1)S(1)} %collective-permute-done.47.refs_1_.refs_2_, ...), custom_call_target="tpu_custom_call" | custom-call | flops 1000 | bytes 1000 | tf_op jit(solution)/shard_map/weight_terms/pallas_call | solution.py:770
  407.8 2.0 collective-permute-done.52
  411.1 7.2 %collective-permute-done.61.down_ref = bf16[128,1152]{1,0:T(8,128)(2,1)S(1)} collective-permute-done((bf16[128,1152]{1,0:T(8,128)(2,1)S(1)}, bf16[128,1152]{1,0:T(8,128)(2,1)S(1)}, u32[]{:S(2)}, u32[]{:S(2)}) %collective-permute-start.61) | collective-permute-done | bytes 294944 | tf_op jit(solution)/shard_map/ppermute | solution.py:103
  423.9 19.3 %collective-permute-done.56 = bf16[256,1920]{1,0:T(8,128)(2,1)S(1)} collective-permute-done((bf16[256,1920]{1,0:T(8,128)(2,1)S(1)}, bf16[256,1920]{1,0:T(8,128)(2,1)S(1)}, u32[]{:S(2)}, u32[]{:S(2)}) %collective-permute-start.56) | collective-permute-done | bytes 983072 | tf_op jit(solution)/shard_map/ppermute | solution.py:100
  445.1 1.8 layer_output.1
  447.0 8.9 %collective-permute-done.66 = bf16[264,1152]{1,0:T(8,128)(2,1)S(1)} collective-permute-done((bf16[264,1152]{1,0:T(8,128)(2,1)S(1)}, bf16[264,1152]{1,0:T(8,128)(2,1)S(1)}, u32[]{:S(2)}, u32[]{:S(2)}) %collective-permute-start.66) | collective-permute-done | bytes 608288 | tf_op jit(solution)/shard_map/ppermute | solution.py:100
  460.9 2.9 first_norm_back.1
  463.8 3.2 collective-permute-done.68
  470.0 3.3 collective-permute-done.72
  476.3 3.7 collective-permute-done.70
  481.6 3.1 collective-permute-done.74
  485.8 7.1 %unpack_mlp.1 = (f32[256,5632]{1,0:T(8,128)}, f32[256,5632]{1,0:T(8,128)}, f32[5632,256]{1,0:T(8,128)}) custom-call(s32[4]{0:T(128)S(1)} %fusion.2.places_ref, bf16[256,2304]{1,0:T(8,128)(2,1)S(1)} %add_convert_fusion.refs_0_, bf16[256,2304]{1,0:T(8,128)(2,1)S(1)} %collective-permute-done.53.refs_1_, bf16[256,2304]{1,0:T(8,128)(2,1)S(1)} %collective-permute-done.54.refs_2_, ...), custom_call_target="tpu_custom_call" | custom-call | flops 1000 | bytes 1000 | tf_op jit(solution)/shard_map/unpack_mlp/pallas_call | solution.py:964
  493.0 4.2 collective-permute-done.78.refs_3_
  499.6 3.6 unpack_heads.1
  (293 shorter events, 106.8 us)
Async XLA Ops:
  3.2 18.7 %collective-permute-start = (bf16[264,1152]{1,0:T(8,128)(2,1)}, bf16[264,1152]{1,0:T(8,128)(2,1)S(1)}, u32[]{:S(2)}, u32[]{:S(2)}) collective-permute-start(bf16[264,1152]{1,0:T(8,128)(2,1)} %pack_heads.1.refs_4_), channel_id=1, source_target_pairs={{8,0},{16,8},{24,16},{28,24},{20,28},{12,20},{4,12},{0,4},{9,1},{1... | collective-permute-start | bytes 1824776 | tf_op jit(solution)/shard_map/ppermute | solution.py:103
  11.0 25.3 %collective-permute-start.2 = (bf16[256,2048]{1,0:T(8,128)(2,1)}, bf16[256,2048]{1,0:T(8,128)(2,1)}, u32[]{:S(2)}, u32[]{:S(2)}) collective-permute-start(bf16[256,2048]{1,0:T(8,128)(2,1)} %permute_features.2.refs_0_.inputs_ref), channel_id=1, source_target_pairs={{0,2},{1,3},{2,0},{3,1},{4,6},{5,7},{6,4},{7,5},{8,10},{9,11},{10,... | collective-permute-start | bytes 3145736 | tf_op jit(solution)/shard_map/ppermute | solution.py:234
  13.0 49.4 %collective-permute-start.5 = (bf16[256,2048]{1,0:T(8,128)(2,1)}, bf16[256,2048]{1,0:T(8,128)(2,1)}, u32[]{:S(2)}, u32[]{:S(2)}) collective-permute-start(bf16[256,2048]{1,0:T(8,128)(2,1)} %permute_features.2.refs_0_.inputs_ref), channel_id=1, source_target_pairs={{0,1},{1,0},{2,3},{3,2},{4,5},{5,4},{6,7},{7,6},{8,9},{9,8},{10,11... | collective-permute-start | bytes 3145736 | tf_op jit(solution)/shard_map/ppermute | solution.py:234
  36.3 26.1 %collective-permute-start.6 = (bf16[256,2048]{1,0:T(8,128)(2,1)}, bf16[256,2048]{1,0:T(8,128)(2,1)S(1)}, u32[]{:S(2)}, u32[]{:S(2)}) collective-permute-start(bf16[256,2048]{1,0:T(8,128)(2,1)} %collective-permute-done.2.refs_1_), channel_id=1, source_target_pairs={{0,1},{1,0},{2,3},{3,2},{4,5},{5,4},{6,7},{7,6},{8,9},{9,8},{10,11... | collective-permute-start | bytes 3145736 | tf_op jit(solution)/shard_map/ppermute | solution.py:234
  62.5 38.3 %collective-permute-start.15 = (bf16[256,2304]{1,0:T(8,128)(2,1)S(1)}, bf16[256,2304]{1,0:T(8,128)(2,1)S(1)}, u32[]{:S(2)}, u32[]{:S(2)}) collective-permute-start(bf16[256,2304]{1,0:T(8,128)(2,1)S(1)} %copy-done.31), channel_id=1, source_target_pairs={{0,8},{8,16},{16,24},{24,28},{28,20},{20,12},{12,4},{4,0},{1,9},{9... | collective-permute-start | bytes 3538952 | tf_op jit(solution)/shard_map/ppermute | solution.py:100
  64.1 36.7 %collective-permute-start.14 = (bf16[256,2304]{1,0:T(8,128)(2,1)S(1)}, bf16[256,2304]{1,0:T(8,128)(2,1)S(1)}, u32[]{:S(2)}, u32[]{:S(2)}) collective-permute-start(bf16[256,2304]{1,0:T(8,128)(2,1)S(1)} %copy-done.31), channel_id=1, source_target_pairs={{8,0},{16,8},{24,16},{28,24},{20,28},{12,20},{4,12},{0,4},{9,1},{1... | collective-permute-start | bytes 3538952 | tf_op jit(solution)/shard_map/ppermute | solution.py:103
  64.5 46.7 %collective-permute-start.11 = (bf16[256,2048]{1,0:T(8,128)(2,1)}, bf16[256,2048]{1,0:T(8,128)(2,1)S(1)}, u32[]{:S(2)}, u32[]{:S(2)}) collective-permute-start(bf16[256,2048]{1,0:T(8,128)(2,1)} %permute_features.3.refs_4_.cot_ref), channel_id=1, source_target_pairs={{0,2},{1,3},{2,0},{3,1},{4,6},{5,7},{6,4},{7,5},{8,10},{9,11},{10,... | collective-permute-start | bytes 3145736 | tf_op jit(solution)/shard_map/ppermute | solution.py:234
  66.1 43.8 %collective-permute-start.12 = (bf16[256,1920]{1,0:T(8,128)(2,1)}, bf16[256,1920]{1,0:T(8,128)(2,1)S(1)}, u32[]{:S(2)}, u32[]{:S(2)}) collective-permute-start(bf16[256,1920]{1,0:T(8,128)(2,1)} %get-tuple-element.315.refs_8_), channel_id=1, source_target_pairs={{0,8},{8,16},{16,24},{24,28},{28,20},{20,12},{12,4},{4,0},{1,9},{9... | collective-permute-start | bytes 2949128 | tf_op jit(solution)/shard_map/ppermute | solution.py:100
  67.6 43.6 %collective-permute-start.13 = (bf16[256,1920]{1,0:T(8,128)(2,1)}, bf16[256,1920]{1,0:T(8,128)(2,1)S(1)}, u32[]{:S(2)}, u32[]{:S(2)}) collective-permute-start(bf16[256,1920]{1,0:T(8,128)(2,1)} %get-tuple-element.315.refs_8_), channel_id=1, source_target_pairs={{8,0},{16,8},{24,16},{28,24},{20,28},{12,20},{4,12},{0,4},{9,1},{1... | collective-permute-start | bytes 2949128 | tf_op jit(solution)/shard_map/ppermute | solution.py:103
  111.2 30.1 %collective-permute-start.18 = (bf16[256,2304]{1,0:T(8,128)(2,1)S(1)}, bf16[256,2304]{1,0:T(8,128)(2,1)S(1)}, u32[]{:S(2)}, u32[]{:S(2)}) collective-permute-start(bf16[256,2304]{1,0:T(8,128)(2,1)S(1)} %collective-permute-done.14.refs_12_), channel_id=1, source_target_pairs={{8,0},{16,8},{24,16},{28,24},{20,28},{12,20},{4,12},{0,4},{9,1},{1... | collective-permute-start | bytes 3538952 | tf_op jit(solution)/shard_map/ppermute | solution.py:103
  111.7 28.0 %collective-permute-start.19 = (bf16[256,2304]{1,0:T(8,128)(2,1)S(1)}, bf16[256,2304]{1,0:T(8,128)(2,1)S(1)}, u32[]{:S(2)}, u32[]{:S(2)}) collective-permute-start(bf16[256,2304]{1,0:T(8,128)(2,1)S(1)} %collective-permute-done.15.refs_9_), channel_id=1, source_target_pairs={{0,8},{8,16},{16,24},{24,28},{28,20},{20,12},{12,4},{4,0},{1,9},{9... | collective-permute-start | bytes 3538952 | tf_op jit(solution)/shard_map/ppermute | solution.py:100
  115.7 26.0 %collective-permute-start.17 = (bf16[256,2048]{1,0:T(8,128)(2,1)S(1)}, bf16[256,2048]{1,0:T(8,128)(2,1)S(1)}, u32[]{:S(2)}, u32[]{:S(2)}) collective-permute-start(bf16[256,2048]{1,0:T(8,128)(2,1)S(1)} %add_convert_fusion.8), channel_id=1, source_target_pairs={{0,2},{1,3},{2,0},{3,1},{4,6},{5,7},{6,4},{7,5},{8,10},{9,11},{10,... | collective-permute-start | bytes 3145736 | tf_op jit(solution)/shard_map/ppermute | solution.py:234
  139.8 27.2 %collective-permute-start.22 = (bf16[256,2304]{1,0:T(8,128)(2,1)S(1)}, bf16[256,2304]{1,0:T(8,128)(2,1)S(1)}, u32[]{:S(2)}, u32[]{:S(2)}) collective-permute-start(bf16[256,2304]{1,0:T(8,128)(2,1)S(1)} %collective-permute-done.19.refs_10_), channel_id=1, source_target_pairs={{0,8},{8,16},{16,24},{24,28},{28,20},{20,12},{12,4},{4,0},{1,9},{9... | collective-permute-start | bytes 3538952 | tf_op jit(solution)/shard_map/ppermute | solution.py:100
  141.3 26.9 %collective-permute-start.21 = (bf16[256,2304]{1,0:T(8,128)(2,1)S(1)}, bf16[256,2304]{1,0:T(8,128)(2,1)S(1)}, u32[]{:S(2)}, u32[]{:S(2)}) collective-permute-start(bf16[256,2304]{1,0:T(8,128)(2,1)S(1)} %collective-permute-done.18.refs_13_), channel_id=1, source_target_pairs={{8,0},{16,8},{24,16},{28,24},{20,28},{12,20},{4,12},{0,4},{9,1},{1... | collective-permute-start | bytes 3538952 | tf_op jit(solution)/shard_map/ppermute | solution.py:103
  143.0 27.3 %collective-permute-start.20 = (bf16[256,2048]{1,0:T(8,128)(2,1)S(1)}, bf16[256,2048]{1,0:T(8,128)(2,1)S(1)}, u32[]{:S(2)}, u32[]{:S(2)}) collective-permute-start(bf16[256,2048]{1,0:T(8,128)(2,1)S(1)} %get-tuple-element.289.refs_0_), channel_id=1, source_target_pairs={{0,2},{1,3},{2,0},{3,1},{4,6},{5,7},{6,4},{7,5},{8,10},{9,11},{10,... | collective-permute-start | bytes 3145736 | tf_op jit(solution)/shard_map/ppermute | solution.py:234
  183.0 27.5 %collective-permute-start.29 = (bf16[256,1920]{1,0:T(8,128)(2,1)S(1)}, bf16[256,1920]{1,0:T(8,128)(2,1)S(1)}, u32[]{:S(2)}, u32[]{:S(2)}) collective-permute-start(bf16[256,1920]{1,0:T(8,128)(2,1)S(1)} %collective-permute-done.12.refs_9_), channel_id=1, source_target_pairs={{0,8},{8,16},{16,24},{24,28},{28,20},{20,12},{12,4},{4,0},{1,9},{9... | collective-permute-start | bytes 2949128 | tf_op jit(solution)/shard_map/ppermute | solution.py:100
  184.5 27.6 %collective-permute-start.31 = (bf16[256,1920]{1,0:T(8,128)(2,1)S(1)}, bf16[256,1920]{1,0:T(8,128)(2,1)S(1)}, u32[]{:S(2)}, u32[]{:S(2)}) collective-permute-start(bf16[256,1920]{1,0:T(8,128)(2,1)S(1)} %collective-permute-done.13.refs_12_), channel_id=1, source_target_pairs={{8,0},{16,8},{24,16},{28,24},{20,28},{12,20},{4,12},{0,4},{9,1},{1... | collective-permute-start | bytes 2949128 | tf_op jit(solution)/shard_map/ppermute | solution.py:103
  210.6 24.7 %collective-permute-start.30 = (bf16[256,1920]{1,0:T(8,128)(2,1)S(1)}, bf16[256,1920]{1,0:T(8,128)(2,1)S(1)}, u32[]{:S(2)}, u32[]{:S(2)}) collective-permute-start(bf16[256,1920]{1,0:T(8,128)(2,1)S(1)} %collective-permute-done.29.refs_10_), channel_id=1, source_target_pairs={{0,8},{8,16},{16,24},{24,28},{28,20},{20,12},{12,4},{4,0},{1,9},{9... | collective-permute-start | bytes 2949128 | tf_op jit(solution)/shard_map/ppermute | solution.py:100
  212.1 24.7 %collective-permute-start.32 = (bf16[256,1920]{1,0:T(8,128)(2,1)S(1)}, bf16[256,1920]{1,0:T(8,128)(2,1)S(1)}, u32[]{:S(2)}, u32[]{:S(2)}) collective-permute-start(bf16[256,1920]{1,0:T(8,128)(2,1)S(1)} %collective-permute-done.31.refs_13_), channel_id=1, source_target_pairs={{8,0},{16,8},{24,16},{28,24},{20,28},{12,20},{4,12},{0,4},{9,1},{1... | collective-permute-start | bytes 2949128 | tf_op jit(solution)/shard_map/ppermute | solution.py:103
  226.4 21.5 %collective-permute-start.35 = (bf16[128,2304]{1,0:T(8,128)(2,1)S(1)}, bf16[128,2304]{1,0:T(8,128)(2,1)S(1)}, u32[]{:S(2)}, u32[]{:S(2)}) collective-permute-start(bf16[128,2304]{1,0:T(8,128)(2,1)S(1)} %get-tuple-element.306), channel_id=1, source_target_pairs={{0,8},{8,16},{16,24},{24,28},{28,20},{20,12},{12,4},{4,0},{1,9},{9... | collective-permute-start | bytes 1769480 | tf_op jit(solution)/shard_map/ppermute | solution.py:100
  227.9 21.5 %collective-permute-start.36 = (bf16[128,2304]{1,0:T(8,128)(2,1)S(1)}, bf16[128,2304]{1,0:T(8,128)(2,1)S(1)}, u32[]{:S(2)}, u32[]{:S(2)}) collective-permute-start(bf16[128,2304]{1,0:T(8,128)(2,1)S(1)} %get-tuple-element.307), channel_id=1, source_target_pairs={{8,0},{16,8},{24,16},{28,24},{20,28},{12,20},{4,12},{0,4},{9,1},{1... | collective-permute-start | bytes 1769480 | tf_op jit(solution)/shard_map/ppermute | solution.py:103
  236.8 17.0 %collective-permute-start.33 = (bf16[128,1920]{1,0:T(8,128)(2,1)S(1)}, bf16[128,1920]{1,0:T(8,128)(2,1)S(1)}, u32[]{:S(2)}, u32[]{:S(2)}) collective-permute-start(bf16[128,1920]{1,0:T(8,128)(2,1)S(1)} %slice.134), channel_id=1, source_target_pairs={{0,8},{8,16},{16,24},{24,28},{28,20},{20,12},{12,4},{4,0},{1,9},{9... | collective-permute-start | bytes 1474568 | tf_op jit(solution)/shard_map/ppermute | solution.py:100
  237.7 17.3 %collective-permute-start.34 = (bf16[128,1920]{1,0:T(8,128)(2,1)S(1)}, bf16[128,1920]{1,0:T(8,128)(2,1)S(1)}, u32[]{:S(2)}, u32[]{:S(2)}) collective-permute-start(bf16[128,1920]{1,0:T(8,128)(2,1)S(1)} %slice.135), channel_id=1, source_target_pairs={{8,0},{16,8},{24,16},{28,24},{20,28},{12,20},{4,12},{0,4},{9,1},{1... | collective-permute-start | bytes 1474568 | tf_op jit(solution)/shard_map/ppermute | solution.py:103
  255.9 30.2 %collective-permute-start.38 = (bf16[256,2304]{1,0:T(8,128)(2,1)}, bf16[256,2304]{1,0:T(8,128)(2,1)}, u32[]{:S(2)}, u32[]{:S(2)}) collective-permute-start(bf16[256,2304]{1,0:T(8,128)(2,1)} %get-tuple-element.314), channel_id=1, source_target_pairs={{0,8},{8,16},{16,24},{24,28},{28,20},{20,12},{12,4},{4,0},{1,9},{9... | collective-permute-start | bytes 3538952 | tf_op jit(solution)/shard_map/ppermute | solution.py:100
  257.0 30.8 %collective-permute-start.37 = (bf16[256,2304]{1,0:T(8,128)(2,1)}, bf16[256,2304]{1,0:T(8,128)(2,1)}, u32[]{:S(2)}, u32[]{:S(2)}) collective-permute-start(bf16[256,2304]{1,0:T(8,128)(2,1)} %get-tuple-element.331), channel_id=1, source_target_pairs={{8,0},{16,8},{24,16},{28,24},{20,28},{12,20},{4,12},{0,4},{9,1},{1... | collective-permute-start | bytes 3538952 | tf_op jit(solution)/shard_map/ppermute | solution.py:103
  289.5 19.5 %collective-permute-start.39 = (bf16[512,2048]{1,0:T(8,128)(2,1)}, bf16[512,2048]{1,0:T(8,128)(2,1)S(1)}, u32[]{:S(2)}, u32[]{:S(2)}) collective-permute-start(bf16[512,2048]{1,0:T(8,128)(2,1)} %get-tuple-element.337), channel_id=1, source_target_pairs={{0,1},{1,0},{2,3},{3,2},{4,5},{5,4},{6,7},{7,6},{8,9},{9,8},{10,11... | collective-permute-start | bytes 6291464 | tf_op jit(solution)/shard_map/ppermute | solution.py:234
  290.0 28.9 %collective-permute-start.44 = (bf16[256,2304]{1,0:T(8,128)(2,1)S(1)}, bf16[256,2304]{1,0:T(8,128)(2,1)}, u32[]{:S(2)}, u32[]{:S(2)}) collective-permute-start(bf16[256,2304]{1,0:T(8,128)(2,1)S(1)} %add_convert_fusion.4), channel_id=1, source_target_pairs={{0,8},{8,16},{16,24},{24,28},{28,20},{20,12},{12,4},{4,0},{1,9},{9... | collective-permute-start | bytes 3538952 | tf_op jit(solution)/shard_map/ppermute | solution.py:100
  291.2 30.5 %collective-permute-start.43 = (bf16[256,2304]{1,0:T(8,128)(2,1)S(1)}, bf16[256,2304]{1,0:T(8,128)(2,1)S(1)}, u32[]{:S(2)}, u32[]{:S(2)}) collective-permute-start(bf16[256,2304]{1,0:T(8,128)(2,1)S(1)} %add_convert_fusion.3), channel_id=1, source_target_pairs={{8,0},{16,8},{24,16},{28,24},{20,28},{12,20},{4,12},{0,4},{9,1},{1... | collective-permute-start | bytes 3538952 | tf_op jit(solution)/shard_map/ppermute | solution.py:103
  297.3 34.1 %collective-permute-start.46 = (bf16[256,2048]{1,0:T(8,128)(2,1)}, bf16[256,2048]{1,0:T(8,128)(2,1)S(1)}, u32[]{:S(2)}, u32[]{:S(2)}) collective-permute-start(bf16[256,2048]{1,0:T(8,128)(2,1)} %add_convert_fusion.7), channel_id=1, source_target_pairs={{0,2},{1,3},{2,0},{3,1},{4,6},{5,7},{6,4},{7,5},{8,10},{9,11},{10,... | collective-permute-start | bytes 3145736 | tf_op jit(solution)/shard_map/ppermute | solution.py:234
  309.1 20.3 %collective-permute-start.41 = (bf16[128,1920]{1,0:T(8,128)(2,1)S(1)}, bf16[128,1920]{1,0:T(8,128)(2,1)S(1)}, u32[]{:S(2)}, u32[]{:S(2)}) collective-permute-start(bf16[128,1920]{1,0:T(8,128)(2,1)S(1)} %get-tuple-element.345), channel_id=1, source_target_pairs={{0,8},{8,16},{16,24},{24,28},{28,20},{20,12},{12,4},{4,0},{1,9},{9... | collective-permute-start | bytes 1474568 | tf_op jit(solution)/shard_map/ppermute | solution.py:100
  310.2 20.3 %collective-permute-start.42 = (bf16[128,1920]{1,0:T(8,128)(2,1)S(1)}, bf16[128,1920]{1,0:T(8,128)(2,1)S(1)}, u32[]{:S(2)}, u32[]{:S(2)}) collective-permute-start(bf16[128,1920]{1,0:T(8,128)(2,1)S(1)} %get-tuple-element.346), channel_id=1, source_target_pairs={{8,0},{16,8},{24,16},{28,24},{20,28},{12,20},{4,12},{0,4},{9,1},{1... | collective-permute-start | bytes 1474568 | tf_op jit(solution)/shard_map/ppermute | solution.py:103
  320.5 33.3 %collective-permute-start.48 = (bf16[256,2304]{1,0:T(8,128)(2,1)S(1)}, bf16[256,2304]{1,0:T(8,128)(2,1)S(1)}, u32[]{:S(2)}, u32[]{:S(2)}) collective-permute-start(bf16[256,2304]{1,0:T(8,128)(2,1)S(1)} %add_convert_fusion.2), channel_id=1, source_target_pairs={{0,8},{8,16},{16,24},{24,28},{28,20},{20,12},{12,4},{4,0},{1,9},{9... | collective-permute-start | bytes 3538952 | tf_op jit(solution)/shard_map/ppermute | solution.py:100
  322.0 32.7 %collective-permute-start.49 = (bf16[256,2304]{1,0:T(8,128)(2,1)S(1)}, bf16[256,2304]{1,0:T(8,128)(2,1)S(1)}, u32[]{:S(2)}, u32[]{:S(2)}) collective-permute-start(bf16[256,2304]{1,0:T(8,128)(2,1)S(1)} %add_convert_fusion.1), channel_id=1, source_target_pairs={{8,0},{16,8},{24,16},{28,24},{20,28},{12,20},{4,12},{0,4},{9,1},{1... | collective-permute-start | bytes 3538952 | tf_op jit(solution)/shard_map/ppermute | solution.py:103
  333.6 25.6 %collective-permute-start.47 = (bf16[256,2048]{1,0:T(8,128)(2,1)S(1)}, bf16[256,2048]{1,0:T(8,128)(2,1)S(1)}, u32[]{:S(2)}, u32[]{:S(2)}) collective-permute-start(bf16[256,2048]{1,0:T(8,128)(2,1)S(1)} %get-tuple-element.368.refs_0_.refs_1_), channel_id=1, source_target_pairs={{0,2},{1,3},{2,0},{3,1},{4,6},{5,7},{6,4},{7,5},{8,10},{9,11},{10,... | collective-permute-start | bytes 3145736 | tf_op jit(solution)/shard_map/ppermute | solution.py:234
  359.2 26.1 %collective-permute-start.45 = (bf16[256,1920]{1,0:T(8,128)(2,1)S(1)}, bf16[256,1920]{1,0:T(8,128)(2,1)S(1)}, u32[]{:S(2)}, u32[]{:S(2)}) collective-permute-start(bf16[256,1920]{1,0:T(8,128)(2,1)S(1)} %get-tuple-element.355), channel_id=1, source_target_pairs={{0,8},{8,16},{16,24},{24,28},{28,20},{20,12},{12,4},{4,0},{1,9},{9... | collective-permute-start | bytes 2949128 | tf_op jit(solution)/shard_map/ppermute | solution.py:100
  360.1 26.4 %collective-permute-start.55 = (bf16[256,1920]{1,0:T(8,128)(2,1)S(1)}, bf16[256,1920]{1,0:T(8,128)(2,1)S(1)}, u32[]{:S(2)}, u32[]{:S(2)}) collective-permute-start(bf16[256,1920]{1,0:T(8,128)(2,1)S(1)} %get-tuple-element.377), channel_id=1, source_target_pairs={{8,0},{16,8},{24,16},{28,24},{20,28},{12,20},{4,12},{0,4},{9,1},{1... | collective-permute-start | bytes 2949128 | tf_op jit(solution)/shard_map/ppermute | solution.py:103
  361.2 27.8 %collective-permute-start.53 = (bf16[256,2304]{1,0:T(8,128)(2,1)S(1)}, bf16[256,2304]{1,0:T(8,128)(2,1)S(1)}, u32[]{:S(2)}, u32[]{:S(2)}) collective-permute-start(bf16[256,2304]{1,0:T(8,128)(2,1)S(1)} %add_convert_fusion.refs_0_), channel_id=1, source_target_pairs={{0,2},{1,3},{2,0},{3,1},{4,6},{5,7},{6,4},{7,5},{8,10},{9,11},{10,... | collective-permute-start | bytes 3538952 | tf_op jit(solution)/shard_map/ppermute | solution.py:234
  362.7 26.3 %collective-permute-start.54 = (bf16[256,2304]{1,0:T(8,128)(2,1)S(1)}, bf16[256,2304]{1,0:T(8,128)(2,1)S(1)}, u32[]{:S(2)}, u32[]{:S(2)}) collective-permute-start(bf16[256,2304]{1,0:T(8,128)(2,1)S(1)} %add_convert_fusion.refs_0_), channel_id=1, source_target_pairs={{0,1},{1,0},{2,3},{3,2},{4,5},{5,4},{6,7},{7,6},{8,9},{9,8},{10,11... | collective-permute-start | bytes 3538952 | tf_op jit(solution)/shard_map/ppermute | solution.py:234
  385.5 24.2 %collective-permute-start.52 = (bf16[256,1920]{1,0:T(8,128)(2,1)S(1)}, bf16[256,1920]{1,0:T(8,128)(2,1)S(1)}, u32[]{:S(2)}, u32[]{:S(2)}) collective-permute-start(bf16[256,1920]{1,0:T(8,128)(2,1)S(1)} %add_convert_fusion.13), channel_id=1, source_target_pairs={{0,8},{8,16},{16,24},{24,28},{28,20},{20,12},{12,4},{4,0},{1,9},{9... | collective-permute-start | bytes 2949128 | tf_op jit(solution)/shard_map/ppermute | solution.py:100
  386.7 24.2 %collective-permute-start.57 = (bf16[256,1920]{1,0:T(8,128)(2,1)S(1)}, bf16[256,1920]{1,0:T(8,128)(2,1)S(1)}, u32[]{:S(2)}, u32[]{:S(2)}) collective-permute-start(bf16[256,1920]{1,0:T(8,128)(2,1)S(1)} %add_convert_fusion.12), channel_id=1, source_target_pairs={{8,0},{16,8},{24,16},{28,24},{20,28},{12,20},{4,12},{0,4},{9,1},{1... | collective-permute-start | bytes 2949128 | tf_op jit(solution)/shard_map/ppermute | solution.py:103
  389.0 29.5 %collective-permute-start.59 = (bf16[256,2048]{1,0:T(8,128)(2,1)}, bf16[256,2048]{1,0:T(8,128)(2,1)S(1)}, u32[]{:S(2)}, u32[]{:S(2)}) collective-permute-start(bf16[256,2048]{1,0:T(8,128)(2,1)} %add_convert_fusion.6), channel_id=1, source_target_pairs={{0,2},{1,3},{2,0},{3,1},{4,6},{5,7},{6,4},{7,5},{8,10},{9,11},{10,... | collective-permute-start | bytes 3145736 | tf_op jit(solution)/shard_map/ppermute | solution.py:234
  390.6 20.6 %collective-permute-start.62 = (bf16[256,2304]{1,0:T(8,128)(2,1)S(1)}, bf16[256,2304]{1,0:T(8,128)(2,1)S(1)}, u32[]{:S(2)}, u32[]{:S(2)}) collective-permute-start(bf16[256,2304]{1,0:T(8,128)(2,1)S(1)} %collective-permute-done.53.refs_1_), channel_id=1, source_target_pairs={{0,1},{1,0},{2,3},{3,2},{4,5},{5,4},{6,7},{7,6},{8,9},{9,8},{10,11... | collective-permute-start | bytes 3538952 | tf_op jit(solution)/shard_map/ppermute | solution.py:234
  418.6 24.6 %collective-permute-start.56 = (bf16[256,1920]{1,0:T(8,128)(2,1)S(1)}, bf16[256,1920]{1,0:T(8,128)(2,1)S(1)}, u32[]{:S(2)}, u32[]{:S(2)}) collective-permute-start(bf16[256,1920]{1,0:T(8,128)(2,1)S(1)} %add_convert_fusion.11), channel_id=1, source_target_pairs={{0,8},{8,16},{16,24},{24,28},{28,20},{20,12},{12,4},{4,0},{1,9},{9... | collective-permute-start | bytes 2949128 | tf_op jit(solution)/shard_map/ppermute | solution.py:100
  419.6 24.6 %collective-permute-start.58 = (bf16[256,1920]{1,0:T(8,128)(2,1)S(1)}, bf16[256,1920]{1,0:T(8,128)(2,1)S(1)}, u32[]{:S(2)}, u32[]{:S(2)}) collective-permute-start(bf16[256,1920]{1,0:T(8,128)(2,1)S(1)} %add_convert_fusion.10), channel_id=1, source_target_pairs={{8,0},{16,8},{24,16},{28,24},{20,28},{12,20},{4,12},{0,4},{9,1},{1... | collective-permute-start | bytes 2949128 | tf_op jit(solution)/shard_map/ppermute | solution.py:103
  420.7 35.1 %collective-permute-start.66 = (bf16[264,1152]{1,0:T(8,128)(2,1)S(1)}, bf16[264,1152]{1,0:T(8,128)(2,1)S(1)}, u32[]{:S(2)}, u32[]{:S(2)}) collective-permute-start(bf16[264,1152]{1,0:T(8,128)(2,1)S(1)} %get-tuple-element.406), channel_id=1, source_target_pairs={{0,8},{8,16},{16,24},{24,28},{28,20},{20,12},{12,4},{4,0},{1,9},{9... | collective-permute-start | bytes 1824776 | tf_op jit(solution)/shard_map/ppermute | solution.py:100
  421.8 34.6 %collective-permute-start.67 = (bf16[264,1152]{1,0:T(8,128)(2,1)S(1)}, bf16[264,1152]{1,0:T(8,128)(2,1)S(1)}, u32[]{:S(2)}, u32[]{:S(2)}) collective-permute-start(bf16[264,1152]{1,0:T(8,128)(2,1)S(1)} %get-tuple-element.416), channel_id=1, source_target_pairs={{8,0},{16,8},{24,16},{28,24},{20,28},{12,20},{4,12},{0,4},{9,1},{1... | collective-permute-start | bytes 1824776 | tf_op jit(solution)/shard_map/ppermute | solution.py:103
  423.4 36.3 %collective-permute-start.64 = (bf16[256,2048]{1,0:T(8,128)(2,1)S(1)}, bf16[256,2048]{1,0:T(8,128)(2,1)S(1)}, u32[]{:S(2)}, u32[]{:S(2)}) collective-permute-start(bf16[256,2048]{1,0:T(8,128)(2,1)S(1)} %add_convert_fusion.5), channel_id=1, source_target_pairs={{0,2},{1,3},{2,0},{3,1},{4,6},{5,7},{6,4},{7,5},{8,10},{9,11},{10,... | collective-permute-start | bytes 3145736 | tf_op jit(solution)/shard_map/ppermute | solution.py:234
  444.6 36.3 %collective-permute-start.76 = (bf16[256,1920]{1,0:T(8,128)(2,1)S(1)}, bf16[256,1920]{1,0:T(8,128)(2,1)S(1)}, u32[]{:S(2)}, u32[]{:S(2)}) collective-permute-start(bf16[256,1920]{1,0:T(8,128)(2,1)S(1)} %add_convert_fusion.9.refs_4_), channel_id=1, source_target_pairs={{0,2},{1,3},{2,0},{3,1},{4,6},{5,7},{6,4},{7,5},{8,10},{9,11},{10,... | collective-permute-start | bytes 2949128 | tf_op jit(solution)/shard_map/ppermute | solution.py:234
  (90 other events, 1838.5 us)
